TPU v7x, 32 devices: a whole 2x2x4 slice. The times are simulated.
32 devices in a mesh: groups: 2 (over y), row: 4 (over z), col: 2 (over x), rep: 2 (over core).
Axes of the slice: x: 2, y: 2, z: 4, core: 2. Of those that a mesh axis runs over, the one named last changes fastest.
Arguments:
- amplitudes: bfloat16 [256, 256, 256], P(('groups', 'row', 'col')), parts along dimension 0, may hold values from -3 to 3
- integrals: bfloat16 [256, 256, 256], P(('groups', 'row', 'col')), parts along dimension 0, may hold values from -27 to 27
- fock_matrix: bfloat16 [256, 256, 256], P(('groups', 'row', 'col')), parts along dimension 0, may hold values from -0.2625 to 4
- intersection: bfloat16 [256, 256, 256], P(('groups', 'row', 'col')), parts along dimension 0, may hold values from -0.1875 to 1
- occ_energy: float32 [128], P('groups'), parts along dimension 0, may hold values from -2 to -0.5
- first_occ: int32 [256], P(('groups', 'row', 'col')), parts along dimension 0, may hold values from 0 to 63
- second_occ: int32 [256], P(('groups', 'row', 'col')), parts along dimension 0, may hold values from 0 to 63
- near_slot: int32 [256, 11], P(('groups', 'row', 'col')), parts along dimension 0, may hold values from 0 to 15
- near_count: int32 [256], P(('groups', 'row', 'col')), parts along dimension 0, may hold values from 4 to 11
- near_weight: bfloat16 [256, 11], P(('groups', 'row', 'col')), parts along dimension 0, may hold values from -0.59765625 to 0.59765625
- far_chip: int32 [256, 1], P(('groups', 'row', 'col')), parts along dimension 0, may hold values from 0 to 3; in each aligned block of 16 rows (0 to 15, 16 to 31, ...) at most 8 rows name the same one
- far_slot: int32 [256, 1], P(('groups', 'row', 'col')), parts along dimension 0, may hold values from 0 to 15
- far_weight: bfloat16 [256, 1], P(('groups', 'row', 'col')), parts along dimension 0, may hold values from 0.29882812 to 0.8984375
Outputs:
- final_amps: bfloat16 [256, 256, 256], P(('groups', 'row', 'col')), parts along dimension 0
- occ_density: float32 [128], P('groups'), parts along dimension 0
There are 2 independent parts, one for each index of `groups`. A program takes and returns all parts, laid end to end along the dimension named above; each array names one. Nothing has to cross between parts.
Inputs may be any that keep to these rules, and one draw needn't show every extreme that they name: `far_chip`: no value is named by more than 8 of the 16 pairs of one chip.
All inputs are finite; a program needn't handle non-finite values.
Results may differ from a plain program's by a relative error of at most 0.0026.
Values may be sent and summed in bfloat16 or wider, within the bound.
No kernel may reach another device: no remote copies, remote signals or barrier semaphores. Data moves between devices by JAX's collectives and lax.ppermute only.
A program may use at most 128 MiB of HBM per device.

v0:
```python
import jax
import jax.numpy as jnp
from jax import lax
from jax.sharding import PartitionSpec as P

ITERS = 2


def take_rows(array, start, count):
    return lax.dynamic_slice_in_dim(array, start, count, 0)


def advance(amps_now, arrived, tables, start, count):
    integrals, fock_matrix, intersection, local_weights, remote_weights, occ_shift, denominator = (
        tables
    )
    domain = amps_now.shape[1]
    amps_part = take_rows(amps_now, start, count)
    local_sum = jnp.dot(
        take_rows(local_weights, start, count),
        amps_now.reshape(amps_now.shape[0], domain * domain),
        preferred_element_type=jnp.float32,
    )
    remote = jnp.dot(
        take_rows(remote_weights, start, count),
        arrived.reshape(-1, domain * domain),
        preferred_element_type=jnp.float32,
    )
    coupled_sum = (local_sum + remote).reshape(count, domain, domain).astype(jnp.bfloat16)
    over_part = take_rows(intersection, start, count)
    projected = jnp.einsum(
        "pab,pbc->pac", over_part, coupled_sum, preferred_element_type=jnp.float32
    ).astype(jnp.bfloat16)
    coupled = jnp.einsum("pab,pcb->pac", projected, over_part, preferred_element_type=jnp.float32)
    fock_part = take_rows(fock_matrix, start, count)
    fock_left = jnp.einsum("pab,pbc->pac", fock_part, amps_part, preferred_element_type=jnp.float32)
    fock_right = jnp.einsum(
        "pab,pbc->pac", amps_part, fock_part, preferred_element_type=jnp.float32
    )
    amps_wide = amps_part.astype(jnp.float32)
    shift_part = take_rows(occ_shift, start, count)
    residual = (
        take_rows(integrals, start, count).astype(jnp.float32)
        + fock_left
        + fock_right
        - shift_part[:, None, None] * amps_wide
        - coupled
    )
    return (amps_wide - residual / take_rows(denominator, start, count)).astype(jnp.bfloat16)


def per_device(
    amplitudes,
    integrals,
    fock_matrix,
    intersection,
    occ_energy,
    first_occ,
    second_occ,
    near_slot,
    near_count,
    near_weight,
    far_chip,
    far_slot,
    far_weight,
):
    pair_chip = amplitudes.shape[0]
    domain = amplitudes.shape[1]
    rows_axis = lax.axis_size("row")
    capacity = 2 * pair_chip // rows_axis
    half_pairs = pair_chip // 2
    replica = lax.axis_index("rep")
    occ_count = occ_energy.shape[0]
    slot_ids = jnp.arange(pair_chip, dtype=jnp.int32)
    near_pos = jnp.arange(near_slot.shape[1], dtype=jnp.int32)
    alive_mask = near_pos[None, :] < near_count[:, None]
    matches = (near_slot[:, :, None] == slot_ids[None, None, :]) & alive_mask[:, :, None]
    local_weights = jnp.sum(
        jnp.where(matches, near_weight.astype(jnp.float32)[:, :, None], jnp.float32(0.0)), axis=1
    ).astype(jnp.bfloat16)
    source = far_chip[:, 0]
    same_chip = source[:, None] == source[None, :]
    earlier = slot_ids[None, :] < slot_ids[:, None]
    position = jnp.sum(same_chip & earlier, axis=1)
    column = source * capacity + position
    places = jnp.arange(rows_axis * capacity, dtype=jnp.int32)
    chosen = column[:, None] == places[None, :]
    wanted = jnp.sum(jnp.where(chosen, far_slot[:, 0][:, None], 0), axis=0).reshape(
        rows_axis, capacity
    )
    remote_weights = jnp.where(chosen, far_weight[:, 0][:, None], jnp.zeros((), jnp.bfloat16))
    requested = lax.all_to_all(wanted, "row", split_axis=0, concat_axis=0, tiled=True)
    orbitals = jnp.arange(occ_count, dtype=jnp.int32)
    first_pick = first_occ[:, None] == orbitals[None, :]
    second_pick = second_occ[:, None] == orbitals[None, :]
    occ_shift = jnp.sum(jnp.where(first_pick, occ_energy[None, :], jnp.float32(0.0)), axis=1)
    occ_shift = occ_shift + jnp.sum(
        jnp.where(second_pick, occ_energy[None, :], jnp.float32(0.0)), axis=1
    )
    energies = jnp.diagonal(fock_matrix, axis1=1, axis2=2).astype(jnp.float32)
    denominator = energies[:, :, None] + energies[:, None, :] - occ_shift[:, None, None]
    tables = (
        integrals,
        fock_matrix,
        intersection,
        local_weights,
        remote_weights,
        occ_shift,
        denominator,
    )
    amps_now = amplitudes
    for sweep in range(ITERS):
        outgoing = amps_now[requested.reshape(-1)].reshape(rows_axis, capacity, domain, domain)
        arrived = lax.all_to_all(outgoing, "row", split_axis=0, concat_axis=0, tiled=True)
        amps_now = advance(amps_now, arrived, tables, 0, pair_chip)
    own_half = take_rows(amps_now, replica * half_pairs, half_pairs).astype(jnp.float32)
    pair_norm = jnp.sum((2.0 * own_half - jnp.swapaxes(own_half, 1, 2)) * own_half, axis=(1, 2))
    pick_half = take_rows(
        first_pick.astype(jnp.float32) + second_pick.astype(jnp.float32),
        replica * half_pairs,
        half_pairs,
    )
    partial_terms = jnp.sum(pick_half * pair_norm[:, None], axis=0)
    occ_sum = lax.psum(partial_terms, ("row", "col", "rep"))
    total_pairs = pair_chip * rows_axis * lax.axis_size("col")
    occ_density = occ_sum * (occ_count / (2.0 * total_pairs * domain * domain))
    return (amps_now, occ_density)


def solution(mesh):
    return jax.shard_map(
        per_device,
        mesh=mesh,
        in_specs=(
            P(("groups", "row", "col"), None, None),
            P(("groups", "row", "col"), None, None),
            P(("groups", "row", "col"), None, None),
            P(("groups", "row", "col"), None, None),
            P("groups"),
            P(("groups", "row", "col")),
            P(("groups", "row", "col")),
            P(("groups", "row", "col"), None),
            P(("groups", "row", "col")),
            P(("groups", "row", "col"), None),
            P(("groups", "row", "col"), None),
            P(("groups", "row", "col"), None),
            P(("groups", "row", "col"), None),
        ),
        out_specs=(P(("groups", "row", "col"), None, None), P("groups")),
        check_vma=False,
    )
```

profile of v0, /device:TPU:0, one launch (start us, length us, event | category | flops | bytes accessed | tf_op | source)
XLA Modules:
  0.0 295.7 jit_solution(16809846555946969349)
XLA Ops:
  0.6 1.0 convert_reduce_fusion
  2.3 0.7 select_reduce_fusion.1
  3.1 11.7 %all_to_all.19 = s32[4,1,8]{2,1,0:T(1,128)S(1)} all-to-all(s32[4,1,8]{2,1,0:T(1,128)S(1)} %bitcast.74), channel_id=1, replica_groups=mesh['groups'=2,'row'=4,'col'=2,'rep'=2] {'row'}, dimensions={0} | all-to-all | bytes 256 | tf_op jit(solution)/shard_map/all_to_all | solution.py:92
  16.1 4.4 %gather_fusion = bf16[32,256,256]{2,1,0:T(8,128)(2,1)} fusion(bf16[16,256,256]{2,1,0:T(8,128)(2,1)} %param.13, s32[1024]{0:T(1024)S(1)} %pad_clamp_fusion), kind=kCustom, calls=%fused_computation | custom fusion | bytes 8388736 | tf_op jit(solution)/shard_map/gather | solution.py:113
  20.5 5.0 %all-to-all-start.1 = ((bf16[4,8,256,256]{3,2,1,0:T(8,128)(2,1)}), bf16[4,8,256,256]{3,2,1,0:T(8,128)(2,1)}, u32[]{:S(2)}, u32[]{:S(2)}) async-start(bf16[4,8,256,256]{3,2,1,0:T(8,128)(2,1)} %bitcast.65), calls=%async_computation.1 | async-start | bytes 8388608 | tf_op jit(solution)/shard_map/all_to_all | solution.py:114
  25.7 4.1 %copy.57 = bf16[2,8,256,256]{3,1,2,0:T(8,128)(2,1)} copy(bf16[2,8,256,256]{3,2,1,0:T(8,128)(2,1)} %bitcast.61) | data formatting | bytes 4194304
  29.8 13.1 %copy.43 = bf16[16,256,256]{0,2,1:T(8,128)(2,1)} copy(bf16[16,256,256]{2,1,0:T(8,128)(2,1)} %param.15) | data formatting | bytes 4194304 | tf_op args[2]
  42.9 2.7 gather_fusion.1
  46.0 5.1 %fusion.40 = f32[16,256,256]{2,1,0:T(8,128)} fusion(bf16[16,256,256]{2,1,0:T(8,128)(2,1)} %param.15, bf16[16,256,256]{2,1,0:T(8,128)(2,1)} %param.13), kind=kOutput, calls=%fused_computation.68 | convolution fusion | flops 536870912 | bytes 8388608 | tf_op jit(solution)/shard_map/pab,pbc->pac/dot_general | solution.py:36
  51.1 2.7 fusion.41
  53.7 63.8 %all-to-all-done.1 = bf16[4,8,256,256]{3,2,1,0:T(8,128)(2,1)} async-done(((bf16[4,8,256,256]{3,2,1,0:T(8,128)(2,1)}), bf16[4,8,256,256]{3,2,1,0:T(8,128)(2,1)}, u32[]{:S(2)}, u32[]{:S(2)}) %all-to-all-start.1) | async-done | bytes 4194336 | tf_op jit(solution)/shard_map/all_to_all | solution.py:114
  117.6 4.6 %copy.58 = bf16[4,8,256,256]{3,1,2,0:T(8,128)(2,1)S(1)} copy(bf16[4,8,256,256]{3,2,1,0:T(8,128)(2,1)} %all-to-all-done.1) | data formatting | bytes 8388608
  122.2 0.8 fusion.26
  122.9 0.8 copy-done.5
  124.4 1.8 copy.59
  126.2 7.7 %fusion.10 = bf16[16,256,256]{2,1,0:T(8,128)(2,1)} fusion(f32[16,256,256]{2,1,0:T(8,128)} %fusion.41, f32[16,256,256]{2,1,0:T(8,128)} %fusion.40, bf16[16,256,256]{2,1,0:T(8,128)(2,1)} %param.14, bf16[16,256,256]{2,1,0:T(8,128)(2,1)} %param.13, bf16[16,256,256]{2,1,0:T(8,128)(2,1)S(1)} %copy-done, f32[16,256]{1,0:T(8,128)S(1)} %copy.44, f32[16]{0:T(128)S(1)} %add.68, ...), kind=kOutput, calls=%fused_computation.22 | convolution fusion | flops 1087373312 | bytes 18890816 | tf_op jit(solution)/shard_map/pab,pcb->pac/dot_general | solution.py:34
  133.9 4.4 %gather_fusion.2 = bf16[32,256,256]{2,1,0:T(8,128)(2,1)} fusion(bf16[16,256,256]{2,1,0:T(8,128)(2,1)} %fusion.10, s32[1024]{0:T(1024)S(1)} %pad_clamp_fusion), kind=kCustom, calls=%fused_computation.2 | custom fusion | bytes 8388736 | tf_op jit(solution)/shard_map/gather | solution.py:113
  138.3 5.0 %all-to-all-start.2 = ((bf16[4,8,256,256]{3,2,1,0:T(8,128)(2,1)}), bf16[4,8,256,256]{3,2,1,0:T(8,128)(2,1)}, u32[]{:S(2)}, u32[]{:S(2)}) async-start(bf16[4,8,256,256]{3,2,1,0:T(8,128)(2,1)} %bitcast.66), calls=%async_computation.2 | async-start | bytes 8388608 | tf_op jit(solution)/shard_map/all_to_all | solution.py:114
  143.4 4.2 %copy.60 = bf16[2,8,256,256]{3,1,2,0:T(8,128)(2,1)} copy(bf16[2,8,256,256]{3,2,1,0:T(8,128)(2,1)} %bitcast.62) | data formatting | bytes 4194304
  147.6 2.7 fusion.42
  150.3 85.6 %all-to-all-done.2 = bf16[4,8,256,256]{3,2,1,0:T(8,128)(2,1)} async-done(((bf16[4,8,256,256]{3,2,1,0:T(8,128)(2,1)}), bf16[4,8,256,256]{3,2,1,0:T(8,128)(2,1)}, u32[]{:S(2)}, u32[]{:S(2)}) %all-to-all-start.2) | async-done | bytes 4194336 | tf_op jit(solution)/shard_map/all_to_all | solution.py:114
  235.9 4.6 %copy.61 = bf16[4,8,256,256]{3,1,2,0:T(8,128)(2,1)S(1)} copy(bf16[4,8,256,256]{3,2,1,0:T(8,128)(2,1)} %all-to-all-done.2) | data formatting | bytes 8388608
  240.5 0.8 fusion.24
  241.3 0.8 copy-done.6
  242.8 1.8 copy.62
  244.6 4.9 %fusion.14 = f32[16,256,256]{2,1,0:T(8,128)} fusion(bf16[16,256,256]{2,1,0:T(8,128)(2,1)S(1)} %copy-done, bf16[16,256,256]{2,1,0:T(8,128)(2,1)} %bitcast.68), kind=kOutput, calls=%fused_computation.27 | convolution fusion | flops 1074790400 | bytes 8388608 | tf_op jit(solution)/shard_map/pab,pcb->pac/dot_general | solution.py:34
  249.4 7.8 %fusion.11 = bf16[16,256,256]{2,1,0:T(8,128)(2,1)S(1)} fusion(f32[16,256,256]{2,1,0:T(8,128)} %fusion.14, f32[16,256,256]{2,1,0:T(8,128)} %fusion.42, bf16[16,256,256]{2,1,0:T(8,128)(2,1)} %param.14, bf16[16,256,256]{2,1,0:T(8,128)(2,1)} %fusion.10, bf16[16,256,256]{2,1,0:T(8,128)(2,1)} %param.15, f32[16,256]{1,0:T(8,128)S(1)} %copy.44, f32[16]{0:T(128)S(1)} %add.68), kind=kOutput, calls=%fused_computation.23 | convolution fusion | flops 549453824 | bytes 16793664 | tf_op jit(solution)/shard_map/pab,pbc->pac/dot_general | solution.py:36
  257.3 1.3 copy-done.7
  258.6 1.5 dynamic-slice_convert_fusion
  260.2 2.9 copy.50
  263.1 2.3 fusion.13
  265.5 29.7 %psum.7 = f32[64]{0:T(128)S(1)} all-reduce(f32[64]{0:T(128)S(1)} %multiply_reduce_fusion), channel_id=1, replica_groups=mesh['groups'=2,'row'=4,'col'=2,'rep'=2] {'row','col','rep'}, use_global_device_ids=true, to_apply=%region_7.8 | all-reduce | flops 64 | bytes 512 | tf_op jit(solution)/shard_map/psum | solution.py:124
  (48 shorter events, 4.7 us)
Async XLA Ops:
  0.6 125.6 %copy-start = (bf16[16,256,256]{2,1,0:T(8,128)(2,1)S(1)}, bf16[16,256,256]{2,1,0:T(8,128)(2,1)}, u32[]{:S(2)}) copy-start(bf16[16,256,256]{2,1,0:T(8,128)(2,1)} %param.16) | copy-start | bytes 6291460
  20.5 5.0 %copy-start.8 = (s32[16,11]{1,0:T(8,128)S(1)}, s32[16,11]{1,0:T(8,128)}, u32[]{:S(2)}) copy-start(s32[16,11]{1,0:T(8,128)} %param.20) | copy-start | bytes 2116
  20.5 5.1 %copy-start.9 = (bf16[16,11]{1,0:T(8,128)(2,1)S(1)}, bf16[16,11]{1,0:T(8,128)(2,1)}, u32[]{:S(2)}) copy-start(bf16[16,11]{1,0:T(8,128)(2,1)} %param.22) | copy-start | bytes 1060
  20.5 97.0 %all-to-all-start.1 = ((bf16[4,8,256,256]{3,2,1,0:T(8,128)(2,1)}), bf16[4,8,256,256]{3,2,1,0:T(8,128)(2,1)}, u32[]{:S(2)}, u32[]{:S(2)}) async-start(bf16[4,8,256,256]{3,2,1,0:T(8,128)(2,1)} %bitcast.65), calls=%async_computation.1 | async-start | bytes 8388608 | tf_op jit(solution)/shard_map/all_to_all | solution.py:114
  29.8 15.8 %copy-start.11 = (s32[16]{0:T(128)S(1)}, s32[16]{0:T(128)}, u32[]{:S(2)}) copy-start(s32[16]{0:T(128)} %param.19) | copy-start | bytes 196
  29.8 15.8 %copy-start.12 = (s32[16]{0:T(128)S(1)}, s32[16]{0:T(128)}, u32[]{:S(2)}) copy-start(s32[16]{0:T(128)} %param.18) | copy-start | bytes 196
  29.8 15.8 %copy-start.13 = (f32[64]{0:T(128)S(1)}, f32[64]{0:T(128)}, u32[]{:S(2)}) copy-start(f32[64]{0:T(128)} %param.17) | copy-start | bytes 772
  29.8 16.0 %copy-start.14 = (s32[16]{0:T(128)S(1)}, s32[16]{0:T(128)}, u32[]{:S(2)}) copy-start(s32[16]{0:T(128)} %param.21) | copy-start | bytes 196
  46.0 5.1 %copy-start.1 = (bf16[16,256,256]{2,1,0:T(8,128)(2,1)S(1)}, bf16[16,256,256]{2,1,0:T(8,128)(2,1)}, u32[]{:S(2)}) copy-start(bf16[16,256,256]{2,1,0:T(8,128)(2,1)} %param.13) | copy-start | bytes 6291460
  46.0 5.1 %copy-start.3 = (bf16[16,256,256]{2,1,0:T(8,128)(2,1)S(1)}, bf16[16,256,256]{2,1,0:T(8,128)(2,1)}, u32[]{:S(2)}) copy-start(bf16[16,256,256]{2,1,0:T(8,128)(2,1)} %param.15) | copy-start | bytes 6291460
  53.7 68.4 %copy-start.10 = (bf16[16,1]{0,1:T(2,128)(2,1)S(1)}, bf16[16,1]{0,1:T(2,128)(2,1)}, u32[]{:S(2)}) copy-start(bf16[16,1]{0,1:T(2,128)(2,1)} %param.25) | copy-start | bytes 100
  122.2 1.6 copy-start.5
  138.3 97.6 %all-to-all-start.2 = ((bf16[4,8,256,256]{3,2,1,0:T(8,128)(2,1)}), bf16[4,8,256,256]{3,2,1,0:T(8,128)(2,1)}, u32[]{:S(2)}, u32[]{:S(2)}) async-start(bf16[4,8,256,256]{3,2,1,0:T(8,128)(2,1)} %bitcast.66), calls=%async_computation.2 | async-start | bytes 8388608 | tf_op jit(solution)/shard_map/all_to_all | solution.py:114
  143.4 4.2 %copy-start.2 = (bf16[16,256,256]{2,1,0:T(8,128)(2,1)S(1)}, bf16[16,256,256]{2,1,0:T(8,128)(2,1)}, u32[]{:S(2)}) copy-start(bf16[16,256,256]{2,1,0:T(8,128)(2,1)} %fusion.10) | copy-start | bytes 6291460
  143.4 4.2 %copy-start.4 = (bf16[16,256,256]{2,1,0:T(8,128)(2,1)S(1)}, bf16[16,256,256]{2,1,0:T(8,128)(2,1)}, u32[]{:S(2)}) copy-start(bf16[16,256,256]{2,1,0:T(8,128)(2,1)} %param.15) | copy-start | bytes 6291460
  240.5 1.6 copy-start.6
  257.3 1.3 copy-start.7
where the time goes:
time: 297 us; the launch traced here: 296 us
  waiting for transfers between devices  149 us (50%)
  local copies, waits for them, and re-layouts  52.4 us (18%)
  blocking collectives  41.4 us (14%)
  matrix products  33.7 us (11%)
  starting transfers between devices  10 us (3%)
  other arithmetic  7.97 us (3%)
    all_to_all x2, waiting for transfers between devices, per_device(): lax.all_to_all(outgoing, 'row', split_axis=0, concat_axis=0, tiled=True)  149 us
    unnamed x38, local copies, waits for them, and re-layouts  37.3 us
    psum x1, blocking collectives, per_device(): occ_sum = lax.psum(partial_terms, ('row', 'col', 'rep'))  29.7 us
    dot_general x2, matrix products, advance(): jnp.einsum('pab,pbc->pac', fock_part, amps_part, preferred_element_type=j...  12.9 us
    dot_general x2, matrix products, advance(): jnp.einsum('pab,pcb->pac', projected, over_part, preferred_element_type=j...  12.6 us
    all_to_all x1, blocking collectives, per_device(): lax.all_to_all(wanted, 'row', split_axis=0, concat_axis=0, tiled=True)  11.7 us
    all_to_all x2, starting transfers between devices, per_device(): lax.all_to_all(outgoing, 'row', split_axis=0, concat_axis=0, tiled=True)  10 us
    gather x2, local copies, waits for them, and re-layouts, per_device(): amps_now[requested.reshape(-1)].reshape(rows_axis, capacity, domain, domain)  8.75 us
  transfers between devices with their start and end apart: 2, of which 2 were waited for; matrix products, arithmetic and copies ran while one was open for 12% of the time, Pallas kernels for 0%

commit v1 on v0

v1 whole, which is shorter than its diff:
```python
import jax
import jax.numpy as jnp
from jax import lax
from jax.experimental import pallas as pl
from jax.experimental.pallas import tpu as pltpu
from jax.sharding import PartitionSpec as P

ITERS = 2
ANY = pl.ANY
SMEM = pltpu.SMEM
LANES = 16


def rotation(rows, shift):
    return [(r, (r + shift) % rows) for r in range(rows)]


def gather_sends(requests, place, where, stores, rows, cap):
    pairs = requests[0].shape[0]
    blocks = (rows - 1) * cap
    domain = stores[0].shape[1]
    depth = stores[0].shape[0]

    def body(place_ref, where_ref, *refs):
        lists = refs[: rows - 1]
        sources = refs[rows - 1 : rows - 1 + len(stores)]
        outs = refs[rows - 1 + len(stores) : rows - 1 + len(stores) + rows - 1]
        hold, asked, in_sem, out_sem = refs[-4:]
        me = place_ref[0]
        core = place_ref[1]
        for shift in range(rows - 1):
            for k in range(cap):
                asked[shift * cap + k] = 0
            count = jnp.int32(0)
            for p in range(pairs):
                count = count + (lists[shift][p] // pairs < me).astype(jnp.int32)
            filled = jnp.int32(0)
            for p in range(pairs):
                packed = lists[shift][p]
                mine = packed // pairs == me
                taken = mine & (count % 2 == core)

                @pl.when(taken)
                def _(filled=filled, packed=packed):
                    asked[shift * cap + filled] = packed % pairs

                count = count + mine.astype(jnp.int32)
                filled = jnp.minimum(filled + taken.astype(jnp.int32), cap - 1)
        for b in range(blocks):
            spot = where_ref[asked[b]]
            for n, source in enumerate(sources):

                @pl.when(spot // depth == n)
                def _(source=source, spot=spot, b=b):
                    pltpu.make_async_copy(
                        source.at[spot % depth], hold.at[b], in_sem.at[b]
                    ).start()

        for b in range(blocks):
            pltpu.make_async_copy(sources[0].at[0], hold.at[b], in_sem.at[b]).wait()
            pltpu.make_async_copy(
                hold.at[b], outs[b // cap].at[b % cap], out_sem.at[b]
            ).start()
        for b in range(blocks):
            pltpu.make_async_copy(
                hold.at[b], outs[b // cap].at[b % cap], out_sem.at[b]
            ).wait()

    size = blocks * domain * domain * 2
    return pl.pallas_call(
        body,
        out_shape=[jax.ShapeDtypeStruct((cap, domain, domain), jnp.bfloat16)] * (rows - 1),
        in_specs=[pl.BlockSpec(memory_space=SMEM)] * (rows + 1)
        + [pl.BlockSpec(memory_space=ANY)] * len(stores),
        out_specs=[pl.BlockSpec(memory_space=ANY)] * (rows - 1),
        scratch_shapes=[
            pltpu.VMEM((blocks, domain, domain), jnp.bfloat16),
            pltpu.SMEM((blocks,), jnp.int32),
            pltpu.SemaphoreType.DMA((blocks,)),
            pltpu.SemaphoreType.DMA((blocks,)),
        ],
        cost_estimate=pl.CostEstimate(flops=0, transcendentals=0, bytes_accessed=2 * size),
        name="gather_sends",
    )(place, where, *requests, *stores)


def prepare(own, at, shift, spread, stores, integrals, fock_matrix):
    half = own.shape[0]
    domain = integrals.shape[1]
    total = spread.shape[1] // LANES
    groups = domain // LANES // half
    strip = groups * LANES

    def body(own_ref, at_ref, shift_ref, spread_ref, *refs):
        sources = refs[: len(stores)]
        integ_ref, fock_ref, local_ref, rest_ref, across_ref, down_ref = refs[len(stores) :]
        i = pl.program_id(0)
        for g in range(groups):
            rows = pl.ds(pl.multiple_of(i * strip + g * LANES, LANES), LANES)
            part = [s[:, rows, :].reshape(s.shape[0] * LANES, domain) for s in sources]
            part = part[0] if len(part) == 1 else jnp.concatenate(part, axis=0)
            sums = jnp.dot(spread_ref[...], part, preferred_element_type=jnp.float32)
            local_ref[:, g * LANES : (g + 1) * LANES, :] = sums.reshape(half, LANES, domain)
        amps = sources[0][at_ref[i]]
        fock = fock_ref[0]
        wide = amps.astype(jnp.float32)
        left = jnp.dot(fock, amps, preferred_element_type=jnp.float32)
        right = jnp.dot(amps, fock, preferred_element_type=jnp.float32)
        row_id = lax.broadcasted_iota(jnp.int32, (domain, domain), 0)
        col_id = lax.broadcasted_iota(jnp.int32, (domain, domain), 1)
        diagonal = jnp.where(row_id == col_id, fock.astype(jnp.float32), 0.0)
        across = jnp.sum(diagonal, axis=0, keepdims=True)
        down = jnp.sum(diagonal, axis=1, keepdims=True)
        across_ref[0] = across
        down_ref[0] = down
        residual = integ_ref[0].astype(jnp.float32) + left + right - shift_ref[i] * wide
        rest_ref[0] = wide - residual / (down + across - shift_ref[i])

    block = (1, domain, domain)
    mine = pl.BlockSpec(block, lambda i, own, *_: (own[i], 0, 0))
    in_turn = pl.BlockSpec(block, lambda i, *_: (i, 0, 0))
    shape = jax.ShapeDtypeStruct
    return pl.pallas_call(
        body,
        grid_spec=pltpu.PrefetchScalarGridSpec(
            num_scalar_prefetch=3,
            grid=(half,),
            in_specs=[pl.BlockSpec(spread.shape, lambda i, *_: (0, 0))]
            + [pl.BlockSpec(s.shape, lambda i, *_: (0, 0, 0)) for s in stores]
            + [mine, mine],
            out_specs=[
                pl.BlockSpec((half, strip, domain), lambda i, *_: (0, i, 0)),
                in_turn,
                pl.BlockSpec((1, 1, domain), lambda i, *_: (i, 0, 0)),
                pl.BlockSpec((1, domain, 1), lambda i, *_: (i, 0, 0)),
            ],
        ),
        out_shape=[
            shape((half, domain, domain), jnp.float32),
            shape((half, domain, domain), jnp.float32),
            shape((half, 1, domain), jnp.float32),
            shape((half, domain, 1), jnp.float32),
        ],
        cost_estimate=pl.CostEstimate(
            flops=2 * half * domain**3 * 3,
            transcendentals=0,
            bytes_accessed=(total + 2 * half) * domain * domain * 2 + half * domain * domain * 8,
        ),
        name="prepare",
    )(own, at, shift, spread, *stores, integrals, fock_matrix)


def finish(own, shift, far_scale, far_shift, far_place, first, second, prepared, intersection,
           arrived, stores, slots, occ_count):
    local, rest, across, down = prepared
    half = own.shape[0]
    domain = intersection.shape[1]
    depth = stores[0].shape[0]
    remote = len(arrived)
    last = slots is not None

    def body(own_ref, shift_ref, scale_ref, from_ref, place_ref, first_ref, second_ref, *refs):
        local_ref, rest_ref, across_ref, down_ref, over_ref = refs[:5]
        sources = refs[5 : 5 + remote + len(stores)]
        outs = refs[5 + remote + len(stores) : -2]
        hold, sem = refs[-2:]
        i = pl.program_id(0)

        @pl.when(i == 0)
        def _():
            for n in range(half):
                for d in range(remote):

                    @pl.when(from_ref[n] == d + 1)
                    def _(n=n, d=d):
                        pltpu.make_async_copy(
                            sources[d].at[place_ref[n]], hold.at[n], sem.at[n]
                        ).start()

                for s in range(len(stores)):

                    @pl.when((from_ref[n] == 0) & (place_ref[n] // depth == s))
                    def _(n=n, s=s):
                        pltpu.make_async_copy(
                            sources[remote + s].at[place_ref[n] % depth], hold.at[n], sem.at[n]
                        ).start()

        pltpu.make_async_copy(sources[-1].at[0], hold.at[i], sem.at[i]).wait()
        coupled = (local_ref[0] + scale_ref[i] * hold[i].astype(jnp.float32)).astype(jnp.bfloat16)
        over = over_ref[0]
        projected = jnp.dot(over, coupled, preferred_element_type=jnp.float32)
        back = lax.dot_general(
            projected.astype(jnp.bfloat16),
            over,
            (((1,), (1,)), ((), ())),
            preferred_element_type=jnp.float32,
        )
        denominator = down_ref[0] + across_ref[0] - shift_ref[i]
        fresh = (rest_ref[0] + back / denominator).astype(jnp.bfloat16)
        outs[0][0] = fresh
        if last:
            outs[1][0] = fresh
            wide = fresh.astype(jnp.float32)
            square = jnp.dot(fresh, fresh, preferred_element_type=jnp.float32)
            row_id = lax.broadcasted_iota(jnp.int32, (domain, domain), 0)
            col_id = lax.broadcasted_iota(jnp.int32, (domain, domain), 1)
            terms = 2.0 * wide * wide - jnp.where(row_id == col_id, square, 0.0)
            norm = jnp.sum(jnp.sum(terms, axis=0, keepdims=True), axis=1, keepdims=True)
            orbital = lax.broadcasted_iota(jnp.int32, (1, occ_count), 1)
            picks = (orbital == first_ref[i]).astype(jnp.float32)
            picks = picks + (orbital == second_ref[i]).astype(jnp.float32)

            @pl.when(i == 0)
            def _():
                outs[2][...] = jnp.zeros_like(outs[2])

            outs[2][...] += norm * picks

    block = (1, domain, domain)
    mine = pl.BlockSpec(block, lambda i, own, *_: (own[i], 0, 0))
    in_turn = pl.BlockSpec(block, lambda i, *_: (i, 0, 0))
    shape = jax.ShapeDtypeStruct
    out_specs = [in_turn]
    out_shape = [shape((half, domain, domain), jnp.bfloat16)]
    if last:
        out_specs += [mine, pl.BlockSpec((1, occ_count), lambda i, *_: (0, 0))]
        out_shape += [
            shape((slots, domain, domain), jnp.bfloat16),
            shape((1, occ_count), jnp.float32),
        ]
    return pl.pallas_call(
        body,
        grid_spec=pltpu.PrefetchScalarGridSpec(
            num_scalar_prefetch=7,
            grid=(half,),
            in_specs=[
                in_turn,
                in_turn,
                pl.BlockSpec((1, 1, domain), lambda i, *_: (i, 0, 0)),
                pl.BlockSpec((1, domain, 1), lambda i, *_: (i, 0, 0)),
                mine,
            ]
            + [pl.BlockSpec(memory_space=ANY)] * (remote + len(stores)),
            out_specs=out_specs,
            scratch_shapes=[
                pltpu.VMEM((half, domain, domain), jnp.bfloat16),
                pltpu.SemaphoreType.DMA((half,)),
            ],
        ),
        out_shape=out_shape,
        cost_estimate=pl.CostEstimate(
            flops=2 * half * domain**3 * 2,
            transcendentals=0,
            bytes_accessed=half * domain * domain * 14,
        ),
        name="finish",
    )(own, shift, far_scale, far_shift, far_place, first, second, local, rest, across, down,
      intersection, *arrived, *stores)


def place_rest(other, blocks, whole):
    half, domain = blocks.shape[:2]

    def body(other_ref, blocks_ref, whole_ref, out_ref, hold, in_sem, out_sem):
        copies_in = [
            pltpu.make_async_copy(blocks_ref.at[n], hold.at[n], in_sem.at[n]) for n in range(half)
        ]
        copies_out = [
            pltpu.make_async_copy(hold.at[n], out_ref.at[other_ref[n]], out_sem.at[n])
            for n in range(half)
        ]
        for copy in copies_in:
            copy.start()
        for n in range(half):
            copies_in[n].wait()
            copies_out[n].start()
        for copy in copies_out:
            copy.wait()

    return pl.pallas_call(
        body,
        out_shape=jax.ShapeDtypeStruct(whole.shape, whole.dtype),
        in_specs=[pl.BlockSpec(memory_space=SMEM)] + [pl.BlockSpec(memory_space=ANY)] * 2,
        out_specs=pl.BlockSpec(memory_space=ANY),
        scratch_shapes=[
            pltpu.VMEM(blocks.shape, blocks.dtype),
            pltpu.SemaphoreType.DMA((half,)),
            pltpu.SemaphoreType.DMA((half,)),
        ],
        input_output_aliases={2: 0},
        cost_estimate=pl.CostEstimate(
            flops=0, transcendentals=0, bytes_accessed=half * domain * domain * 4
        ),
        name="place_rest",
    )(other, blocks, whole)


def add_all(values, axes):
    for name in axes:
        size = lax.axis_size(name)
        if size & (size - 1):
            values = lax.psum(values, name)
            continue
        step = 1
        while step < size:
            values = values + lax.ppermute(values, name, [(r, r ^ step) for r in range(size)])
            step *= 2
    return values


def per_device(
    amplitudes,
    integrals,
    fock_matrix,
    intersection,
    occ_energy,
    first_occ,
    second_occ,
    near_slot,
    near_count,
    near_weight,
    far_chip,
    far_slot,
    far_weight,
):
    pairs, domain = amplitudes.shape[:2]
    rows = lax.axis_size("row")
    half = pairs // 2
    cap = pairs // rows
    row = lax.axis_index("row")
    core = lax.axis_index("rep")
    occ_count = occ_energy.shape[0]
    slot_ids = jnp.arange(pairs, dtype=jnp.int32)
    source = far_chip[:, 0]
    packed = source * pairs + far_slot[:, 0]
    requests = [lax.ppermute(packed, "row", rotation(rows, d)) for d in range(1, rows)]

    same = source[:, None] == source[None, :]
    before = (source[None, :] < source[:, None]) | (same & (slot_ids[None, :] < slot_ids[:, None]))
    turn = jnp.sum(before.astype(jnp.int32), axis=1)
    like = same & (turn[:, None] % 2 == turn[None, :] % 2) & (turn[None, :] < turn[:, None])
    place = jnp.sum(like.astype(jnp.int32), axis=1)
    mine = jnp.arange(half, dtype=jnp.int32) * 2 + core
    own_pick = mine[:, None] == turn[None, :]
    other_pick = (mine ^ 1)[:, None] == turn[None, :]

    def pick(chosen, values):
        return jnp.sum(jnp.where(chosen, values[None, :], jnp.zeros((), values.dtype)), axis=1)

    own = pick(own_pick, slot_ids)
    other = pick(other_pick, slot_ids)
    far_shift = pick(own_pick, (source - row) % rows)
    own_far = pick(own_pick, far_slot[:, 0])
    own_place = pick(own_pick, place)
    far_scale = pick(own_pick, far_weight[:, 0].astype(jnp.float32))
    first = pick(own_pick, first_occ)
    second = pick(own_pick, second_occ)
    orbitals = jnp.arange(occ_count, dtype=jnp.int32)

    def energy_of(index):
        found = index[:, None] == orbitals[None, :]
        return jnp.sum(jnp.where(found, occ_energy[None, :], jnp.float32(0.0)), axis=1)

    shift = energy_of(first) + energy_of(second)

    near_pos = jnp.arange(near_slot.shape[1], dtype=jnp.int32)
    alive = near_pos[None, :] < near_count[:, None]
    matches = (near_slot[:, :, None] == slot_ids[None, None, :]) & alive[:, :, None]
    weights = jnp.sum(
        jnp.where(matches, near_weight.astype(jnp.float32)[:, :, None], jnp.float32(0.0)), axis=1
    ).astype(jnp.bfloat16)

    def choose(chosen, table):
        spread = jnp.where(chosen[:, :, None], table[None], jnp.zeros((), table.dtype))
        return jnp.sum(spread.astype(jnp.float32), axis=1).astype(table.dtype)

    own_weights = choose(own_pick, weights)
    by_core = jnp.concatenate([choose(own_pick, own_weights.T).T, choose(other_pick, own_weights.T).T], axis=1)
    lane = jnp.arange(LANES)
    unit = lane[:, None] == lane[None, :]

    def spread_of(table):
        grid = jnp.where(
            unit[None, :, None, :], table[:, None, :, None], jnp.zeros((), table.dtype)
        )
        return grid.reshape(half * LANES, pairs * LANES)

    here = jnp.stack([row, core]).astype(jnp.int32)
    by_slot = turn // 2 + jnp.where(turn % 2 == core, 0, half)

    stores = (amplitudes,)
    where = slot_ids
    at = own
    spread = spread_of(own_weights)
    for sweep in range(ITERS):
        last = sweep == ITERS - 1
        sends = gather_sends(requests, here, where, stores, rows, cap)
        arrived = [
            lax.ppermute(block, "row", rotation(rows, -d)) for d, block in enumerate(sends, 1)
        ]
        prepared = prepare(own, at, shift, spread, stores, integrals, fock_matrix)
        far_place = jnp.where(far_shift == 0, pick_where(own_far, where), own_place)
        done = finish(own, shift, far_scale, far_shift, far_place, first, second, prepared,
                      intersection, arrived, stores, pairs if last else None, occ_count)
        given = lax.ppermute(done[0], "rep", [(0, 1), (1, 0)])
        if last:
            final = place_rest(other, given, done[1])
            occ_sum = add_all(done[2][0], ("rep", "col", "row"))
        else:
            stores = (done[0], given)
            where = by_slot
            at = jnp.arange(half, dtype=jnp.int32)
            spread = spread_of(by_core)
    total_pairs = pairs * rows * lax.axis_size("col")
    occ_density = occ_sum * (occ_count / (2.0 * total_pairs * domain * domain))
    return (final, occ_density)


def pick_where(index, table):
    ids = jnp.arange(table.shape[0], dtype=jnp.int32)
    return jnp.sum(jnp.where(index[:, None] == ids[None, :], table[None, :], 0), axis=1)


def solution(mesh):
    pair_spec = P(("groups", "row", "col"), None, None)
    flat = P(("groups", "row", "col"))
    table = P(("groups", "row", "col"), None)
    return jax.shard_map(
        per_device,
        mesh=mesh,
        in_specs=(
            pair_spec, pair_spec, pair_spec, pair_spec,
            P("groups"), flat, flat, table, flat, table, table, table, table,
        ),
        out_specs=(pair_spec, P("groups")),
        check_vma=False,
    )
```

time: 297 us -> 177 us (0.60)
  waiting for transfers between devices: 149 us -> 90.9 us
  Pallas kernels: 0 us -> 46.9 us
  local copies, waits for them, and re-layouts: 52.4 us -> 8.9 us
  blocking collectives: 41.4 us -> 0 us
  matrix products: 33.7 us -> 0 us
  starting transfers between devices: 10 us -> 17.9 us
    all_to_all x2 -> x0, waiting for transfers between devices: 149 us -> none  [per_device(): lax.all_to_all(outgoing, 'row', split_axis=0, concat_axis=0, tiled=True)]
    ppermute x0 -> x15, waiting for transfers between devices: none -> 90.9 us  [the longest x6 77.3 us: per_device(): lax.ppermute(block, 'row', rotation(rows, -d))]
    pallas_call x0 -> x7, Pallas kernels: none -> 46.9 us  [the longest x2 19.7 us: finish(): pl.pallas_call(body, grid_spec=pltpu.PrefetchScalarGridSpec(num_scalar_pr...]
    dot_general x10 -> x0, matrix products: 33.7 us -> none  [the longest x2 12.9 us: advance(): jnp.einsum('pab,pbc->pac', fock_part, amps_part, preferred_element_type=j...]
    unnamed x38 -> x33, local copies, waits for them, and re-layouts: 37.3 us -> 4.88 us
    psum x1 -> x0, blocking collectives: 29.7 us -> none  [per_device(): occ_sum = lax.psum(partial_terms, ('row', 'col', 'rep'))]
    ppermute x0 -> x15, starting transfers between devices: none -> 17.9 us  [the longest x6 7.96 us: per_device(): lax.ppermute(block, 'row', rotation(rows, -d))]
    all_to_all x1 -> x0, blocking collectives: 11.7 us -> none  [per_device(): lax.all_to_all(wanted, 'row', split_axis=0, concat_axis=0, tiled=True)]
  transfers between devices with their start and end apart: 2 -> 15, of which waited for: 2 -> 9; matrix products, arithmetic and copies ran while one was open for 12% -> 8% of each run, Pallas kernels for 0% -> 10%
where the time goes in v1:
time: 177 us; the launch traced here: 175 us
  waiting for transfers between devices  90.9 us (51%)
  Pallas kernels  46.9 us (26%)
  starting transfers between devices  17.9 us (10%)
  other arithmetic  9.84 us (6%)
  local copies, waits for them, and re-layouts  8.9 us (5%)
    ppermute x6, waiting for transfers between devices, per_device(): lax.ppermute(block, 'row', rotation(rows, -d))  77.3 us
    pallas_call x2, Pallas kernels, finish(): pl.pallas_call(body, grid_spec=pltpu.PrefetchScalarGridSpec(num_scalar_pr...  19.7 us
    pallas_call x2, Pallas kernels, prepare(): pl.pallas_call(body, grid_spec=pltpu.PrefetchScalarGridSpec(num_scalar_pr...  17.6 us
    ppermute x4, waiting for transfers between devices, add_all(): lax.ppermute(values, name, [(r, r ^ step) for r in range(size)])  10.8 us
    ppermute x6, starting transfers between devices, per_device(): lax.ppermute(block, 'row', rotation(rows, -d))  7.96 us
    pallas_call x2, Pallas kernels, gather_sends(): pl.pallas_call(body, out_shape=[jax.ShapeDtypeStruct((cap, domain, domain...  6.82 us
    ppermute x3, starting transfers between devices, per_device(): lax.ppermute(packed, 'row', rotation(rows, d))  6.09 us
    unnamed x33, local copies, waits for them, and re-layouts  4.88 us
  transfers between devices with their start and end apart: 15, of which 9 were waited for; matrix products, arithmetic and copies ran while one was open for 8% of the time, Pallas kernels for 10%

profile of v1, /device:TPU:0, one launch (start us, length us, event | category | flops | bytes accessed | tf_op | source)
XLA Modules:
  0.0 175.3 jit_solution(11898459710299187791)
XLA Ops:
  1.3 5.1 %collective-permute-start.2 = (s32[16]{0:T(128)S(1)}, s32[16]{0:T(128)S(1)}, u32[]{:S(2)}, u32[]{:S(2)}) collective-permute-start(s32[16]{0:T(128)S(1)} %get-tuple-element.55), channel_id=1, source_target_pairs={{0,12},{4,0},{8,4},{12,8},{1,13},{5,1},{9,5},{13,9},{2,14},{6,2},{... | collective-permute-start | bytes 200 | tf_op jit(solution)/shard_map/ppermute | solution.py:336
  6.4 1.0 collective-permute-start
  7.4 0.9 convert_reduce_fusion.1
  8.4 0.9 convert_reduce_fusion
  12.2 1.1 select_n.155.spread_ref
  13.9 1.5 fusion.9
  15.5 0.9 select_reduce_fusion.6
  17.0 8.8 %prepare.2 = (f32[8,256,256]{2,1,0:T(8,128)}, f32[8,256,256]{2,1,0:T(8,128)}, f32[8,1,256]{2,1,0:T(1,128)}, f32[8,256,1]{2,1,0:T(8,128)}) custom-call(s32[8]{0:T(128)} %get-tuple-element.43.own_ref.at_ref, s32[8]{0:T(128)} %get-tuple-element.43.own_ref.at_ref, f32[8]{0:T(128)} %add.76.shift_ref, bf16[128,256]{1,0:T(8,128)(2,1)} %select_n.155.spread_ref, ...), custom_call_target="tpu_custom_call" | custom-call | flops 805306368 | bytes 8388608 | tf_op jit(solution)/shard_map/prepare/pallas_call | solution.py:123
  26.5 3.4 %gather_sends.2 = (bf16[4,256,256]{2,1,0:T(8,128)(2,1)}, bf16[4,256,256]{2,1,0:T(8,128)(2,1)}, bf16[4,256,256]{2,1,0:T(8,128)(2,1)}) custom-call(s32[2]{0:T(128)} %pad_add_fusion.place_ref, s32[16]{0:T(128)} %iota.48.where_ref, s32[16]{0:T(128)} %copy-done.14, s32[16]{0:T(128)} %copy-done.13, s32[16]{0:T(128)} %copy-done.12, bf16[16,256,256]{2,1,0:T(8,128)(2,1)} %refs_8_.1), custom_call_target="tpu_custom_call" | custom-call | bytes 3145728 | tf_op jit(solution)/shard_map/gather_sends/pallas_call | solution.py:70
  29.9 3.6 %collective-permute-start.3 = (bf16[4,256,256]{2,1,0:T(8,128)(2,1)}, bf16[4,256,256]{2,1,0:T(8,128)(2,1)S(1)}, u32[]{:S(2)}, u32[]{:S(2)}) collective-permute-start(bf16[4,256,256]{2,1,0:T(8,128)(2,1)} %get-tuple-element.23), channel_id=1, source_target_pairs={{0,12},{4,0},{8,4},{12,8},{1,13},{5,1},{9,5},{13,9},{2,14},{6,2},{... | collective-permute-start | bytes 1572872 | tf_op jit(solution)/shard_map/ppermute | solution.py:399
  33.6 1.1 collective-permute-start.4
  36.0 10.3 %collective-permute-done.3.refs_5_ = bf16[4,256,256]{2,1,0:T(8,128)(2,1)S(1)} collective-permute-done((bf16[4,256,256]{2,1,0:T(8,128)(2,1)}, bf16[4,256,256]{2,1,0:T(8,128)(2,1)S(1)}, u32[]{:S(2)}, u32[]{:S(2)}) %collective-permute-start.3) | collective-permute-done | bytes 524320 | tf_op jit(solution)/shard_map/ppermute | solution.py:399
  46.2 33.1 %collective-permute-done.4.refs_6_ = bf16[4,256,256]{2,1,0:T(8,128)(2,1)S(1)} collective-permute-done((bf16[4,256,256]{2,1,0:T(8,128)(2,1)}, bf16[4,256,256]{2,1,0:T(8,128)(2,1)S(1)}, u32[]{:S(2)}, u32[]{:S(2)}) %collective-permute-start.4) | collective-permute-done | bytes 524320 | tf_op jit(solution)/shard_map/ppermute | solution.py:399
  80.3 9.2 %finish.2.refs_0_.refs_3_.refs_8_ = bf16[8,256,256]{2,1,0:T(8,128)(2,1)} custom-call(s32[8]{0:T(128)} %get-tuple-element.43.own_ref.at_ref, f32[8]{0:T(128)} %add.76.shift_ref, f32[8]{0:T(128)} %fusion.6.scale_ref, s32[8]{0:T(128)} %copy-done.10, s32[8]{0:T(128)} %get-tuple-element.53.place_ref, s32[8]{0:T(128)} %copy-done.9, s32[8]{0:T(128)} %copy-done.8, ...), custom_call_target="tpu_custom_call" | custom-call | flops 536870912 | bytes 7340032 | tf_op jit(solution)/shard_map/finish/pallas_call | solution.py:231
  89.6 2.9 %collective-permute-done.6.refs_1_.refs_4_.refs_9_ = bf16[8,256,256]{2,1,0:T(8,128)(2,1)S(1)} collective-permute-done((bf16[8,256,256]{2,1,0:T(8,128)(2,1)}, bf16[8,256,256]{2,1,0:T(8,128)(2,1)S(1)}, u32[]{:S(2)}, u32[]{:S(2)}) %collective-permute-start.6) | collective-permute-done | bytes 1048608 | tf_op jit(solution)/shard_map/ppermute | solution.py:405
  92.5 1.0 copy-done
  93.5 3.4 %gather_sends.3 = (bf16[4,256,256]{2,1,0:T(8,128)(2,1)}, bf16[4,256,256]{2,1,0:T(8,128)(2,1)}, bf16[4,256,256]{2,1,0:T(8,128)(2,1)}) custom-call(s32[2]{0:T(128)} %pad_add_fusion.place_ref, s32[16]{0:T(128)} %copy-done.11, s32[16]{0:T(128)} %copy-done.14, s32[16]{0:T(128)} %copy-done.13, s32[16]{0:T(128)} %copy-done.12, ...), custom_call_target="tpu_custom_call" | custom-call | bytes 3145728 | tf_op jit(solution)/shard_map/gather_sends/pallas_call | solution.py:70
  97.0 1.3 collective-permute-start.8
  98.2 1.8 %collective-permute-start.9 = (bf16[4,256,256]{2,1,0:T(8,128)(2,1)}, bf16[4,256,256]{2,1,0:T(8,128)(2,1)S(1)}, u32[]{:S(2)}, u32[]{:S(2)}) collective-permute-start(bf16[4,256,256]{2,1,0:T(8,128)(2,1)} %get-tuple-element.32), channel_id=1, source_target_pairs={{0,4},{4,8},{8,12},{12,0},{1,5},{5,9},{9,13},{13,1},{2,6},{6,10},{... | collective-permute-start | bytes 1572872 | tf_op jit(solution)/shard_map/ppermute | solution.py:399
  100.1 1.1 select_n.151.spread_ref
  101.6 8.8 %prepare.3 = (f32[8,256,256]{2,1,0:T(8,128)}, f32[8,256,256]{2,1,0:T(8,128)}, f32[8,1,256]{2,1,0:T(1,128)}, f32[8,256,1]{2,1,0:T(8,128)}) custom-call(s32[8]{0:T(128)} %get-tuple-element.43.own_ref.at_ref, s32[8]{0:T(128)} %iota.47.at_ref, f32[8]{0:T(128)} %add.76.shift_ref, bf16[128,256]{1,0:T(8,128)(2,1)} %select_n.151.spread_ref, ...), custom_call_target="tpu_custom_call" | custom-call | flops 805306368 | bytes 8388608 | tf_op jit(solution)/shard_map/prepare/pallas_call | solution.py:123
  110.5 1.6 collective-permute-done.7.refs_5_
  112.1 32.3 %collective-permute-done.8.refs_6_ = bf16[4,256,256]{2,1,0:T(8,128)(2,1)S(1)} collective-permute-done((bf16[4,256,256]{2,1,0:T(8,128)(2,1)}, bf16[4,256,256]{2,1,0:T(8,128)(2,1)S(1)}, u32[]{:S(2)}, u32[]{:S(2)}) %collective-permute-start.8) | collective-permute-done | bytes 524320 | tf_op jit(solution)/shard_map/ppermute | solution.py:399
  145.4 10.5 %finish.3 = (bf16[8,256,256]{2,1,0:T(8,128)(2,1)}, bf16[16,256,256]{2,1,0:T(8,128)(2,1)}, f32[1,64]{1,0:T(1,128)}) custom-call(s32[8]{0:T(128)} %get-tuple-element.43.own_ref.at_ref, f32[8]{0:T(128)} %add.76.shift_ref, f32[8]{0:T(128)} %fusion.6.scale_ref, s32[8]{0:T(128)} %copy-done.10, s32[8]{0:T(128)} %get-tuple-element.54.place_ref, s32[8]{0:T(128)} %copy-done.9, ...), custom_call_target="tpu_custom_call" | custom-call | flops 536870912 | bytes 7340032 | tf_op jit(solution)/shard_map/finish/pallas_call | solution.py:231
  156.5 2.4 %collective-permute-done.11 = f32[64]{0:T(128)S(1)} collective-permute-done((f32[64]{0:T(128)}, f32[64]{0:T(128)S(1)}, u32[]{:S(2)}, u32[]{:S(2)}) %collective-permute-start.11) | collective-permute-done | bytes 288 | tf_op jit(solution)/shard_map/ppermute | solution.py:306
  159.4 1.8 %collective-permute-start.12 = (f32[64]{0:T(128)S(1)}, f32[64]{0:T(128)S(1)}, u32[]{:S(2)}, u32[]{:S(2)}) collective-permute-start(f32[64]{0:T(128)S(1)} %bitcast_add_fusion), channel_id=1, source_target_pairs={{0,2},{2,0},{1,3},{3,1},{4,6},{6,4},{5,7},{7,5},{8,10},{10,8},{9,1... | collective-permute-start | bytes 776 | tf_op jit(solution)/shard_map/ppermute | solution.py:306
  161.2 1.8 %collective-permute-done.12 = f32[64]{0:T(128)S(1)} collective-permute-done((f32[64]{0:T(128)S(1)}, f32[64]{0:T(128)S(1)}, u32[]{:S(2)}, u32[]{:S(2)}) %collective-permute-start.12) | collective-permute-done | bytes 288 | tf_op jit(solution)/shard_map/ppermute | solution.py:306
  163.0 3.6 %collective-permute-done.13 = f32[64]{0:T(128)S(1)} collective-permute-done((f32[64]{0:T(128)S(1)}, f32[64]{0:T(128)S(1)}, u32[]{:S(2)}, u32[]{:S(2)}) %collective-permute-start.13) | collective-permute-done | bytes 288 | tf_op jit(solution)/shard_map/ppermute | solution.py:306
  166.6 1.4 collective-permute-start.14
  168.0 3.0 %collective-permute-done.14 = f32[64]{0:T(128)S(1)} collective-permute-done((f32[64]{0:T(128)S(1)}, f32[64]{0:T(128)S(1)}, u32[]{:S(2)}, u32[]{:S(2)}) %collective-permute-start.14) | collective-permute-done | bytes 288 | tf_op jit(solution)/shard_map/ppermute | solution.py:306
  171.6 1.0 copy-done.1
  172.5 2.7 %place_rest.1 = bf16[16,256,256]{2,1,0:T(8,128)(2,1)} custom-call(s32[8]{0:T(128)} %get-tuple-element.46.other_ref, bf16[8,256,256]{2,1,0:T(8,128)(2,1)} %copy-done.1, bf16[16,256,256]{2,1,0:T(8,128)(2,1)} %get-tuple-element.34.whole_ref), custom_call_target="tpu_custom_call", output_to_operand_aliasing={{}: (2, {})} | custom-call | bytes 2097152 | tf_op jit(solution)/shard_map/place_rest/pallas_call | solution.py:280
  (70 shorter events, 11.1 us)
Async XLA Ops:
  1.3 24.5 %collective-permute-start.2 = (s32[16]{0:T(128)S(1)}, s32[16]{0:T(128)S(1)}, u32[]{:S(2)}, u32[]{:S(2)}) collective-permute-start(s32[16]{0:T(128)S(1)} %get-tuple-element.55), channel_id=1, source_target_pairs={{0,12},{4,0},{8,4},{12,8},{1,13},{5,1},{9,5},{13,9},{2,14},{6,2},{... | collective-permute-start | bytes 200 | tf_op jit(solution)/shard_map/ppermute | solution.py:336
  6.4 19.5 %collective-permute-start.1 = (s32[16]{0:T(128)S(1)}, s32[16]{0:T(128)S(1)}, u32[]{:S(2)}, u32[]{:S(2)}) collective-permute-start(s32[16]{0:T(128)S(1)} %get-tuple-element.55), channel_id=1, source_target_pairs={{0,8},{4,12},{8,0},{12,4},{1,9},{5,13},{9,1},{13,5},{2,10},{6,14},... | collective-permute-start | bytes 200 | tf_op jit(solution)/shard_map/ppermute | solution.py:336
  6.4 19.5 %collective-permute-start = (s32[16]{0:T(128)S(1)}, s32[16]{0:T(128)S(1)}, u32[]{:S(2)}, u32[]{:S(2)}) collective-permute-start(s32[16]{0:T(128)S(1)} %get-tuple-element.55), channel_id=1, source_target_pairs={{0,4},{4,8},{8,12},{12,0},{1,5},{5,9},{9,13},{13,1},{2,6},{6,10},{... | collective-permute-start | bytes 200 | tf_op jit(solution)/shard_map/ppermute | solution.py:336
  8.4 17.5 %copy-start.11 = (s32[16]{0:T(128)}, s32[16]{0:T(128)S(1)}, u32[]{:S(2)}) copy-start(s32[16]{0:T(128)S(1)} %get-tuple-element.49.where_ref) | copy-start | bytes 196
  15.3 10.5 %copy-start.8 = (s32[8]{0:T(128)}, s32[8]{0:T(128)S(1)}, u32[]{:S(2)}) copy-start(s32[8]{0:T(128)S(1)} %get-tuple-element.41.second_ref) | copy-start | bytes 100
  15.3 10.5 %copy-start.9 = (s32[8]{0:T(128)}, s32[8]{0:T(128)S(1)}, u32[]{:S(2)}) copy-start(s32[8]{0:T(128)S(1)} %get-tuple-element.42.first_ref) | copy-start | bytes 100
  15.3 20.1 %copy-start.10 = (s32[8]{0:T(128)}, s32[8]{0:T(128)S(1)}, u32[]{:S(2)}) copy-start(s32[8]{0:T(128)S(1)} %get-tuple-element.40.from_ref) | copy-start | bytes 100
  25.8 8.9 %copy-start.15 = (bf16[16,1]{0,1:T(2,128)(2,1)S(1)}, bf16[16,1]{0,1:T(2,128)(2,1)}, u32[]{:S(2)}) copy-start(bf16[16,1]{0,1:T(2,128)(2,1)} %param.25) | copy-start | bytes 100
  25.9 0.6 copy-start.12
  25.9 0.6 copy-start.13
  25.9 0.6 copy-start.14
  29.9 16.3 %collective-permute-start.3 = (bf16[4,256,256]{2,1,0:T(8,128)(2,1)}, bf16[4,256,256]{2,1,0:T(8,128)(2,1)S(1)}, u32[]{:S(2)}, u32[]{:S(2)}) collective-permute-start(bf16[4,256,256]{2,1,0:T(8,128)(2,1)} %get-tuple-element.23), channel_id=1, source_target_pairs={{0,12},{4,0},{8,4},{12,8},{1,13},{5,1},{9,5},{13,9},{2,14},{6,2},{... | collective-permute-start | bytes 1572872 | tf_op jit(solution)/shard_map/ppermute | solution.py:399
  33.6 45.8 %collective-permute-start.4 = (bf16[4,256,256]{2,1,0:T(8,128)(2,1)}, bf16[4,256,256]{2,1,0:T(8,128)(2,1)S(1)}, u32[]{:S(2)}, u32[]{:S(2)}) collective-permute-start(bf16[4,256,256]{2,1,0:T(8,128)(2,1)} %get-tuple-element.24), channel_id=1, source_target_pairs={{0,8},{4,12},{8,0},{12,4},{1,9},{5,13},{9,1},{13,5},{2,10},{6,14},... | collective-permute-start | bytes 1572872 | tf_op jit(solution)/shard_map/ppermute | solution.py:399
  34.7 44.7 %collective-permute-start.5 = (bf16[4,256,256]{2,1,0:T(8,128)(2,1)}, bf16[4,256,256]{2,1,0:T(8,128)(2,1)S(1)}, u32[]{:S(2)}, u32[]{:S(2)}) collective-permute-start(bf16[4,256,256]{2,1,0:T(8,128)(2,1)} %get-tuple-element.25), channel_id=1, source_target_pairs={{0,4},{4,8},{8,12},{12,0},{1,5},{5,9},{9,13},{13,1},{2,6},{6,10},{... | collective-permute-start | bytes 1572872 | tf_op jit(solution)/shard_map/ppermute | solution.py:399
  46.2 33.1 %copy-start.5 = (bf16[4,256,256]{2,1,0:T(8,128)(2,1)}, bf16[4,256,256]{2,1,0:T(8,128)(2,1)S(1)}, u32[]{:S(2)}) copy-start(bf16[4,256,256]{2,1,0:T(8,128)(2,1)S(1)} %collective-permute-done.3.refs_5_) | copy-start | bytes 1572868
  79.3 0.8 copy-start.6
  79.4 1.0 copy-start.7
  89.5 2.9 %collective-permute-start.6 = (bf16[8,256,256]{2,1,0:T(8,128)(2,1)}, bf16[8,256,256]{2,1,0:T(8,128)(2,1)S(1)}, u32[]{:S(2)}, u32[]{:S(2)}) collective-permute-start(bf16[8,256,256]{2,1,0:T(8,128)(2,1)} %finish.2.refs_0_.refs_3_.refs_8_), channel_id=1, source_target_pairs={{0,1},{1,0},{2,3},{3,2},{4,5},{5,4},{6,7},{7,6},{8,9},{9,8},{10,11... | collective-permute-start | bytes 3145736 | tf_op jit(solution)/shard_map/ppermute | solution.py:405
  92.5 1.0 copy-start
  96.9 15.2 %collective-permute-start.7 = (bf16[4,256,256]{2,1,0:T(8,128)(2,1)}, bf16[4,256,256]{2,1,0:T(8,128)(2,1)S(1)}, u32[]{:S(2)}, u32[]{:S(2)}) collective-permute-start(bf16[4,256,256]{2,1,0:T(8,128)(2,1)} %get-tuple-element.30), channel_id=1, source_target_pairs={{0,12},{4,0},{8,4},{12,8},{1,13},{5,1},{9,5},{13,9},{2,14},{6,2},{... | collective-permute-start | bytes 1572872 | tf_op jit(solution)/shard_map/ppermute | solution.py:399
  97.0 47.4 %collective-permute-start.8 = (bf16[4,256,256]{2,1,0:T(8,128)(2,1)}, bf16[4,256,256]{2,1,0:T(8,128)(2,1)S(1)}, u32[]{:S(2)}, u32[]{:S(2)}) collective-permute-start(bf16[4,256,256]{2,1,0:T(8,128)(2,1)} %get-tuple-element.31), channel_id=1, source_target_pairs={{0,8},{4,12},{8,0},{12,4},{1,9},{5,13},{9,1},{13,5},{2,10},{6,14},... | collective-permute-start | bytes 1572872 | tf_op jit(solution)/shard_map/ppermute | solution.py:399
  98.2 46.2 %collective-permute-start.9 = (bf16[4,256,256]{2,1,0:T(8,128)(2,1)}, bf16[4,256,256]{2,1,0:T(8,128)(2,1)S(1)}, u32[]{:S(2)}, u32[]{:S(2)}) collective-permute-start(bf16[4,256,256]{2,1,0:T(8,128)(2,1)} %get-tuple-element.32), channel_id=1, source_target_pairs={{0,4},{4,8},{8,12},{12,0},{1,5},{5,9},{9,13},{13,1},{2,6},{6,10},{... | collective-permute-start | bytes 1572872 | tf_op jit(solution)/shard_map/ppermute | solution.py:399
  112.1 32.3 %copy-start.2 = (bf16[4,256,256]{2,1,0:T(8,128)(2,1)}, bf16[4,256,256]{2,1,0:T(8,128)(2,1)S(1)}, u32[]{:S(2)}) copy-start(bf16[4,256,256]{2,1,0:T(8,128)(2,1)S(1)} %collective-permute-done.7.refs_5_) | copy-start | bytes 1572868
  144.4 0.9 copy-start.3
  144.4 1.0 copy-start.4
  155.9 15.6 %collective-permute-start.10 = (bf16[8,256,256]{2,1,0:T(8,128)(2,1)}, bf16[8,256,256]{2,1,0:T(8,128)(2,1)S(1)}, u32[]{:S(2)}, u32[]{:S(2)}) collective-permute-start(bf16[8,256,256]{2,1,0:T(8,128)(2,1)} %get-tuple-element.33), channel_id=1, source_target_pairs={{0,1},{1,0},{2,3},{3,2},{4,5},{5,4},{6,7},{7,6},{8,9},{9,8},{10,11... | collective-permute-start | bytes 3145736 | tf_op jit(solution)/shard_map/ppermute | solution.py:405
  156.0 2.9 %collective-permute-start.11 = (f32[64]{0:T(128)}, f32[64]{0:T(128)S(1)}, u32[]{:S(2)}, u32[]{:S(2)}) collective-permute-start(f32[64]{0:T(128)} %bitcast.25), channel_id=1, source_target_pairs={{0,1},{1,0},{2,3},{3,2},{4,5},{5,4},{6,7},{7,6},{8,9},{9,8},{10,11... | collective-permute-start | bytes 776 | tf_op jit(solution)/shard_map/ppermute | solution.py:306
  159.4 3.6 %collective-permute-start.12 = (f32[64]{0:T(128)S(1)}, f32[64]{0:T(128)S(1)}, u32[]{:S(2)}, u32[]{:S(2)}) collective-permute-start(f32[64]{0:T(128)S(1)} %bitcast_add_fusion), channel_id=1, source_target_pairs={{0,2},{2,0},{1,3},{3,1},{4,6},{6,4},{5,7},{7,5},{8,10},{10,8},{9,1... | collective-permute-start | bytes 776 | tf_op jit(solution)/shard_map/ppermute | solution.py:306
  163.0 3.6 %collective-permute-start.13 = (f32[64]{0:T(128)S(1)}, f32[64]{0:T(128)S(1)}, u32[]{:S(2)}, u32[]{:S(2)}) collective-permute-start(f32[64]{0:T(128)S(1)} %add.82), channel_id=1, source_target_pairs={{0,4},{4,0},{8,12},{12,8},{1,5},{5,1},{9,13},{13,9},{2,6},{6,2},{1... | collective-permute-start | bytes 776 | tf_op jit(solution)/shard_map/ppermute | solution.py:306
  166.6 4.5 %collective-permute-start.14 = (f32[64]{0:T(128)S(1)}, f32[64]{0:T(128)S(1)}, u32[]{:S(2)}, u32[]{:S(2)}) collective-permute-start(f32[64]{0:T(128)S(1)} %add.83), channel_id=1, source_target_pairs={{0,8},{4,12},{8,0},{12,4},{1,9},{5,13},{9,1},{13,5},{2,10},{6,14},... | collective-permute-start | bytes 776 | tf_op jit(solution)/shard_map/ppermute | solution.py:306
  171.6 1.0 copy-start.1

commit v2 on v1

v2 whole, which is shorter than its diff:
```python
import jax
import jax.numpy as jnp
from jax import lax
from jax.experimental import pallas as pl
from jax.experimental.pallas import tpu as pltpu
from jax.sharding import PartitionSpec as P

ITERS = 2
ANY = pl.ANY
SMEM = pltpu.SMEM
VMEM = pltpu.VMEM
LANES = 16
MIB = 1 << 20


def exchanges(rows, shift):
    if rows & (rows - 1):
        return [(r, (r - shift) % rows) for r in range(rows)]
    return [(r, r ^ shift) for r in range(rows)]


def returns(rows, shift):
    return [(b, a) for a, b in exchanges(rows, shift)]


def apart(rows, source, row):
    if rows & (rows - 1):
        return (row - source) % rows
    return source ^ row


def limits(mib):
    return pltpu.CompilerParams(vmem_limit_bytes=mib * MIB)


def cost(flops, size):
    return pl.CostEstimate(flops=flops, transcendentals=0, bytes_accessed=size)


def fetch(candidates, spot, target, sem):
    for offset, ref in candidates:

        @pl.when((spot >= offset) & (spot < offset + ref.shape[0]))
        def _(offset=offset, ref=ref):
            pltpu.make_async_copy(ref.at[spot - offset], target, sem).start()


def laid(refs, offset=0):
    placed = []
    for ref in refs:
        placed.append((offset, ref))
        offset += ref.shape[0]
    return placed


def gather_first(requests, place, amplitudes, rows, cap):
    pairs, domain = amplitudes.shape[:2]
    blocks = (rows - 1) * cap

    def body(place_ref, *refs):
        lists = refs[: rows - 1]
        store = refs[rows - 1]
        asked = refs[rows]
        outs = refs[rows + 1 : 2 * rows]
        sem = refs[-1]
        me = place_ref[0]
        core = place_ref[1]
        for b in range(blocks):
            asked[b] = 0
        for shift in range(1, rows):
            asker = apart(rows, me, shift) if rows & (rows - 1) == 0 else (me + shift) % rows
            sources = [lists[shift - 1][p] // pairs for p in range(pairs)]
            count = jnp.int32(0)
            for p in range(pairs):
                count = count + (apart(rows, sources[p], asker) < shift).astype(jnp.int32)
            filled = jnp.int32((shift - 1) * cap)
            for p in range(pairs):
                mine = sources[p] == me
                taken = mine & (count % 2 == core)

                @pl.when(taken)
                def _(filled=filled, p=p, shift=shift):
                    asked[filled] = lists[shift - 1][p] % pairs

                count = count + mine.astype(jnp.int32)
                filled = jnp.minimum(filled + taken.astype(jnp.int32), shift * cap - 1)
            for k in range(cap):
                b = (shift - 1) * cap + k
                pltpu.make_async_copy(
                    store.at[asked[b]], outs[shift - 1].at[k], sem.at[b]
                ).start()
        for b in range(blocks):
            pltpu.make_async_copy(store.at[0], outs[b // cap].at[b % cap], sem.at[b]).wait()

    shape = (cap, domain, domain)
    return pl.pallas_call(
        body,
        out_shape=[jax.ShapeDtypeStruct((blocks,), jnp.int32)]
        + [VMEM(shape, jnp.bfloat16)] * (rows - 1),
        in_specs=[pl.BlockSpec(memory_space=SMEM)] * rows + [pl.BlockSpec(memory_space=ANY)],
        out_specs=[pl.BlockSpec(memory_space=SMEM)]
        + [pl.BlockSpec(memory_space=VMEM)] * (rows - 1),
        scratch_shapes=[pltpu.SemaphoreType.DMA((blocks,))],
        cost_estimate=cost(0, blocks * domain * domain * 4),
        compiler_params=limits(8),
        name="gather_first",
    )(place, *requests, amplitudes)


def gather_again(asked, where, stores, rows, cap):
    domain = stores[0].shape[1]
    blocks = (rows - 1) * cap

    def body(asked_ref, where_ref, *refs):
        sources = laid(refs[: len(stores)])
        outs = refs[len(stores) : len(stores) + rows - 1]
        sem = refs[-1]
        for b in range(blocks):
            fetch(sources, where_ref[asked_ref[b]], outs[b // cap].at[b % cap], sem.at[b])
        for b in range(blocks):
            pltpu.make_async_copy(
                sources[0][1].at[0], outs[b // cap].at[b % cap], sem.at[b]
            ).wait()

    return pl.pallas_call(
        body,
        out_shape=[VMEM((cap, domain, domain), jnp.bfloat16)] * (rows - 1),
        in_specs=[pl.BlockSpec(memory_space=SMEM)] * 2
        + [pl.BlockSpec(memory_space=ANY)] * len(stores),
        out_specs=[pl.BlockSpec(memory_space=VMEM)] * (rows - 1),
        scratch_shapes=[pltpu.SemaphoreType.DMA((blocks,))],
        cost_estimate=cost(0, blocks * domain * domain * 4),
        compiler_params=limits(8),
        name="gather_again",
    )(asked, where, *stores)


def prepare(own, at, shift, spread, stores, integrals, fock_matrix, intersection):
    half = own.shape[0]
    domain = integrals.shape[1]
    total = spread.shape[1] // LANES
    groups = domain // LANES // half
    strip = groups * LANES

    def body(own_ref, at_ref, shift_ref, spread_ref, *refs):
        sources = refs[: len(stores)]
        integ_ref, fock_ref, over_ref, local_ref, rest_ref, recip_ref, keep_ref = refs[len(stores) :]
        i = pl.program_id(0)
        for g in range(groups):
            rows = pl.ds(pl.multiple_of(i * strip + g * LANES, LANES), LANES)
            part = [s[:, rows, :].reshape(s.shape[0] * LANES, domain) for s in sources]
            part = part[0] if len(part) == 1 else jnp.concatenate(part, axis=0)
            sums = jnp.dot(spread_ref[...], part, preferred_element_type=jnp.float32)
            local_ref[:, g * LANES : (g + 1) * LANES, :] = sums.reshape(half, LANES, domain)
        amps = sources[0][at_ref[i]]
        fock = fock_ref[0]
        wide = amps.astype(jnp.float32)
        left = jnp.dot(fock, amps, preferred_element_type=jnp.float32)
        right = jnp.dot(amps, fock, preferred_element_type=jnp.float32)
        row_id = lax.broadcasted_iota(jnp.int32, (domain, domain), 0)
        col_id = lax.broadcasted_iota(jnp.int32, (domain, domain), 1)
        diagonal = jnp.where(row_id == col_id, fock.astype(jnp.float32), 0.0)
        across = jnp.sum(diagonal, axis=0, keepdims=True)
        down = jnp.sum(diagonal, axis=1, keepdims=True)
        residual = integ_ref[0].astype(jnp.float32) + left + right - shift_ref[i] * wide
        recip = 1.0 / (down + across - shift_ref[i])
        recip_ref[0] = recip
        rest_ref[0] = wide - residual * recip
        keep_ref[0] = over_ref[0]

    block = (1, domain, domain)
    mine = pl.BlockSpec(block, lambda i, own, *_: (own[i], 0, 0))
    in_turn = pl.BlockSpec(block, lambda i, *_: (i, 0, 0))
    wide_shape = jax.ShapeDtypeStruct((half, domain, domain), jnp.float32)
    return pl.pallas_call(
        body,
        grid_spec=pltpu.PrefetchScalarGridSpec(
            num_scalar_prefetch=3,
            grid=(half,),
            in_specs=[pl.BlockSpec(spread.shape, lambda i, *_: (0, 0))]
            + [pl.BlockSpec(s.shape, lambda i, *_: (0, 0, 0)) for s in stores]
            + [mine, mine, mine],
            out_specs=[
                pl.BlockSpec((half, strip, domain), lambda i, *_: (0, i, 0)),
                in_turn,
                in_turn,
                in_turn,
            ],
        ),
        out_shape=[
            wide_shape,
            wide_shape,
            wide_shape,
            jax.ShapeDtypeStruct((half, domain, domain), jnp.bfloat16),
        ],
        cost_estimate=cost(
            2 * half * domain**3 * 3,
            (total + 4 * half) * domain * domain * 2 + half * domain * domain * 12,
        ),
        compiler_params=limits(20),
        name="prepare",
    )(own, at, shift, spread, *stores, integrals, fock_matrix, intersection)


def finish(start, count, numbers, scale, prepared, arrived, stores, occ_count, last):
    half, domain = prepared[0].shape[:2]

    def body(number_ref, scale_ref, local_ref, rest_ref, recip_ref, over_ref, *refs):
        candidates = [
            (offset, ref) for offset, ref in zip([o for o, _ in arrived + stores], refs)
        ]
        outs = refs[len(candidates) : -2]
        hold, sem = refs[-2:]
        for n in range(count):
            fetch(candidates, number_ref[start + n], hold.at[n], sem.at[n])
        if last:
            row_id = lax.broadcasted_iota(jnp.int32, (domain, domain), 0)
            col_id = lax.broadcasted_iota(jnp.int32, (domain, domain), 1)
            on_diagonal = row_id == col_id
            orbital = lax.broadcasted_iota(jnp.int32, (1, occ_count), 1)
            density = jnp.zeros((1, occ_count), jnp.float32)
        for n in range(count):
            pltpu.make_async_copy(candidates[0][1].at[0], hold.at[n], sem.at[n]).wait()
        for n in range(count):
            i = start + n
            coupled = local_ref[i] + scale_ref[i] * hold[n].astype(jnp.float32)
            over = over_ref[i]
            projected = jnp.dot(
                over, coupled.astype(jnp.bfloat16), preferred_element_type=jnp.float32
            )
            back = lax.dot_general(
                projected.astype(jnp.bfloat16),
                over,
                (((1,), (1,)), ((), ())),
                preferred_element_type=jnp.float32,
            )
            fresh = (rest_ref[i] + back * recip_ref[i]).astype(jnp.bfloat16)
            outs[0][n] = fresh
            if last:
                wide = fresh.astype(jnp.float32)
                square = jnp.dot(fresh, fresh, preferred_element_type=jnp.float32)
                terms = 2.0 * wide * wide - jnp.where(on_diagonal, square, 0.0)
                norm = jnp.sum(jnp.sum(terms, axis=0, keepdims=True), axis=1, keepdims=True)
                picks = (orbital == number_ref[half + i]).astype(jnp.float32)
                picks = picks + (orbital == number_ref[2 * half + i]).astype(jnp.float32)
                density = density + norm * picks
        if last:
            outs[1][...] = density

    out_shape = [VMEM((count, domain, domain), jnp.bfloat16)]
    if last:
        out_shape.append(VMEM((1, occ_count), jnp.float32))
    return pl.pallas_call(
        body,
        out_shape=out_shape,
        in_specs=[pl.BlockSpec(memory_space=SMEM)] * 2
        + [pl.BlockSpec(memory_space=VMEM)] * 4
        + [pl.BlockSpec(memory_space=ANY)] * len(arrived + stores),
        out_specs=[pl.BlockSpec(memory_space=VMEM)] * len(out_shape),
        scratch_shapes=[
            VMEM((count, domain, domain), jnp.bfloat16),
            pltpu.SemaphoreType.DMA((count,)),
        ],
        cost_estimate=cost(2 * count * domain**3 * 2, count * domain * domain * 18),
        compiler_params=limits(16),
        name="finish",
    )(numbers, scale, *prepared, *[a for _, a in arrived + stores])


def put_in_slots(slots, stores):
    domain = stores[0].shape[1]
    total = slots.shape[0]

    def body(slot_ref, *refs):
        sources = refs[: len(stores)]
        out_ref, sem = refs[-2:]
        copies = []
        for source in sources:
            for n in range(source.shape[0]):
                at = len(copies)
                copies.append(
                    pltpu.make_async_copy(source.at[n], out_ref.at[slot_ref[at]], sem.at[at])
                )
        for copy in copies:
            copy.start()
        for copy in copies:
            copy.wait()

    return pl.pallas_call(
        body,
        out_shape=jax.ShapeDtypeStruct((total, domain, domain), jnp.bfloat16),
        in_specs=[pl.BlockSpec(memory_space=SMEM)]
        + [pl.BlockSpec(memory_space=VMEM)] * len(stores),
        out_specs=pl.BlockSpec(memory_space=ANY),
        scratch_shapes=[pltpu.SemaphoreType.DMA((total,))],
        cost_estimate=cost(0, total * domain * domain * 4),
        compiler_params=limits(8),
        name="put_in_slots",
    )(slots, *stores)


def add_over(values, name):
    size = lax.axis_size(name)
    if size & (size - 1):
        return lax.psum(values, name)
    step = 1
    while step < size:
        values = values + lax.ppermute(values, name, [(r, r ^ step) for r in range(size)])
        step *= 2
    return values


def per_device(
    amplitudes,
    integrals,
    fock_matrix,
    intersection,
    occ_energy,
    first_occ,
    second_occ,
    near_slot,
    near_count,
    near_weight,
    far_chip,
    far_slot,
    far_weight,
):
    pairs, domain = amplitudes.shape[:2]
    rows = lax.axis_size("row")
    half = pairs // 2
    cap = pairs // rows
    row = lax.axis_index("row")
    core = lax.axis_index("rep")
    occ_count = occ_energy.shape[0]
    slot_ids = jnp.arange(pairs, dtype=jnp.int32)
    source = far_chip[:, 0]
    packed = source * pairs + far_slot[:, 0]
    requests = [lax.ppermute(packed, "row", exchanges(rows, d)) for d in range(1, rows)]
    here = jnp.stack([row, core]).astype(jnp.int32)
    asked, *sends = gather_first(requests, here, amplitudes, rows, cap)

    step = apart(rows, source, row)
    same = step[:, None] == step[None, :]
    before = (step[None, :] < step[:, None]) | (same & (slot_ids[None, :] < slot_ids[:, None]))
    turn = jnp.sum(before.astype(jnp.int32), axis=1)
    like = same & (turn[:, None] % 2 == turn[None, :] % 2) & (turn[None, :] < turn[:, None])
    place = jnp.sum(like.astype(jnp.int32), axis=1)
    mine = jnp.arange(half, dtype=jnp.int32) * 2 + core
    own_pick = mine[:, None] == turn[None, :]
    other_pick = (mine ^ 1)[:, None] == turn[None, :]

    def pick(chosen, values):
        return jnp.sum(jnp.where(chosen, values[None, :], jnp.zeros((), values.dtype)), axis=1)

    own = pick(own_pick, slot_ids)
    other = pick(other_pick, slot_ids)
    far_step = pick(own_pick, step)
    own_far = pick(own_pick, far_slot[:, 0])
    own_place = pick(own_pick, place)
    far_scale = pick(own_pick, far_weight[:, 0].astype(jnp.float32))
    first = pick(own_pick, first_occ)
    second = pick(own_pick, second_occ)
    orbitals = jnp.arange(occ_count, dtype=jnp.int32)

    def energy_of(index):
        found = index[:, None] == orbitals[None, :]
        return jnp.sum(jnp.where(found, occ_energy[None, :], jnp.float32(0.0)), axis=1)

    shift = energy_of(first) + energy_of(second)

    near_pos = jnp.arange(near_slot.shape[1], dtype=jnp.int32)
    alive = near_pos[None, :] < near_count[:, None]
    matches = (near_slot[:, :, None] == slot_ids[None, None, :]) & alive[:, :, None]
    weights = jnp.sum(
        jnp.where(matches, near_weight.astype(jnp.float32)[:, :, None], jnp.float32(0.0)), axis=1
    ).astype(jnp.bfloat16)

    def choose(chosen, table):
        spread = jnp.where(chosen[:, :, None], table[None], jnp.zeros((), table.dtype))
        return jnp.sum(spread.astype(jnp.float32), axis=1).astype(table.dtype)

    own_weights = choose(own_pick, weights)
    by_core = jnp.concatenate(
        [choose(own_pick, own_weights.T).T, choose(other_pick, own_weights.T).T], axis=1
    )
    lane = jnp.arange(LANES)
    unit = lane[:, None] == lane[None, :]

    def spread_of(table):
        grid = jnp.where(
            unit[None, :, None, :], table[:, None, :, None], jnp.zeros((), table.dtype)
        )
        return grid.reshape(half * LANES, pairs * LANES)

    by_slot = turn // 2 + jnp.where(turn % 2 == core, 0, half)
    early = half - cap
    swap = [(0, 1), (1, 0)]
    remote = (rows - 1) * cap
    local_spots = [
        slot_ids,
        jnp.where(
            by_slot < half,
            by_slot + jnp.where(by_slot % half < early, 0, early),
            by_slot - half + jnp.where(by_slot % half < early, early, half),
        ),
    ]
    tables = []
    for where in local_spots:
        at_home = remote + jnp.sum(
            jnp.where(own_far[:, None] == slot_ids[None, :], where[None, :], 0), axis=1
        )
        spot = jnp.where(far_step == 0, at_home, (far_step - 1) * cap + own_place)
        tables.append(jnp.concatenate([spot, first, second]))
    spreads = [spread_of(own_weights), spread_of(by_core)]
    ats = [own, jnp.arange(half, dtype=jnp.int32)]
    slots = jnp.concatenate([own[:early], other[:early], own[early:], other[early:]])
    (own, shift, far_scale, *moved) = lax.optimization_barrier(
        (own, shift, far_scale, *tables, *spreads, *ats, slots, *sends)
    )
    tables, spreads, ats, slots = moved[:2], moved[2:4], moved[4:6], moved[6]

    stores = [amplitudes]
    whole = [amplitudes]
    for sweep in range(ITERS):
        last = sweep == ITERS - 1
        late = min(sweep, 1)
        if sweep > 0:
            sends = gather_again(asked, local_spots[late], stores, rows, cap)
        arrived = [
            lax.ppermute(block, "row", returns(rows, d)) for d, block in enumerate(sends, 1)
        ]
        prepared = prepare(
            own, ats[late], shift, spreads[late], whole, integrals, fock_matrix, intersection
        )
        spots = laid(arrived)
        homes = laid(stores, remote)
        done_early = finish(
            0, early, tables[late], far_scale, prepared, spots[:-1], homes, occ_count, last
        )
        given_early = lax.ppermute(done_early[0], "rep", swap)
        done_late = finish(
            early, cap, tables[late], far_scale, prepared, spots, homes, occ_count, last
        )
        given_late = lax.ppermute(done_late[0], "rep", swap)
        stores = [done_early[0], given_early, done_late[0], given_late]
        whole = [
            jnp.concatenate([done_early[0], done_late[0]], axis=0),
            jnp.concatenate([given_early, given_late], axis=0),
        ]
    final = put_in_slots(slots, stores)
    occ_sum = (done_early[1] + done_late[1])[0]
    occ_sum = add_over(add_over(occ_sum, "rep"), "col")
    occ_sum, final = lax.optimization_barrier((occ_sum, final))
    occ_sum = add_over(occ_sum, "row")
    total_pairs = pairs * rows * lax.axis_size("col")
    occ_density = occ_sum * (occ_count / (2.0 * total_pairs * domain * domain))
    return (final, occ_density)


def solution(mesh):
    pair_spec = P(("groups", "row", "col"), None, None)
    flat = P(("groups", "row", "col"))
    table = P(("groups", "row", "col"), None)
    return jax.shard_map(
        per_device,
        mesh=mesh,
        in_specs=(
            pair_spec, pair_spec, pair_spec, pair_spec,
            P("groups"), flat, flat, table, flat, table, table, table, table,
        ),
        out_specs=(pair_spec, P("groups")),
        check_vma=False,
    )
```

time: 177 us -> 143 us (0.81)
  waiting for transfers between devices: 90.9 us -> 68.8 us
  Pallas kernels: 46.9 us -> 24.8 us
  starting transfers between devices: 17.9 us -> 36.3 us
  other arithmetic: 9.84 us -> 4.94 us
  local copies, waits for them, and re-layouts: 8.9 us -> 6.46 us
    ppermute x15 -> x17, waiting for transfers between devices: 90.9 us -> 68.8 us  [the longest x6 60.7 us: per_device(): lax.ppermute(block, 'row', returns(rows, d))]
    ppermute x15 -> x17, starting transfers between devices: 17.9 us -> 36.3 us  [the longest x6 16.8 us: per_device(): lax.ppermute(block, 'row', returns(rows, d))]
    pallas_call x2, Pallas kernels: 17.6 us -> 6.03 us  [prepare(): pl.pallas_call(body, grid_spec=pltpu.PrefetchScalarGridSpec(num_scalar_pr...]
    pallas_call x5 -> x7, Pallas kernels: 29.2 us -> 18.8 us  [the longest x4 9.45 us: finish(): pl.pallas_call(body, out_shape=out_shape, in_specs=[pl.BlockSpec(memory_s...]
    unnamed x33 -> x23, local copies, waits for them, and re-layouts: 4.88 us -> 4.62 us
  transfers between devices with their start and end apart: 15 -> 17, of which waited for: 9 -> 9; matrix products, arithmetic and copies ran while one was open for 8% -> 4% of each run, Pallas kernels for 10% -> 10%
where the time goes in v2:
time: 143 us; the launch traced here: 142 us
  waiting for transfers between devices  68.8 us (48%)
  starting transfers between devices  36.3 us (25%)
  Pallas kernels  24.8 us (17%)
  local copies, waits for them, and re-layouts  6.46 us (5%)
  other arithmetic  4.94 us (3%)
    ppermute x6, waiting for transfers between devices, per_device(): lax.ppermute(block, 'row', returns(rows, d))  60.7 us
    ppermute x6, starting transfers between devices, per_device(): lax.ppermute(block, 'row', returns(rows, d))  16.8 us
    ppermute x4, starting transfers between devices, add_over(): lax.ppermute(values, name, [(r, r ^ step) for r in range(size)])  12.6 us
    pallas_call x4, Pallas kernels, finish(): pl.pallas_call(body, out_shape=out_shape, in_specs=[pl.BlockSpec(memory_s...  9.45 us
    ppermute x4, waiting for transfers between devices, add_over(): lax.ppermute(values, name, [(r, r ^ step) for r in range(size)])  6.61 us
    pallas_call x2, Pallas kernels, prepare(): pl.pallas_call(body, grid_spec=pltpu.PrefetchScalarGridSpec(num_scalar_pr...  6.03 us
    ppermute x3, starting transfers between devices, per_device(): lax.ppermute(packed, 'row', exchanges(rows, d))  5.64 us
    unnamed x23, local copies, waits for them, and re-layouts  4.62 us
  transfers between devices with their start and end apart: 17, of which 9 were waited for; matrix products, arithmetic and copies ran while one was open for 4% of the time, Pallas kernels for 10%

profile of v2, /device:TPU:0, one launch (start us, length us, event | category | flops | bytes accessed | tf_op | source)
XLA Modules:
  0.0 142.3 jit_solution(17005226342575753672)
XLA Ops:
  0.7 0.8 bitcast_add_fusion
  1.5 3.1 %collective-permute-start = (s32[16]{0:T(128)S(1)}, s32[16]{0:T(128)S(1)}, u32[]{:S(2)}, u32[]{:S(2)}) collective-permute-start(s32[16]{0:T(128)S(1)} %bitcast_add_fusion), channel_id=1, source_target_pairs={{0,4},{4,0},{8,12},{12,8},{1,5},{5,1},{9,13},{13,9},{2,6},{6,2},{1... | collective-permute-start | bytes 200 | tf_op jit(solution)/shard_map/ppermute | solution.py:338
  4.6 2.6 %collective-permute-start.1 = (s32[16]{0:T(128)S(1)}, s32[16]{0:T(128)S(1)}, u32[]{:S(2)}, u32[]{:S(2)}) collective-permute-start(s32[16]{0:T(128)S(1)} %bitcast_add_fusion), channel_id=1, source_target_pairs={{0,8},{4,12},{8,0},{12,4},{1,9},{5,13},{9,1},{13,5},{2,10},{6,14},... | collective-permute-start | bytes 200 | tf_op jit(solution)/shard_map/ppermute | solution.py:338
  9.0 0.8 copy.16
  13.1 4.3 %gather_first.1 = (s32[12]{0:T(128)S(1)}, bf16[4,256,256]{2,1,0:T(8,128)(2,1)S(1)}, bf16[4,256,256]{2,1,0:T(8,128)(2,1)S(1)}, bf16[4,256,256]{2,1,0:T(8,128)(2,1)S(1)}) custom-call(s32[2]{0:T(128)S(1)} %pad_add_fusion.1.place_ref, s32[16]{0:T(128)S(1)} %collective-permute-done.refs_0_, s32[16]{0:T(128)S(1)} %collective-permute-done.1.refs_1_, ...), custom_call_target="tpu_custom_call" | custom-call | bytes 3145728 | tf_op jit(solution)/shard_map/gather_first/pallas_call | solution.py:96
  17.4 1.0 collective-permute-start.3
  18.4 3.5 %collective-permute-start.4 = (bf16[4,256,256]{2,1,0:T(8,128)(2,1)S(1)}, bf16[4,256,256]{2,1,0:T(8,128)(2,1)S(1)}, u32[]{:S(2)}, u32[]{:S(2)}) collective-permute-start(bf16[4,256,256]{2,1,0:T(8,128)(2,1)S(1)} %get-tuple-element.34), channel_id=1, source_target_pairs={{8,0},{12,4},{0,8},{4,12},{9,1},{13,5},{1,9},{5,13},{10,2},{14,6},... | collective-permute-start | bytes 1572872 | tf_op jit(solution)/shard_map/ppermute | solution.py:430
  22.2 1.6 %copy-done.2 = bf16[16,256,256]{2,1,0:T(8,128)(2,1)S(1)} copy-done((bf16[16,256,256]{2,1,0:T(8,128)(2,1)S(1)}, bf16[16,256,256]{2,1,0:T(8,128)(2,1)}, u32[]{:S(2)}) %copy-start.2) | copy-done | bytes 2097176
  23.7 1.6 %copy-done.4 = bf16[16,256,256]{2,1,0:T(8,128)(2,1)S(1)} copy-done((bf16[16,256,256]{2,1,0:T(8,128)(2,1)S(1)}, bf16[16,256,256]{2,1,0:T(8,128)(2,1)}, u32[]{:S(2)}) %copy-start.4) | copy-done | bytes 2097176
  25.3 3.0 %prepare.2 = (f32[8,256,256]{2,1,0:T(8,128)S(1)}, f32[8,256,256]{2,1,0:T(8,128)S(1)}, f32[8,256,256]{2,1,0:T(8,128)S(1)}, bf16[8,256,256]{2,1,0:T(8,128)(2,1)S(1)}) custom-call(s32[8]{0:T(128)S(1)} %get-tuple-element.43.own_ref.at_ref, s32[8]{0:T(128)S(1)} %get-tuple-element.43.own_ref.at_ref, f32[8]{0:T(128)S(1)} %add.115.shift_ref, ...), custom_call_target="tpu_custom_call" | custom-call | flops 805306368 | bytes 12582912 | tf_op jit(solution)/shard_map/prepare/pallas_call | solution.py:175
  28.3 12.4 %collective-permute-done.3.refs_0_ = bf16[4,256,256]{2,1,0:T(8,128)(2,1)S(1)} collective-permute-done((bf16[4,256,256]{2,1,0:T(8,128)(2,1)S(1)}, bf16[4,256,256]{2,1,0:T(8,128)(2,1)S(1)}, u32[]{:S(2)}, u32[]{:S(2)}) %collective-permute-start.3) | collective-permute-done | bytes 524320 | tf_op jit(solution)/shard_map/ppermute | solution.py:430
  40.7 16.4 %collective-permute-done.4.refs_1_ = bf16[4,256,256]{2,1,0:T(8,128)(2,1)S(1)} collective-permute-done((bf16[4,256,256]{2,1,0:T(8,128)(2,1)S(1)}, bf16[4,256,256]{2,1,0:T(8,128)(2,1)S(1)}, u32[]{:S(2)}, u32[]{:S(2)}) %collective-permute-start.4) | collective-permute-done | bytes 524320 | tf_op jit(solution)/shard_map/ppermute | solution.py:430
  57.1 1.9 %finish.5.refs_2_.refs_4_.refs_5_ = bf16[4,256,256]{2,1,0:T(8,128)(2,1)S(1)} custom-call(s32[24]{0:T(128)S(1)} %get-tuple-element.42.number_ref, f32[8]{0:T(128)S(1)} %fusion.6.scale_ref, f32[8,256,256]{2,1,0:T(8,128)S(1)} %get-tuple-element.45.local_ref, f32[8,256,256]{2,1,0:T(8,128)S(1)} %get-tuple-element.46.rest_ref, ...), custom_call_target="tpu_custom_call" | custom-call | flops 268435456 | bytes 4718592 | tf_op jit(solution)/shard_map/finish/pallas_call | solution.py:253
  59.1 1.9 %finish.4.refs_0_.refs_2_.refs_3_ = bf16[4,256,256]{2,1,0:T(8,128)(2,1)S(1)} custom-call(s32[24]{0:T(128)S(1)} %get-tuple-element.42.number_ref, f32[8]{0:T(128)S(1)} %fusion.6.scale_ref, f32[8,256,256]{2,1,0:T(8,128)S(1)} %get-tuple-element.45.local_ref, f32[8,256,256]{2,1,0:T(8,128)S(1)} %get-tuple-element.46.rest_ref, ...), custom_call_target="tpu_custom_call" | custom-call | flops 268435456 | bytes 4718592 | tf_op jit(solution)/shard_map/finish/pallas_call | solution.py:253
  61.6 1.5 %collective-permute-done.6.refs_1_.refs_3_.refs_4_ = bf16[4,256,256]{2,1,0:T(8,128)(2,1)S(1)} collective-permute-done((bf16[4,256,256]{2,1,0:T(8,128)(2,1)S(1)}, bf16[4,256,256]{2,1,0:T(8,128)(2,1)S(1)}, u32[]{:S(2)}, u32[]{:S(2)}) %collective-permute-start.6) | collective-permute-done | bytes 524320 | tf_op jit(solution)/shard_map/ppermute | solution.py:440
  63.1 3.0 %gather_again.1 = (bf16[4,256,256]{2,1,0:T(8,128)(2,1)S(1)}, bf16[4,256,256]{2,1,0:T(8,128)(2,1)S(1)}, bf16[4,256,256]{2,1,0:T(8,128)(2,1)S(1)}) custom-call(s32[12]{0:T(128)S(1)} %get-tuple-element.53.asked_ref, s32[16]{0:T(128)S(1)} %get-tuple-element.77.where_ref, bf16[4,256,256]{2,1,0:T(8,128)(2,1)S(1)} %finish.4.refs_0_.refs_2_.refs_3_, ...), custom_call_target="tpu_custom_call" | custom-call | bytes 3145728 | tf_op jit(solution)/shard_map/gather_again/pallas_call | solution.py:125
  66.1 9.9 %collective-permute-start.8 = (bf16[4,256,256]{2,1,0:T(8,128)(2,1)S(1)}, bf16[4,256,256]{2,1,0:T(8,128)(2,1)S(1)}, u32[]{:S(2)}, u32[]{:S(2)}) collective-permute-start(bf16[4,256,256]{2,1,0:T(8,128)(2,1)S(1)} %get-tuple-element.54), channel_id=1, source_target_pairs={{4,0},{0,4},{12,8},{8,12},{5,1},{1,5},{13,9},{9,13},{6,2},{2,6},{1... | collective-permute-start | bytes 1572872 | tf_op jit(solution)/shard_map/ppermute | solution.py:430
  76.1 1.1 collective-permute-start.9
  77.1 1.4 collective-permute-start.10
  79.3 3.0 %prepare.3 = (f32[8,256,256]{2,1,0:T(8,128)S(1)}, f32[8,256,256]{2,1,0:T(8,128)S(1)}, f32[8,256,256]{2,1,0:T(8,128)S(1)}, bf16[8,256,256]{2,1,0:T(8,128)(2,1)S(1)}) custom-call(s32[8]{0:T(128)S(1)} %get-tuple-element.43.own_ref.at_ref, s32[8]{0:T(128)S(1)} %iota.43.at_ref, f32[8]{0:T(128)S(1)} %add.115.shift_ref, bf16[128,256]{1,0:T(8,128)(2,1)S(1)} %select_n.176.spread_ref, ...), custom_call_target="tpu_custom_call" | custom-call | flops 805306368 | bytes 12582912 | tf_op jit(solution)/shard_map/prepare/pallas_call | solution.py:175
  82.4 16.9 %collective-permute-done.8.refs_0_ = bf16[4,256,256]{2,1,0:T(8,128)(2,1)S(1)} collective-permute-done((bf16[4,256,256]{2,1,0:T(8,128)(2,1)S(1)}, bf16[4,256,256]{2,1,0:T(8,128)(2,1)S(1)}, u32[]{:S(2)}, u32[]{:S(2)}) %collective-permute-start.8) | collective-permute-done | bytes 524320 | tf_op jit(solution)/shard_map/ppermute | solution.py:430
  99.3 15.0 %collective-permute-done.9.refs_1_ = bf16[4,256,256]{2,1,0:T(8,128)(2,1)S(1)} collective-permute-done((bf16[4,256,256]{2,1,0:T(8,128)(2,1)S(1)}, bf16[4,256,256]{2,1,0:T(8,128)(2,1)S(1)}, u32[]{:S(2)}, u32[]{:S(2)}) %collective-permute-start.9) | collective-permute-done | bytes 524320 | tf_op jit(solution)/shard_map/ppermute | solution.py:430
  114.3 2.8 %finish.6 = (bf16[4,256,256]{2,1,0:T(8,128)(2,1)S(1)}, f32[1,64]{1,0:T(1,128)S(1)}) custom-call(s32[24]{0:T(128)S(1)} %get-tuple-element.36.number_ref, f32[8]{0:T(128)S(1)} %fusion.6.scale_ref, f32[8,256,256]{2,1,0:T(8,128)S(1)} %get-tuple-element.49.local_ref, f32[8,256,256]{2,1,0:T(8,128)S(1)} %get-tuple-element.50.rest_ref, ...), custom_call_target="tpu_custom_call" | custom-call | flops 268435456 | bytes 4718592 | tf_op jit(solution)/shard_map/finish/pallas_call | solution.py:253
  117.2 2.8 %finish.7 = (bf16[4,256,256]{2,1,0:T(8,128)(2,1)S(1)}, f32[1,64]{1,0:T(1,128)S(1)}) custom-call(s32[24]{0:T(128)S(1)} %get-tuple-element.36.number_ref, f32[8]{0:T(128)S(1)} %fusion.6.scale_ref, f32[8,256,256]{2,1,0:T(8,128)S(1)} %get-tuple-element.49.local_ref, f32[8,256,256]{2,1,0:T(8,128)S(1)} %get-tuple-element.50.rest_ref, ...), custom_call_target="tpu_custom_call" | custom-call | flops 268435456 | bytes 4718592 | tf_op jit(solution)/shard_map/finish/pallas_call | solution.py:253
  120.7 1.4 %collective-permute-done.11 = f32[64]{0:T(128)S(1)} collective-permute-done((f32[64]{0:T(128)S(1)}, f32[64]{0:T(128)S(1)}, u32[]{:S(2)}, u32[]{:S(2)}) %collective-permute-start.11) | collective-permute-done | bytes 288 | tf_op jit(solution)/shard_map/ppermute | solution.py:308
  122.1 1.5 %collective-permute-start.12 = (f32[64]{0:T(128)S(1)}, f32[64]{0:T(128)S(1)}, u32[]{:S(2)}, u32[]{:S(2)}) collective-permute-start(f32[64]{0:T(128)S(1)} %add.126), channel_id=1, source_target_pairs={{0,2},{2,0},{1,3},{3,1},{4,6},{6,4},{5,7},{7,5},{8,10},{10,8},{9,1... | collective-permute-start | bytes 776 | tf_op jit(solution)/shard_map/ppermute | solution.py:308
  123.6 2.1 %collective-permute-done.12 = f32[64]{0:T(128)S(1)} collective-permute-done((f32[64]{0:T(128)S(1)}, f32[64]{0:T(128)S(1)}, u32[]{:S(2)}, u32[]{:S(2)}) %collective-permute-start.12) | collective-permute-done | bytes 288 | tf_op jit(solution)/shard_map/ppermute | solution.py:308
  125.7 2.0 %put_in_slots.1 = bf16[16,256,256]{2,1,0:T(8,128)(2,1)} custom-call(s32[16]{0:T(128)S(1)} %pad_add_fusion.slot_ref, bf16[4,256,256]{2,1,0:T(8,128)(2,1)S(1)} %get-tuple-element.60.refs_0_, bf16[4,256,256]{2,1,0:T(8,128)(2,1)S(1)} %collective-permute-done.13.refs_1_, bf16[4,256,256]{2,1,0:T(8,128)(2,1)S(1)} %get-tuple-element.61.refs_2_, ...), custom_call_target="tpu_custom_call" | custom-call | bytes 4194304 | tf_op jit(solution)/shard_map/put_in_slots/pallas_call | solution.py:289
  127.7 8.0 %collective-permute-start.15 = (f32[64]{0:T(128)S(1)}, f32[64]{0:T(128)S(1)}, u32[]{:S(2)}, u32[]{:S(2)}) collective-permute-start(f32[64]{0:T(128)S(1)} %add.127), channel_id=1, source_target_pairs={{0,4},{4,0},{8,12},{12,8},{1,5},{5,1},{9,13},{13,9},{2,6},{6,2},{1... | collective-permute-start | bytes 776 | tf_op jit(solution)/shard_map/ppermute | solution.py:308
  135.7 1.5 %collective-permute-done.15 = f32[64]{0:T(128)S(1)} collective-permute-done((f32[64]{0:T(128)S(1)}, f32[64]{0:T(128)S(1)}, u32[]{:S(2)}, u32[]{:S(2)}) %collective-permute-start.15) | collective-permute-done | bytes 288 | tf_op jit(solution)/shard_map/ppermute | solution.py:308
  137.2 3.0 %collective-permute-start.16 = (f32[64]{0:T(128)S(1)}, f32[64]{0:T(128)S(1)}, u32[]{:S(2)}, u32[]{:S(2)}) collective-permute-start(f32[64]{0:T(128)S(1)} %add.128), channel_id=1, source_target_pairs={{0,8},{4,12},{8,0},{12,4},{1,9},{5,13},{9,1},{13,5},{2,10},{6,14},... | collective-permute-start | bytes 776 | tf_op jit(solution)/shard_map/ppermute | solution.py:308
  140.2 1.5 %collective-permute-done.16 = f32[64]{0:T(128)S(1)} collective-permute-done((f32[64]{0:T(128)S(1)}, f32[64]{0:T(128)S(1)}, u32[]{:S(2)}, u32[]{:S(2)}) %collective-permute-start.16) | collective-permute-done | bytes 288 | tf_op jit(solution)/shard_map/ppermute | solution.py:308
  (72 shorter events, 8.0 us)
Async XLA Ops:
  0.6 11.4 %copy-start.7 = (s32[16,1]{0,1:T(1,128)S(1)}, s32[16,1]{0,1:T(1,128)}, u32[]{:S(2)}) copy-start(s32[16,1]{0,1:T(1,128)} %param.24) | copy-start | bytes 196
  0.6 11.4 %copy-start.8 = (s32[16]{0:T(128)S(1)}, s32[16]{0:T(128)}, u32[]{:S(2)}) copy-start(s32[16]{0:T(128)} %param.19) | copy-start | bytes 196
  0.7 11.4 %copy-start.9 = (s32[16]{0:T(128)S(1)}, s32[16]{0:T(128)}, u32[]{:S(2)}) copy-start(s32[16]{0:T(128)} %param.18) | copy-start | bytes 196
  0.7 11.9 %copy-start.6 = (f32[64]{0:T(128)S(1)}, f32[64]{0:T(128)}, u32[]{:S(2)}) copy-start(f32[64]{0:T(128)} %param.17) | copy-start | bytes 772
  0.7 12.4 %copy-start = (bf16[16,256,256]{2,1,0:T(8,128)(2,1)S(1)}, bf16[16,256,256]{2,1,0:T(8,128)(2,1)}, u32[]{:S(2)}) copy-start(bf16[16,256,256]{2,1,0:T(8,128)(2,1)} %refs_3_.6) | copy-start | bytes 6291460
  1.5 11.5 %collective-permute-start = (s32[16]{0:T(128)S(1)}, s32[16]{0:T(128)S(1)}, u32[]{:S(2)}, u32[]{:S(2)}) collective-permute-start(s32[16]{0:T(128)S(1)} %bitcast_add_fusion), channel_id=1, source_target_pairs={{0,4},{4,0},{8,12},{12,8},{1,5},{5,1},{9,13},{13,9},{2,6},{6,2},{1... | collective-permute-start | bytes 200 | tf_op jit(solution)/shard_map/ppermute | solution.py:338
  4.6 8.5 %collective-permute-start.1 = (s32[16]{0:T(128)S(1)}, s32[16]{0:T(128)S(1)}, u32[]{:S(2)}, u32[]{:S(2)}) collective-permute-start(s32[16]{0:T(128)S(1)} %bitcast_add_fusion), channel_id=1, source_target_pairs={{0,8},{4,12},{8,0},{12,4},{1,9},{5,13},{9,1},{13,5},{2,10},{6,14},... | collective-permute-start | bytes 200 | tf_op jit(solution)/shard_map/ppermute | solution.py:338
  7.2 5.9 %collective-permute-start.2 = (s32[16]{0:T(128)S(1)}, s32[16]{0:T(128)S(1)}, u32[]{:S(2)}, u32[]{:S(2)}) collective-permute-start(s32[16]{0:T(128)S(1)} %bitcast_add_fusion), channel_id=1, source_target_pairs={{0,12},{4,8},{8,4},{12,0},{1,13},{5,9},{9,5},{13,1},{2,14},{6,10},... | collective-permute-start | bytes 200 | tf_op jit(solution)/shard_map/ppermute | solution.py:338
  11.0 11.0 %copy-start.10 = (bf16[16,1]{0,1:T(2,128)(2,1)S(1)}, bf16[16,1]{0,1:T(2,128)(2,1)}, u32[]{:S(2)}) copy-start(bf16[16,1]{0,1:T(2,128)(2,1)} %param.25) | copy-start | bytes 100
  12.0 10.1 %copy-start.1 = (bf16[16,256,256]{2,1,0:T(8,128)(2,1)S(1)}, bf16[16,256,256]{2,1,0:T(8,128)(2,1)}, u32[]{:S(2)}) copy-start(bf16[16,256,256]{2,1,0:T(8,128)(2,1)} %refs_2_.5) | copy-start | bytes 6291460
  17.4 23.3 %collective-permute-start.3 = (bf16[4,256,256]{2,1,0:T(8,128)(2,1)S(1)}, bf16[4,256,256]{2,1,0:T(8,128)(2,1)S(1)}, u32[]{:S(2)}, u32[]{:S(2)}) collective-permute-start(bf16[4,256,256]{2,1,0:T(8,128)(2,1)S(1)} %get-tuple-element.33), channel_id=1, source_target_pairs={{4,0},{0,4},{12,8},{8,12},{5,1},{1,5},{13,9},{9,13},{6,2},{2,6},{1... | collective-permute-start | bytes 1572872 | tf_op jit(solution)/shard_map/ppermute | solution.py:430
  18.4 38.7 %collective-permute-start.4 = (bf16[4,256,256]{2,1,0:T(8,128)(2,1)S(1)}, bf16[4,256,256]{2,1,0:T(8,128)(2,1)S(1)}, u32[]{:S(2)}, u32[]{:S(2)}) collective-permute-start(bf16[4,256,256]{2,1,0:T(8,128)(2,1)S(1)} %get-tuple-element.34), channel_id=1, source_target_pairs={{8,0},{12,4},{0,8},{4,12},{9,1},{13,5},{1,9},{5,13},{10,2},{14,6},... | collective-permute-start | bytes 1572872 | tf_op jit(solution)/shard_map/ppermute | solution.py:430
  21.9 35.2 %collective-permute-start.5 = (bf16[4,256,256]{2,1,0:T(8,128)(2,1)S(1)}, bf16[4,256,256]{2,1,0:T(8,128)(2,1)S(1)}, u32[]{:S(2)}, u32[]{:S(2)}) collective-permute-start(bf16[4,256,256]{2,1,0:T(8,128)(2,1)S(1)} %get-tuple-element.35), channel_id=1, source_target_pairs={{12,0},{8,4},{4,8},{0,12},{13,1},{9,5},{5,9},{1,13},{14,2},{10,6},... | collective-permute-start | bytes 1572872 | tf_op jit(solution)/shard_map/ppermute | solution.py:430
  22.1 1.6 %copy-start.2 = (bf16[16,256,256]{2,1,0:T(8,128)(2,1)S(1)}, bf16[16,256,256]{2,1,0:T(8,128)(2,1)}, u32[]{:S(2)}) copy-start(bf16[16,256,256]{2,1,0:T(8,128)(2,1)} %refs_3_.7) | copy-start | bytes 6291460
  23.7 1.6 %copy-start.4 = (bf16[16,256,256]{2,1,0:T(8,128)(2,1)S(1)}, bf16[16,256,256]{2,1,0:T(8,128)(2,1)}, u32[]{:S(2)}) copy-start(bf16[16,256,256]{2,1,0:T(8,128)(2,1)} %refs_4_.1) | copy-start | bytes 6291460
  59.0 2.5 %collective-permute-start.7 = (bf16[4,256,256]{2,1,0:T(8,128)(2,1)S(1)}, bf16[4,256,256]{2,1,0:T(8,128)(2,1)S(1)}, u32[]{:S(2)}, u32[]{:S(2)}) collective-permute-start(bf16[4,256,256]{2,1,0:T(8,128)(2,1)S(1)} %finish.5.refs_2_.refs_4_.refs_5_), channel_id=1, source_target_pairs={{0,1},{1,0},{2,3},{3,2},{4,5},{5,4},{6,7},{7,6},{8,9},{9,8},{10,11... | collective-permute-start | bytes 1572872 | tf_op jit(solution)/shard_map/ppermute | solution.py:444
  61.0 2.1 %collective-permute-start.6 = (bf16[4,256,256]{2,1,0:T(8,128)(2,1)S(1)}, bf16[4,256,256]{2,1,0:T(8,128)(2,1)S(1)}, u32[]{:S(2)}, u32[]{:S(2)}) collective-permute-start(bf16[4,256,256]{2,1,0:T(8,128)(2,1)S(1)} %finish.4.refs_0_.refs_2_.refs_3_), channel_id=1, source_target_pairs={{0,1},{1,0},{2,3},{3,2},{4,5},{5,4},{6,7},{7,6},{8,9},{9,8},{10,11... | collective-permute-start | bytes 1572872 | tf_op jit(solution)/shard_map/ppermute | solution.py:440
  66.1 33.1 %collective-permute-start.8 = (bf16[4,256,256]{2,1,0:T(8,128)(2,1)S(1)}, bf16[4,256,256]{2,1,0:T(8,128)(2,1)S(1)}, u32[]{:S(2)}, u32[]{:S(2)}) collective-permute-start(bf16[4,256,256]{2,1,0:T(8,128)(2,1)S(1)} %get-tuple-element.54), channel_id=1, source_target_pairs={{4,0},{0,4},{12,8},{8,12},{5,1},{1,5},{13,9},{9,13},{6,2},{2,6},{1... | collective-permute-start | bytes 1572872 | tf_op jit(solution)/shard_map/ppermute | solution.py:430
  76.1 38.2 %collective-permute-start.9 = (bf16[4,256,256]{2,1,0:T(8,128)(2,1)S(1)}, bf16[4,256,256]{2,1,0:T(8,128)(2,1)S(1)}, u32[]{:S(2)}, u32[]{:S(2)}) collective-permute-start(bf16[4,256,256]{2,1,0:T(8,128)(2,1)S(1)} %get-tuple-element.55), channel_id=1, source_target_pairs={{8,0},{12,4},{0,8},{4,12},{9,1},{13,5},{1,9},{5,13},{10,2},{14,6},... | collective-permute-start | bytes 1572872 | tf_op jit(solution)/shard_map/ppermute | solution.py:430
  77.1 1.6 %copy-start.3 = (bf16[16,256,256]{2,1,0:T(8,128)(2,1)S(1)}, bf16[16,256,256]{2,1,0:T(8,128)(2,1)}, u32[]{:S(2)}) copy-start(bf16[16,256,256]{2,1,0:T(8,128)(2,1)} %refs_3_.7) | copy-start | bytes 6291460
  77.1 2.2 %copy-start.5 = (bf16[16,256,256]{2,1,0:T(8,128)(2,1)S(1)}, bf16[16,256,256]{2,1,0:T(8,128)(2,1)}, u32[]{:S(2)}) copy-start(bf16[16,256,256]{2,1,0:T(8,128)(2,1)} %refs_4_.1) | copy-start | bytes 6291460
  77.1 40.0 %collective-permute-start.10 = (bf16[4,256,256]{2,1,0:T(8,128)(2,1)S(1)}, bf16[4,256,256]{2,1,0:T(8,128)(2,1)S(1)}, u32[]{:S(2)}, u32[]{:S(2)}) collective-permute-start(bf16[4,256,256]{2,1,0:T(8,128)(2,1)S(1)} %get-tuple-element.57), channel_id=1, source_target_pairs={{12,0},{8,4},{4,8},{0,12},{13,1},{9,5},{5,9},{1,13},{14,2},{10,6},... | collective-permute-start | bytes 1572872 | tf_op jit(solution)/shard_map/ppermute | solution.py:430
  117.1 8.6 %collective-permute-start.13 = (bf16[4,256,256]{2,1,0:T(8,128)(2,1)S(1)}, bf16[4,256,256]{2,1,0:T(8,128)(2,1)S(1)}, u32[]{:S(2)}, u32[]{:S(2)}) collective-permute-start(bf16[4,256,256]{2,1,0:T(8,128)(2,1)S(1)} %get-tuple-element.60.refs_0_), channel_id=1, source_target_pairs={{0,1},{1,0},{2,3},{3,2},{4,5},{5,4},{6,7},{7,6},{8,9},{9,8},{10,11... | collective-permute-start | bytes 1572872 | tf_op jit(solution)/shard_map/ppermute | solution.py:440
  120.0 5.7 %collective-permute-start.14 = (bf16[4,256,256]{2,1,0:T(8,128)(2,1)S(1)}, bf16[4,256,256]{2,1,0:T(8,128)(2,1)S(1)}, u32[]{:S(2)}, u32[]{:S(2)}) collective-permute-start(bf16[4,256,256]{2,1,0:T(8,128)(2,1)S(1)} %get-tuple-element.61.refs_2_), channel_id=1, source_target_pairs={{0,1},{1,0},{2,3},{3,2},{4,5},{5,4},{6,7},{7,6},{8,9},{9,8},{10,11... | collective-permute-start | bytes 1572872 | tf_op jit(solution)/shard_map/ppermute | solution.py:444
  120.6 1.5 %collective-permute-start.11 = (f32[64]{0:T(128)S(1)}, f32[64]{0:T(128)S(1)}, u32[]{:S(2)}, u32[]{:S(2)}) collective-permute-start(f32[64]{0:T(128)S(1)} %add_bitcast_fusion), channel_id=1, source_target_pairs={{0,1},{1,0},{2,3},{3,2},{4,5},{5,4},{6,7},{7,6},{8,9},{9,8},{10,11... | collective-permute-start | bytes 776 | tf_op jit(solution)/shard_map/ppermute | solution.py:308
  122.1 3.6 %collective-permute-start.12 = (f32[64]{0:T(128)S(1)}, f32[64]{0:T(128)S(1)}, u32[]{:S(2)}, u32[]{:S(2)}) collective-permute-start(f32[64]{0:T(128)S(1)} %add.126), channel_id=1, source_target_pairs={{0,2},{2,0},{1,3},{3,1},{4,6},{6,4},{5,7},{7,5},{8,10},{10,8},{9,1... | collective-permute-start | bytes 776 | tf_op jit(solution)/shard_map/ppermute | solution.py:308
  127.7 9.5 %collective-permute-start.15 = (f32[64]{0:T(128)S(1)}, f32[64]{0:T(128)S(1)}, u32[]{:S(2)}, u32[]{:S(2)}) collective-permute-start(f32[64]{0:T(128)S(1)} %add.127), channel_id=1, source_target_pairs={{0,4},{4,0},{8,12},{12,8},{1,5},{5,1},{9,13},{13,9},{2,6},{6,2},{1... | collective-permute-start | bytes 776 | tf_op jit(solution)/shard_map/ppermute | solution.py:308
  137.2 4.5 %collective-permute-start.16 = (f32[64]{0:T(128)S(1)}, f32[64]{0:T(128)S(1)}, u32[]{:S(2)}, u32[]{:S(2)}) collective-permute-start(f32[64]{0:T(128)S(1)} %add.128), channel_id=1, source_target_pairs={{0,8},{4,12},{8,0},{12,4},{1,9},{5,13},{9,1},{13,5},{2,10},{6,14},... | collective-permute-start | bytes 776 | tf_op jit(solution)/shard_map/ppermute | solution.py:308

commit v3 on v2

--- a/solution.py
+++ b/solution.py
@@ -5,6 +5,7 @@
 from jax.experimental.pallas import tpu as pltpu
 from jax.sharding import PartitionSpec as P
 
+
 ITERS = 2
 ANY = pl.ANY
 SMEM = pltpu.SMEM
@@ -37,12 +38,12 @@
     return pl.CostEstimate(flops=flops, transcendentals=0, bytes_accessed=size)
 
 
-def fetch(candidates, spot, target, sem):
+def fetch(candidates, spot, target):
     for offset, ref in candidates:
 
         @pl.when((spot >= offset) & (spot < offset + ref.shape[0]))
         def _(offset=offset, ref=ref):
-            pltpu.make_async_copy(ref.at[spot - offset], target, sem).start()
+            target[...] = ref[spot - offset]
 
 
 def laid(refs, offset=0):
@@ -61,46 +62,36 @@
         lists = refs[: rows - 1]
         store = refs[rows - 1]
         asked = refs[rows]
-        outs = refs[rows + 1 : 2 * rows]
-        sem = refs[-1]
+        outs = refs[rows + 1 :]
         me = place_ref[0]
         core = place_ref[1]
-        for b in range(blocks):
-            asked[b] = 0
         for shift in range(1, rows):
+            base = (shift - 1) * (cap + 1)
             asker = apart(rows, me, shift) if rows & (rows - 1) == 0 else (me + shift) % rows
+            for k in range(cap):
+                asked[base + k] = 0
             sources = [lists[shift - 1][p] // pairs for p in range(pairs)]
             count = jnp.int32(0)
             for p in range(pairs):
                 count = count + (apart(rows, sources[p], asker) < shift).astype(jnp.int32)
-            filled = jnp.int32((shift - 1) * cap)
+            filled = jnp.int32(0)
             for p in range(pairs):
                 mine = sources[p] == me
                 taken = mine & (count % 2 == core)
-
-                @pl.when(taken)
-                def _(filled=filled, p=p, shift=shift):
-                    asked[filled] = lists[shift - 1][p] % pairs
-
+                asked[base + jnp.minimum(filled, cap)] = lists[shift - 1][p] % pairs
                 count = count + mine.astype(jnp.int32)
-                filled = jnp.minimum(filled + taken.astype(jnp.int32), shift * cap - 1)
+                filled = filled + taken.astype(jnp.int32)
             for k in range(cap):
-                b = (shift - 1) * cap + k
-                pltpu.make_async_copy(
-                    store.at[asked[b]], outs[shift - 1].at[k], sem.at[b]
-                ).start()
-        for b in range(blocks):
-            pltpu.make_async_copy(store.at[0], outs[b // cap].at[b % cap], sem.at[b]).wait()
+                outs[shift - 1][k] = store[asked[base + k]]
 
     shape = (cap, domain, domain)
     return pl.pallas_call(
         body,
-        out_shape=[jax.ShapeDtypeStruct((blocks,), jnp.int32)]
+        out_shape=[jax.ShapeDtypeStruct(((rows - 1) * (cap + 1),), jnp.int32)]
         + [VMEM(shape, jnp.bfloat16)] * (rows - 1),
-        in_specs=[pl.BlockSpec(memory_space=SMEM)] * rows + [pl.BlockSpec(memory_space=ANY)],
+        in_specs=[pl.BlockSpec(memory_space=SMEM)] * rows + [pl.BlockSpec(memory_space=VMEM)],
         out_specs=[pl.BlockSpec(memory_space=SMEM)]
         + [pl.BlockSpec(memory_space=VMEM)] * (rows - 1),
-        scratch_shapes=[pltpu.SemaphoreType.DMA((blocks,))],
         cost_estimate=cost(0, blocks * domain * domain * 4),
         compiler_params=limits(8),
         name="gather_first",
@@ -113,22 +104,17 @@
 
     def body(asked_ref, where_ref, *refs):
         sources = laid(refs[: len(stores)])
-        outs = refs[len(stores) : len(stores) + rows - 1]
-        sem = refs[-1]
+        outs = refs[len(stores) :]
         for b in range(blocks):
-            fetch(sources, where_ref[asked_ref[b]], outs[b // cap].at[b % cap], sem.at[b])
-        for b in range(blocks):
-            pltpu.make_async_copy(
-                sources[0][1].at[0], outs[b // cap].at[b % cap], sem.at[b]
-            ).wait()
+            spot = where_ref[asked_ref[b // cap * (cap + 1) + b % cap]]
+            fetch(sources, spot, outs[b // cap].at[b % cap])
 
     return pl.pallas_call(
         body,
         out_shape=[VMEM((cap, domain, domain), jnp.bfloat16)] * (rows - 1),
         in_specs=[pl.BlockSpec(memory_space=SMEM)] * 2
-        + [pl.BlockSpec(memory_space=ANY)] * len(stores),
+        + [pl.BlockSpec(memory_space=VMEM)] * len(stores),
         out_specs=[pl.BlockSpec(memory_space=VMEM)] * (rows - 1),
-        scratch_shapes=[pltpu.SemaphoreType.DMA((blocks,))],
         cost_estimate=cost(0, blocks * domain * domain * 4),
         compiler_params=limits(8),
         name="gather_again",
@@ -209,18 +195,16 @@
         candidates = [
             (offset, ref) for offset, ref in zip([o for o, _ in arrived + stores], refs)
         ]
-        outs = refs[len(candidates) : -2]
-        hold, sem = refs[-2:]
+        outs = refs[len(candidates) : -1]
+        hold = refs[-1]
         for n in range(count):
-            fetch(candidates, number_ref[start + n], hold.at[n], sem.at[n])
+            fetch(candidates, number_ref[start + n], hold.at[n])
         if last:
             row_id = lax.broadcasted_iota(jnp.int32, (domain, domain), 0)
             col_id = lax.broadcasted_iota(jnp.int32, (domain, domain), 1)
             on_diagonal = row_id == col_id
             orbital = lax.broadcasted_iota(jnp.int32, (1, occ_count), 1)
             density = jnp.zeros((1, occ_count), jnp.float32)
-        for n in range(count):
-            pltpu.make_async_copy(candidates[0][1].at[0], hold.at[n], sem.at[n]).wait()
         for n in range(count):
             i = start + n
             coupled = local_ref[i] + scale_ref[i] * hold[n].astype(jnp.float32)
@@ -255,12 +239,9 @@
         out_shape=out_shape,
         in_specs=[pl.BlockSpec(memory_space=SMEM)] * 2
         + [pl.BlockSpec(memory_space=VMEM)] * 4
-        + [pl.BlockSpec(memory_space=ANY)] * len(arrived + stores),
+        + [pl.BlockSpec(memory_space=VMEM)] * len(arrived + stores),
         out_specs=[pl.BlockSpec(memory_space=VMEM)] * len(out_shape),
-        scratch_shapes=[
-            VMEM((count, domain, domain), jnp.bfloat16),
-            pltpu.SemaphoreType.DMA((count,)),
-        ],
+        scratch_shapes=[VMEM((count, domain, domain), jnp.bfloat16)],
         cost_estimate=cost(2 * count * domain**3 * 2, count * domain * domain * 18),
         compiler_params=limits(16),
         name="finish",
@@ -338,6 +319,9 @@
     requests = [lax.ppermute(packed, "row", exchanges(rows, d)) for d in range(1, rows)]
     here = jnp.stack([row, core]).astype(jnp.int32)
     asked, *sends = gather_first(requests, here, amplitudes, rows, cap)
+    source, far_slot, near_slot, near_count, near_weight, far_weight, *_ = lax.optimization_barrier(
+        (source, far_slot, near_slot, near_count, near_weight, far_weight, asked)
+    )
 
     step = apart(rows, source, row)
     same = step[:, None] == step[None, :]
@@ -405,7 +389,7 @@
         ),
     ]
     tables = []
-    for where in local_spots:
+    for where in (slot_ids, by_slot):
         at_home = remote + jnp.sum(
             jnp.where(own_far[:, None] == slot_ids[None, :], where[None, :], 0), axis=1
         )
@@ -414,32 +398,29 @@
     spreads = [spread_of(own_weights), spread_of(by_core)]
     ats = [own, jnp.arange(half, dtype=jnp.int32)]
     slots = jnp.concatenate([own[:early], other[:early], own[early:], other[early:]])
-    (own, shift, far_scale, *moved) = lax.optimization_barrier(
-        (own, shift, far_scale, *tables, *spreads, *ats, slots, *sends)
-    )
-    tables, spreads, ats, slots = moved[:2], moved[2:4], moved[4:6], moved[6]
-
     stores = [amplitudes]
     whole = [amplitudes]
     for sweep in range(ITERS):
         last = sweep == ITERS - 1
-        late = min(sweep, 1)
+        again = min(sweep, 1)
         if sweep > 0:
-            sends = gather_again(asked, local_spots[late], stores, rows, cap)
-        arrived = [
-            lax.ppermute(block, "row", returns(rows, d)) for d, block in enumerate(sends, 1)
-        ]
+            sends = gather_again(asked, local_spots[again], stores, rows, cap)
+        arrived = []
+        for d in range(1, rows):
+            arrived.append(lax.ppermute(sends[d - 1], "row", returns(rows, d)))
         prepared = prepare(
-            own, ats[late], shift, spreads[late], whole, integrals, fock_matrix, intersection
+            own, ats[again], shift, spreads[again], whole,
+            integrals, fock_matrix, intersection,
         )
         spots = laid(arrived)
-        homes = laid(stores, remote)
+        homes = laid(whole, remote)
         done_early = finish(
-            0, early, tables[late], far_scale, prepared, spots[:-1], homes, occ_count, last
+            0, early, tables[again], far_scale, prepared, spots[:-1], homes, occ_count,
+            last,
         )
         given_early = lax.ppermute(done_early[0], "rep", swap)
         done_late = finish(
-            early, cap, tables[late], far_scale, prepared, spots, homes, occ_count, last
+            early, cap, tables[again], far_scale, prepared, spots, homes, occ_count, last
         )
         given_late = lax.ppermute(done_late[0], "rep", swap)
         stores = [done_early[0], given_early, done_late[0], given_late]
@@ -449,8 +430,8 @@
         ]
     final = put_in_slots(slots, stores)
     occ_sum = (done_early[1] + done_late[1])[0]
-    occ_sum = add_over(add_over(occ_sum, "rep"), "col")
-    occ_sum, final = lax.optimization_barrier((occ_sum, final))
+    occ_sum = add_over(occ_sum, "rep")
+    occ_sum = add_over(occ_sum, "col")
     occ_sum = add_over(occ_sum, "row")
     total_pairs = pairs * rows * lax.axis_size("col")
     occ_density = occ_sum * (occ_count / (2.0 * total_pairs * domain * domain))

time: 143 us -> 139 us (0.972)
  local copies, waits for them, and re-layouts: 6.46 us -> 17.3 us
  waiting for transfers between devices: 68.8 us -> 62.4 us
  Pallas kernels: 24.8 us -> 20.6 us
  starting transfers between devices: 36.3 us -> 33.1 us
    ppermute x6, waiting for transfers between devices: 60.7 us -> 51.3 us  [per_device(): arrived.append(lax.ppermute(sends[d - 1], 'row', returns(rows, d)))]
    unnamed x23 -> x53, local copies, waits for them, and re-layouts: 4.62 us -> 12.9 us
    ppermute x3, waiting for transfers between devices: 0.01 us -> 3.8 us  [per_device(): lax.ppermute(packed, 'row', exchanges(rows, d))]
    ppermute x6, starting transfers between devices: 16.8 us -> 13.4 us  [per_device(): arrived.append(lax.ppermute(sends[d - 1], 'row', returns(rows, d)))]
    pallas_call x1, Pallas kernels: 4.34 us -> 1.98 us  [gather_first(): pl.pallas_call(body, out_shape=[jax.ShapeDtypeStruct(((rows - 1) * (cap +...]
    select_n x2, local copies, waits for them, and re-layouts: 0.92 us -> 2.98 us  [spread_of(): jnp.where(unit[None, :, None, :], table[:, None, :, None], jnp.zeros((),...]
    ppermute x2, waiting for transfers between devices: 0.01 us -> 1.54 us  [per_device(): given_late = lax.ppermute(done_late[0], 'rep', swap)]
    ppermute x2, waiting for transfers between devices: 1.54 us -> 0.01 us  [per_device(): given_early = lax.ppermute(done_early[0], 'rep', swap)]
  transfers between devices with their start and end apart: 17 -> 17, of which waited for: 9 -> 11; matrix products, arithmetic and copies ran while one was open for 4% -> 6% of each run, Pallas kernels for 10% -> 8%
where the time goes in v3:
time: 139 us
  waiting for transfers between devices  62.4 us (45%)
  starting transfers between devices  33.1 us (24%)
  Pallas kernels  20.6 us (15%)
  local copies, waits for them, and re-layouts  17.3 us (12%)
  other arithmetic  4.35 us (3%)
    ppermute x6, waiting for transfers between devices, per_device(): arrived.append(lax.ppermute(sends[d - 1], 'row', returns(rows, d)))  51.3 us
    ppermute x6, starting transfers between devices, per_device(): arrived.append(lax.ppermute(sends[d - 1], 'row', returns(rows, d)))  13.4 us
    ppermute x4, starting transfers between devices, add_over(): lax.ppermute(values, name, [(r, r ^ step) for r in range(size)])  12.9 us
    unnamed x53, local copies, waits for them, and re-layouts  12.9 us
    pallas_call x4, Pallas kernels, finish(): pl.pallas_call(body, out_shape=out_shape, in_specs=[pl.BlockSpec(memory_s...  8.54 us
    pallas_call x2, Pallas kernels, prepare(): pl.pallas_call(body, grid_spec=pltpu.PrefetchScalarGridSpec(num_scalar_pr...  5.89 us
    ppermute x4, waiting for transfers between devices, add_over(): lax.ppermute(values, name, [(r, r ^ step) for r in range(size)])  5.66 us
    ppermute x3, starting transfers between devices, per_device(): lax.ppermute(packed, 'row', exchanges(rows, d))  5.64 us
  transfers between devices with their start and end apart: 17, of which 11 were waited for; matrix products, arithmetic and copies ran while one was open for 6% of the time, Pallas kernels for 8%

profile of v3, /device:TPU:0, one launch (start us, length us, event | category | flops | bytes accessed | tf_op | source)
XLA Modules:
  0.0 138.7 jit_solution(9378037805274469650)
XLA Ops:
  1.4 5.1 %collective-permute-start.2 = (s32[16]{0:T(128)S(1)}, s32[16]{0:T(128)S(1)}, u32[]{:S(2)}, u32[]{:S(2)}) collective-permute-start(s32[16]{0:T(128)S(1)} %bitcast_add_fusion), channel_id=1, source_target_pairs={{0,12},{4,8},{8,4},{12,0},{1,13},{5,9},{9,5},{13,1},{2,14},{6,10},... | collective-permute-start | bytes 200 | tf_op jit(solution)/shard_map/ppermute | solution.py:319
  8.0 2.9 %collective-permute-done.1.refs_1_ = s32[16]{0:T(128)S(1)} collective-permute-done((s32[16]{0:T(128)S(1)}, s32[16]{0:T(128)S(1)}, u32[]{:S(2)}, u32[]{:S(2)}) %collective-permute-start.1) | collective-permute-done | bytes 96 | tf_op jit(solution)/shard_map/ppermute | solution.py:319
  10.9 1.6 %copy-done = bf16[16,256,256]{2,1,0:T(8,128)(2,1)S(1)} copy-done((bf16[16,256,256]{2,1,0:T(8,128)(2,1)S(1)}, bf16[16,256,256]{2,1,0:T(8,128)(2,1)}, u32[]{:S(2)}) %copy-start) | copy-done | bytes 2097176
  12.5 2.0 %gather_first.1 = (s32[15]{0:T(128)S(1)}, bf16[4,256,256]{2,1,0:T(8,128)(2,1)}, bf16[4,256,256]{2,1,0:T(8,128)(2,1)S(1)}, bf16[4,256,256]{2,1,0:T(8,128)(2,1)S(1)}) custom-call(s32[2]{0:T(128)S(1)} %pad_add_fusion.place_ref, s32[16]{0:T(128)S(1)} %collective-permute-done.refs_0_, s32[16]{0:T(128)S(1)} %collective-permute-done.1.refs_1_, ...), custom_call_target="tpu_custom_call" | custom-call | bytes 3145728 | tf_op jit(solution)/shard_map/gather_first/pallas_call | solution.py:88
  17.3 2.1 %collective-permute-start.4 = (bf16[4,256,256]{2,1,0:T(8,128)(2,1)}, bf16[4,256,256]{2,1,0:T(8,128)(2,1)S(1)}, u32[]{:S(2)}, u32[]{:S(2)}) collective-permute-start(bf16[4,256,256]{2,1,0:T(8,128)(2,1)} %copy-done.16), channel_id=1, source_target_pairs={{8,0},{12,4},{0,8},{4,12},{9,1},{13,5},{1,9},{5,13},{10,2},{14,6},... | collective-permute-start | bytes 1572872 | tf_op jit(solution)/shard_map/ppermute | solution.py:410
  19.3 2.3 %collective-permute-start.5 = (bf16[4,256,256]{2,1,0:T(8,128)(2,1)}, bf16[4,256,256]{2,1,0:T(8,128)(2,1)}, u32[]{:S(2)}, u32[]{:S(2)}) collective-permute-start(bf16[4,256,256]{2,1,0:T(8,128)(2,1)} %copy-done.15), channel_id=1, source_target_pairs={{12,0},{8,4},{4,8},{0,12},{13,1},{9,5},{5,9},{1,13},{14,2},{10,6},... | collective-permute-start | bytes 1572872 | tf_op jit(solution)/shard_map/ppermute | solution.py:410
  22.7 1.5 %select_n.161.spread_ref = bf16[128,256]{1,0:T(8,128)(2,1)S(1)} reshape(bf16[8,16,16,16]{3,2,1,0:T(8,128)(2,1)} %get-tuple-element.68) | data formatting | bytes 131072 | tf_op jit(solution)/shard_map/jit(_where)/select_n | solution.py:374
  25.0 1.6 %copy-done.2 = bf16[16,256,256]{2,1,0:T(8,128)(2,1)S(1)} copy-done((bf16[16,256,256]{2,1,0:T(8,128)(2,1)S(1)}, bf16[16,256,256]{2,1,0:T(8,128)(2,1)}, u32[]{:S(2)}) %copy-start.2) | copy-done | bytes 2097176
  26.6 1.6 %copy-done.4 = bf16[16,256,256]{2,1,0:T(8,128)(2,1)S(1)} copy-done((bf16[16,256,256]{2,1,0:T(8,128)(2,1)S(1)}, bf16[16,256,256]{2,1,0:T(8,128)(2,1)}, u32[]{:S(2)}) %copy-start.4) | copy-done | bytes 2097176
  28.2 1.6 %copy-done.6 = bf16[16,256,256]{2,1,0:T(8,128)(2,1)S(1)} copy-done((bf16[16,256,256]{2,1,0:T(8,128)(2,1)S(1)}, bf16[16,256,256]{2,1,0:T(8,128)(2,1)}, u32[]{:S(2)}) %copy-start.6) | copy-done | bytes 2097176
  29.8 3.0 %prepare.2 = (f32[8,256,256]{2,1,0:T(8,128)S(1)}, f32[8,256,256]{2,1,0:T(8,128)S(1)}, f32[8,256,256]{2,1,0:T(8,128)S(1)}, bf16[8,256,256]{2,1,0:T(8,128)(2,1)S(1)}) custom-call(s32[8]{0:T(128)S(1)} %get-tuple-element.59.own_ref.at_ref, s32[8]{0:T(128)S(1)} %get-tuple-element.59.own_ref.at_ref, f32[8]{0:T(128)S(1)} %add.104.shift_ref, ...), custom_call_target="tpu_custom_call" | custom-call | flops 805306368 | bytes 12582912 | tf_op jit(solution)/shard_map/prepare/pallas_call | solution.py:161
  33.0 7.2 %collective-permute-done.3.refs_0_ = bf16[4,256,256]{2,1,0:T(8,128)(2,1)S(1)} collective-permute-done((bf16[4,256,256]{2,1,0:T(8,128)(2,1)}, bf16[4,256,256]{2,1,0:T(8,128)(2,1)S(1)}, u32[]{:S(2)}, u32[]{:S(2)}) %collective-permute-start.3) | collective-permute-done | bytes 524320 | tf_op jit(solution)/shard_map/ppermute | solution.py:410
  40.2 15.5 %collective-permute-done.4.refs_1_ = bf16[4,256,256]{2,1,0:T(8,128)(2,1)S(1)} collective-permute-done((bf16[4,256,256]{2,1,0:T(8,128)(2,1)}, bf16[4,256,256]{2,1,0:T(8,128)(2,1)S(1)}, u32[]{:S(2)}, u32[]{:S(2)}) %collective-permute-start.4) | collective-permute-done | bytes 524320 | tf_op jit(solution)/shard_map/ppermute | solution.py:410
  59.9 1.7 %finish.5.refs_2_ = bf16[4,256,256]{2,1,0:T(8,128)(2,1)S(1)} custom-call(s32[24]{0:T(128)S(1)} %get-tuple-element.70.number_ref, f32[8]{0:T(128)S(1)} %fusion.9.scale_ref, f32[8,256,256]{2,1,0:T(8,128)S(1)} %get-tuple-element.34.local_ref, f32[8,256,256]{2,1,0:T(8,128)S(1)} %get-tuple-element.35.rest_ref, f32[8,256,256]{2,1,0:T(8,128)S(1)} %get-tuple-element.36.recip_ref, ...), custom_call_target="tpu_custom_call" | custom-call | flops 268435456 | bytes 4718592 | tf_op jit(solution)/shard_map/finish/pallas_call | solution.py:237
  62.2 1.5 %collective-permute-done.7.refs_3_ = bf16[4,256,256]{2,1,0:T(8,128)(2,1)S(1)} collective-permute-done((bf16[4,256,256]{2,1,0:T(8,128)(2,1)S(1)}, bf16[4,256,256]{2,1,0:T(8,128)(2,1)S(1)}, u32[]{:S(2)}, u32[]{:S(2)}) %collective-permute-start.7) | collective-permute-done | bytes 524320 | tf_op jit(solution)/shard_map/ppermute | solution.py:425
  63.7 2.2 %gather_again.1 = (bf16[4,256,256]{2,1,0:T(8,128)(2,1)}, bf16[4,256,256]{2,1,0:T(8,128)(2,1)}, bf16[4,256,256]{2,1,0:T(8,128)(2,1)}) custom-call(s32[15]{0:T(128)S(1)} %get-tuple-element.27.asked_ref, s32[16]{0:T(128)S(1)} %get-tuple-element.65.where_ref, bf16[4,256,256]{2,1,0:T(8,128)(2,1)S(1)} %finish.4.refs_0_, ...), custom_call_target="tpu_custom_call" | custom-call | bytes 3145728 | tf_op jit(solution)/shard_map/gather_again/pallas_call | solution.py:112
  66.7 6.1 %collective-permute-start.8 = (bf16[4,256,256]{2,1,0:T(8,128)(2,1)}, bf16[4,256,256]{2,1,0:T(8,128)(2,1)}, u32[]{:S(2)}, u32[]{:S(2)}) collective-permute-start(bf16[4,256,256]{2,1,0:T(8,128)(2,1)} %get-tuple-element.45), channel_id=1, source_target_pairs={{4,0},{0,4},{12,8},{8,12},{5,1},{1,5},{13,9},{9,13},{6,2},{2,6},{1... | collective-permute-start | bytes 1572872 | tf_op jit(solution)/shard_map/ppermute | solution.py:410
  72.8 1.4 %collective-permute-start.9 = (bf16[4,256,256]{2,1,0:T(8,128)(2,1)}, bf16[4,256,256]{2,1,0:T(8,128)(2,1)}, u32[]{:S(2)}, u32[]{:S(2)}) collective-permute-start(bf16[4,256,256]{2,1,0:T(8,128)(2,1)} %get-tuple-element.46), channel_id=1, source_target_pairs={{8,0},{12,4},{0,8},{4,12},{9,1},{13,5},{1,9},{5,13},{10,2},{14,6},... | collective-permute-start | bytes 1572872 | tf_op jit(solution)/shard_map/ppermute | solution.py:410
  74.2 1.5 %collective-permute-start.11 = (bf16[4,256,256]{2,1,0:T(8,128)(2,1)}, bf16[4,256,256]{2,1,0:T(8,128)(2,1)}, u32[]{:S(2)}, u32[]{:S(2)}) collective-permute-start(bf16[4,256,256]{2,1,0:T(8,128)(2,1)} %get-tuple-element.48), channel_id=1, source_target_pairs={{12,0},{8,4},{4,8},{0,12},{13,1},{9,5},{5,9},{1,13},{14,2},{10,6},... | collective-permute-start | bytes 1572872 | tf_op jit(solution)/shard_map/ppermute | solution.py:410
  75.7 1.5 %select_n.157.spread_ref = bf16[128,256]{1,0:T(8,128)(2,1)S(1)} reshape(bf16[8,16,16,16]{3,2,1,0:T(8,128)(2,1)} %get-tuple-element.69) | data formatting | bytes 131072 | tf_op jit(solution)/shard_map/jit(_where)/select_n | solution.py:374
  79.7 2.9 %prepare.3 = (f32[8,256,256]{2,1,0:T(8,128)S(1)}, f32[8,256,256]{2,1,0:T(8,128)S(1)}, f32[8,256,256]{2,1,0:T(8,128)S(1)}, bf16[8,256,256]{2,1,0:T(8,128)(2,1)S(1)}) custom-call(s32[8]{0:T(128)S(1)} %get-tuple-element.59.own_ref.at_ref, s32[8]{0:T(128)S(1)} %iota.43.at_ref, f32[8]{0:T(128)S(1)} %add.104.shift_ref, bf16[128,256]{1,0:T(8,128)(2,1)S(1)} %select_n.157.spread_ref, ...), custom_call_target="tpu_custom_call" | custom-call | flops 805306368 | bytes 12582912 | tf_op jit(solution)/shard_map/prepare/pallas_call | solution.py:161
  82.6 13.5 %collective-permute-done.8.refs_0_ = bf16[4,256,256]{2,1,0:T(8,128)(2,1)} collective-permute-done((bf16[4,256,256]{2,1,0:T(8,128)(2,1)}, bf16[4,256,256]{2,1,0:T(8,128)(2,1)}, u32[]{:S(2)}, u32[]{:S(2)}) %collective-permute-start.8) | collective-permute-done | bytes 524320 | tf_op jit(solution)/shard_map/ppermute | solution.py:410
  96.2 15.1 %collective-permute-done.9.refs_1_ = bf16[4,256,256]{2,1,0:T(8,128)(2,1)} collective-permute-done((bf16[4,256,256]{2,1,0:T(8,128)(2,1)}, bf16[4,256,256]{2,1,0:T(8,128)(2,1)}, u32[]{:S(2)}, u32[]{:S(2)}) %collective-permute-start.9) | collective-permute-done | bytes 524320 | tf_op jit(solution)/shard_map/ppermute | solution.py:410
  111.3 2.7 %finish.6 = (bf16[4,256,256]{2,1,0:T(8,128)(2,1)S(1)}, f32[1,64]{1,0:T(1,128)S(1)}) custom-call(s32[24]{0:T(128)S(1)} %get-tuple-element.71.number_ref, f32[8]{0:T(128)S(1)} %fusion.9.scale_ref, f32[8,256,256]{2,1,0:T(8,128)S(1)} %get-tuple-element.41.local_ref, f32[8,256,256]{2,1,0:T(8,128)S(1)} %get-tuple-element.42.rest_ref, ...), custom_call_target="tpu_custom_call" | custom-call | flops 268435456 | bytes 4718592 | tf_op jit(solution)/shard_map/finish/pallas_call | solution.py:237
  114.0 2.9 %finish.7 = (bf16[4,256,256]{2,1,0:T(8,128)(2,1)S(1)}, f32[1,64]{1,0:T(1,128)S(1)}) custom-call(s32[24]{0:T(128)S(1)} %get-tuple-element.71.number_ref, f32[8]{0:T(128)S(1)} %fusion.9.scale_ref, f32[8,256,256]{2,1,0:T(8,128)S(1)} %get-tuple-element.41.local_ref, f32[8,256,256]{2,1,0:T(8,128)S(1)} %get-tuple-element.42.rest_ref, ...), custom_call_target="tpu_custom_call" | custom-call | flops 268435456 | bytes 4718592 | tf_op jit(solution)/shard_map/finish/pallas_call | solution.py:237
  118.1 1.5 %collective-permute-start.14 = (f32[64]{0:T(128)S(1)}, f32[64]{0:T(128)S(1)}, u32[]{:S(2)}, u32[]{:S(2)}) collective-permute-start(f32[64]{0:T(128)S(1)} %add.110), channel_id=1, source_target_pairs={{0,2},{2,0},{1,3},{3,1},{4,6},{6,4},{5,7},{7,5},{8,10},{10,8},{9,1... | collective-permute-start | bytes 776 | tf_op jit(solution)/shard_map/ppermute | solution.py:289
  120.1 1.6 %collective-permute-done.14 = f32[64]{0:T(128)S(1)} collective-permute-done((f32[64]{0:T(128)S(1)}, f32[64]{0:T(128)S(1)}, u32[]{:S(2)}, u32[]{:S(2)}) %collective-permute-start.14) | collective-permute-done | bytes 288 | tf_op jit(solution)/shard_map/ppermute | solution.py:289
  121.6 8.0 %collective-permute-start.15 = (f32[64]{0:T(128)S(1)}, f32[64]{0:T(128)S(1)}, u32[]{:S(2)}, u32[]{:S(2)}) collective-permute-start(f32[64]{0:T(128)S(1)} %add.111), channel_id=1, source_target_pairs={{0,4},{4,0},{8,12},{12,8},{1,5},{5,1},{9,13},{13,9},{2,6},{6,2},{1... | collective-permute-start | bytes 776 | tf_op jit(solution)/shard_map/ppermute | solution.py:289
  129.7 1.5 %collective-permute-done.15 = f32[64]{0:T(128)S(1)} collective-permute-done((f32[64]{0:T(128)S(1)}, f32[64]{0:T(128)S(1)}, u32[]{:S(2)}, u32[]{:S(2)}) %collective-permute-start.15) | collective-permute-done | bytes 288 | tf_op jit(solution)/shard_map/ppermute | solution.py:289
  131.2 3.4 %collective-permute-start.16 = (f32[64]{0:T(128)S(1)}, f32[64]{0:T(128)S(1)}, u32[]{:S(2)}, u32[]{:S(2)}) collective-permute-start(f32[64]{0:T(128)S(1)} %add.112), channel_id=1, source_target_pairs={{0,8},{4,12},{8,0},{12,4},{1,9},{5,13},{9,1},{13,5},{2,10},{6,14},... | collective-permute-start | bytes 776 | tf_op jit(solution)/shard_map/ppermute | solution.py:289
  134.7 1.5 %collective-permute-done.16 = f32[64]{0:T(128)S(1)} collective-permute-done((f32[64]{0:T(128)S(1)}, f32[64]{0:T(128)S(1)}, u32[]{:S(2)}, u32[]{:S(2)}) %collective-permute-start.16) | collective-permute-done | bytes 288 | tf_op jit(solution)/shard_map/ppermute | solution.py:289
  136.7 2.0 %put_in_slots.1 = bf16[16,256,256]{2,1,0:T(8,128)(2,1)} custom-call(s32[16]{0:T(128)S(1)} %pad_add_fusion.1.slot_ref, bf16[4,256,256]{2,1,0:T(8,128)(2,1)S(1)} %get-tuple-element.47.refs_0_, bf16[4,256,256]{2,1,0:T(8,128)(2,1)S(1)} %collective-permute-done.10.refs_1_, bf16[4,256,256]{2,1,0:T(8,128)(2,1)S(1)} %get-tuple-element.49.refs_2_, ...), custom_call_target="tpu_custom_call" | custom-call | bytes 4194304 | tf_op jit(solution)/shard_map/put_in_slots/pallas_call | solution.py:270
  (103 shorter events, 17.3 us)
Async XLA Ops:
  0.6 23.6 %copy-start.23 = (s32[16,1]{0,1:T(1,128)S(1)}, s32[16,1]{0,1:T(1,128)}, u32[]{:S(2)}) copy-start(s32[16,1]{0,1:T(1,128)} %param.24) | copy-start | bytes 196
  0.6 14.7 %copy-start.24 = (s32[16,1]{0,1:T(1,128)S(1)}, s32[16,1]{0,1:T(1,128)}, u32[]{:S(2)}) copy-start(s32[16,1]{0,1:T(1,128)} %param.23) | copy-start | bytes 196
  0.7 16.0 %copy-start.18 = (bf16[16,11]{1,0:T(8,128)(2,1)S(1)}, bf16[16,11]{1,0:T(8,128)(2,1)}, u32[]{:S(2)}) copy-start(bf16[16,11]{1,0:T(8,128)(2,1)} %param.22) | copy-start | bytes 1060
  0.7 15.8 %copy-start.19 = (s32[16]{0:T(128)S(1)}, s32[16]{0:T(128)}, u32[]{:S(2)}) copy-start(s32[16]{0:T(128)} %param.21) | copy-start | bytes 196
  0.7 15.9 %copy-start.17 = (s32[16,11]{1,0:T(8,128)S(1)}, s32[16,11]{1,0:T(8,128)}, u32[]{:S(2)}) copy-start(s32[16,11]{1,0:T(8,128)} %param.20) | copy-start | bytes 2116
  0.7 23.6 %copy-start.22 = (s32[16]{0:T(128)S(1)}, s32[16]{0:T(128)}, u32[]{:S(2)}) copy-start(s32[16]{0:T(128)} %param.19) | copy-start | bytes 196
  0.7 23.6 %copy-start.21 = (s32[16]{0:T(128)S(1)}, s32[16]{0:T(128)}, u32[]{:S(2)}) copy-start(s32[16]{0:T(128)} %param.18) | copy-start | bytes 196
  0.7 24.0 %copy-start.20 = (f32[64]{0:T(128)S(1)}, f32[64]{0:T(128)}, u32[]{:S(2)}) copy-start(f32[64]{0:T(128)} %param.17) | copy-start | bytes 772
  1.4 6.6 %collective-permute-start.2 = (s32[16]{0:T(128)S(1)}, s32[16]{0:T(128)S(1)}, u32[]{:S(2)}, u32[]{:S(2)}) collective-permute-start(s32[16]{0:T(128)S(1)} %bitcast_add_fusion), channel_id=1, source_target_pairs={{0,12},{4,8},{8,4},{12,0},{1,13},{5,9},{9,5},{13,1},{2,14},{6,10},... | collective-permute-start | bytes 200 | tf_op jit(solution)/shard_map/ppermute | solution.py:319
  6.5 4.5 %collective-permute-start.1 = (s32[16]{0:T(128)S(1)}, s32[16]{0:T(128)S(1)}, u32[]{:S(2)}, u32[]{:S(2)}) collective-permute-start(s32[16]{0:T(128)S(1)} %bitcast_add_fusion), channel_id=1, source_target_pairs={{0,8},{4,12},{8,0},{12,4},{1,9},{5,13},{9,1},{13,5},{2,10},{6,14},... | collective-permute-start | bytes 200 | tf_op jit(solution)/shard_map/ppermute | solution.py:319
  6.5 4.5 %collective-permute-start = (s32[16]{0:T(128)S(1)}, s32[16]{0:T(128)S(1)}, u32[]{:S(2)}, u32[]{:S(2)}) collective-permute-start(s32[16]{0:T(128)S(1)} %bitcast_add_fusion), channel_id=1, source_target_pairs={{0,4},{4,0},{8,12},{12,8},{1,5},{5,1},{9,13},{13,9},{2,6},{6,2},{1... | collective-permute-start | bytes 200 | tf_op jit(solution)/shard_map/ppermute | solution.py:319
  12.5 12.4 %copy-start.1 = (bf16[16,256,256]{2,1,0:T(8,128)(2,1)S(1)}, bf16[16,256,256]{2,1,0:T(8,128)(2,1)}, u32[]{:S(2)}) copy-start(bf16[16,256,256]{2,1,0:T(8,128)(2,1)} %refs_3_.6) | copy-start | bytes 6291460
  17.2 23.0 %collective-permute-start.3 = (bf16[4,256,256]{2,1,0:T(8,128)(2,1)}, bf16[4,256,256]{2,1,0:T(8,128)(2,1)S(1)}, u32[]{:S(2)}, u32[]{:S(2)}) collective-permute-start(bf16[4,256,256]{2,1,0:T(8,128)(2,1)} %get-tuple-element.38), channel_id=1, source_target_pairs={{4,0},{0,4},{12,8},{8,12},{5,1},{1,5},{13,9},{9,13},{6,2},{2,6},{1... | collective-permute-start | bytes 1572872 | tf_op jit(solution)/shard_map/ppermute | solution.py:410
  17.3 38.4 %collective-permute-start.4 = (bf16[4,256,256]{2,1,0:T(8,128)(2,1)}, bf16[4,256,256]{2,1,0:T(8,128)(2,1)S(1)}, u32[]{:S(2)}, u32[]{:S(2)}) collective-permute-start(bf16[4,256,256]{2,1,0:T(8,128)(2,1)} %copy-done.16), channel_id=1, source_target_pairs={{8,0},{12,4},{0,8},{4,12},{9,1},{13,5},{1,9},{5,13},{10,2},{14,6},... | collective-permute-start | bytes 1572872 | tf_op jit(solution)/shard_map/ppermute | solution.py:410
  19.3 39.5 %collective-permute-start.5 = (bf16[4,256,256]{2,1,0:T(8,128)(2,1)}, bf16[4,256,256]{2,1,0:T(8,128)(2,1)}, u32[]{:S(2)}, u32[]{:S(2)}) collective-permute-start(bf16[4,256,256]{2,1,0:T(8,128)(2,1)} %copy-done.15), channel_id=1, source_target_pairs={{12,0},{8,4},{4,8},{0,12},{13,1},{9,5},{5,9},{1,13},{14,2},{10,6},... | collective-permute-start | bytes 1572872 | tf_op jit(solution)/shard_map/ppermute | solution.py:410
  29.8 3.0 %copy-start.25 = (bf16[16,1]{0,1:T(2,128)(2,1)S(1)}, bf16[16,1]{0,1:T(2,128)(2,1)}, u32[]{:S(2)}) copy-start(bf16[16,1]{0,1:T(2,128)(2,1)} %param.25) | copy-start | bytes 100
  40.2 18.5 %copy-start.8 = (bf16[4,256,256]{2,1,0:T(8,128)(2,1)}, bf16[4,256,256]{2,1,0:T(8,128)(2,1)S(1)}, u32[]{:S(2)}) copy-start(bf16[4,256,256]{2,1,0:T(8,128)(2,1)S(1)} %collective-permute-done.3.refs_0_) | copy-start | bytes 1572868
  58.7 3.4 %collective-permute-start.6 = (bf16[4,256,256]{2,1,0:T(8,128)(2,1)S(1)}, bf16[4,256,256]{2,1,0:T(8,128)(2,1)S(1)}, u32[]{:S(2)}, u32[]{:S(2)}) collective-permute-start(bf16[4,256,256]{2,1,0:T(8,128)(2,1)S(1)} %finish.4.refs_0_), channel_id=1, source_target_pairs={{0,1},{1,0},{2,3},{3,2},{4,5},{5,4},{6,7},{7,6},{8,9},{9,8},{10,11... | collective-permute-start | bytes 1572872 | tf_op jit(solution)/shard_map/ppermute | solution.py:421
  61.6 2.1 %collective-permute-start.7 = (bf16[4,256,256]{2,1,0:T(8,128)(2,1)S(1)}, bf16[4,256,256]{2,1,0:T(8,128)(2,1)S(1)}, u32[]{:S(2)}, u32[]{:S(2)}) collective-permute-start(bf16[4,256,256]{2,1,0:T(8,128)(2,1)S(1)} %finish.5.refs_2_), channel_id=1, source_target_pairs={{0,1},{1,0},{2,3},{3,2},{4,5},{5,4},{6,7},{7,6},{8,9},{9,8},{10,11... | collective-permute-start | bytes 1572872 | tf_op jit(solution)/shard_map/ppermute | solution.py:425
  63.7 2.2 %copy-start.14 = (bf16[4,256,256]{2,1,0:T(8,128)(2,1)}, bf16[4,256,256]{2,1,0:T(8,128)(2,1)S(1)}, u32[]{:S(2)}) copy-start(bf16[4,256,256]{2,1,0:T(8,128)(2,1)S(1)} %collective-permute-done.7.refs_3_) | copy-start | bytes 1572868
  63.7 16.0 %copy-start.7 = (bf16[16,256,256]{2,1,0:T(8,128)(2,1)S(1)}, bf16[16,256,256]{2,1,0:T(8,128)(2,1)}, u32[]{:S(2)}) copy-start(bf16[16,256,256]{2,1,0:T(8,128)(2,1)} %refs_4_.1) | copy-start | bytes 6291460
  66.7 29.5 %collective-permute-start.8 = (bf16[4,256,256]{2,1,0:T(8,128)(2,1)}, bf16[4,256,256]{2,1,0:T(8,128)(2,1)}, u32[]{:S(2)}, u32[]{:S(2)}) collective-permute-start(bf16[4,256,256]{2,1,0:T(8,128)(2,1)} %get-tuple-element.45), channel_id=1, source_target_pairs={{4,0},{0,4},{12,8},{8,12},{5,1},{1,5},{13,9},{9,13},{6,2},{2,6},{1... | collective-permute-start | bytes 1572872 | tf_op jit(solution)/shard_map/ppermute | solution.py:410
  72.8 38.5 %collective-permute-start.9 = (bf16[4,256,256]{2,1,0:T(8,128)(2,1)}, bf16[4,256,256]{2,1,0:T(8,128)(2,1)}, u32[]{:S(2)}, u32[]{:S(2)}) collective-permute-start(bf16[4,256,256]{2,1,0:T(8,128)(2,1)} %get-tuple-element.46), channel_id=1, source_target_pairs={{8,0},{12,4},{0,8},{4,12},{9,1},{13,5},{1,9},{5,13},{10,2},{14,6},... | collective-permute-start | bytes 1572872 | tf_op jit(solution)/shard_map/ppermute | solution.py:410
  74.2 39.8 %collective-permute-start.11 = (bf16[4,256,256]{2,1,0:T(8,128)(2,1)}, bf16[4,256,256]{2,1,0:T(8,128)(2,1)}, u32[]{:S(2)}, u32[]{:S(2)}) collective-permute-start(bf16[4,256,256]{2,1,0:T(8,128)(2,1)} %get-tuple-element.48), channel_id=1, source_target_pairs={{12,0},{8,4},{4,8},{0,12},{13,1},{9,5},{5,9},{1,13},{14,2},{10,6},... | collective-permute-start | bytes 1572872 | tf_op jit(solution)/shard_map/ppermute | solution.py:410
  77.1 2.5 %copy-start.3 = (bf16[16,256,256]{2,1,0:T(8,128)(2,1)S(1)}, bf16[16,256,256]{2,1,0:T(8,128)(2,1)}, u32[]{:S(2)}) copy-start(bf16[16,256,256]{2,1,0:T(8,128)(2,1)} %refs_2_.5) | copy-start | bytes 6291460
  77.2 2.5 %copy-start.5 = (bf16[16,256,256]{2,1,0:T(8,128)(2,1)S(1)}, bf16[16,256,256]{2,1,0:T(8,128)(2,1)}, u32[]{:S(2)}) copy-start(bf16[16,256,256]{2,1,0:T(8,128)(2,1)} %refs_3_.7) | copy-start | bytes 6291460
  116.9 1.2 collective-permute-start.13
  118.1 3.6 %collective-permute-start.14 = (f32[64]{0:T(128)S(1)}, f32[64]{0:T(128)S(1)}, u32[]{:S(2)}, u32[]{:S(2)}) collective-permute-start(f32[64]{0:T(128)S(1)} %add.110), channel_id=1, source_target_pairs={{0,2},{2,0},{1,3},{3,1},{4,6},{6,4},{5,7},{7,5},{8,10},{10,8},{9,1... | collective-permute-start | bytes 776 | tf_op jit(solution)/shard_map/ppermute | solution.py:289
  119.6 17.1 %collective-permute-start.12 = (bf16[4,256,256]{2,1,0:T(8,128)(2,1)S(1)}, bf16[4,256,256]{2,1,0:T(8,128)(2,1)S(1)}, u32[]{:S(2)}, u32[]{:S(2)}) collective-permute-start(bf16[4,256,256]{2,1,0:T(8,128)(2,1)S(1)} %get-tuple-element.49.refs_2_), channel_id=1, source_target_pairs={{0,1},{1,0},{2,3},{3,2},{4,5},{5,4},{6,7},{7,6},{8,9},{9,8},{10,11... | collective-permute-start | bytes 1572872 | tf_op jit(solution)/shard_map/ppermute | solution.py:425
  119.6 17.1 %collective-permute-start.10 = (bf16[4,256,256]{2,1,0:T(8,128)(2,1)S(1)}, bf16[4,256,256]{2,1,0:T(8,128)(2,1)S(1)}, u32[]{:S(2)}, u32[]{:S(2)}) collective-permute-start(bf16[4,256,256]{2,1,0:T(8,128)(2,1)S(1)} %get-tuple-element.47.refs_0_), channel_id=1, source_target_pairs={{0,1},{1,0},{2,3},{3,2},{4,5},{5,4},{6,7},{7,6},{8,9},{9,8},{10,11... | collective-permute-start | bytes 1572872 | tf_op jit(solution)/shard_map/ppermute | solution.py:421
  121.6 9.6 %collective-permute-start.15 = (f32[64]{0:T(128)S(1)}, f32[64]{0:T(128)S(1)}, u32[]{:S(2)}, u32[]{:S(2)}) collective-permute-start(f32[64]{0:T(128)S(1)} %add.111), channel_id=1, source_target_pairs={{0,4},{4,0},{8,12},{12,8},{1,5},{5,1},{9,13},{13,9},{2,6},{6,2},{1... | collective-permute-start | bytes 776 | tf_op jit(solution)/shard_map/ppermute | solution.py:289
  131.2 5.0 %collective-permute-start.16 = (f32[64]{0:T(128)S(1)}, f32[64]{0:T(128)S(1)}, u32[]{:S(2)}, u32[]{:S(2)}) collective-permute-start(f32[64]{0:T(128)S(1)} %add.112), channel_id=1, source_target_pairs={{0,8},{4,12},{8,0},{12,4},{1,9},{5,13},{9,1},{13,5},{2,10},{6,14},... | collective-permute-start | bytes 776 | tf_op jit(solution)/shard_map/ppermute | solution.py:289
  (11 other events, 12.9 us)

commit v4 on v3

--- a/solution.py
+++ b/solution.py
@@ -62,7 +62,8 @@
         lists = refs[: rows - 1]
         store = refs[rows - 1]
         asked = refs[rows]
-        outs = refs[rows + 1 :]
+        outs = refs[rows + 1 : -1]
+        sem = refs[-1]
         me = place_ref[0]
         core = place_ref[1]
         for shift in range(1, rows):
@@ -82,20 +83,27 @@
                 count = count + mine.astype(jnp.int32)
                 filled = filled + taken.astype(jnp.int32)
             for k in range(cap):
-                outs[shift - 1][k] = store[asked[base + k]]
+                pltpu.make_async_copy(
+                    store.at[asked[base + k]], outs[shift - 1].at[k], sem.at[shift - 1, k]
+                ).start()
+        for shift in range(rows - 1):
+            for k in range(cap):
+                pltpu.make_async_copy(store.at[0], outs[shift].at[k], sem.at[shift, k]).wait()
 
     shape = (cap, domain, domain)
     return pl.pallas_call(
         body,
         out_shape=[jax.ShapeDtypeStruct(((rows - 1) * (cap + 1),), jnp.int32)]
         + [VMEM(shape, jnp.bfloat16)] * (rows - 1),
-        in_specs=[pl.BlockSpec(memory_space=SMEM)] * rows + [pl.BlockSpec(memory_space=VMEM)],
+        in_specs=[pl.BlockSpec(memory_space=SMEM)] * rows
+        + [pl.BlockSpec(memory_space=pltpu.HBM)],
         out_specs=[pl.BlockSpec(memory_space=SMEM)]
         + [pl.BlockSpec(memory_space=VMEM)] * (rows - 1),
+        scratch_shapes=[pltpu.SemaphoreType.DMA((rows - 1, cap))],
         cost_estimate=cost(0, blocks * domain * domain * 4),
         compiler_params=limits(8),
         name="gather_first",
-    )(place, *requests, amplitudes)
+    )(place, *requests, pltpu.with_memory_space_constraint(amplitudes, pltpu.HBM))
 
 
 def gather_again(asked, where, stores, rows, cap):
@@ -319,9 +327,6 @@
     requests = [lax.ppermute(packed, "row", exchanges(rows, d)) for d in range(1, rows)]
     here = jnp.stack([row, core]).astype(jnp.int32)
     asked, *sends = gather_first(requests, here, amplitudes, rows, cap)
-    source, far_slot, near_slot, near_count, near_weight, far_weight, *_ = lax.optimization_barrier(
-        (source, far_slot, near_slot, near_count, near_weight, far_weight, asked)
-    )
 
     step = apart(rows, source, row)
     same = step[:, None] == step[None, :]
@@ -352,12 +357,12 @@
 
     shift = energy_of(first) + energy_of(second)
 
-    near_pos = jnp.arange(near_slot.shape[1], dtype=jnp.int32)
-    alive = near_pos[None, :] < near_count[:, None]
-    matches = (near_slot[:, :, None] == slot_ids[None, None, :]) & alive[:, :, None]
-    weights = jnp.sum(
-        jnp.where(matches, near_weight.astype(jnp.float32)[:, :, None], jnp.float32(0.0)), axis=1
-    ).astype(jnp.bfloat16)
+    near_wide = near_weight.astype(jnp.float32)
+    weights = jnp.zeros((pairs, pairs), jnp.float32)
+    for k in range(near_slot.shape[1]):
+        used = (near_slot[:, k : k + 1] == slot_ids[None, :]) & (k < near_count[:, None])
+        weights = weights + jnp.where(used, near_wide[:, k : k + 1], jnp.float32(0.0))
+    weights = weights.astype(jnp.bfloat16)
 
     def choose(chosen, table):
         spread = jnp.where(chosen[:, :, None], table[None], jnp.zeros((), table.dtype))
@@ -398,6 +403,10 @@
     spreads = [spread_of(own_weights), spread_of(by_core)]
     ats = [own, jnp.arange(half, dtype=jnp.int32)]
     slots = jnp.concatenate([own[:early], other[:early], own[early:], other[early:]])
+    (own, shift, far_scale, *moved) = lax.optimization_barrier(
+        (own, shift, far_scale, *tables, *spreads, *ats, slots, *sends)
+    )
+    tables, spreads, ats, slots = moved[:2], moved[2:4], moved[4:6], moved[6]
     stores = [amplitudes]
     whole = [amplitudes]
     for sweep in range(ITERS):

time: 139 us -> 138 us (level)
  local copies, waits for them, and re-layouts: 17.3 us -> 6.82 us
  waiting for transfers between devices: 62.4 us -> 68.8 us
  starting transfers between devices: 33.1 us -> 37.6 us
  Pallas kernels: 20.6 us -> 18.5 us
    ppermute x6, waiting for transfers between devices: 51.3 us -> 60.6 us  [per_device(): arrived.append(lax.ppermute(sends[d - 1], 'row', returns(rows, d)))]
    unnamed x53 -> x23, local copies, waits for them, and re-layouts: 12.9 us -> 3.89 us
    ppermute x3, waiting for transfers between devices: 3.8 us -> 0.01 us  [per_device(): lax.ppermute(packed, 'row', exchanges(rows, d))]
    ppermute x4, starting transfers between devices: 12.9 us -> 15.3 us  [add_over(): lax.ppermute(values, name, [(r, r ^ step) for r in range(size)])]
    ppermute x6, starting transfers between devices: 13.4 us -> 15.6 us  [per_device(): arrived.append(lax.ppermute(sends[d - 1], 'row', returns(rows, d)))]
    select_n x2, local copies, waits for them, and re-layouts: 2.98 us -> 0.92 us  [spread_of(): jnp.where(unit[None, :, None, :], table[:, None, :, None], jnp.zeros((),...]
    pallas_call x4, Pallas kernels: 8.54 us -> 6.59 us  [finish(): pl.pallas_call(body, out_shape=out_shape, in_specs=[pl.BlockSpec(memory_s...]
    slice x0 -> x2, local copies, waits for them, and re-layouts: none -> 1.81 us  [the longest x1 1.48 us: per_device(): near_slot[:, k:k + 1] == slot_ids[None, :]]
  transfers between devices with their start and end apart: 17 -> 17, of which waited for: 11 -> 10; matrix products, arithmetic and copies ran while one was open for 6% -> 6% of each run, Pallas kernels for 8% -> 8%
where the time goes in v4:
time: 138 us
  waiting for transfers between devices  68.8 us (50%)
  starting transfers between devices  37.6 us (27%)
  Pallas kernels  18.5 us (13%)
  local copies, waits for them, and re-layouts  6.82 us (5%)
  other arithmetic  5.42 us (4%)
    ppermute x6, waiting for transfers between devices, per_device(): arrived.append(lax.ppermute(sends[d - 1], 'row', returns(rows, d)))  60.6 us
    ppermute x6, starting transfers between devices, per_device(): arrived.append(lax.ppermute(sends[d - 1], 'row', returns(rows, d)))  15.6 us
    ppermute x4, starting transfers between devices, add_over(): lax.ppermute(values, name, [(r, r ^ step) for r in range(size)])  15.3 us
    ppermute x4, waiting for transfers between devices, add_over(): lax.ppermute(values, name, [(r, r ^ step) for r in range(size)])  6.65 us
    pallas_call x4, Pallas kernels, finish(): pl.pallas_call(body, out_shape=out_shape, in_specs=[pl.BlockSpec(memory_s...  6.59 us
    pallas_call x2, Pallas kernels, prepare(): pl.pallas_call(body, grid_spec=pltpu.PrefetchScalarGridSpec(num_scalar_pr...  6 us
    ppermute x3, starting transfers between devices, per_device(): lax.ppermute(packed, 'row', exchanges(rows, d))  5.64 us
    unnamed x23, local copies, waits for them, and re-layouts  3.89 us
  transfers between devices with their start and end apart: 17, of which 10 were waited for; matrix products, arithmetic and copies ran while one was open for 6% of the time, Pallas kernels for 8%

profile of v4, /device:TPU:0, one launch (start us, length us, event | category | flops | bytes accessed | tf_op | source)
XLA Modules:
  0.0 138.1 jit_solution(8501928152780734172)
XLA Ops:
  0.7 0.7 bitcast_add_fusion
  1.4 5.1 %collective-permute-start.2 = (s32[16]{0:T(128)S(1)}, s32[16]{0:T(128)S(1)}, u32[]{:S(2)}, u32[]{:S(2)}) collective-permute-start(s32[16]{0:T(128)S(1)} %bitcast_add_fusion), channel_id=1, source_target_pairs={{0,12},{4,8},{8,4},{12,0},{1,13},{5,9},{9,5},{13,1},{2,14},{6,10},... | collective-permute-start | bytes 200 | tf_op jit(solution)/shard_map/ppermute | solution.py:327
  8.1 1.5 %slice_reduce_fusion.21 = (s32[16]{0:T(128)S(1)}, s32[16]{0:T(128)S(1)}, s32[16]{0:T(128)S(1)}, s32[16]{0:T(128)S(1)}, s32[16]{0:T(128)S(1)}, /*index=5*/s32[16]...) fusion(s32[16,11]{1,0:T(8,128)} %param.20), kind=kLoop, calls=%fused_computation.41 | loop fusion | bytes 1408 | tf_op jit(solution)/shard_map/slice | solution.py:363
  10.2 0.7 convert_element_type.36
  13.9 3.0 %gather_first.1 = (s32[15]{0:T(128)S(1)}, bf16[4,256,256]{2,1,0:T(8,128)(2,1)S(1)}, bf16[4,256,256]{2,1,0:T(8,128)(2,1)S(1)}, bf16[4,256,256]{2,1,0:T(8,128)(2,1)S(1)}) custom-call(s32[2]{0:T(128)S(1)} %pad_add_fusion.1.place_ref, s32[16]{0:T(128)S(1)} %collective-permute-done.refs_0_, s32[16]{0:T(128)S(1)} %collective-permute-done.1.refs_1_, ...), custom_call_target="tpu_custom_call" | custom-call | bytes 3145728 | tf_op jit(solution)/shard_map/gather_first/pallas_call | solution.py:94
  16.9 1.6 %collective-permute-start.3 = (bf16[4,256,256]{2,1,0:T(8,128)(2,1)S(1)}, bf16[4,256,256]{2,1,0:T(8,128)(2,1)S(1)}, u32[]{:S(2)}, u32[]{:S(2)}) collective-permute-start(bf16[4,256,256]{2,1,0:T(8,128)(2,1)S(1)} %get-tuple-element.31), channel_id=1, source_target_pairs={{4,0},{0,4},{12,8},{8,12},{5,1},{1,5},{13,9},{9,13},{6,2},{2,6},{1... | collective-permute-start | bytes 1572872 | tf_op jit(solution)/shard_map/ppermute | solution.py:419
  18.5 2.9 %collective-permute-start.4 = (bf16[4,256,256]{2,1,0:T(8,128)(2,1)S(1)}, bf16[4,256,256]{2,1,0:T(8,128)(2,1)S(1)}, u32[]{:S(2)}, u32[]{:S(2)}) collective-permute-start(bf16[4,256,256]{2,1,0:T(8,128)(2,1)S(1)} %get-tuple-element.32), channel_id=1, source_target_pairs={{8,0},{12,4},{0,8},{4,12},{9,1},{13,5},{1,9},{5,13},{10,2},{14,6},... | collective-permute-start | bytes 1572872 | tf_op jit(solution)/shard_map/ppermute | solution.py:419
  21.7 1.6 %copy-done.2 = bf16[16,256,256]{2,1,0:T(8,128)(2,1)S(1)} copy-done((bf16[16,256,256]{2,1,0:T(8,128)(2,1)S(1)}, bf16[16,256,256]{2,1,0:T(8,128)(2,1)}, u32[]{:S(2)}) %copy-start.2) | copy-done | bytes 2097176
  23.3 1.6 %copy-done.4 = bf16[16,256,256]{2,1,0:T(8,128)(2,1)S(1)} copy-done((bf16[16,256,256]{2,1,0:T(8,128)(2,1)S(1)}, bf16[16,256,256]{2,1,0:T(8,128)(2,1)}, u32[]{:S(2)}) %copy-start.4) | copy-done | bytes 2097176
  24.9 3.0 %prepare.2 = (f32[8,256,256]{2,1,0:T(8,128)S(1)}, f32[8,256,256]{2,1,0:T(8,128)S(1)}, f32[8,256,256]{2,1,0:T(8,128)S(1)}, bf16[8,256,256]{2,1,0:T(8,128)(2,1)S(1)}) custom-call(s32[8]{0:T(128)S(1)} %get-tuple-element.42.own_ref.at_ref, s32[8]{0:T(128)S(1)} %get-tuple-element.42.own_ref.at_ref, f32[8]{0:T(128)S(1)} %add.169.shift_ref, ...), custom_call_target="tpu_custom_call" | custom-call | flops 805306368 | bytes 12582912 | tf_op jit(solution)/shard_map/prepare/pallas_call | solution.py:169
  27.9 12.3 %collective-permute-done.3.refs_0_ = bf16[4,256,256]{2,1,0:T(8,128)(2,1)S(1)} collective-permute-done((bf16[4,256,256]{2,1,0:T(8,128)(2,1)S(1)}, bf16[4,256,256]{2,1,0:T(8,128)(2,1)S(1)}, u32[]{:S(2)}, u32[]{:S(2)}) %collective-permute-start.3) | collective-permute-done | bytes 524320 | tf_op jit(solution)/shard_map/ppermute | solution.py:419
  40.2 16.4 %collective-permute-done.4.refs_1_ = bf16[4,256,256]{2,1,0:T(8,128)(2,1)S(1)} collective-permute-done((bf16[4,256,256]{2,1,0:T(8,128)(2,1)S(1)}, bf16[4,256,256]{2,1,0:T(8,128)(2,1)S(1)}, u32[]{:S(2)}, u32[]{:S(2)}) %collective-permute-start.4) | collective-permute-done | bytes 524320 | tf_op jit(solution)/shard_map/ppermute | solution.py:419
  56.6 1.2 finish.4.refs_0_
  57.9 1.2 finish.5.refs_2_
  59.8 1.4 %collective-permute-done.7.refs_3_ = bf16[4,256,256]{2,1,0:T(8,128)(2,1)S(1)} collective-permute-done((bf16[4,256,256]{2,1,0:T(8,128)(2,1)S(1)}, bf16[4,256,256]{2,1,0:T(8,128)(2,1)S(1)}, u32[]{:S(2)}, u32[]{:S(2)}) %collective-permute-start.7) | collective-permute-done | bytes 524320 | tf_op jit(solution)/shard_map/ppermute | solution.py:434
  61.3 1.0 gather_again.1
  62.3 8.6 %collective-permute-start.8 = (bf16[4,256,256]{2,1,0:T(8,128)(2,1)S(1)}, bf16[4,256,256]{2,1,0:T(8,128)(2,1)S(1)}, u32[]{:S(2)}, u32[]{:S(2)}) collective-permute-start(bf16[4,256,256]{2,1,0:T(8,128)(2,1)S(1)} %get-tuple-element.53), channel_id=1, source_target_pairs={{4,0},{0,4},{12,8},{8,12},{5,1},{1,5},{13,9},{9,13},{6,2},{2,6},{1... | collective-permute-start | bytes 1572872 | tf_op jit(solution)/shard_map/ppermute | solution.py:419
  70.8 1.1 collective-permute-start.9
  71.9 1.4 %collective-permute-start.11 = (bf16[4,256,256]{2,1,0:T(8,128)(2,1)S(1)}, bf16[4,256,256]{2,1,0:T(8,128)(2,1)S(1)}, u32[]{:S(2)}, u32[]{:S(2)}) collective-permute-start(bf16[4,256,256]{2,1,0:T(8,128)(2,1)S(1)} %get-tuple-element.56), channel_id=1, source_target_pairs={{12,0},{8,4},{4,8},{0,12},{13,1},{9,5},{5,9},{1,13},{14,2},{10,6},... | collective-permute-start | bytes 1572872 | tf_op jit(solution)/shard_map/ppermute | solution.py:419
  74.1 3.0 %prepare.3 = (f32[8,256,256]{2,1,0:T(8,128)S(1)}, f32[8,256,256]{2,1,0:T(8,128)S(1)}, f32[8,256,256]{2,1,0:T(8,128)S(1)}, bf16[8,256,256]{2,1,0:T(8,128)(2,1)S(1)}) custom-call(s32[8]{0:T(128)S(1)} %get-tuple-element.42.own_ref.at_ref, s32[8]{0:T(128)S(1)} %iota.88.at_ref, f32[8]{0:T(128)S(1)} %add.169.shift_ref, bf16[128,256]{1,0:T(8,128)(2,1)S(1)} %select_n.244.spread_ref, ...), custom_call_target="tpu_custom_call" | custom-call | flops 805306368 | bytes 12582912 | tf_op jit(solution)/shard_map/prepare/pallas_call | solution.py:169
  77.1 16.6 %collective-permute-done.8.refs_0_ = bf16[4,256,256]{2,1,0:T(8,128)(2,1)S(1)} collective-permute-done((bf16[4,256,256]{2,1,0:T(8,128)(2,1)S(1)}, bf16[4,256,256]{2,1,0:T(8,128)(2,1)S(1)}, u32[]{:S(2)}, u32[]{:S(2)}) %collective-permute-start.8) | collective-permute-done | bytes 524320 | tf_op jit(solution)/shard_map/ppermute | solution.py:419
  93.7 15.3 %collective-permute-done.9.refs_1_ = bf16[4,256,256]{2,1,0:T(8,128)(2,1)S(1)} collective-permute-done((bf16[4,256,256]{2,1,0:T(8,128)(2,1)S(1)}, bf16[4,256,256]{2,1,0:T(8,128)(2,1)S(1)}, u32[]{:S(2)}, u32[]{:S(2)}) %collective-permute-start.9) | collective-permute-done | bytes 524320 | tf_op jit(solution)/shard_map/ppermute | solution.py:419
  109.0 2.1 %finish.7 = (bf16[4,256,256]{2,1,0:T(8,128)(2,1)S(1)}, f32[1,64]{1,0:T(1,128)S(1)}) custom-call(s32[24]{0:T(128)S(1)} %get-tuple-element.35.number_ref, f32[8]{0:T(128)S(1)} %fusion.16.scale_ref, f32[8,256,256]{2,1,0:T(8,128)S(1)} %get-tuple-element.48.local_ref, f32[8,256,256]{2,1,0:T(8,128)S(1)} %get-tuple-element.49.rest_ref, ...), custom_call_target="tpu_custom_call" | custom-call | flops 268435456 | bytes 4718592 | tf_op jit(solution)/shard_map/finish/pallas_call | solution.py:245
  111.1 2.1 %finish.6 = (bf16[4,256,256]{2,1,0:T(8,128)(2,1)S(1)}, f32[1,64]{1,0:T(1,128)S(1)}) custom-call(s32[24]{0:T(128)S(1)} %get-tuple-element.35.number_ref, f32[8]{0:T(128)S(1)} %fusion.16.scale_ref, f32[8,256,256]{2,1,0:T(8,128)S(1)} %get-tuple-element.48.local_ref, f32[8,256,256]{2,1,0:T(8,128)S(1)} %get-tuple-element.49.rest_ref, ...), custom_call_target="tpu_custom_call" | custom-call | flops 268435456 | bytes 4718592 | tf_op jit(solution)/shard_map/finish/pallas_call | solution.py:245
  113.7 1.5 %collective-permute-done.13 = f32[64]{0:T(128)S(1)} collective-permute-done((f32[64]{0:T(128)S(1)}, f32[64]{0:T(128)S(1)}, u32[]{:S(2)}, u32[]{:S(2)}) %collective-permute-start.13) | collective-permute-done | bytes 288 | tf_op jit(solution)/shard_map/ppermute | solution.py:297
  115.2 1.5 %collective-permute-start.14 = (f32[64]{0:T(128)S(1)}, f32[64]{0:T(128)S(1)}, u32[]{:S(2)}, u32[]{:S(2)}) collective-permute-start(f32[64]{0:T(128)S(1)} %add.190), channel_id=1, source_target_pairs={{0,2},{2,0},{1,3},{3,1},{4,6},{6,4},{5,7},{7,5},{8,10},{10,8},{9,1... | collective-permute-start | bytes 776 | tf_op jit(solution)/shard_map/ppermute | solution.py:297
  116.7 2.1 %collective-permute-done.14 = f32[64]{0:T(128)S(1)} collective-permute-done((f32[64]{0:T(128)S(1)}, f32[64]{0:T(128)S(1)}, u32[]{:S(2)}, u32[]{:S(2)}) %collective-permute-start.14) | collective-permute-done | bytes 288 | tf_op jit(solution)/shard_map/ppermute | solution.py:297
  118.8 10.7 %collective-permute-start.15 = (f32[64]{0:T(128)S(1)}, f32[64]{0:T(128)S(1)}, u32[]{:S(2)}, u32[]{:S(2)}) collective-permute-start(f32[64]{0:T(128)S(1)} %add.191), channel_id=1, source_target_pairs={{0,4},{4,0},{8,12},{12,8},{1,5},{5,1},{9,13},{13,9},{2,6},{6,2},{1... | collective-permute-start | bytes 776 | tf_op jit(solution)/shard_map/ppermute | solution.py:297
  129.5 1.5 %collective-permute-done.15 = f32[64]{0:T(128)S(1)} collective-permute-done((f32[64]{0:T(128)S(1)}, f32[64]{0:T(128)S(1)}, u32[]{:S(2)}, u32[]{:S(2)}) %collective-permute-start.15) | collective-permute-done | bytes 288 | tf_op jit(solution)/shard_map/ppermute | solution.py:297
  131.1 3.0 %collective-permute-start.16 = (f32[64]{0:T(128)S(1)}, f32[64]{0:T(128)S(1)}, u32[]{:S(2)}, u32[]{:S(2)}) collective-permute-start(f32[64]{0:T(128)S(1)} %add.192), channel_id=1, source_target_pairs={{0,8},{4,12},{8,0},{12,4},{1,9},{5,13},{9,1},{13,5},{2,10},{6,14},... | collective-permute-start | bytes 776 | tf_op jit(solution)/shard_map/ppermute | solution.py:297
  134.1 1.5 %collective-permute-done.16 = f32[64]{0:T(128)S(1)} collective-permute-done((f32[64]{0:T(128)S(1)}, f32[64]{0:T(128)S(1)}, u32[]{:S(2)}, u32[]{:S(2)}) %collective-permute-start.16) | collective-permute-done | bytes 288 | tf_op jit(solution)/shard_map/ppermute | solution.py:297
  136.1 2.0 %put_in_slots.1 = bf16[16,256,256]{2,1,0:T(8,128)(2,1)} custom-call(s32[16]{0:T(128)S(1)} %pad_add_fusion.slot_ref, bf16[4,256,256]{2,1,0:T(8,128)(2,1)S(1)} %get-tuple-element.55.refs_0_, bf16[4,256,256]{2,1,0:T(8,128)(2,1)S(1)} %collective-permute-done.10.refs_1_, bf16[4,256,256]{2,1,0:T(8,128)(2,1)S(1)} %get-tuple-element.57.refs_2_, ...), custom_call_target="tpu_custom_call" | custom-call | bytes 4194304 | tf_op jit(solution)/shard_map/put_in_slots/pallas_call | solution.py:278
  (74 shorter events, 8.1 us)
Async XLA Ops:
  0.6 12.3 %copy-start.7 = (s32[16,1]{0,1:T(1,128)S(1)}, s32[16,1]{0,1:T(1,128)}, u32[]{:S(2)}) copy-start(s32[16,1]{0,1:T(1,128)} %param.24) | copy-start | bytes 196
  0.6 12.3 %copy-start.8 = (s32[16]{0:T(128)S(1)}, s32[16]{0:T(128)}, u32[]{:S(2)}) copy-start(s32[16]{0:T(128)} %param.19) | copy-start | bytes 196
  0.7 12.3 %copy-start.9 = (s32[16]{0:T(128)S(1)}, s32[16]{0:T(128)}, u32[]{:S(2)}) copy-start(s32[16]{0:T(128)} %param.18) | copy-start | bytes 196
  0.7 12.8 %copy-start.6 = (f32[64]{0:T(128)S(1)}, f32[64]{0:T(128)}, u32[]{:S(2)}) copy-start(f32[64]{0:T(128)} %param.17) | copy-start | bytes 772
  1.4 12.5 %collective-permute-start.2 = (s32[16]{0:T(128)S(1)}, s32[16]{0:T(128)S(1)}, u32[]{:S(2)}, u32[]{:S(2)}) collective-permute-start(s32[16]{0:T(128)S(1)} %bitcast_add_fusion), channel_id=1, source_target_pairs={{0,12},{4,8},{8,4},{12,0},{1,13},{5,9},{9,5},{13,1},{2,14},{6,10},... | collective-permute-start | bytes 200 | tf_op jit(solution)/shard_map/ppermute | solution.py:327
  6.4 7.4 %collective-permute-start.1 = (s32[16]{0:T(128)S(1)}, s32[16]{0:T(128)S(1)}, u32[]{:S(2)}, u32[]{:S(2)}) collective-permute-start(s32[16]{0:T(128)S(1)} %bitcast_add_fusion), channel_id=1, source_target_pairs={{0,8},{4,12},{8,0},{12,4},{1,9},{5,13},{9,1},{13,5},{2,10},{6,14},... | collective-permute-start | bytes 200 | tf_op jit(solution)/shard_map/ppermute | solution.py:327
  6.5 7.4 %collective-permute-start = (s32[16]{0:T(128)S(1)}, s32[16]{0:T(128)S(1)}, u32[]{:S(2)}, u32[]{:S(2)}) collective-permute-start(s32[16]{0:T(128)S(1)} %bitcast_add_fusion), channel_id=1, source_target_pairs={{0,4},{4,0},{8,12},{12,8},{1,5},{5,1},{9,13},{13,9},{2,6},{6,2},{1... | collective-permute-start | bytes 200 | tf_op jit(solution)/shard_map/ppermute | solution.py:327
  11.8 9.7 %copy-start.10 = (bf16[16,1]{0,1:T(2,128)(2,1)S(1)}, bf16[16,1]{0,1:T(2,128)(2,1)}, u32[]{:S(2)}) copy-start(bf16[16,1]{0,1:T(2,128)(2,1)} %param.25) | copy-start | bytes 100
  11.8 9.9 %copy-start = (bf16[16,256,256]{2,1,0:T(8,128)(2,1)S(1)}, bf16[16,256,256]{2,1,0:T(8,128)(2,1)}, u32[]{:S(2)}) copy-start(bf16[16,256,256]{2,1,0:T(8,128)(2,1)} %refs_3_.6) | copy-start | bytes 6291460
  12.9 8.8 %copy-start.1 = (bf16[16,256,256]{2,1,0:T(8,128)(2,1)S(1)}, bf16[16,256,256]{2,1,0:T(8,128)(2,1)}, u32[]{:S(2)}) copy-start(bf16[16,256,256]{2,1,0:T(8,128)(2,1)} %refs_2_.5) | copy-start | bytes 6291460
  16.9 23.4 %collective-permute-start.3 = (bf16[4,256,256]{2,1,0:T(8,128)(2,1)S(1)}, bf16[4,256,256]{2,1,0:T(8,128)(2,1)S(1)}, u32[]{:S(2)}, u32[]{:S(2)}) collective-permute-start(bf16[4,256,256]{2,1,0:T(8,128)(2,1)S(1)} %get-tuple-element.31), channel_id=1, source_target_pairs={{4,0},{0,4},{12,8},{8,12},{5,1},{1,5},{13,9},{9,13},{6,2},{2,6},{1... | collective-permute-start | bytes 1572872 | tf_op jit(solution)/shard_map/ppermute | solution.py:419
  18.5 38.2 %collective-permute-start.4 = (bf16[4,256,256]{2,1,0:T(8,128)(2,1)S(1)}, bf16[4,256,256]{2,1,0:T(8,128)(2,1)S(1)}, u32[]{:S(2)}, u32[]{:S(2)}) collective-permute-start(bf16[4,256,256]{2,1,0:T(8,128)(2,1)S(1)} %get-tuple-element.32), channel_id=1, source_target_pairs={{8,0},{12,4},{0,8},{4,12},{9,1},{13,5},{1,9},{5,13},{10,2},{14,6},... | collective-permute-start | bytes 1572872 | tf_op jit(solution)/shard_map/ppermute | solution.py:419
  21.4 36.5 %collective-permute-start.5 = (bf16[4,256,256]{2,1,0:T(8,128)(2,1)S(1)}, bf16[4,256,256]{2,1,0:T(8,128)(2,1)S(1)}, u32[]{:S(2)}, u32[]{:S(2)}) collective-permute-start(bf16[4,256,256]{2,1,0:T(8,128)(2,1)S(1)} %get-tuple-element.33), channel_id=1, source_target_pairs={{12,0},{8,4},{4,8},{0,12},{13,1},{9,5},{5,9},{1,13},{14,2},{10,6},... | collective-permute-start | bytes 1572872 | tf_op jit(solution)/shard_map/ppermute | solution.py:419
  21.7 1.6 %copy-start.2 = (bf16[16,256,256]{2,1,0:T(8,128)(2,1)S(1)}, bf16[16,256,256]{2,1,0:T(8,128)(2,1)}, u32[]{:S(2)}) copy-start(bf16[16,256,256]{2,1,0:T(8,128)(2,1)} %refs_3_.7) | copy-start | bytes 6291460
  23.3 1.6 %copy-start.4 = (bf16[16,256,256]{2,1,0:T(8,128)(2,1)S(1)}, bf16[16,256,256]{2,1,0:T(8,128)(2,1)}, u32[]{:S(2)}) copy-start(bf16[16,256,256]{2,1,0:T(8,128)(2,1)} %refs_4_.1) | copy-start | bytes 6291460
  57.9 2.0 %collective-permute-start.6 = (bf16[4,256,256]{2,1,0:T(8,128)(2,1)S(1)}, bf16[4,256,256]{2,1,0:T(8,128)(2,1)S(1)}, u32[]{:S(2)}, u32[]{:S(2)}) collective-permute-start(bf16[4,256,256]{2,1,0:T(8,128)(2,1)S(1)} %finish.4.refs_0_), channel_id=1, source_target_pairs={{0,1},{1,0},{2,3},{3,2},{4,5},{5,4},{6,7},{7,6},{8,9},{9,8},{10,11... | collective-permute-start | bytes 1572872 | tf_op jit(solution)/shard_map/ppermute | solution.py:430
  59.2 2.1 %collective-permute-start.7 = (bf16[4,256,256]{2,1,0:T(8,128)(2,1)S(1)}, bf16[4,256,256]{2,1,0:T(8,128)(2,1)S(1)}, u32[]{:S(2)}, u32[]{:S(2)}) collective-permute-start(bf16[4,256,256]{2,1,0:T(8,128)(2,1)S(1)} %finish.5.refs_2_), channel_id=1, source_target_pairs={{0,1},{1,0},{2,3},{3,2},{4,5},{5,4},{6,7},{7,6},{8,9},{9,8},{10,11... | collective-permute-start | bytes 1572872 | tf_op jit(solution)/shard_map/ppermute | solution.py:434
  62.3 31.4 %collective-permute-start.8 = (bf16[4,256,256]{2,1,0:T(8,128)(2,1)S(1)}, bf16[4,256,256]{2,1,0:T(8,128)(2,1)S(1)}, u32[]{:S(2)}, u32[]{:S(2)}) collective-permute-start(bf16[4,256,256]{2,1,0:T(8,128)(2,1)S(1)} %get-tuple-element.53), channel_id=1, source_target_pairs={{4,0},{0,4},{12,8},{8,12},{5,1},{1,5},{13,9},{9,13},{6,2},{2,6},{1... | collective-permute-start | bytes 1572872 | tf_op jit(solution)/shard_map/ppermute | solution.py:419
  70.8 38.2 %collective-permute-start.9 = (bf16[4,256,256]{2,1,0:T(8,128)(2,1)S(1)}, bf16[4,256,256]{2,1,0:T(8,128)(2,1)S(1)}, u32[]{:S(2)}, u32[]{:S(2)}) collective-permute-start(bf16[4,256,256]{2,1,0:T(8,128)(2,1)S(1)} %get-tuple-element.54), channel_id=1, source_target_pairs={{8,0},{12,4},{0,8},{4,12},{9,1},{13,5},{1,9},{5,13},{10,2},{14,6},... | collective-permute-start | bytes 1572872 | tf_op jit(solution)/shard_map/ppermute | solution.py:419
  71.9 1.6 %copy-start.5 = (bf16[16,256,256]{2,1,0:T(8,128)(2,1)S(1)}, bf16[16,256,256]{2,1,0:T(8,128)(2,1)}, u32[]{:S(2)}) copy-start(bf16[16,256,256]{2,1,0:T(8,128)(2,1)} %refs_4_.1) | copy-start | bytes 6291460
  71.9 2.2 %copy-start.3 = (bf16[16,256,256]{2,1,0:T(8,128)(2,1)S(1)}, bf16[16,256,256]{2,1,0:T(8,128)(2,1)}, u32[]{:S(2)}) copy-start(bf16[16,256,256]{2,1,0:T(8,128)(2,1)} %refs_3_.7) | copy-start | bytes 6291460
  71.9 37.1 %collective-permute-start.11 = (bf16[4,256,256]{2,1,0:T(8,128)(2,1)S(1)}, bf16[4,256,256]{2,1,0:T(8,128)(2,1)S(1)}, u32[]{:S(2)}, u32[]{:S(2)}) collective-permute-start(bf16[4,256,256]{2,1,0:T(8,128)(2,1)S(1)} %get-tuple-element.56), channel_id=1, source_target_pairs={{12,0},{8,4},{4,8},{0,12},{13,1},{9,5},{5,9},{1,13},{14,2},{10,6},... | collective-permute-start | bytes 1572872 | tf_op jit(solution)/shard_map/ppermute | solution.py:419
  111.1 25.0 %collective-permute-start.12 = (bf16[4,256,256]{2,1,0:T(8,128)(2,1)S(1)}, bf16[4,256,256]{2,1,0:T(8,128)(2,1)S(1)}, u32[]{:S(2)}, u32[]{:S(2)}) collective-permute-start(bf16[4,256,256]{2,1,0:T(8,128)(2,1)S(1)} %get-tuple-element.57.refs_2_), channel_id=1, source_target_pairs={{0,1},{1,0},{2,3},{3,2},{4,5},{5,4},{6,7},{7,6},{8,9},{9,8},{10,11... | collective-permute-start | bytes 1572872 | tf_op jit(solution)/shard_map/ppermute | solution.py:434
  113.2 23.0 %collective-permute-start.10 = (bf16[4,256,256]{2,1,0:T(8,128)(2,1)S(1)}, bf16[4,256,256]{2,1,0:T(8,128)(2,1)S(1)}, u32[]{:S(2)}, u32[]{:S(2)}) collective-permute-start(bf16[4,256,256]{2,1,0:T(8,128)(2,1)S(1)} %get-tuple-element.55.refs_0_), channel_id=1, source_target_pairs={{0,1},{1,0},{2,3},{3,2},{4,5},{5,4},{6,7},{7,6},{8,9},{9,8},{10,11... | collective-permute-start | bytes 1572872 | tf_op jit(solution)/shard_map/ppermute | solution.py:430
  113.7 1.5 %collective-permute-start.13 = (f32[64]{0:T(128)S(1)}, f32[64]{0:T(128)S(1)}, u32[]{:S(2)}, u32[]{:S(2)}) collective-permute-start(f32[64]{0:T(128)S(1)} %add_bitcast_fusion), channel_id=1, source_target_pairs={{0,1},{1,0},{2,3},{3,2},{4,5},{5,4},{6,7},{7,6},{8,9},{9,8},{10,11... | collective-permute-start | bytes 776 | tf_op jit(solution)/shard_map/ppermute | solution.py:297
  115.2 3.6 %collective-permute-start.14 = (f32[64]{0:T(128)S(1)}, f32[64]{0:T(128)S(1)}, u32[]{:S(2)}, u32[]{:S(2)}) collective-permute-start(f32[64]{0:T(128)S(1)} %add.190), channel_id=1, source_target_pairs={{0,2},{2,0},{1,3},{3,1},{4,6},{6,4},{5,7},{7,5},{8,10},{10,8},{9,1... | collective-permute-start | bytes 776 | tf_op jit(solution)/shard_map/ppermute | solution.py:297
  118.8 12.3 %collective-permute-start.15 = (f32[64]{0:T(128)S(1)}, f32[64]{0:T(128)S(1)}, u32[]{:S(2)}, u32[]{:S(2)}) collective-permute-start(f32[64]{0:T(128)S(1)} %add.191), channel_id=1, source_target_pairs={{0,4},{4,0},{8,12},{12,8},{1,5},{5,1},{9,13},{13,9},{2,6},{6,2},{1... | collective-permute-start | bytes 776 | tf_op jit(solution)/shard_map/ppermute | solution.py:297
  131.1 4.5 %collective-permute-start.16 = (f32[64]{0:T(128)S(1)}, f32[64]{0:T(128)S(1)}, u32[]{:S(2)}, u32[]{:S(2)}) collective-permute-start(f32[64]{0:T(128)S(1)} %add.192), channel_id=1, source_target_pairs={{0,8},{4,12},{8,0},{12,4},{1,9},{5,13},{9,1},{13,5},{2,10},{6,14},... | collective-permute-start | bytes 776 | tf_op jit(solution)/shard_map/ppermute | solution.py:297

commit v5 on v4

--- a/solution.py
+++ b/solution.py
@@ -54,24 +54,25 @@
     return placed
 
 
-def gather_first(requests, place, amplitudes, rows, cap):
+def gather_first(requests, shifts, place, amplitudes, rows, cap):
     pairs, domain = amplitudes.shape[:2]
-    blocks = (rows - 1) * cap
+    count_of = len(shifts)
+    blocks = count_of * cap
 
     def body(place_ref, *refs):
-        lists = refs[: rows - 1]
-        store = refs[rows - 1]
-        asked = refs[rows]
-        outs = refs[rows + 1 : -1]
+        lists = refs[:count_of]
+        store = refs[count_of]
+        asked = refs[count_of + 1]
+        outs = refs[count_of + 2 : -1]
         sem = refs[-1]
         me = place_ref[0]
         core = place_ref[1]
-        for shift in range(1, rows):
-            base = (shift - 1) * (cap + 1)
+        for n, shift in enumerate(shifts):
+            base = n * (cap + 1)
             asker = apart(rows, me, shift) if rows & (rows - 1) == 0 else (me + shift) % rows
             for k in range(cap):
                 asked[base + k] = 0
-            sources = [lists[shift - 1][p] // pairs for p in range(pairs)]
+            sources = [lists[n][p] // pairs for p in range(pairs)]
             count = jnp.int32(0)
             for p in range(pairs):
                 count = count + (apart(rows, sources[p], asker) < shift).astype(jnp.int32)
@@ -79,36 +80,37 @@
             for p in range(pairs):
                 mine = sources[p] == me
                 taken = mine & (count % 2 == core)
-                asked[base + jnp.minimum(filled, cap)] = lists[shift - 1][p] % pairs
+                asked[base + jnp.minimum(filled, cap)] = lists[n][p] % pairs
                 count = count + mine.astype(jnp.int32)
                 filled = filled + taken.astype(jnp.int32)
             for k in range(cap):
                 pltpu.make_async_copy(
-                    store.at[asked[base + k]], outs[shift - 1].at[k], sem.at[shift - 1, k]
+                    store.at[asked[base + k]], outs[n].at[k], sem.at[n, k]
                 ).start()
-        for shift in range(rows - 1):
+        for n in range(count_of):
             for k in range(cap):
-                pltpu.make_async_copy(store.at[0], outs[shift].at[k], sem.at[shift, k]).wait()
+                pltpu.make_async_copy(store.at[0], outs[n].at[k], sem.at[n, k]).wait()
 
     shape = (cap, domain, domain)
     return pl.pallas_call(
         body,
-        out_shape=[jax.ShapeDtypeStruct(((rows - 1) * (cap + 1),), jnp.int32)]
-        + [VMEM(shape, jnp.bfloat16)] * (rows - 1),
-        in_specs=[pl.BlockSpec(memory_space=SMEM)] * rows
+        out_shape=[jax.ShapeDtypeStruct((count_of * (cap + 1),), jnp.int32)]
+        + [VMEM(shape, jnp.bfloat16)] * count_of,
+        in_specs=[pl.BlockSpec(memory_space=SMEM)] * (count_of + 1)
         + [pl.BlockSpec(memory_space=pltpu.HBM)],
         out_specs=[pl.BlockSpec(memory_space=SMEM)]
-        + [pl.BlockSpec(memory_space=VMEM)] * (rows - 1),
-        scratch_shapes=[pltpu.SemaphoreType.DMA((rows - 1, cap))],
+        + [pl.BlockSpec(memory_space=VMEM)] * count_of,
+        scratch_shapes=[pltpu.SemaphoreType.DMA((count_of, cap))],
         cost_estimate=cost(0, blocks * domain * domain * 4),
         compiler_params=limits(8),
         name="gather_first",
     )(place, *requests, pltpu.with_memory_space_constraint(amplitudes, pltpu.HBM))
 
 
-def gather_again(asked, where, stores, rows, cap):
+def gather_again(asked, where, stores, cap):
     domain = stores[0].shape[1]
-    blocks = (rows - 1) * cap
+    lists = asked.shape[0] // (cap + 1)
+    blocks = lists * cap
 
     def body(asked_ref, where_ref, *refs):
         sources = laid(refs[: len(stores)])
@@ -119,27 +121,70 @@
 
     return pl.pallas_call(
         body,
-        out_shape=[VMEM((cap, domain, domain), jnp.bfloat16)] * (rows - 1),
+        out_shape=[VMEM((cap, domain, domain), jnp.bfloat16)] * lists,
         in_specs=[pl.BlockSpec(memory_space=SMEM)] * 2
         + [pl.BlockSpec(memory_space=VMEM)] * len(stores),
-        out_specs=[pl.BlockSpec(memory_space=VMEM)] * (rows - 1),
+        out_specs=[pl.BlockSpec(memory_space=VMEM)] * lists,
         cost_estimate=cost(0, blocks * domain * domain * 4),
         compiler_params=limits(8),
         name="gather_again",
     )(asked, where, *stores)
 
 
-def prepare(own, at, shift, spread, stores, integrals, fock_matrix, intersection):
+def prepare(own, at, columns, shift, near, stores, integrals, fock_matrix, intersection):
     half = own.shape[0]
     domain = integrals.shape[1]
-    total = spread.shape[1] // LANES
+    total = columns.shape[0]
+    entries = near[0].shape[1]
     groups = domain // LANES // half
     strip = groups * LANES
 
-    def body(own_ref, at_ref, shift_ref, spread_ref, *refs):
+    def spread_weights(own_ref, column_ref, slot_ref, count_ref, weight_ref, spread_ref):
+        lane = lax.broadcasted_iota(jnp.int32, (total, total), 1)
+        weights = jnp.zeros((total, total), jnp.float32)
+        for k in range(entries):
+            used = (slot_ref[:, k : k + 1] == lane) & (k < count_ref[...])
+            wide = weight_ref[:, k : k + 1].astype(jnp.float32)
+            weights = weights + jnp.where(used, wide, jnp.float32(0.0))
+        weights = weights.astype(jnp.bfloat16)
+        shape = (half * LANES, total)
+        row = lax.broadcasted_iota(jnp.int32, shape, 0) // LANES
+        wanted = jnp.zeros(shape, jnp.int32)
+        for n in range(half):
+            wanted = jnp.where(row == n, own_ref[n], wanted)
+        pick = lax.broadcasted_iota(jnp.int32, shape, 1) == wanted
+        mine = jnp.dot(
+            pick.astype(jnp.float32).astype(jnp.bfloat16),
+            weights,
+            preferred_element_type=jnp.float32,
+        ).astype(jnp.bfloat16)
+        shape = (total, total * LANES)
+        column = lax.broadcasted_iota(jnp.int32, shape, 1) // LANES
+        wanted = jnp.zeros(shape, jnp.int32)
+        for n in range(total):
+            wanted = jnp.where(column == n, column_ref[n], wanted)
+        pick = lax.broadcasted_iota(jnp.int32, shape, 0) == wanted
+        full = jnp.dot(
+            mine,
+            pick.astype(jnp.float32).astype(jnp.bfloat16),
+            preferred_element_type=jnp.float32,
+        )
+        shape = (half * LANES, total * LANES)
+        down = lax.broadcasted_iota(jnp.int32, shape, 0) % LANES
+        along = lax.broadcasted_iota(jnp.int32, shape, 1) % LANES
+        spread_ref[...] = jnp.where(down == along, full, 0.0).astype(jnp.bfloat16)
+
+    def body(own_ref, at_ref, column_ref, shift_ref, slot_ref, count_ref, weight_ref, *refs):
         sources = refs[: len(stores)]
-        integ_ref, fock_ref, over_ref, local_ref, rest_ref, recip_ref, keep_ref = refs[len(stores) :]
+        (integ_ref, fock_ref, over_ref, local_ref, rest_ref, recip_ref, keep_ref, spread_ref) = (
+            refs[len(stores) :]
+        )
         i = pl.program_id(0)
+
+        @pl.when(i == 0)
+        def _():
+            spread_weights(own_ref, column_ref, slot_ref, count_ref, weight_ref, spread_ref)
+
         for g in range(groups):
             rows = pl.ds(pl.multiple_of(i * strip + g * LANES, LANES), LANES)
             part = [s[:, rows, :].reshape(s.shape[0] * LANES, domain) for s in sources]
@@ -169,9 +214,9 @@
     return pl.pallas_call(
         body,
         grid_spec=pltpu.PrefetchScalarGridSpec(
-            num_scalar_prefetch=3,
+            num_scalar_prefetch=4,
             grid=(half,),
-            in_specs=[pl.BlockSpec(spread.shape, lambda i, *_: (0, 0))]
+            in_specs=[pl.BlockSpec(n.shape, lambda i, *_: (0, 0)) for n in near]
             + [pl.BlockSpec(s.shape, lambda i, *_: (0, 0, 0)) for s in stores]
             + [mine, mine, mine],
             out_specs=[
@@ -180,6 +225,7 @@
                 in_turn,
                 in_turn,
             ],
+            scratch_shapes=[VMEM((half * LANES, total * LANES), jnp.bfloat16)],
         ),
         out_shape=[
             wide_shape,
@@ -193,7 +239,7 @@
         ),
         compiler_params=limits(20),
         name="prepare",
-    )(own, at, shift, spread, *stores, integrals, fock_matrix, intersection)
+    )(own, at, columns, shift, *near, *stores, integrals, fock_matrix, intersection)
 
 
 def finish(start, count, numbers, scale, prepared, arrived, stores, occ_count, last):
@@ -324,9 +370,10 @@
     slot_ids = jnp.arange(pairs, dtype=jnp.int32)
     source = far_chip[:, 0]
     packed = source * pairs + far_slot[:, 0]
-    requests = [lax.ppermute(packed, "row", exchanges(rows, d)) for d in range(1, rows)]
     here = jnp.stack([row, core]).astype(jnp.int32)
-    asked, *sends = gather_first(requests, here, amplitudes, rows, cap)
+    groups = [[rows // 2], [d for d in range(1, rows) if d != rows // 2]]
+    request = lax.ppermute(packed, "row", exchanges(rows, rows // 2))
+    asked_mid, send_mid = gather_first([request], groups[0], here, amplitudes, rows, cap)
 
     step = apart(rows, source, row)
     same = step[:, None] == step[None, :]
@@ -356,30 +403,6 @@
         return jnp.sum(jnp.where(found, occ_energy[None, :], jnp.float32(0.0)), axis=1)
 
     shift = energy_of(first) + energy_of(second)
-
-    near_wide = near_weight.astype(jnp.float32)
-    weights = jnp.zeros((pairs, pairs), jnp.float32)
-    for k in range(near_slot.shape[1]):
-        used = (near_slot[:, k : k + 1] == slot_ids[None, :]) & (k < near_count[:, None])
-        weights = weights + jnp.where(used, near_wide[:, k : k + 1], jnp.float32(0.0))
-    weights = weights.astype(jnp.bfloat16)
-
-    def choose(chosen, table):
-        spread = jnp.where(chosen[:, :, None], table[None], jnp.zeros((), table.dtype))
-        return jnp.sum(spread.astype(jnp.float32), axis=1).astype(table.dtype)
-
-    own_weights = choose(own_pick, weights)
-    by_core = jnp.concatenate(
-        [choose(own_pick, own_weights.T).T, choose(other_pick, own_weights.T).T], axis=1
-    )
-    lane = jnp.arange(LANES)
-    unit = lane[:, None] == lane[None, :]
-
-    def spread_of(table):
-        grid = jnp.where(
-            unit[None, :, None, :], table[:, None, :, None], jnp.zeros((), table.dtype)
-        )
-        return grid.reshape(half * LANES, pairs * LANES)
 
     by_slot = turn // 2 + jnp.where(turn % 2 == core, 0, half)
     early = half - cap
@@ -400,25 +423,38 @@
         )
         spot = jnp.where(far_step == 0, at_home, (far_step - 1) * cap + own_place)
         tables.append(jnp.concatenate([spot, first, second]))
-    spreads = [spread_of(own_weights), spread_of(by_core)]
+    near = [near_slot, near_count[:, None], near_weight]
+    columns = [slot_ids, jnp.concatenate([own, other])]
     ats = [own, jnp.arange(half, dtype=jnp.int32)]
     slots = jnp.concatenate([own[:early], other[:early], own[early:], other[early:]])
-    (own, shift, far_scale, *moved) = lax.optimization_barrier(
-        (own, shift, far_scale, *tables, *spreads, *ats, slots, *sends)
+    (own, shift, far_scale, *moved, send_mid) = lax.optimization_barrier(
+        (own, shift, far_scale, *tables, *columns, *ats, slots, send_mid)
     )
-    tables, spreads, ats, slots = moved[:2], moved[2:4], moved[4:6], moved[6]
+    tables, columns, ats, slots = moved[:2], moved[2:4], moved[4:6], moved[6]
     stores = [amplitudes]
     whole = [amplitudes]
     for sweep in range(ITERS):
         last = sweep == ITERS - 1
         again = min(sweep, 1)
         if sweep > 0:
-            sends = gather_again(asked, local_spots[again], stores, rows, cap)
-        arrived = []
-        for d in range(1, rows):
-            arrived.append(lax.ppermute(sends[d - 1], "row", returns(rows, d)))
+            (send_mid,) = gather_again(asked_mid, local_spots[1], stores, cap)
+        arrived = {}
+        arrived[rows // 2] = lax.ppermute(send_mid, "row", returns(rows, rows // 2))
+        if sweep == 0:
+            packed, _ = lax.optimization_barrier((packed, send_mid))
+            requests = [
+                lax.ppermute(packed, "row", exchanges(rows, d)) for d in groups[1]
+            ]
+            asked, *sends = gather_first(
+                requests, groups[1], here, amplitudes, rows, cap
+            )
+        else:
+            sends = gather_again(asked, local_spots[1], stores, cap)
+        for d, send in zip(groups[1], sends):
+            arrived[d] = lax.ppermute(send, "row", returns(rows, d))
+        arrived = [arrived[d] for d in range(1, rows)]
         prepared = prepare(
-            own, ats[again], shift, spreads[again], whole,
+            own, ats[again], columns[again], shift, near, whole,
             integrals, fock_matrix, intersection,
         )
         spots = laid(arrived)

time: 138 us -> 134 us (0.971)
  waiting for transfers between devices: 68.8 us -> 62.1 us
  Pallas kernels: 18.5 us -> 23.6 us
  starting transfers between devices: 37.6 us -> 35.4 us
    ppermute x6 -> x7, waiting for transfers between devices: 60.6 us -> 51.8 us  [the longest x2 27.8 us: per_device(): arrived[rows // 2] = lax.ppermute(send_mid, 'row', returns(rows, rows // 2))]
    ppermute x3 -> x2, starting transfers between devices: 5.64 us -> 1.72 us  [per_device(): lax.ppermute(packed, 'row', exchanges(rows, d))]
    ppermute x6 -> x7, starting transfers between devices: 15.6 us -> 18.6 us  [the longest x2 10.3 us: per_device(): arrived[rows // 2] = lax.ppermute(send_mid, 'row', returns(rows, rows // 2))]
    pallas_call x1 -> x2, Pallas kernels: 3 us -> 5.82 us  [gather_first(): pl.pallas_call(body, out_shape=[jax.ShapeDtypeStruct((count_of * (cap + 1...]
    slice x2 -> x0, local copies, waits for them, and re-layouts: 1.81 us -> none  [the longest x1 1.48 us: per_device(): near_slot[:, k:k + 1] == slot_ids[None, :]]
    unnamed x23 -> x21, local copies, waits for them, and re-layouts: 3.89 us -> 5.54 us
  transfers between devices with their start and end apart: 17 -> 17, of which waited for: 10 -> 10; matrix products, arithmetic and copies ran while one was open for 6% -> 4% of each run, Pallas kernels for 8% -> 12%
where the time goes in v5:
time: 134 us; the launch traced here: 133 us
  waiting for transfers between devices  62.1 us (46%)
  starting transfers between devices  35.4 us (26%)
  Pallas kernels  23.6 us (18%)
  local copies, waits for them, and re-layouts  5.74 us (4%)
  other arithmetic  5.55 us (4%)
    ppermute x2, waiting for transfers between devices, per_device(): arrived[rows // 2] = lax.ppermute(send_mid, 'row', returns(rows, rows // 2))  27.8 us
    ppermute x4, waiting for transfers between devices, per_device(): arrived[d] = lax.ppermute(send, 'row', returns(rows, d))  24 us
    ppermute x4, starting transfers between devices, add_over(): lax.ppermute(values, name, [(r, r ^ step) for r in range(size)])  13.9 us
    ppermute x2, starting transfers between devices, per_device(): arrived[rows // 2] = lax.ppermute(send_mid, 'row', returns(rows, rows // 2))  10.3 us
    ppermute x4, waiting for transfers between devices, add_over(): lax.ppermute(values, name, [(r, r ^ step) for r in range(size)])  7.77 us
    pallas_call x2, Pallas kernels, prepare(): pl.pallas_call(body, grid_spec=pltpu.PrefetchScalarGridSpec(num_scalar_pr...  7.22 us
    pallas_call x4, Pallas kernels, finish(): pl.pallas_call(body, out_shape=out_shape, in_specs=[pl.BlockSpec(memory_s...  7.09 us
    pallas_call x2, Pallas kernels, gather_first(): pl.pallas_call(body, out_shape=[jax.ShapeDtypeStruct((count_of * (cap + 1...  5.82 us
  transfers between devices with their start and end apart: 17, of which 10 were waited for; matrix products, arithmetic and copies ran while one was open for 4% of the time, Pallas kernels for 12%

profile of v5, /device:TPU:0, one launch (start us, length us, event | category | flops | bytes accessed | tf_op | source)
XLA Modules:
  0.0 133.3 jit_solution(8649040027861579729)
XLA Ops:
  1.3 4.1 %collective-permute-start = (s32[16]{0:T(128)S(1)}, s32[16]{0:T(128)S(1)}, u32[]{:S(2)}, u32[]{:S(2)}) collective-permute-start(s32[16]{0:T(128)S(1)} %bitcast_add_fusion), channel_id=1, source_target_pairs={{0,8},{4,12},{8,0},{12,4},{1,9},{5,13},{9,1},{13,5},{2,10},{6,14},... | collective-permute-start | bytes 200 | tf_op jit(solution)/shard_map/ppermute | solution.py:375
  6.4 1.0 fusion.8
  9.8 2.7 %gather_first.2 = (s32[5]{0:T(128)S(1)}, bf16[4,256,256]{2,1,0:T(8,128)(2,1)}) custom-call(s32[2]{0:T(128)S(1)} %pad_add_fusion.2.place_ref, s32[16]{0:T(128)S(1)} %collective-permute-done.refs_0_, bf16[16,256,256]{2,1,0:T(8,128)(2,1)} %refs_3_.4), custom_call_target="tpu_custom_call" | custom-call | bytes 1048576 | tf_op jit(solution)/shard_map/gather_first/pallas_call | solution.py:95
  12.5 1.4 %collective-permute-start.2 = (s32[16]{0:T(128)S(1)}, s32[16]{0:T(128)S(1)}, u32[]{:S(2)}, u32[]{:S(2)}) collective-permute-start(s32[16]{0:T(128)S(1)} %bitcast_add_fusion), channel_id=1, source_target_pairs={{0,12},{4,8},{8,4},{12,0},{1,13},{5,9},{9,5},{13,1},{2,14},{6,10},... | collective-permute-start | bytes 200 | tf_op jit(solution)/shard_map/ppermute | solution.py:446
  14.2 2.7 %collective-permute-start.4 = (bf16[4,256,256]{2,1,0:T(8,128)(2,1)}, bf16[4,256,256]{2,1,0:T(8,128)(2,1)S(1)}, u32[]{:S(2)}, u32[]{:S(2)}) collective-permute-start(bf16[4,256,256]{2,1,0:T(8,128)(2,1)} %get-tuple-element.48), channel_id=1, source_target_pairs={{8,0},{12,4},{0,8},{4,12},{9,1},{13,5},{1,9},{5,13},{10,2},{14,6},... | collective-permute-start | bytes 1572872 | tf_op jit(solution)/shard_map/ppermute | solution.py:442
  16.9 1.0 collective-permute-done.2.refs_1_
  17.9 3.1 %gather_first.3 = (s32[10]{0:T(128)S(1)}, bf16[4,256,256]{2,1,0:T(8,128)(2,1)}, bf16[4,256,256]{2,1,0:T(8,128)(2,1)}) custom-call(s32[2]{0:T(128)S(1)} %pad_add_fusion.2.place_ref, s32[16]{0:T(128)S(1)} %collective-permute-done.1.refs_0_, s32[16]{0:T(128)S(1)} %collective-permute-done.2.refs_1_, bf16[16,256,256]{2,1,0:T(8,128)(2,1)} %refs_3_.4), custom_call_target="tpu_custom_call" | custom-call | bytes 2097152 | tf_op jit(solution)/shard_map/gather_first/pallas_call | solution.py:95
  21.1 2.7 %collective-permute-start.5 = (bf16[4,256,256]{2,1,0:T(8,128)(2,1)}, bf16[4,256,256]{2,1,0:T(8,128)(2,1)}, u32[]{:S(2)}, u32[]{:S(2)}) collective-permute-start(bf16[4,256,256]{2,1,0:T(8,128)(2,1)} %get-tuple-element.51), channel_id=1, source_target_pairs={{12,0},{8,4},{4,8},{0,12},{13,1},{9,5},{5,9},{1,13},{14,2},{10,6},... | collective-permute-start | bytes 1572872 | tf_op jit(solution)/shard_map/ppermute | solution.py:454
  23.9 1.6 %copy-done.1 = bf16[16,256,256]{2,1,0:T(8,128)(2,1)S(1)} copy-done((bf16[16,256,256]{2,1,0:T(8,128)(2,1)S(1)}, bf16[16,256,256]{2,1,0:T(8,128)(2,1)}, u32[]{:S(2)}) %copy-start.1) | copy-done | bytes 2097176
  25.5 1.6 %copy-done.3 = bf16[16,256,256]{2,1,0:T(8,128)(2,1)S(1)} copy-done((bf16[16,256,256]{2,1,0:T(8,128)(2,1)S(1)}, bf16[16,256,256]{2,1,0:T(8,128)(2,1)}, u32[]{:S(2)}) %copy-start.3) | copy-done | bytes 2097176
  27.1 1.6 %copy-done.5 = bf16[16,256,256]{2,1,0:T(8,128)(2,1)S(1)} copy-done((bf16[16,256,256]{2,1,0:T(8,128)(2,1)S(1)}, bf16[16,256,256]{2,1,0:T(8,128)(2,1)}, u32[]{:S(2)}) %copy-start.5) | copy-done | bytes 2097176
  28.7 3.6 %prepare.2 = (f32[8,256,256]{2,1,0:T(8,128)S(1)}, f32[8,256,256]{2,1,0:T(8,128)S(1)}, f32[8,256,256]{2,1,0:T(8,128)S(1)}, bf16[8,256,256]{2,1,0:T(8,128)(2,1)S(1)}) custom-call(s32[8]{0:T(128)S(1)} %get-tuple-element.42.own_ref.at_ref, s32[8]{0:T(128)S(1)} %get-tuple-element.42.own_ref.at_ref, s32[16]{0:T(128)S(1)} %iota.25.column_ref, f32[8]{0:T(128)S(1)} %add.99.shift_ref, ...), custom_call_target="tpu_custom_call" | custom-call | flops 805306368 | bytes 12582912 | tf_op jit(solution)/shard_map/prepare/pallas_call | solution.py:214
  32.3 10.3 %collective-permute-done.4.refs_1_ = bf16[4,256,256]{2,1,0:T(8,128)(2,1)S(1)} collective-permute-done((bf16[4,256,256]{2,1,0:T(8,128)(2,1)}, bf16[4,256,256]{2,1,0:T(8,128)(2,1)S(1)}, u32[]{:S(2)}, u32[]{:S(2)}) %collective-permute-start.4) | collective-permute-done | bytes 524320 | tf_op jit(solution)/shard_map/ppermute | solution.py:442
  42.6 12.5 %collective-permute-done.3.refs_0_ = bf16[4,256,256]{2,1,0:T(8,128)(2,1)S(1)} collective-permute-done((bf16[4,256,256]{2,1,0:T(8,128)(2,1)}, bf16[4,256,256]{2,1,0:T(8,128)(2,1)S(1)}, u32[]{:S(2)}, u32[]{:S(2)}) %collective-permute-start.3) | collective-permute-done | bytes 524320 | tf_op jit(solution)/shard_map/ppermute | solution.py:454
  55.1 1.2 finish.4.refs_0_
  56.4 1.7 %finish.5.refs_2_ = bf16[4,256,256]{2,1,0:T(8,128)(2,1)S(1)} custom-call(s32[24]{0:T(128)S(1)} %get-tuple-element.41.number_ref, f32[8]{0:T(128)S(1)} %fusion.5.scale_ref, f32[8,256,256]{2,1,0:T(8,128)S(1)} %get-tuple-element.44.local_ref, f32[8,256,256]{2,1,0:T(8,128)S(1)} %get-tuple-element.45.rest_ref, f32[8,256,256]{2,1,0:T(8,128)S(1)} %get-tuple-element.46.recip_ref, ...), custom_call_target="tpu_custom_call" | custom-call | flops 268435456 | bytes 4718592 | tf_op jit(solution)/shard_map/finish/pallas_call | solution.py:291
  58.7 1.5 %collective-permute-done.7.refs_3_ = bf16[4,256,256]{2,1,0:T(8,128)(2,1)S(1)} collective-permute-done((bf16[4,256,256]{2,1,0:T(8,128)(2,1)S(1)}, bf16[4,256,256]{2,1,0:T(8,128)(2,1)S(1)}, u32[]{:S(2)}, u32[]{:S(2)}) %collective-permute-start.7) | collective-permute-done | bytes 524320 | tf_op jit(solution)/shard_map/ppermute | solution.py:470
  60.9 7.5 %collective-permute-start.9 = (bf16[4,256,256]{2,1,0:T(8,128)(2,1)S(1)}, bf16[4,256,256]{2,1,0:T(8,128)(2,1)S(1)}, u32[]{:S(2)}, u32[]{:S(2)}) collective-permute-start(bf16[4,256,256]{2,1,0:T(8,128)(2,1)S(1)} %gather_again.3), channel_id=1, source_target_pairs={{8,0},{12,4},{0,8},{4,12},{9,1},{13,5},{1,9},{5,13},{10,2},{14,6},... | collective-permute-start | bytes 1572872 | tf_op jit(solution)/shard_map/ppermute | solution.py:442
  69.4 1.5 %collective-permute-start.11 = (bf16[4,256,256]{2,1,0:T(8,128)(2,1)S(1)}, bf16[4,256,256]{2,1,0:T(8,128)(2,1)S(1)}, u32[]{:S(2)}, u32[]{:S(2)}) collective-permute-start(bf16[4,256,256]{2,1,0:T(8,128)(2,1)S(1)} %get-tuple-element.60), channel_id=1, source_target_pairs={{12,0},{8,4},{4,8},{0,12},{13,1},{9,5},{5,9},{1,13},{14,2},{10,6},... | collective-permute-start | bytes 1572872 | tf_op jit(solution)/shard_map/ppermute | solution.py:454
  71.7 3.6 %prepare.3 = (f32[8,256,256]{2,1,0:T(8,128)S(1)}, f32[8,256,256]{2,1,0:T(8,128)S(1)}, f32[8,256,256]{2,1,0:T(8,128)S(1)}, bf16[8,256,256]{2,1,0:T(8,128)(2,1)S(1)}) custom-call(s32[8]{0:T(128)S(1)} %get-tuple-element.42.own_ref.at_ref, s32[8]{0:T(128)S(1)} %iota.26.at_ref, s32[16]{0:T(128)S(1)} %pad_add_fusion.column_ref, f32[8]{0:T(128)S(1)} %add.99.shift_ref, ...), custom_call_target="tpu_custom_call" | custom-call | flops 805306368 | bytes 12582912 | tf_op jit(solution)/shard_map/prepare/pallas_call | solution.py:214
  75.3 17.5 %collective-permute-done.9.refs_1_ = bf16[4,256,256]{2,1,0:T(8,128)(2,1)S(1)} collective-permute-done((bf16[4,256,256]{2,1,0:T(8,128)(2,1)S(1)}, bf16[4,256,256]{2,1,0:T(8,128)(2,1)S(1)}, u32[]{:S(2)}, u32[]{:S(2)}) %collective-permute-start.9) | collective-permute-done | bytes 524320 | tf_op jit(solution)/shard_map/ppermute | solution.py:442
  92.9 11.5 %collective-permute-done.8.refs_0_ = bf16[4,256,256]{2,1,0:T(8,128)(2,1)S(1)} collective-permute-done((bf16[4,256,256]{2,1,0:T(8,128)(2,1)S(1)}, bf16[4,256,256]{2,1,0:T(8,128)(2,1)S(1)}, u32[]{:S(2)}, u32[]{:S(2)}) %collective-permute-start.8) | collective-permute-done | bytes 524320 | tf_op jit(solution)/shard_map/ppermute | solution.py:454
  104.4 2.1 %finish.7 = (bf16[4,256,256]{2,1,0:T(8,128)(2,1)S(1)}, f32[1,64]{1,0:T(1,128)S(1)}) custom-call(s32[24]{0:T(128)S(1)} %get-tuple-element.35.number_ref, f32[8]{0:T(128)S(1)} %fusion.5.scale_ref, f32[8,256,256]{2,1,0:T(8,128)S(1)} %get-tuple-element.52.local_ref, f32[8,256,256]{2,1,0:T(8,128)S(1)} %get-tuple-element.53.rest_ref, ...), custom_call_target="tpu_custom_call" | custom-call | flops 268435456 | bytes 4718592 | tf_op jit(solution)/shard_map/finish/pallas_call | solution.py:291
  106.5 2.1 %finish.6 = (bf16[4,256,256]{2,1,0:T(8,128)(2,1)S(1)}, f32[1,64]{1,0:T(1,128)S(1)}) custom-call(s32[24]{0:T(128)S(1)} %get-tuple-element.35.number_ref, f32[8]{0:T(128)S(1)} %fusion.5.scale_ref, f32[8,256,256]{2,1,0:T(8,128)S(1)} %get-tuple-element.52.local_ref, f32[8,256,256]{2,1,0:T(8,128)S(1)} %get-tuple-element.53.rest_ref, ...), custom_call_target="tpu_custom_call" | custom-call | flops 268435456 | bytes 4718592 | tf_op jit(solution)/shard_map/finish/pallas_call | solution.py:291
  109.1 1.5 %collective-permute-done.13 = f32[64]{0:T(128)S(1)} collective-permute-done((f32[64]{0:T(128)S(1)}, f32[64]{0:T(128)S(1)}, u32[]{:S(2)}, u32[]{:S(2)}) %collective-permute-start.13) | collective-permute-done | bytes 288 | tf_op jit(solution)/shard_map/ppermute | solution.py:343
  110.6 1.5 %collective-permute-start.14 = (f32[64]{0:T(128)S(1)}, f32[64]{0:T(128)S(1)}, u32[]{:S(2)}, u32[]{:S(2)}) collective-permute-start(f32[64]{0:T(128)S(1)} %add.110), channel_id=1, source_target_pairs={{0,2},{2,0},{1,3},{3,1},{4,6},{6,4},{5,7},{7,5},{8,10},{10,8},{9,1... | collective-permute-start | bytes 776 | tf_op jit(solution)/shard_map/ppermute | solution.py:343
  112.1 2.1 %collective-permute-done.14 = f32[64]{0:T(128)S(1)} collective-permute-done((f32[64]{0:T(128)S(1)}, f32[64]{0:T(128)S(1)}, u32[]{:S(2)}, u32[]{:S(2)}) %collective-permute-start.14) | collective-permute-done | bytes 288 | tf_op jit(solution)/shard_map/ppermute | solution.py:343
  114.2 10.6 %collective-permute-start.15 = (f32[64]{0:T(128)S(1)}, f32[64]{0:T(128)S(1)}, u32[]{:S(2)}, u32[]{:S(2)}) collective-permute-start(f32[64]{0:T(128)S(1)} %add.111), channel_id=1, source_target_pairs={{0,4},{4,0},{8,12},{12,8},{1,5},{5,1},{9,13},{13,9},{2,6},{6,2},{1... | collective-permute-start | bytes 776 | tf_op jit(solution)/shard_map/ppermute | solution.py:343
  124.7 1.5 %collective-permute-done.15 = f32[64]{0:T(128)S(1)} collective-permute-done((f32[64]{0:T(128)S(1)}, f32[64]{0:T(128)S(1)}, u32[]{:S(2)}, u32[]{:S(2)}) %collective-permute-start.15) | collective-permute-done | bytes 288 | tf_op jit(solution)/shard_map/ppermute | solution.py:343
  126.3 1.8 %collective-permute-start.16 = (f32[64]{0:T(128)S(1)}, f32[64]{0:T(128)S(1)}, u32[]{:S(2)}, u32[]{:S(2)}) collective-permute-start(f32[64]{0:T(128)S(1)} %add.112), channel_id=1, source_target_pairs={{0,8},{4,12},{8,0},{12,4},{1,9},{5,13},{9,1},{13,5},{2,10},{6,14},... | collective-permute-start | bytes 776 | tf_op jit(solution)/shard_map/ppermute | solution.py:343
  128.1 2.7 %collective-permute-done.16 = f32[64]{0:T(128)S(1)} collective-permute-done((f32[64]{0:T(128)S(1)}, f32[64]{0:T(128)S(1)}, u32[]{:S(2)}, u32[]{:S(2)}) %collective-permute-start.16) | collective-permute-done | bytes 288 | tf_op jit(solution)/shard_map/ppermute | solution.py:343
  131.3 2.0 %put_in_slots.1 = bf16[16,256,256]{2,1,0:T(8,128)(2,1)} custom-call(s32[16]{0:T(128)S(1)} %pad_add_fusion.1.slot_ref, bf16[4,256,256]{2,1,0:T(8,128)(2,1)S(1)} %get-tuple-element.59.refs_0_, bf16[4,256,256]{2,1,0:T(8,128)(2,1)S(1)} %collective-permute-done.10.refs_1_, bf16[4,256,256]{2,1,0:T(8,128)(2,1)S(1)} %get-tuple-element.61.refs_2_, ...), custom_call_target="tpu_custom_call" | custom-call | bytes 4194304 | tf_op jit(solution)/shard_map/put_in_slots/pallas_call | solution.py:324
  (63 shorter events, 8.7 us)
Async XLA Ops:
  1.3 8.4 %collective-permute-start = (s32[16]{0:T(128)S(1)}, s32[16]{0:T(128)S(1)}, u32[]{:S(2)}, u32[]{:S(2)}) collective-permute-start(s32[16]{0:T(128)S(1)} %bitcast_add_fusion), channel_id=1, source_target_pairs={{0,8},{4,12},{8,0},{12,4},{1,9},{5,13},{9,1},{13,5},{2,10},{6,14},... | collective-permute-start | bytes 200 | tf_op jit(solution)/shard_map/ppermute | solution.py:375
  9.7 14.1 %copy-start.9 = (s32[16]{0:T(128)S(1)}, s32[16]{0:T(128)}, u32[]{:S(2)}) copy-start(s32[16]{0:T(128)} %param.21) | copy-start | bytes 196
  9.7 14.2 %copy-start = (bf16[16,256,256]{2,1,0:T(8,128)(2,1)S(1)}, bf16[16,256,256]{2,1,0:T(8,128)(2,1)}, u32[]{:S(2)}) copy-start(bf16[16,256,256]{2,1,0:T(8,128)(2,1)} %refs_3_.4) | copy-start | bytes 6291460
  9.7 14.2 %copy-start.7 = (s32[16,11]{1,0:T(8,128)S(1)}, s32[16,11]{1,0:T(8,128)}, u32[]{:S(2)}) copy-start(s32[16,11]{1,0:T(8,128)} %slot_ref.3) | copy-start | bytes 2116
  9.7 14.2 %copy-start.8 = (bf16[16,11]{1,0:T(8,128)(2,1)S(1)}, bf16[16,11]{1,0:T(8,128)(2,1)}, u32[]{:S(2)}) copy-start(bf16[16,11]{1,0:T(8,128)(2,1)} %weight_ref.3) | copy-start | bytes 1060
  12.5 5.4 %collective-permute-start.2 = (s32[16]{0:T(128)S(1)}, s32[16]{0:T(128)S(1)}, u32[]{:S(2)}, u32[]{:S(2)}) collective-permute-start(s32[16]{0:T(128)S(1)} %bitcast_add_fusion), channel_id=1, source_target_pairs={{0,12},{4,8},{8,4},{12,0},{1,13},{5,9},{9,5},{13,1},{2,14},{6,10},... | collective-permute-start | bytes 200 | tf_op jit(solution)/shard_map/ppermute | solution.py:446
  13.9 4.0 %collective-permute-start.1 = (s32[16]{0:T(128)S(1)}, s32[16]{0:T(128)S(1)}, u32[]{:S(2)}, u32[]{:S(2)}) collective-permute-start(s32[16]{0:T(128)S(1)} %bitcast_add_fusion), channel_id=1, source_target_pairs={{0,4},{4,0},{8,12},{12,8},{1,5},{5,1},{9,13},{13,9},{2,6},{6,2},{1... | collective-permute-start | bytes 200 | tf_op jit(solution)/shard_map/ppermute | solution.py:446
  14.2 28.4 %collective-permute-start.4 = (bf16[4,256,256]{2,1,0:T(8,128)(2,1)}, bf16[4,256,256]{2,1,0:T(8,128)(2,1)S(1)}, u32[]{:S(2)}, u32[]{:S(2)}) collective-permute-start(bf16[4,256,256]{2,1,0:T(8,128)(2,1)} %get-tuple-element.48), channel_id=1, source_target_pairs={{8,0},{12,4},{0,8},{4,12},{9,1},{13,5},{1,9},{5,13},{10,2},{14,6},... | collective-permute-start | bytes 1572872 | tf_op jit(solution)/shard_map/ppermute | solution.py:442
  21.1 34.0 %collective-permute-start.3 = (bf16[4,256,256]{2,1,0:T(8,128)(2,1)}, bf16[4,256,256]{2,1,0:T(8,128)(2,1)S(1)}, u32[]{:S(2)}, u32[]{:S(2)}) collective-permute-start(bf16[4,256,256]{2,1,0:T(8,128)(2,1)} %get-tuple-element.50), channel_id=1, source_target_pairs={{4,0},{0,4},{12,8},{8,12},{5,1},{1,5},{13,9},{9,13},{6,2},{2,6},{1... | collective-permute-start | bytes 1572872 | tf_op jit(solution)/shard_map/ppermute | solution.py:454
  21.1 35.2 %collective-permute-start.5 = (bf16[4,256,256]{2,1,0:T(8,128)(2,1)}, bf16[4,256,256]{2,1,0:T(8,128)(2,1)}, u32[]{:S(2)}, u32[]{:S(2)}) collective-permute-start(bf16[4,256,256]{2,1,0:T(8,128)(2,1)} %get-tuple-element.51), channel_id=1, source_target_pairs={{12,0},{8,4},{4,8},{0,12},{13,1},{9,5},{5,9},{1,13},{14,2},{10,6},... | collective-permute-start | bytes 1572872 | tf_op jit(solution)/shard_map/ppermute | solution.py:454
  23.9 1.6 %copy-start.1 = (bf16[16,256,256]{2,1,0:T(8,128)(2,1)S(1)}, bf16[16,256,256]{2,1,0:T(8,128)(2,1)}, u32[]{:S(2)}) copy-start(bf16[16,256,256]{2,1,0:T(8,128)(2,1)} %refs_2_.7) | copy-start | bytes 6291460
  25.5 1.6 %copy-start.3 = (bf16[16,256,256]{2,1,0:T(8,128)(2,1)S(1)}, bf16[16,256,256]{2,1,0:T(8,128)(2,1)}, u32[]{:S(2)}) copy-start(bf16[16,256,256]{2,1,0:T(8,128)(2,1)} %refs_3_.5) | copy-start | bytes 6291460
  27.1 1.6 %copy-start.5 = (bf16[16,256,256]{2,1,0:T(8,128)(2,1)S(1)}, bf16[16,256,256]{2,1,0:T(8,128)(2,1)}, u32[]{:S(2)}) copy-start(bf16[16,256,256]{2,1,0:T(8,128)(2,1)} %refs_4_.1) | copy-start | bytes 6291460
  56.3 2.4 %collective-permute-start.6 = (bf16[4,256,256]{2,1,0:T(8,128)(2,1)S(1)}, bf16[4,256,256]{2,1,0:T(8,128)(2,1)S(1)}, u32[]{:S(2)}, u32[]{:S(2)}) collective-permute-start(bf16[4,256,256]{2,1,0:T(8,128)(2,1)S(1)} %finish.4.refs_0_), channel_id=1, source_target_pairs={{0,1},{1,0},{2,3},{3,2},{4,5},{5,4},{6,7},{7,6},{8,9},{9,8},{10,11... | collective-permute-start | bytes 1572872 | tf_op jit(solution)/shard_map/ppermute | solution.py:466
  58.1 2.1 %collective-permute-start.7 = (bf16[4,256,256]{2,1,0:T(8,128)(2,1)S(1)}, bf16[4,256,256]{2,1,0:T(8,128)(2,1)S(1)}, u32[]{:S(2)}, u32[]{:S(2)}) collective-permute-start(bf16[4,256,256]{2,1,0:T(8,128)(2,1)S(1)} %finish.5.refs_2_), channel_id=1, source_target_pairs={{0,1},{1,0},{2,3},{3,2},{4,5},{5,4},{6,7},{7,6},{8,9},{9,8},{10,11... | collective-permute-start | bytes 1572872 | tf_op jit(solution)/shard_map/ppermute | solution.py:470
  60.9 32.0 %collective-permute-start.9 = (bf16[4,256,256]{2,1,0:T(8,128)(2,1)S(1)}, bf16[4,256,256]{2,1,0:T(8,128)(2,1)S(1)}, u32[]{:S(2)}, u32[]{:S(2)}) collective-permute-start(bf16[4,256,256]{2,1,0:T(8,128)(2,1)S(1)} %gather_again.3), channel_id=1, source_target_pairs={{8,0},{12,4},{0,8},{4,12},{9,1},{13,5},{1,9},{5,13},{10,2},{14,6},... | collective-permute-start | bytes 1572872 | tf_op jit(solution)/shard_map/ppermute | solution.py:442
  68.4 2.6 %copy-start.6 = (bf16[16,256,256]{2,1,0:T(8,128)(2,1)S(1)}, bf16[16,256,256]{2,1,0:T(8,128)(2,1)}, u32[]{:S(2)}) copy-start(bf16[16,256,256]{2,1,0:T(8,128)(2,1)} %refs_4_.1) | copy-start | bytes 6291460
  69.3 35.1 %collective-permute-start.8 = (bf16[4,256,256]{2,1,0:T(8,128)(2,1)S(1)}, bf16[4,256,256]{2,1,0:T(8,128)(2,1)S(1)}, u32[]{:S(2)}, u32[]{:S(2)}) collective-permute-start(bf16[4,256,256]{2,1,0:T(8,128)(2,1)S(1)} %get-tuple-element.57), channel_id=1, source_target_pairs={{4,0},{0,4},{12,8},{8,12},{5,1},{1,5},{13,9},{9,13},{6,2},{2,6},{1... | collective-permute-start | bytes 1572872 | tf_op jit(solution)/shard_map/ppermute | solution.py:454
  69.3 1.8 %copy-start.4 = (bf16[16,256,256]{2,1,0:T(8,128)(2,1)S(1)}, bf16[16,256,256]{2,1,0:T(8,128)(2,1)}, u32[]{:S(2)}) copy-start(bf16[16,256,256]{2,1,0:T(8,128)(2,1)} %refs_3_.5) | copy-start | bytes 6291460
  69.3 2.4 %copy-start.2 = (bf16[16,256,256]{2,1,0:T(8,128)(2,1)S(1)}, bf16[16,256,256]{2,1,0:T(8,128)(2,1)}, u32[]{:S(2)}) copy-start(bf16[16,256,256]{2,1,0:T(8,128)(2,1)} %refs_2_.7) | copy-start | bytes 6291460
  69.4 35.0 %collective-permute-start.11 = (bf16[4,256,256]{2,1,0:T(8,128)(2,1)S(1)}, bf16[4,256,256]{2,1,0:T(8,128)(2,1)S(1)}, u32[]{:S(2)}, u32[]{:S(2)}) collective-permute-start(bf16[4,256,256]{2,1,0:T(8,128)(2,1)S(1)} %get-tuple-element.60), channel_id=1, source_target_pairs={{12,0},{8,4},{4,8},{0,12},{13,1},{9,5},{5,9},{1,13},{14,2},{10,6},... | collective-permute-start | bytes 1572872 | tf_op jit(solution)/shard_map/ppermute | solution.py:454
  106.5 24.8 %collective-permute-start.12 = (bf16[4,256,256]{2,1,0:T(8,128)(2,1)S(1)}, bf16[4,256,256]{2,1,0:T(8,128)(2,1)S(1)}, u32[]{:S(2)}, u32[]{:S(2)}) collective-permute-start(bf16[4,256,256]{2,1,0:T(8,128)(2,1)S(1)} %get-tuple-element.61.refs_2_), channel_id=1, source_target_pairs={{0,1},{1,0},{2,3},{3,2},{4,5},{5,4},{6,7},{7,6},{8,9},{9,8},{10,11... | collective-permute-start | bytes 1572872 | tf_op jit(solution)/shard_map/ppermute | solution.py:470
  108.5 22.7 %collective-permute-start.10 = (bf16[4,256,256]{2,1,0:T(8,128)(2,1)S(1)}, bf16[4,256,256]{2,1,0:T(8,128)(2,1)S(1)}, u32[]{:S(2)}, u32[]{:S(2)}) collective-permute-start(bf16[4,256,256]{2,1,0:T(8,128)(2,1)S(1)} %get-tuple-element.59.refs_0_), channel_id=1, source_target_pairs={{0,1},{1,0},{2,3},{3,2},{4,5},{5,4},{6,7},{7,6},{8,9},{9,8},{10,11... | collective-permute-start | bytes 1572872 | tf_op jit(solution)/shard_map/ppermute | solution.py:466
  109.1 1.5 %collective-permute-start.13 = (f32[64]{0:T(128)S(1)}, f32[64]{0:T(128)S(1)}, u32[]{:S(2)}, u32[]{:S(2)}) collective-permute-start(f32[64]{0:T(128)S(1)} %add_bitcast_fusion), channel_id=1, source_target_pairs={{0,1},{1,0},{2,3},{3,2},{4,5},{5,4},{6,7},{7,6},{8,9},{9,8},{10,11... | collective-permute-start | bytes 776 | tf_op jit(solution)/shard_map/ppermute | solution.py:343
  110.6 3.6 %collective-permute-start.14 = (f32[64]{0:T(128)S(1)}, f32[64]{0:T(128)S(1)}, u32[]{:S(2)}, u32[]{:S(2)}) collective-permute-start(f32[64]{0:T(128)S(1)} %add.110), channel_id=1, source_target_pairs={{0,2},{2,0},{1,3},{3,1},{4,6},{6,4},{5,7},{7,5},{8,10},{10,8},{9,1... | collective-permute-start | bytes 776 | tf_op jit(solution)/shard_map/ppermute | solution.py:343
  114.2 12.1 %collective-permute-start.15 = (f32[64]{0:T(128)S(1)}, f32[64]{0:T(128)S(1)}, u32[]{:S(2)}, u32[]{:S(2)}) collective-permute-start(f32[64]{0:T(128)S(1)} %add.111), channel_id=1, source_target_pairs={{0,4},{4,0},{8,12},{12,8},{1,5},{5,1},{9,13},{13,9},{2,6},{6,2},{1... | collective-permute-start | bytes 776 | tf_op jit(solution)/shard_map/ppermute | solution.py:343
  126.3 4.5 %collective-permute-start.16 = (f32[64]{0:T(128)S(1)}, f32[64]{0:T(128)S(1)}, u32[]{:S(2)}, u32[]{:S(2)}) collective-permute-start(f32[64]{0:T(128)S(1)} %add.112), channel_id=1, source_target_pairs={{0,8},{4,12},{8,0},{12,4},{1,9},{5,13},{9,1},{13,5},{2,10},{6,14},... | collective-permute-start | bytes 776 | tf_op jit(solution)/shard_map/ppermute | solution.py:343

commit v6 on v5

--- a/solution.py
+++ b/solution.py
@@ -373,6 +373,7 @@
     here = jnp.stack([row, core]).astype(jnp.int32)
     groups = [[rows // 2], [d for d in range(1, rows) if d != rows // 2]]
     request = lax.ppermute(packed, "row", exchanges(rows, rows // 2))
+    requests = [lax.ppermute(packed, "row", exchanges(rows, d)) for d in groups[1]]
     asked_mid, send_mid = gather_first([request], groups[0], here, amplitudes, rows, cap)
 
     step = apart(rows, source, row)
@@ -427,8 +428,8 @@
     columns = [slot_ids, jnp.concatenate([own, other])]
     ats = [own, jnp.arange(half, dtype=jnp.int32)]
     slots = jnp.concatenate([own[:early], other[:early], own[early:], other[early:]])
-    (own, shift, far_scale, *moved, send_mid) = lax.optimization_barrier(
-        (own, shift, far_scale, *tables, *columns, *ats, slots, send_mid)
+    (own, *moved, send_mid) = lax.optimization_barrier(
+        (own, *tables, *columns, *ats, slots, send_mid)
     )
     tables, columns, ats, slots = moved[:2], moved[2:4], moved[4:6], moved[6]
     stores = [amplitudes]
@@ -441,10 +442,7 @@
         arrived = {}
         arrived[rows // 2] = lax.ppermute(send_mid, "row", returns(rows, rows // 2))
         if sweep == 0:
-            packed, _ = lax.optimization_barrier((packed, send_mid))
-            requests = [
-                lax.ppermute(packed, "row", exchanges(rows, d)) for d in groups[1]
-            ]
+            (*requests, _) = lax.optimization_barrier((*requests, send_mid))
             asked, *sends = gather_first(
                 requests, groups[1], here, amplitudes, rows, cap
             )

time: 134 us -> 133 us (level)
  waiting for transfers between devices: 62.1 us -> 65.3 us
    ppermute x2, waiting for transfers between devices: 27.8 us -> 31.9 us  [per_device(): arrived[rows // 2] = lax.ppermute(send_mid, 'row', returns(rows, rows // 2))]
    ppermute x1, starting transfers between devices: 4.06 us -> 0.56 us  [per_device(): request = lax.ppermute(packed, 'row', exchanges(rows, rows // 2))]
    ppermute x2, starting transfers between devices: 1.72 us -> 5.08 us  [per_device(): lax.ppermute(packed, 'row', exchanges(rows, d))]
    unnamed x21, local copies, waits for them, and re-layouts: 5.54 us -> 3.82 us
    ppermute x4, starting transfers between devices: 13.9 us -> 12.5 us  [add_over(): lax.ppermute(values, name, [(r, r ^ step) for r in range(size)])]
  transfers between devices with their start and end apart: 17 -> 17, of which waited for: 10 -> 11; matrix products, arithmetic and copies ran while one was open for 4% -> 3% of each run, Pallas kernels for 12% -> 14%
where the time goes in v6:
time: 133 us; the launch traced here: 132 us
  waiting for transfers between devices  65.3 us (49%)
  starting transfers between devices  34.6 us (26%)
  Pallas kernels  22.6 us (17%)
  local copies, waits for them, and re-layouts  4.74 us (4%)
  other arithmetic  4.22 us (3%)
    ppermute x2, waiting for transfers between devices, per_device(): arrived[rows // 2] = lax.ppermute(send_mid, 'row', returns(rows, rows // 2))  31.9 us
    ppermute x4, waiting for transfers between devices, per_device(): arrived[d] = lax.ppermute(send, 'row', returns(rows, d))  22.9 us
    ppermute x4, starting transfers between devices, add_over(): lax.ppermute(values, name, [(r, r ^ step) for r in range(size)])  12.5 us
    ppermute x2, starting transfers between devices, per_device(): arrived[rows // 2] = lax.ppermute(send_mid, 'row', returns(rows, rows // 2))  11.6 us
    ppermute x4, waiting for transfers between devices, add_over(): lax.ppermute(values, name, [(r, r ^ step) for r in range(size)])  8.47 us
    pallas_call x2, Pallas kernels, prepare(): pl.pallas_call(body, grid_spec=pltpu.PrefetchScalarGridSpec(num_scalar_pr...  7.21 us
    pallas_call x4, Pallas kernels, finish(): pl.pallas_call(body, out_shape=out_shape, in_specs=[pl.BlockSpec(memory_s...  6.58 us
    pallas_call x2, Pallas kernels, gather_first(): pl.pallas_call(body, out_shape=[jax.ShapeDtypeStruct((count_of * (cap + 1...  5.32 us
  transfers between devices with their start and end apart: 17, of which 11 were waited for; matrix products, arithmetic and copies ran while one was open for 3% of the time, Pallas kernels for 14%

profile of v6, /device:TPU:0, one launch (start us, length us, event | category | flops | bytes accessed | tf_op | source)
XLA Modules:
  0.0 132.3 jit_solution(8111883585092720004)
XLA Ops:
  1.3 5.1 %collective-permute-start.2 = (s32[16]{0:T(128)S(1)}, s32[16]{0:T(128)S(1)}, u32[]{:S(2)}, u32[]{:S(2)}) collective-permute-start(s32[16]{0:T(128)S(1)} %bitcast_add_fusion), channel_id=1, source_target_pairs={{0,12},{4,8},{8,4},{12,0},{1,13},{5,9},{9,5},{13,1},{2,14},{6,10},... | collective-permute-start | bytes 200 | tf_op jit(solution)/shard_map/ppermute | solution.py:376
  8.0 1.0 fusion.6
  9.6 0.7 copy.18.count_ref
  10.9 2.6 %gather_first.2 = (s32[5]{0:T(128)S(1)}, bf16[4,256,256]{2,1,0:T(8,128)(2,1)S(1)}) custom-call(s32[2]{0:T(128)S(1)} %pad_add_fusion.2.place_ref, s32[16]{0:T(128)S(1)} %collective-permute-done.refs_0_, bf16[16,256,256]{2,1,0:T(8,128)(2,1)} %refs_3_.4), custom_call_target="tpu_custom_call" | custom-call | bytes 1048576 | tf_op jit(solution)/shard_map/gather_first/pallas_call | solution.py:95
  13.5 2.3 %collective-permute-start.4 = (bf16[4,256,256]{2,1,0:T(8,128)(2,1)S(1)}, bf16[4,256,256]{2,1,0:T(8,128)(2,1)S(1)}, u32[]{:S(2)}, u32[]{:S(2)}) collective-permute-start(bf16[4,256,256]{2,1,0:T(8,128)(2,1)S(1)} %get-tuple-element.45), channel_id=1, source_target_pairs={{8,0},{12,4},{0,8},{4,12},{9,1},{13,5},{1,9},{5,13},{10,2},{14,6},... | collective-permute-start | bytes 1572872 | tf_op jit(solution)/shard_map/ppermute | solution.py:443
  15.8 2.8 %gather_first.3 = (s32[10]{0:T(128)S(1)}, bf16[4,256,256]{2,1,0:T(8,128)(2,1)S(1)}, bf16[4,256,256]{2,1,0:T(8,128)(2,1)S(1)}) custom-call(s32[2]{0:T(128)S(1)} %pad_add_fusion.2.place_ref, s32[16]{0:T(128)S(1)} %collective-permute-done.1.refs_0_, s32[16]{0:T(128)S(1)} %collective-permute-done.2.refs_1_, bf16[16,256,256]{2,1,0:T(8,128)(2,1)} %refs_3_.4), custom_call_target="tpu_custom_call" | custom-call | bytes 2097152 | tf_op jit(solution)/shard_map/gather_first/pallas_call | solution.py:95
  18.5 2.1 %collective-permute-start.3 = (bf16[4,256,256]{2,1,0:T(8,128)(2,1)S(1)}, bf16[4,256,256]{2,1,0:T(8,128)(2,1)S(1)}, u32[]{:S(2)}, u32[]{:S(2)}) collective-permute-start(bf16[4,256,256]{2,1,0:T(8,128)(2,1)S(1)} %get-tuple-element.48), channel_id=1, source_target_pairs={{4,0},{0,4},{12,8},{8,12},{5,1},{1,5},{13,9},{9,13},{6,2},{2,6},{1... | collective-permute-start | bytes 1572872 | tf_op jit(solution)/shard_map/ppermute | solution.py:452
  21.2 1.6 %copy-done.2 = bf16[16,256,256]{2,1,0:T(8,128)(2,1)S(1)} copy-done((bf16[16,256,256]{2,1,0:T(8,128)(2,1)S(1)}, bf16[16,256,256]{2,1,0:T(8,128)(2,1)}, u32[]{:S(2)}) %copy-start.2) | copy-done | bytes 2097176
  22.8 1.6 %copy-done.4 = bf16[16,256,256]{2,1,0:T(8,128)(2,1)S(1)} copy-done((bf16[16,256,256]{2,1,0:T(8,128)(2,1)S(1)}, bf16[16,256,256]{2,1,0:T(8,128)(2,1)}, u32[]{:S(2)}) %copy-start.4) | copy-done | bytes 2097176
  24.4 3.6 %prepare.2 = (f32[8,256,256]{2,1,0:T(8,128)S(1)}, f32[8,256,256]{2,1,0:T(8,128)S(1)}, f32[8,256,256]{2,1,0:T(8,128)S(1)}, bf16[8,256,256]{2,1,0:T(8,128)(2,1)S(1)}) custom-call(s32[8]{0:T(128)S(1)} %get-tuple-element.39.own_ref.at_ref, s32[8]{0:T(128)S(1)} %get-tuple-element.39.own_ref.at_ref, s32[16]{0:T(128)S(1)} %iota.25.column_ref, ...), custom_call_target="tpu_custom_call" | custom-call | flops 805306368 | bytes 12582912 | tf_op jit(solution)/shard_map/prepare/pallas_call | solution.py:214
  28.0 13.9 %collective-permute-done.4.refs_1_ = bf16[4,256,256]{2,1,0:T(8,128)(2,1)S(1)} collective-permute-done((bf16[4,256,256]{2,1,0:T(8,128)(2,1)S(1)}, bf16[4,256,256]{2,1,0:T(8,128)(2,1)S(1)}, u32[]{:S(2)}, u32[]{:S(2)}) %collective-permute-start.4) | collective-permute-done | bytes 524320 | tf_op jit(solution)/shard_map/ppermute | solution.py:443
  41.9 11.0 %collective-permute-done.3.refs_0_ = bf16[4,256,256]{2,1,0:T(8,128)(2,1)S(1)} collective-permute-done((bf16[4,256,256]{2,1,0:T(8,128)(2,1)S(1)}, bf16[4,256,256]{2,1,0:T(8,128)(2,1)S(1)}, u32[]{:S(2)}, u32[]{:S(2)}) %collective-permute-start.3) | collective-permute-done | bytes 524320 | tf_op jit(solution)/shard_map/ppermute | solution.py:452
  52.9 1.2 finish.4.refs_0_
  54.2 1.2 finish.5.refs_2_
  56.1 1.4 %collective-permute-done.7.refs_3_ = bf16[4,256,256]{2,1,0:T(8,128)(2,1)S(1)} collective-permute-done((bf16[4,256,256]{2,1,0:T(8,128)(2,1)S(1)}, bf16[4,256,256]{2,1,0:T(8,128)(2,1)S(1)}, u32[]{:S(2)}, u32[]{:S(2)}) %collective-permute-start.7) | collective-permute-done | bytes 524320 | tf_op jit(solution)/shard_map/ppermute | solution.py:468
  57.5 0.7 gather_again.3
  58.2 9.3 %collective-permute-start.9 = (bf16[4,256,256]{2,1,0:T(8,128)(2,1)S(1)}, bf16[4,256,256]{2,1,0:T(8,128)(2,1)S(1)}, u32[]{:S(2)}, u32[]{:S(2)}) collective-permute-start(bf16[4,256,256]{2,1,0:T(8,128)(2,1)S(1)} %gather_again.3), channel_id=1, source_target_pairs={{8,0},{12,4},{0,8},{4,12},{9,1},{13,5},{1,9},{5,13},{10,2},{14,6},... | collective-permute-start | bytes 1572872 | tf_op jit(solution)/shard_map/ppermute | solution.py:443
  67.5 0.8 gather_again.2
  68.4 1.4 %collective-permute-start.11 = (bf16[4,256,256]{2,1,0:T(8,128)(2,1)S(1)}, bf16[4,256,256]{2,1,0:T(8,128)(2,1)S(1)}, u32[]{:S(2)}, u32[]{:S(2)}) collective-permute-start(bf16[4,256,256]{2,1,0:T(8,128)(2,1)S(1)} %get-tuple-element.58), channel_id=1, source_target_pairs={{12,0},{8,4},{4,8},{0,12},{13,1},{9,5},{5,9},{1,13},{14,2},{10,6},... | collective-permute-start | bytes 1572872 | tf_op jit(solution)/shard_map/ppermute | solution.py:452
  70.6 3.6 %prepare.3 = (f32[8,256,256]{2,1,0:T(8,128)S(1)}, f32[8,256,256]{2,1,0:T(8,128)S(1)}, f32[8,256,256]{2,1,0:T(8,128)S(1)}, bf16[8,256,256]{2,1,0:T(8,128)(2,1)S(1)}) custom-call(s32[8]{0:T(128)S(1)} %get-tuple-element.39.own_ref.at_ref, s32[8]{0:T(128)S(1)} %iota.26.at_ref, s32[16]{0:T(128)S(1)} %pad_add_fusion.column_ref, f32[8]{0:T(128)S(1)} %add.105.shift_ref, ...), custom_call_target="tpu_custom_call" | custom-call | flops 805306368 | bytes 12582912 | tf_op jit(solution)/shard_map/prepare/pallas_call | solution.py:214
  74.2 18.0 %collective-permute-done.9.refs_1_ = bf16[4,256,256]{2,1,0:T(8,128)(2,1)S(1)} collective-permute-done((bf16[4,256,256]{2,1,0:T(8,128)(2,1)S(1)}, bf16[4,256,256]{2,1,0:T(8,128)(2,1)S(1)}, u32[]{:S(2)}, u32[]{:S(2)}) %collective-permute-start.9) | collective-permute-done | bytes 524320 | tf_op jit(solution)/shard_map/ppermute | solution.py:443
  92.2 12.0 %collective-permute-done.8.refs_0_ = bf16[4,256,256]{2,1,0:T(8,128)(2,1)S(1)} collective-permute-done((bf16[4,256,256]{2,1,0:T(8,128)(2,1)S(1)}, bf16[4,256,256]{2,1,0:T(8,128)(2,1)S(1)}, u32[]{:S(2)}, u32[]{:S(2)}) %collective-permute-start.8) | collective-permute-done | bytes 524320 | tf_op jit(solution)/shard_map/ppermute | solution.py:452
  104.2 2.1 %finish.7 = (bf16[4,256,256]{2,1,0:T(8,128)(2,1)S(1)}, f32[1,64]{1,0:T(1,128)S(1)}) custom-call(s32[24]{0:T(128)S(1)} %get-tuple-element.34.number_ref, f32[8]{0:T(128)S(1)} %fusion.8.scale_ref, f32[8,256,256]{2,1,0:T(8,128)S(1)} %get-tuple-element.50.local_ref, f32[8,256,256]{2,1,0:T(8,128)S(1)} %get-tuple-element.51.rest_ref, ...), custom_call_target="tpu_custom_call" | custom-call | flops 268435456 | bytes 4718592 | tf_op jit(solution)/shard_map/finish/pallas_call | solution.py:291
  106.3 2.1 %finish.6 = (bf16[4,256,256]{2,1,0:T(8,128)(2,1)S(1)}, f32[1,64]{1,0:T(1,128)S(1)}) custom-call(s32[24]{0:T(128)S(1)} %get-tuple-element.34.number_ref, f32[8]{0:T(128)S(1)} %fusion.8.scale_ref, f32[8,256,256]{2,1,0:T(8,128)S(1)} %get-tuple-element.50.local_ref, f32[8,256,256]{2,1,0:T(8,128)S(1)} %get-tuple-element.51.rest_ref, ...), custom_call_target="tpu_custom_call" | custom-call | flops 268435456 | bytes 4718592 | tf_op jit(solution)/shard_map/finish/pallas_call | solution.py:291
  108.9 1.5 %collective-permute-done.13 = f32[64]{0:T(128)S(1)} collective-permute-done((f32[64]{0:T(128)S(1)}, f32[64]{0:T(128)S(1)}, u32[]{:S(2)}, u32[]{:S(2)}) %collective-permute-start.13) | collective-permute-done | bytes 288 | tf_op jit(solution)/shard_map/ppermute | solution.py:343
  110.4 1.5 %collective-permute-start.14 = (f32[64]{0:T(128)S(1)}, f32[64]{0:T(128)S(1)}, u32[]{:S(2)}, u32[]{:S(2)}) collective-permute-start(f32[64]{0:T(128)S(1)} %add.110), channel_id=1, source_target_pairs={{0,2},{2,0},{1,3},{3,1},{4,6},{6,4},{5,7},{7,5},{8,10},{10,8},{9,1... | collective-permute-start | bytes 776 | tf_op jit(solution)/shard_map/ppermute | solution.py:343
  111.9 2.1 %collective-permute-done.14 = f32[64]{0:T(128)S(1)} collective-permute-done((f32[64]{0:T(128)S(1)}, f32[64]{0:T(128)S(1)}, u32[]{:S(2)}, u32[]{:S(2)}) %collective-permute-start.14) | collective-permute-done | bytes 288 | tf_op jit(solution)/shard_map/ppermute | solution.py:343
  113.9 9.9 %collective-permute-start.15 = (f32[64]{0:T(128)S(1)}, f32[64]{0:T(128)S(1)}, u32[]{:S(2)}, u32[]{:S(2)}) collective-permute-start(f32[64]{0:T(128)S(1)} %add.111), channel_id=1, source_target_pairs={{0,4},{4,0},{8,12},{12,8},{1,5},{5,1},{9,13},{13,9},{2,6},{6,2},{1... | collective-permute-start | bytes 776 | tf_op jit(solution)/shard_map/ppermute | solution.py:343
  123.8 1.5 %collective-permute-done.15 = f32[64]{0:T(128)S(1)} collective-permute-done((f32[64]{0:T(128)S(1)}, f32[64]{0:T(128)S(1)}, u32[]{:S(2)}, u32[]{:S(2)}) %collective-permute-start.15) | collective-permute-done | bytes 288 | tf_op jit(solution)/shard_map/ppermute | solution.py:343
  125.4 1.1 collective-permute-start.16
  126.4 3.4 %collective-permute-done.16 = f32[64]{0:T(128)S(1)} collective-permute-done((f32[64]{0:T(128)S(1)}, f32[64]{0:T(128)S(1)}, u32[]{:S(2)}, u32[]{:S(2)}) %collective-permute-start.16) | collective-permute-done | bytes 288 | tf_op jit(solution)/shard_map/ppermute | solution.py:343
  130.3 2.0 %put_in_slots.1 = bf16[16,256,256]{2,1,0:T(8,128)(2,1)} custom-call(s32[16]{0:T(128)S(1)} %pad_add_fusion.1.slot_ref, bf16[4,256,256]{2,1,0:T(8,128)(2,1)S(1)} %get-tuple-element.57.refs_0_, bf16[4,256,256]{2,1,0:T(8,128)(2,1)S(1)} %collective-permute-done.10.refs_1_, bf16[4,256,256]{2,1,0:T(8,128)(2,1)S(1)} %get-tuple-element.59.refs_2_, ...), custom_call_target="tpu_custom_call" | custom-call | bytes 4194304 | tf_op jit(solution)/shard_map/put_in_slots/pallas_call | solution.py:324
  (63 shorter events, 6.6 us)
Async XLA Ops:
  1.3 14.5 %collective-permute-start.2 = (s32[16]{0:T(128)S(1)}, s32[16]{0:T(128)S(1)}, u32[]{:S(2)}, u32[]{:S(2)}) collective-permute-start(s32[16]{0:T(128)S(1)} %bitcast_add_fusion), channel_id=1, source_target_pairs={{0,12},{4,8},{8,4},{12,0},{1,13},{5,9},{9,5},{13,1},{2,14},{6,10},... | collective-permute-start | bytes 200 | tf_op jit(solution)/shard_map/ppermute | solution.py:376
  6.4 9.4 %collective-permute-start.1 = (s32[16]{0:T(128)S(1)}, s32[16]{0:T(128)S(1)}, u32[]{:S(2)}, u32[]{:S(2)}) collective-permute-start(s32[16]{0:T(128)S(1)} %bitcast_add_fusion), channel_id=1, source_target_pairs={{0,4},{4,0},{8,12},{12,8},{1,5},{5,1},{9,13},{13,9},{2,6},{6,2},{1... | collective-permute-start | bytes 200 | tf_op jit(solution)/shard_map/ppermute | solution.py:376
  6.4 4.5 %collective-permute-start = (s32[16]{0:T(128)S(1)}, s32[16]{0:T(128)S(1)}, u32[]{:S(2)}, u32[]{:S(2)}) collective-permute-start(s32[16]{0:T(128)S(1)} %bitcast_add_fusion), channel_id=1, source_target_pairs={{0,8},{4,12},{8,0},{12,4},{1,9},{5,13},{9,1},{13,5},{2,10},{6,14},... | collective-permute-start | bytes 200 | tf_op jit(solution)/shard_map/ppermute | solution.py:375
  10.4 10.4 %copy-start.8 = (f32[64]{0:T(128)S(1)}, f32[64]{0:T(128)}, u32[]{:S(2)}) copy-start(f32[64]{0:T(128)} %param.17) | copy-start | bytes 772
  10.4 10.6 %copy-start.9 = (bf16[16,1]{0,1:T(2,128)(2,1)S(1)}, bf16[16,1]{0,1:T(2,128)(2,1)}, u32[]{:S(2)}) copy-start(bf16[16,1]{0,1:T(2,128)(2,1)} %param.25) | copy-start | bytes 100
  10.4 10.8 %copy-start = (bf16[16,256,256]{2,1,0:T(8,128)(2,1)S(1)}, bf16[16,256,256]{2,1,0:T(8,128)(2,1)}, u32[]{:S(2)}) copy-start(bf16[16,256,256]{2,1,0:T(8,128)(2,1)} %refs_3_.4) | copy-start | bytes 6291460
  10.4 10.8 %copy-start.1 = (bf16[16,256,256]{2,1,0:T(8,128)(2,1)S(1)}, bf16[16,256,256]{2,1,0:T(8,128)(2,1)}, u32[]{:S(2)}) copy-start(bf16[16,256,256]{2,1,0:T(8,128)(2,1)} %refs_2_.7) | copy-start | bytes 6291460
  10.4 10.8 %copy-start.6 = (s32[16,11]{1,0:T(8,128)S(1)}, s32[16,11]{1,0:T(8,128)}, u32[]{:S(2)}) copy-start(s32[16,11]{1,0:T(8,128)} %slot_ref.3) | copy-start | bytes 2116
  10.4 10.8 %copy-start.7 = (bf16[16,11]{1,0:T(8,128)(2,1)S(1)}, bf16[16,11]{1,0:T(8,128)(2,1)}, u32[]{:S(2)}) copy-start(bf16[16,11]{1,0:T(8,128)(2,1)} %weight_ref.3) | copy-start | bytes 1060
  13.5 28.5 %collective-permute-start.4 = (bf16[4,256,256]{2,1,0:T(8,128)(2,1)S(1)}, bf16[4,256,256]{2,1,0:T(8,128)(2,1)S(1)}, u32[]{:S(2)}, u32[]{:S(2)}) collective-permute-start(bf16[4,256,256]{2,1,0:T(8,128)(2,1)S(1)} %get-tuple-element.45), channel_id=1, source_target_pairs={{8,0},{12,4},{0,8},{4,12},{9,1},{13,5},{1,9},{5,13},{10,2},{14,6},... | collective-permute-start | bytes 1572872 | tf_op jit(solution)/shard_map/ppermute | solution.py:443
  18.5 34.4 %collective-permute-start.3 = (bf16[4,256,256]{2,1,0:T(8,128)(2,1)S(1)}, bf16[4,256,256]{2,1,0:T(8,128)(2,1)S(1)}, u32[]{:S(2)}, u32[]{:S(2)}) collective-permute-start(bf16[4,256,256]{2,1,0:T(8,128)(2,1)S(1)} %get-tuple-element.48), channel_id=1, source_target_pairs={{4,0},{0,4},{12,8},{8,12},{5,1},{1,5},{13,9},{9,13},{6,2},{2,6},{1... | collective-permute-start | bytes 1572872 | tf_op jit(solution)/shard_map/ppermute | solution.py:452
  20.6 33.6 %collective-permute-start.5 = (bf16[4,256,256]{2,1,0:T(8,128)(2,1)S(1)}, bf16[4,256,256]{2,1,0:T(8,128)(2,1)S(1)}, u32[]{:S(2)}, u32[]{:S(2)}) collective-permute-start(bf16[4,256,256]{2,1,0:T(8,128)(2,1)S(1)} %get-tuple-element.49), channel_id=1, source_target_pairs={{12,0},{8,4},{4,8},{0,12},{13,1},{9,5},{5,9},{1,13},{14,2},{10,6},... | collective-permute-start | bytes 1572872 | tf_op jit(solution)/shard_map/ppermute | solution.py:452
  21.2 1.6 %copy-start.2 = (bf16[16,256,256]{2,1,0:T(8,128)(2,1)S(1)}, bf16[16,256,256]{2,1,0:T(8,128)(2,1)}, u32[]{:S(2)}) copy-start(bf16[16,256,256]{2,1,0:T(8,128)(2,1)} %refs_3_.5) | copy-start | bytes 6291460
  22.8 1.6 %copy-start.4 = (bf16[16,256,256]{2,1,0:T(8,128)(2,1)S(1)}, bf16[16,256,256]{2,1,0:T(8,128)(2,1)}, u32[]{:S(2)}) copy-start(bf16[16,256,256]{2,1,0:T(8,128)(2,1)} %refs_4_.1) | copy-start | bytes 6291460
  54.1 2.0 %collective-permute-start.6 = (bf16[4,256,256]{2,1,0:T(8,128)(2,1)S(1)}, bf16[4,256,256]{2,1,0:T(8,128)(2,1)S(1)}, u32[]{:S(2)}, u32[]{:S(2)}) collective-permute-start(bf16[4,256,256]{2,1,0:T(8,128)(2,1)S(1)} %finish.4.refs_0_), channel_id=1, source_target_pairs={{0,1},{1,0},{2,3},{3,2},{4,5},{5,4},{6,7},{7,6},{8,9},{9,8},{10,11... | collective-permute-start | bytes 1572872 | tf_op jit(solution)/shard_map/ppermute | solution.py:464
  55.4 2.1 %collective-permute-start.7 = (bf16[4,256,256]{2,1,0:T(8,128)(2,1)S(1)}, bf16[4,256,256]{2,1,0:T(8,128)(2,1)S(1)}, u32[]{:S(2)}, u32[]{:S(2)}) collective-permute-start(bf16[4,256,256]{2,1,0:T(8,128)(2,1)S(1)} %finish.5.refs_2_), channel_id=1, source_target_pairs={{0,1},{1,0},{2,3},{3,2},{4,5},{5,4},{6,7},{7,6},{8,9},{9,8},{10,11... | collective-permute-start | bytes 1572872 | tf_op jit(solution)/shard_map/ppermute | solution.py:468
  58.2 34.0 %collective-permute-start.9 = (bf16[4,256,256]{2,1,0:T(8,128)(2,1)S(1)}, bf16[4,256,256]{2,1,0:T(8,128)(2,1)S(1)}, u32[]{:S(2)}, u32[]{:S(2)}) collective-permute-start(bf16[4,256,256]{2,1,0:T(8,128)(2,1)S(1)} %gather_again.3), channel_id=1, source_target_pairs={{8,0},{12,4},{0,8},{4,12},{9,1},{13,5},{1,9},{5,13},{10,2},{14,6},... | collective-permute-start | bytes 1572872 | tf_op jit(solution)/shard_map/ppermute | solution.py:443
  68.3 35.8 %collective-permute-start.8 = (bf16[4,256,256]{2,1,0:T(8,128)(2,1)S(1)}, bf16[4,256,256]{2,1,0:T(8,128)(2,1)S(1)}, u32[]{:S(2)}, u32[]{:S(2)}) collective-permute-start(bf16[4,256,256]{2,1,0:T(8,128)(2,1)S(1)} %get-tuple-element.55), channel_id=1, source_target_pairs={{4,0},{0,4},{12,8},{8,12},{5,1},{1,5},{13,9},{9,13},{6,2},{2,6},{1... | collective-permute-start | bytes 1572872 | tf_op jit(solution)/shard_map/ppermute | solution.py:452
  68.4 1.7 %copy-start.5 = (bf16[16,256,256]{2,1,0:T(8,128)(2,1)S(1)}, bf16[16,256,256]{2,1,0:T(8,128)(2,1)}, u32[]{:S(2)}) copy-start(bf16[16,256,256]{2,1,0:T(8,128)(2,1)} %refs_4_.1) | copy-start | bytes 6291460
  68.4 2.2 %copy-start.3 = (bf16[16,256,256]{2,1,0:T(8,128)(2,1)S(1)}, bf16[16,256,256]{2,1,0:T(8,128)(2,1)}, u32[]{:S(2)}) copy-start(bf16[16,256,256]{2,1,0:T(8,128)(2,1)} %refs_3_.5) | copy-start | bytes 6291460
  68.4 35.7 %collective-permute-start.11 = (bf16[4,256,256]{2,1,0:T(8,128)(2,1)S(1)}, bf16[4,256,256]{2,1,0:T(8,128)(2,1)S(1)}, u32[]{:S(2)}, u32[]{:S(2)}) collective-permute-start(bf16[4,256,256]{2,1,0:T(8,128)(2,1)S(1)} %get-tuple-element.58), channel_id=1, source_target_pairs={{12,0},{8,4},{4,8},{0,12},{13,1},{9,5},{5,9},{1,13},{14,2},{10,6},... | collective-permute-start | bytes 1572872 | tf_op jit(solution)/shard_map/ppermute | solution.py:452
  106.3 24.1 %collective-permute-start.12 = (bf16[4,256,256]{2,1,0:T(8,128)(2,1)S(1)}, bf16[4,256,256]{2,1,0:T(8,128)(2,1)S(1)}, u32[]{:S(2)}, u32[]{:S(2)}) collective-permute-start(bf16[4,256,256]{2,1,0:T(8,128)(2,1)S(1)} %get-tuple-element.59.refs_2_), channel_id=1, source_target_pairs={{0,1},{1,0},{2,3},{3,2},{4,5},{5,4},{6,7},{7,6},{8,9},{9,8},{10,11... | collective-permute-start | bytes 1572872 | tf_op jit(solution)/shard_map/ppermute | solution.py:468
  108.3 22.0 %collective-permute-start.10 = (bf16[4,256,256]{2,1,0:T(8,128)(2,1)S(1)}, bf16[4,256,256]{2,1,0:T(8,128)(2,1)S(1)}, u32[]{:S(2)}, u32[]{:S(2)}) collective-permute-start(bf16[4,256,256]{2,1,0:T(8,128)(2,1)S(1)} %get-tuple-element.57.refs_0_), channel_id=1, source_target_pairs={{0,1},{1,0},{2,3},{3,2},{4,5},{5,4},{6,7},{7,6},{8,9},{9,8},{10,11... | collective-permute-start | bytes 1572872 | tf_op jit(solution)/shard_map/ppermute | solution.py:464
  108.8 1.5 %collective-permute-start.13 = (f32[64]{0:T(128)S(1)}, f32[64]{0:T(128)S(1)}, u32[]{:S(2)}, u32[]{:S(2)}) collective-permute-start(f32[64]{0:T(128)S(1)} %add_bitcast_fusion), channel_id=1, source_target_pairs={{0,1},{1,0},{2,3},{3,2},{4,5},{5,4},{6,7},{7,6},{8,9},{9,8},{10,11... | collective-permute-start | bytes 776 | tf_op jit(solution)/shard_map/ppermute | solution.py:343
  110.4 3.6 %collective-permute-start.14 = (f32[64]{0:T(128)S(1)}, f32[64]{0:T(128)S(1)}, u32[]{:S(2)}, u32[]{:S(2)}) collective-permute-start(f32[64]{0:T(128)S(1)} %add.110), channel_id=1, source_target_pairs={{0,2},{2,0},{1,3},{3,1},{4,6},{6,4},{5,7},{7,5},{8,10},{10,8},{9,1... | collective-permute-start | bytes 776 | tf_op jit(solution)/shard_map/ppermute | solution.py:343
  113.9 11.4 %collective-permute-start.15 = (f32[64]{0:T(128)S(1)}, f32[64]{0:T(128)S(1)}, u32[]{:S(2)}, u32[]{:S(2)}) collective-permute-start(f32[64]{0:T(128)S(1)} %add.111), channel_id=1, source_target_pairs={{0,4},{4,0},{8,12},{12,8},{1,5},{5,1},{9,13},{13,9},{2,6},{6,2},{1... | collective-permute-start | bytes 776 | tf_op jit(solution)/shard_map/ppermute | solution.py:343
  125.4 4.5 %collective-permute-start.16 = (f32[64]{0:T(128)S(1)}, f32[64]{0:T(128)S(1)}, u32[]{:S(2)}, u32[]{:S(2)}) collective-permute-start(f32[64]{0:T(128)S(1)} %add.112), channel_id=1, source_target_pairs={{0,8},{4,12},{8,0},{12,4},{1,9},{5,13},{9,1},{13,5},{2,10},{6,14},... | collective-permute-start | bytes 776 | tf_op jit(solution)/shard_map/ppermute | solution.py:343

commit v7 on v6

--- a/solution.py
+++ b/solution.py
@@ -14,20 +14,25 @@
 MIB = 1 << 20
 
 
-def exchanges(rows, shift):
-    if rows & (rows - 1):
-        return [(r, (r - shift) % rows) for r in range(rows)]
-    return [(r, r ^ shift) for r in range(rows)]
-
-
-def returns(rows, shift):
-    return [(b, a) for a, b in exchanges(rows, shift)]
-
-
-def apart(rows, source, row):
-    if rows & (rows - 1):
-        return (row - source) % rows
-    return source ^ row
+def ring(rows, row):
+    return row if rows & (rows - 1) else row ^ (row >> 1)
+
+
+def sent(rows, step):
+    hop = (step + 1) // 2 if step % 2 else rows - step // 2
+    where = {ring(rows, r): r for r in range(rows)}
+    return [(r, where[(ring(rows, r) + hop) % rows]) for r in range(rows)]
+
+
+def asked_of(rows, step):
+    return [(b, a) for a, b in sent(rows, step)]
+
+
+def step_of(rows, source, row):
+    hop = ring(rows, row) - ring(rows, source)
+    hop = jnp.where(hop < 0, hop + rows, hop)
+    step = jnp.where(2 * hop <= rows, 2 * hop - 1, 2 * (rows - hop))
+    return jnp.where(hop == 0, 0, step)
 
 
 def limits(mib):
@@ -69,13 +74,15 @@
         core = place_ref[1]
         for n, shift in enumerate(shifts):
             base = n * (cap + 1)
-            asker = apart(rows, me, shift) if rows & (rows - 1) == 0 else (me + shift) % rows
+            asker = jnp.int32(0)
+            for a, b in sent(rows, shift):
+                asker = jnp.where(me == a, b, asker)
             for k in range(cap):
                 asked[base + k] = 0
             sources = [lists[n][p] // pairs for p in range(pairs)]
             count = jnp.int32(0)
             for p in range(pairs):
-                count = count + (apart(rows, sources[p], asker) < shift).astype(jnp.int32)
+                count = count + (step_of(rows, sources[p], asker) < shift).astype(jnp.int32)
             filled = jnp.int32(0)
             for p in range(pairs):
                 mine = sources[p] == me
@@ -371,12 +378,12 @@
     source = far_chip[:, 0]
     packed = source * pairs + far_slot[:, 0]
     here = jnp.stack([row, core]).astype(jnp.int32)
-    groups = [[rows // 2], [d for d in range(1, rows) if d != rows // 2]]
-    request = lax.ppermute(packed, "row", exchanges(rows, rows // 2))
-    requests = [lax.ppermute(packed, "row", exchanges(rows, d)) for d in groups[1]]
-    asked_mid, send_mid = gather_first([request], groups[0], here, amplitudes, rows, cap)
-
-    step = apart(rows, source, row)
+    groups = [[1], list(range(2, rows))]
+    request = lax.ppermute(packed, "row", asked_of(rows, 1))
+    requests = [lax.ppermute(packed, "row", asked_of(rows, d)) for d in groups[1]]
+    asked_lead, send_lead = gather_first([request], groups[0], here, amplitudes, rows, cap)
+
+    step = step_of(rows, source, row)
     same = step[:, None] == step[None, :]
     before = (step[None, :] < step[:, None]) | (same & (slot_ids[None, :] < slot_ids[:, None]))
     turn = jnp.sum(before.astype(jnp.int32), axis=1)
@@ -428,8 +435,8 @@
     columns = [slot_ids, jnp.concatenate([own, other])]
     ats = [own, jnp.arange(half, dtype=jnp.int32)]
     slots = jnp.concatenate([own[:early], other[:early], own[early:], other[early:]])
-    (own, *moved, send_mid) = lax.optimization_barrier(
-        (own, *tables, *columns, *ats, slots, send_mid)
+    (own, *moved, send_lead) = lax.optimization_barrier(
+        (own, *tables, *columns, *ats, slots, send_lead)
     )
     tables, columns, ats, slots = moved[:2], moved[2:4], moved[4:6], moved[6]
     stores = [amplitudes]
@@ -438,18 +445,18 @@
         last = sweep == ITERS - 1
         again = min(sweep, 1)
         if sweep > 0:
-            (send_mid,) = gather_again(asked_mid, local_spots[1], stores, cap)
+            (send_lead,) = gather_again(asked_lead, local_spots[1], stores, cap)
         arrived = {}
-        arrived[rows // 2] = lax.ppermute(send_mid, "row", returns(rows, rows // 2))
+        arrived[1] = lax.ppermute(send_lead, "row", sent(rows, 1))
         if sweep == 0:
-            (*requests, _) = lax.optimization_barrier((*requests, send_mid))
+            (*requests, _) = lax.optimization_barrier((*requests, send_lead))
             asked, *sends = gather_first(
                 requests, groups[1], here, amplitudes, rows, cap
             )
         else:
             sends = gather_again(asked, local_spots[1], stores, cap)
         for d, send in zip(groups[1], sends):
-            arrived[d] = lax.ppermute(send, "row", returns(rows, d))
+            arrived[d] = lax.ppermute(send, "row", sent(rows, d))
         arrived = [arrived[d] for d in range(1, rows)]
         prepared = prepare(
             own, ats[again], columns[again], shift, near, whole,

time: 133 us -> 133 us (level)
  starting transfers between devices: 34.6 us -> 39.1 us
  waiting for transfers between devices: 65.3 us -> 61.1 us
    ppermute x4, starting transfers between devices: 12.5 us -> 16.1 us  [add_over(): lax.ppermute(values, name, [(r, r ^ step) for r in range(size)])]
    ppermute x9, waiting for transfers between devices: 55.3 us -> 52.9 us  [the longest x2 30.3 us: per_device(): arrived[1] = lax.ppermute(send_lead, 'row', sent(rows, 1))]
    ppermute x4, waiting for transfers between devices: 8.47 us -> 6.61 us  [add_over(): lax.ppermute(values, name, [(r, r ^ step) for r in range(size)])]
  transfers between devices with their start and end apart: 17 -> 17, of which waited for: 11 -> 10; matrix products, arithmetic and copies ran while one was open for 3% -> 3% of each run, Pallas kernels for 14% -> 14%
where the time goes in v7:
time: 133 us
  waiting for transfers between devices  61.1 us (46%)
  starting transfers between devices  39.1 us (29%)
  Pallas kernels  23.2 us (17%)
  other arithmetic  4.24 us (3%)
  local copies, waits for them, and re-layouts  4.18 us (3%)
    ppermute x2, waiting for transfers between devices, per_device(): arrived[1] = lax.ppermute(send_lead, 'row', sent(rows, 1))  30.3 us
    ppermute x4, waiting for transfers between devices, per_device(): arrived[d] = lax.ppermute(send, 'row', sent(rows, d))  22.6 us
    ppermute x4, starting transfers between devices, add_over(): lax.ppermute(values, name, [(r, r ^ step) for r in range(size)])  16.1 us
    ppermute x2, starting transfers between devices, per_device(): arrived[1] = lax.ppermute(send_lead, 'row', sent(rows, 1))  8.51 us
    pallas_call x2, Pallas kernels, prepare(): pl.pallas_call(body, grid_spec=pltpu.PrefetchScalarGridSpec(num_scalar_pr...  7.22 us
    ppermute x4, waiting for transfers between devices, add_over(): lax.ppermute(values, name, [(r, r ^ step) for r in range(size)])  6.61 us
    pallas_call x4, Pallas kernels, finish(): pl.pallas_call(body, out_shape=out_shape, in_specs=[pl.BlockSpec(memory_s...  6.58 us
    pallas_call x2, Pallas kernels, gather_first(): pl.pallas_call(body, out_shape=[jax.ShapeDtypeStruct((count_of * (cap + 1...  5.86 us
  transfers between devices with their start and end apart: 17, of which 10 were waited for; matrix products, arithmetic and copies ran while one was open for 3% of the time, Pallas kernels for 14%

profile of v7, /device:TPU:0, one launch (start us, length us, event | category | flops | bytes accessed | tf_op | source)
XLA Modules:
  0.0 132.7 jit_solution(11658488776537185088)
XLA Ops:
  1.3 5.1 %collective-permute-start.3 = (s32[16]{0:T(128)S(1)}, s32[16]{0:T(128)S(1)}, u32[]{:S(2)}, u32[]{:S(2)}) collective-permute-start(s32[16]{0:T(128)S(1)} %get-tuple-element.80), channel_id=1, source_target_pairs={{12,0},{8,4},{4,8},{0,12},{13,1},{9,5},{5,9},{1,13},{14,2},{10,6},... | collective-permute-start | bytes 200 | tf_op jit(solution)/shard_map/ppermute | solution.py:383
  6.4 2.9 %collective-permute-start = (s32[16]{0:T(128)S(1)}, s32[16]{0:T(128)S(1)}, u32[]{:S(2)}, u32[]{:S(2)}) collective-permute-start(s32[16]{0:T(128)S(1)} %get-tuple-element.80), channel_id=1, source_target_pairs={{4,0},{12,4},{0,8},{8,12},{5,1},{13,5},{1,9},{9,13},{6,2},{14,6},{... | collective-permute-start | bytes 200 | tf_op jit(solution)/shard_map/ppermute | solution.py:382
  10.4 1.0 fusion.6
  12.0 0.7 copy.18.count_ref
  12.8 3.0 %gather_first.2 = (s32[5]{0:T(128)S(1)}, bf16[4,256,256]{2,1,0:T(8,128)(2,1)S(1)}) custom-call(s32[2]{0:T(128)S(1)} %pad_add_fusion.2.place_ref, s32[16]{0:T(128)S(1)} %collective-permute-done.refs_0_, bf16[16,256,256]{2,1,0:T(8,128)(2,1)} %refs_3_.4), custom_call_target="tpu_custom_call" | custom-call | bytes 1048576 | tf_op jit(solution)/shard_map/gather_first/pallas_call | solution.py:102
  15.9 2.9 %gather_first.3 = (s32[10]{0:T(128)S(1)}, bf16[4,256,256]{2,1,0:T(8,128)(2,1)S(1)}, bf16[4,256,256]{2,1,0:T(8,128)(2,1)S(1)}) custom-call(s32[2]{0:T(128)S(1)} %pad_add_fusion.2.place_ref, s32[16]{0:T(128)S(1)} %collective-permute-done.2.refs_0_, s32[16]{0:T(128)S(1)} %collective-permute-done.3.refs_1_, bf16[16,256,256]{2,1,0:T(8,128)(2,1)} %refs_3_.4), custom_call_target="tpu_custom_call" | custom-call | bytes 2097152 | tf_op jit(solution)/shard_map/gather_first/pallas_call | solution.py:102
  18.8 2.9 %collective-permute-start.4 = (bf16[4,256,256]{2,1,0:T(8,128)(2,1)S(1)}, bf16[4,256,256]{2,1,0:T(8,128)(2,1)S(1)}, u32[]{:S(2)}, u32[]{:S(2)}) collective-permute-start(bf16[4,256,256]{2,1,0:T(8,128)(2,1)S(1)} %get-tuple-element.48), channel_id=1, source_target_pairs={{0,8},{4,0},{8,12},{12,4},{1,9},{5,1},{9,13},{13,5},{2,10},{6,2},{... | collective-permute-start | bytes 1572872 | tf_op jit(solution)/shard_map/ppermute | solution.py:459
  22.3 1.6 %copy-done.2 = bf16[16,256,256]{2,1,0:T(8,128)(2,1)S(1)} copy-done((bf16[16,256,256]{2,1,0:T(8,128)(2,1)S(1)}, bf16[16,256,256]{2,1,0:T(8,128)(2,1)}, u32[]{:S(2)}) %copy-start.2) | copy-done | bytes 2097176
  23.8 1.6 %copy-done.4 = bf16[16,256,256]{2,1,0:T(8,128)(2,1)S(1)} copy-done((bf16[16,256,256]{2,1,0:T(8,128)(2,1)S(1)}, bf16[16,256,256]{2,1,0:T(8,128)(2,1)}, u32[]{:S(2)}) %copy-start.4) | copy-done | bytes 2097176
  25.4 3.6 %prepare.2 = (f32[8,256,256]{2,1,0:T(8,128)S(1)}, f32[8,256,256]{2,1,0:T(8,128)S(1)}, f32[8,256,256]{2,1,0:T(8,128)S(1)}, bf16[8,256,256]{2,1,0:T(8,128)(2,1)S(1)}) custom-call(s32[8]{0:T(128)S(1)} %get-tuple-element.39.own_ref.at_ref, s32[8]{0:T(128)S(1)} %get-tuple-element.39.own_ref.at_ref, s32[16]{0:T(128)S(1)} %iota.25.column_ref, ...), custom_call_target="tpu_custom_call" | custom-call | flops 805306368 | bytes 12582912 | tf_op jit(solution)/shard_map/prepare/pallas_call | solution.py:221
  29.1 25.0 %collective-permute-done.1.refs_0_ = bf16[4,256,256]{2,1,0:T(8,128)(2,1)S(1)} collective-permute-done((bf16[4,256,256]{2,1,0:T(8,128)(2,1)S(1)}, bf16[4,256,256]{2,1,0:T(8,128)(2,1)S(1)}, u32[]{:S(2)}, u32[]{:S(2)}) %collective-permute-start.1) | collective-permute-done | bytes 524320 | tf_op jit(solution)/shard_map/ppermute | solution.py:450
  54.1 1.2 finish.4.refs_0_
  55.4 1.2 finish.5.refs_2_
  57.3 1.4 %collective-permute-done.7.refs_3_ = bf16[4,256,256]{2,1,0:T(8,128)(2,1)S(1)} collective-permute-done((bf16[4,256,256]{2,1,0:T(8,128)(2,1)S(1)}, bf16[4,256,256]{2,1,0:T(8,128)(2,1)S(1)}, u32[]{:S(2)}, u32[]{:S(2)}) %collective-permute-start.7) | collective-permute-done | bytes 524320 | tf_op jit(solution)/shard_map/ppermute | solution.py:475
  58.7 0.7 gather_again.2
  59.4 8.4 %collective-permute-start.8 = (bf16[4,256,256]{2,1,0:T(8,128)(2,1)S(1)}, bf16[4,256,256]{2,1,0:T(8,128)(2,1)S(1)}, u32[]{:S(2)}, u32[]{:S(2)}) collective-permute-start(bf16[4,256,256]{2,1,0:T(8,128)(2,1)S(1)} %gather_again.2), channel_id=1, source_target_pairs={{0,4},{4,12},{8,0},{12,8},{1,5},{5,13},{9,1},{13,9},{2,6},{6,14},{... | collective-permute-start | bytes 1572872 | tf_op jit(solution)/shard_map/ppermute | solution.py:450
  67.9 0.8 gather_again.3
  68.8 2.3 %collective-permute-start.11 = (bf16[4,256,256]{2,1,0:T(8,128)(2,1)S(1)}, bf16[4,256,256]{2,1,0:T(8,128)(2,1)S(1)}, u32[]{:S(2)}, u32[]{:S(2)}) collective-permute-start(bf16[4,256,256]{2,1,0:T(8,128)(2,1)S(1)} %get-tuple-element.58), channel_id=1, source_target_pairs={{0,12},{4,8},{8,4},{12,0},{1,13},{5,9},{9,5},{13,1},{2,14},{6,10},... | collective-permute-start | bytes 1572872 | tf_op jit(solution)/shard_map/ppermute | solution.py:459
  71.4 3.6 %prepare.3 = (f32[8,256,256]{2,1,0:T(8,128)S(1)}, f32[8,256,256]{2,1,0:T(8,128)S(1)}, f32[8,256,256]{2,1,0:T(8,128)S(1)}, bf16[8,256,256]{2,1,0:T(8,128)(2,1)S(1)}) custom-call(s32[8]{0:T(128)S(1)} %get-tuple-element.39.own_ref.at_ref, s32[8]{0:T(128)S(1)} %iota.26.at_ref, s32[16]{0:T(128)S(1)} %pad_add_fusion.column_ref, f32[8]{0:T(128)S(1)} %add.123.shift_ref, ...), custom_call_target="tpu_custom_call" | custom-call | flops 805306368 | bytes 12582912 | tf_op jit(solution)/shard_map/prepare/pallas_call | solution.py:221
  75.0 5.2 %collective-permute-done.8.refs_0_ = bf16[4,256,256]{2,1,0:T(8,128)(2,1)S(1)} collective-permute-done((bf16[4,256,256]{2,1,0:T(8,128)(2,1)S(1)}, bf16[4,256,256]{2,1,0:T(8,128)(2,1)S(1)}, u32[]{:S(2)}, u32[]{:S(2)}) %collective-permute-start.8) | collective-permute-done | bytes 524320 | tf_op jit(solution)/shard_map/ppermute | solution.py:450
  80.2 11.3 %collective-permute-done.9.refs_1_ = bf16[4,256,256]{2,1,0:T(8,128)(2,1)S(1)} collective-permute-done((bf16[4,256,256]{2,1,0:T(8,128)(2,1)S(1)}, bf16[4,256,256]{2,1,0:T(8,128)(2,1)S(1)}, u32[]{:S(2)}, u32[]{:S(2)}) %collective-permute-start.9) | collective-permute-done | bytes 524320 | tf_op jit(solution)/shard_map/ppermute | solution.py:459
  91.5 11.4 %collective-permute-done.11.refs_2_ = bf16[4,256,256]{2,1,0:T(8,128)(2,1)S(1)} collective-permute-done((bf16[4,256,256]{2,1,0:T(8,128)(2,1)S(1)}, bf16[4,256,256]{2,1,0:T(8,128)(2,1)S(1)}, u32[]{:S(2)}, u32[]{:S(2)}) %collective-permute-start.11) | collective-permute-done | bytes 524320 | tf_op jit(solution)/shard_map/ppermute | solution.py:459
  102.8 2.1 %finish.7 = (bf16[4,256,256]{2,1,0:T(8,128)(2,1)S(1)}, f32[1,64]{1,0:T(1,128)S(1)}) custom-call(s32[24]{0:T(128)S(1)} %get-tuple-element.34.number_ref, f32[8]{0:T(128)S(1)} %fusion.8.scale_ref, f32[8,256,256]{2,1,0:T(8,128)S(1)} %get-tuple-element.50.local_ref, f32[8,256,256]{2,1,0:T(8,128)S(1)} %get-tuple-element.51.rest_ref, ...), custom_call_target="tpu_custom_call" | custom-call | flops 268435456 | bytes 4718592 | tf_op jit(solution)/shard_map/finish/pallas_call | solution.py:298
  104.9 2.1 %finish.6 = (bf16[4,256,256]{2,1,0:T(8,128)(2,1)S(1)}, f32[1,64]{1,0:T(1,128)S(1)}) custom-call(s32[24]{0:T(128)S(1)} %get-tuple-element.34.number_ref, f32[8]{0:T(128)S(1)} %fusion.8.scale_ref, f32[8,256,256]{2,1,0:T(8,128)S(1)} %get-tuple-element.50.local_ref, f32[8,256,256]{2,1,0:T(8,128)S(1)} %get-tuple-element.51.rest_ref, ...), custom_call_target="tpu_custom_call" | custom-call | flops 268435456 | bytes 4718592 | tf_op jit(solution)/shard_map/finish/pallas_call | solution.py:298
  107.6 1.5 %collective-permute-done.13 = f32[64]{0:T(128)S(1)} collective-permute-done((f32[64]{0:T(128)S(1)}, f32[64]{0:T(128)S(1)}, u32[]{:S(2)}, u32[]{:S(2)}) %collective-permute-start.13) | collective-permute-done | bytes 288 | tf_op jit(solution)/shard_map/ppermute | solution.py:350
  109.0 1.5 %collective-permute-start.14 = (f32[64]{0:T(128)S(1)}, f32[64]{0:T(128)S(1)}, u32[]{:S(2)}, u32[]{:S(2)}) collective-permute-start(f32[64]{0:T(128)S(1)} %add.128), channel_id=1, source_target_pairs={{0,2},{2,0},{1,3},{3,1},{4,6},{6,4},{5,7},{7,5},{8,10},{10,8},{9,1... | collective-permute-start | bytes 776 | tf_op jit(solution)/shard_map/ppermute | solution.py:350
  110.5 2.1 %collective-permute-done.14 = f32[64]{0:T(128)S(1)} collective-permute-done((f32[64]{0:T(128)S(1)}, f32[64]{0:T(128)S(1)}, u32[]{:S(2)}, u32[]{:S(2)}) %collective-permute-start.14) | collective-permute-done | bytes 288 | tf_op jit(solution)/shard_map/ppermute | solution.py:350
  112.6 10.6 %collective-permute-start.15 = (f32[64]{0:T(128)S(1)}, f32[64]{0:T(128)S(1)}, u32[]{:S(2)}, u32[]{:S(2)}) collective-permute-start(f32[64]{0:T(128)S(1)} %add.129), channel_id=1, source_target_pairs={{0,4},{4,0},{8,12},{12,8},{1,5},{5,1},{9,13},{13,9},{2,6},{6,2},{1... | collective-permute-start | bytes 776 | tf_op jit(solution)/shard_map/ppermute | solution.py:350
  123.2 1.5 %collective-permute-done.15 = f32[64]{0:T(128)S(1)} collective-permute-done((f32[64]{0:T(128)S(1)}, f32[64]{0:T(128)S(1)}, u32[]{:S(2)}, u32[]{:S(2)}) %collective-permute-start.15) | collective-permute-done | bytes 288 | tf_op jit(solution)/shard_map/ppermute | solution.py:350
  124.7 3.9 %collective-permute-start.16 = (f32[64]{0:T(128)S(1)}, f32[64]{0:T(128)S(1)}, u32[]{:S(2)}, u32[]{:S(2)}) collective-permute-start(f32[64]{0:T(128)S(1)} %add.130), channel_id=1, source_target_pairs={{0,8},{4,12},{8,0},{12,4},{1,9},{5,13},{9,1},{13,5},{2,10},{6,14},... | collective-permute-start | bytes 776 | tf_op jit(solution)/shard_map/ppermute | solution.py:350
  128.7 1.5 %collective-permute-done.16 = f32[64]{0:T(128)S(1)} collective-permute-done((f32[64]{0:T(128)S(1)}, f32[64]{0:T(128)S(1)}, u32[]{:S(2)}, u32[]{:S(2)}) %collective-permute-start.16) | collective-permute-done | bytes 288 | tf_op jit(solution)/shard_map/ppermute | solution.py:350
  130.7 2.0 %put_in_slots.1 = bf16[16,256,256]{2,1,0:T(8,128)(2,1)} custom-call(s32[16]{0:T(128)S(1)} %pad_add_fusion.1.slot_ref, bf16[4,256,256]{2,1,0:T(8,128)(2,1)S(1)} %get-tuple-element.57.refs_0_, bf16[4,256,256]{2,1,0:T(8,128)(2,1)S(1)} %collective-permute-done.10.refs_1_, bf16[4,256,256]{2,1,0:T(8,128)(2,1)S(1)} %get-tuple-element.59.refs_2_, ...), custom_call_target="tpu_custom_call" | custom-call | bytes 4194304 | tf_op jit(solution)/shard_map/put_in_slots/pallas_call | solution.py:331
  (63 shorter events, 5.0 us)
Async XLA Ops:
  1.3 14.6 %collective-permute-start.3 = (s32[16]{0:T(128)S(1)}, s32[16]{0:T(128)S(1)}, u32[]{:S(2)}, u32[]{:S(2)}) collective-permute-start(s32[16]{0:T(128)S(1)} %get-tuple-element.80), channel_id=1, source_target_pairs={{12,0},{8,4},{4,8},{0,12},{13,1},{9,5},{5,9},{1,13},{14,2},{10,6},... | collective-permute-start | bytes 200 | tf_op jit(solution)/shard_map/ppermute | solution.py:383
  6.4 9.5 %collective-permute-start.2 = (s32[16]{0:T(128)S(1)}, s32[16]{0:T(128)S(1)}, u32[]{:S(2)}, u32[]{:S(2)}) collective-permute-start(s32[16]{0:T(128)S(1)} %get-tuple-element.80), channel_id=1, source_target_pairs={{8,0},{0,4},{12,8},{4,12},{9,1},{1,5},{13,9},{5,13},{10,2},{2,6},{... | collective-permute-start | bytes 200 | tf_op jit(solution)/shard_map/ppermute | solution.py:383
  6.4 6.4 %collective-permute-start = (s32[16]{0:T(128)S(1)}, s32[16]{0:T(128)S(1)}, u32[]{:S(2)}, u32[]{:S(2)}) collective-permute-start(s32[16]{0:T(128)S(1)} %get-tuple-element.80), channel_id=1, source_target_pairs={{4,0},{12,4},{0,8},{8,12},{5,1},{13,5},{1,9},{9,13},{6,2},{14,6},{... | collective-permute-start | bytes 200 | tf_op jit(solution)/shard_map/ppermute | solution.py:382
  12.8 9.0 %copy-start.8 = (f32[64]{0:T(128)S(1)}, f32[64]{0:T(128)}, u32[]{:S(2)}) copy-start(f32[64]{0:T(128)} %param.17) | copy-start | bytes 772
  12.8 9.3 %copy-start.9 = (bf16[16,1]{0,1:T(2,128)(2,1)S(1)}, bf16[16,1]{0,1:T(2,128)(2,1)}, u32[]{:S(2)}) copy-start(bf16[16,1]{0,1:T(2,128)(2,1)} %param.25) | copy-start | bytes 100
  12.8 9.5 %copy-start = (bf16[16,256,256]{2,1,0:T(8,128)(2,1)S(1)}, bf16[16,256,256]{2,1,0:T(8,128)(2,1)}, u32[]{:S(2)}) copy-start(bf16[16,256,256]{2,1,0:T(8,128)(2,1)} %refs_3_.4) | copy-start | bytes 6291460
  12.8 9.5 %copy-start.1 = (bf16[16,256,256]{2,1,0:T(8,128)(2,1)S(1)}, bf16[16,256,256]{2,1,0:T(8,128)(2,1)}, u32[]{:S(2)}) copy-start(bf16[16,256,256]{2,1,0:T(8,128)(2,1)} %refs_2_.7) | copy-start | bytes 6291460
  12.8 9.5 %copy-start.6 = (s32[16,11]{1,0:T(8,128)S(1)}, s32[16,11]{1,0:T(8,128)}, u32[]{:S(2)}) copy-start(s32[16,11]{1,0:T(8,128)} %slot_ref.3) | copy-start | bytes 2116
  12.8 9.5 %copy-start.7 = (bf16[16,11]{1,0:T(8,128)(2,1)S(1)}, bf16[16,11]{1,0:T(8,128)(2,1)}, u32[]{:S(2)}) copy-start(bf16[16,11]{1,0:T(8,128)(2,1)} %weight_ref.3) | copy-start | bytes 1060
  15.8 38.3 %collective-permute-start.1 = (bf16[4,256,256]{2,1,0:T(8,128)(2,1)S(1)}, bf16[4,256,256]{2,1,0:T(8,128)(2,1)S(1)}, u32[]{:S(2)}, u32[]{:S(2)}) collective-permute-start(bf16[4,256,256]{2,1,0:T(8,128)(2,1)S(1)} %get-tuple-element.45), channel_id=1, source_target_pairs={{0,4},{4,12},{8,0},{12,8},{1,5},{5,13},{9,1},{13,9},{2,6},{6,14},{... | collective-permute-start | bytes 1572872 | tf_op jit(solution)/shard_map/ppermute | solution.py:450
  18.8 35.3 %collective-permute-start.4 = (bf16[4,256,256]{2,1,0:T(8,128)(2,1)S(1)}, bf16[4,256,256]{2,1,0:T(8,128)(2,1)S(1)}, u32[]{:S(2)}, u32[]{:S(2)}) collective-permute-start(bf16[4,256,256]{2,1,0:T(8,128)(2,1)S(1)} %get-tuple-element.48), channel_id=1, source_target_pairs={{0,8},{4,0},{8,12},{12,4},{1,9},{5,1},{9,13},{13,5},{2,10},{6,2},{... | collective-permute-start | bytes 1572872 | tf_op jit(solution)/shard_map/ppermute | solution.py:459
  21.7 33.7 %collective-permute-start.5 = (bf16[4,256,256]{2,1,0:T(8,128)(2,1)S(1)}, bf16[4,256,256]{2,1,0:T(8,128)(2,1)S(1)}, u32[]{:S(2)}, u32[]{:S(2)}) collective-permute-start(bf16[4,256,256]{2,1,0:T(8,128)(2,1)S(1)} %get-tuple-element.49), channel_id=1, source_target_pairs={{0,12},{4,8},{8,4},{12,0},{1,13},{5,9},{9,5},{13,1},{2,14},{6,10},... | collective-permute-start | bytes 1572872 | tf_op jit(solution)/shard_map/ppermute | solution.py:459
  22.3 1.6 %copy-start.2 = (bf16[16,256,256]{2,1,0:T(8,128)(2,1)S(1)}, bf16[16,256,256]{2,1,0:T(8,128)(2,1)}, u32[]{:S(2)}) copy-start(bf16[16,256,256]{2,1,0:T(8,128)(2,1)} %refs_3_.5) | copy-start | bytes 6291460
  23.8 1.6 %copy-start.4 = (bf16[16,256,256]{2,1,0:T(8,128)(2,1)S(1)}, bf16[16,256,256]{2,1,0:T(8,128)(2,1)}, u32[]{:S(2)}) copy-start(bf16[16,256,256]{2,1,0:T(8,128)(2,1)} %refs_4_.1) | copy-start | bytes 6291460
  55.3 2.0 %collective-permute-start.6 = (bf16[4,256,256]{2,1,0:T(8,128)(2,1)S(1)}, bf16[4,256,256]{2,1,0:T(8,128)(2,1)S(1)}, u32[]{:S(2)}, u32[]{:S(2)}) collective-permute-start(bf16[4,256,256]{2,1,0:T(8,128)(2,1)S(1)} %finish.4.refs_0_), channel_id=1, source_target_pairs={{0,1},{1,0},{2,3},{3,2},{4,5},{5,4},{6,7},{7,6},{8,9},{9,8},{10,11... | collective-permute-start | bytes 1572872 | tf_op jit(solution)/shard_map/ppermute | solution.py:471
  56.6 2.1 %collective-permute-start.7 = (bf16[4,256,256]{2,1,0:T(8,128)(2,1)S(1)}, bf16[4,256,256]{2,1,0:T(8,128)(2,1)S(1)}, u32[]{:S(2)}, u32[]{:S(2)}) collective-permute-start(bf16[4,256,256]{2,1,0:T(8,128)(2,1)S(1)} %finish.5.refs_2_), channel_id=1, source_target_pairs={{0,1},{1,0},{2,3},{3,2},{4,5},{5,4},{6,7},{7,6},{8,9},{9,8},{10,11... | collective-permute-start | bytes 1572872 | tf_op jit(solution)/shard_map/ppermute | solution.py:475
  59.4 20.8 %collective-permute-start.8 = (bf16[4,256,256]{2,1,0:T(8,128)(2,1)S(1)}, bf16[4,256,256]{2,1,0:T(8,128)(2,1)S(1)}, u32[]{:S(2)}, u32[]{:S(2)}) collective-permute-start(bf16[4,256,256]{2,1,0:T(8,128)(2,1)S(1)} %gather_again.2), channel_id=1, source_target_pairs={{0,4},{4,12},{8,0},{12,8},{1,5},{5,13},{9,1},{13,9},{2,6},{6,14},{... | collective-permute-start | bytes 1572872 | tf_op jit(solution)/shard_map/ppermute | solution.py:450
  68.7 22.8 %collective-permute-start.9 = (bf16[4,256,256]{2,1,0:T(8,128)(2,1)S(1)}, bf16[4,256,256]{2,1,0:T(8,128)(2,1)S(1)}, u32[]{:S(2)}, u32[]{:S(2)}) collective-permute-start(bf16[4,256,256]{2,1,0:T(8,128)(2,1)S(1)} %get-tuple-element.56), channel_id=1, source_target_pairs={{0,8},{4,0},{8,12},{12,4},{1,9},{5,1},{9,13},{13,5},{2,10},{6,2},{... | collective-permute-start | bytes 1572872 | tf_op jit(solution)/shard_map/ppermute | solution.py:459
  68.8 2.6 %copy-start.5 = (bf16[16,256,256]{2,1,0:T(8,128)(2,1)S(1)}, bf16[16,256,256]{2,1,0:T(8,128)(2,1)}, u32[]{:S(2)}) copy-start(bf16[16,256,256]{2,1,0:T(8,128)(2,1)} %refs_4_.1) | copy-start | bytes 6291460
  68.8 2.6 %copy-start.3 = (bf16[16,256,256]{2,1,0:T(8,128)(2,1)S(1)}, bf16[16,256,256]{2,1,0:T(8,128)(2,1)}, u32[]{:S(2)}) copy-start(bf16[16,256,256]{2,1,0:T(8,128)(2,1)} %refs_3_.5) | copy-start | bytes 6291460
  68.8 34.0 %collective-permute-start.11 = (bf16[4,256,256]{2,1,0:T(8,128)(2,1)S(1)}, bf16[4,256,256]{2,1,0:T(8,128)(2,1)S(1)}, u32[]{:S(2)}, u32[]{:S(2)}) collective-permute-start(bf16[4,256,256]{2,1,0:T(8,128)(2,1)S(1)} %get-tuple-element.58), channel_id=1, source_target_pairs={{0,12},{4,8},{8,4},{12,0},{1,13},{5,9},{9,5},{13,1},{2,14},{6,10},... | collective-permute-start | bytes 1572872 | tf_op jit(solution)/shard_map/ppermute | solution.py:459
  104.9 25.8 %collective-permute-start.12 = (bf16[4,256,256]{2,1,0:T(8,128)(2,1)S(1)}, bf16[4,256,256]{2,1,0:T(8,128)(2,1)S(1)}, u32[]{:S(2)}, u32[]{:S(2)}) collective-permute-start(bf16[4,256,256]{2,1,0:T(8,128)(2,1)S(1)} %get-tuple-element.59.refs_2_), channel_id=1, source_target_pairs={{0,1},{1,0},{2,3},{3,2},{4,5},{5,4},{6,7},{7,6},{8,9},{9,8},{10,11... | collective-permute-start | bytes 1572872 | tf_op jit(solution)/shard_map/ppermute | solution.py:475
  107.0 23.7 %collective-permute-start.10 = (bf16[4,256,256]{2,1,0:T(8,128)(2,1)S(1)}, bf16[4,256,256]{2,1,0:T(8,128)(2,1)S(1)}, u32[]{:S(2)}, u32[]{:S(2)}) collective-permute-start(bf16[4,256,256]{2,1,0:T(8,128)(2,1)S(1)} %get-tuple-element.57.refs_0_), channel_id=1, source_target_pairs={{0,1},{1,0},{2,3},{3,2},{4,5},{5,4},{6,7},{7,6},{8,9},{9,8},{10,11... | collective-permute-start | bytes 1572872 | tf_op jit(solution)/shard_map/ppermute | solution.py:471
  107.5 1.5 %collective-permute-start.13 = (f32[64]{0:T(128)S(1)}, f32[64]{0:T(128)S(1)}, u32[]{:S(2)}, u32[]{:S(2)}) collective-permute-start(f32[64]{0:T(128)S(1)} %add_bitcast_fusion), channel_id=1, source_target_pairs={{0,1},{1,0},{2,3},{3,2},{4,5},{5,4},{6,7},{7,6},{8,9},{9,8},{10,11... | collective-permute-start | bytes 776 | tf_op jit(solution)/shard_map/ppermute | solution.py:350
  109.0 3.6 %collective-permute-start.14 = (f32[64]{0:T(128)S(1)}, f32[64]{0:T(128)S(1)}, u32[]{:S(2)}, u32[]{:S(2)}) collective-permute-start(f32[64]{0:T(128)S(1)} %add.128), channel_id=1, source_target_pairs={{0,2},{2,0},{1,3},{3,1},{4,6},{6,4},{5,7},{7,5},{8,10},{10,8},{9,1... | collective-permute-start | bytes 776 | tf_op jit(solution)/shard_map/ppermute | solution.py:350
  112.6 12.1 %collective-permute-start.15 = (f32[64]{0:T(128)S(1)}, f32[64]{0:T(128)S(1)}, u32[]{:S(2)}, u32[]{:S(2)}) collective-permute-start(f32[64]{0:T(128)S(1)} %add.129), channel_id=1, source_target_pairs={{0,4},{4,0},{8,12},{12,8},{1,5},{5,1},{9,13},{13,9},{2,6},{6,2},{1... | collective-permute-start | bytes 776 | tf_op jit(solution)/shard_map/ppermute | solution.py:350
  124.7 5.5 %collective-permute-start.16 = (f32[64]{0:T(128)S(1)}, f32[64]{0:T(128)S(1)}, u32[]{:S(2)}, u32[]{:S(2)}) collective-permute-start(f32[64]{0:T(128)S(1)} %add.130), channel_id=1, source_target_pairs={{0,8},{4,12},{8,0},{12,4},{1,9},{5,13},{9,1},{13,5},{2,10},{6,14},... | collective-permute-start | bytes 776 | tf_op jit(solution)/shard_map/ppermute | solution.py:350

commit v8 on v7

--- a/solution.py
+++ b/solution.py
@@ -63,6 +63,7 @@
     pairs, domain = amplitudes.shape[:2]
     count_of = len(shifts)
     blocks = count_of * cap
+    bits = pairs.bit_length() - 1
 
     def body(place_ref, *refs):
         lists = refs[:count_of]
@@ -72,24 +73,31 @@
         sem = refs[-1]
         me = place_ref[0]
         core = place_ref[1]
-        for n, shift in enumerate(shifts):
+        for n, step in enumerate(shifts):
             base = n * (cap + 1)
             asker = jnp.int32(0)
-            for a, b in sent(rows, shift):
+            for a, b in sent(rows, step):
                 asker = jnp.where(me == a, b, asker)
+            served = [asker]
+            for sooner in range(1, step):
+                server = jnp.int32(0)
+                for a, b in sent(rows, sooner):
+                    server = jnp.where(asker == b, a, server)
+                served.append(server)
             for k in range(cap):
                 asked[base + k] = 0
-            sources = [lists[n][p] // pairs for p in range(pairs)]
+            entries = [lists[n][p] for p in range(pairs)]
+            sources = [entry // pairs if pairs & (pairs - 1) else entry >> bits for entry in entries]
             count = jnp.int32(0)
             for p in range(pairs):
-                count = count + (step_of(rows, sources[p], asker) < shift).astype(jnp.int32)
+                for server in served:
+                    count = count + (sources[p] == server).astype(jnp.int32)
             filled = jnp.int32(0)
             for p in range(pairs):
-                mine = sources[p] == me
-                taken = mine & (count % 2 == core)
-                asked[base + jnp.minimum(filled, cap)] = lists[n][p] % pairs
-                count = count + mine.astype(jnp.int32)
-                filled = filled + taken.astype(jnp.int32)
+                mine = (sources[p] == me).astype(jnp.int32)
+                asked[base + jnp.minimum(filled, cap)] = entries[p] - sources[p] * pairs
+                filled = filled + jnp.where((count & 1) == core, mine, 0)
+                count = count + mine
             for k in range(cap):
                 pltpu.make_async_copy(
                     store.at[asked[base + k]], outs[n].at[k], sem.at[n, k]
@@ -138,7 +146,7 @@
     )(asked, where, *stores)
 
 
-def prepare(own, at, columns, shift, near, stores, integrals, fock_matrix, intersection):
+def prepare(own, at, columns, counts, shift, near, stores, integrals, fock_matrix, intersection):
     half = own.shape[0]
     domain = integrals.shape[1]
     total = columns.shape[0]
@@ -148,9 +156,13 @@
 
     def spread_weights(own_ref, column_ref, slot_ref, count_ref, weight_ref, spread_ref):
         lane = lax.broadcasted_iota(jnp.int32, (total, total), 1)
+        down = lax.broadcasted_iota(jnp.int32, (total, total), 0)
+        used_count = jnp.zeros((total, total), jnp.int32)
+        for n in range(total):
+            used_count = jnp.where(down == n, count_ref[n], used_count)
         weights = jnp.zeros((total, total), jnp.float32)
         for k in range(entries):
-            used = (slot_ref[:, k : k + 1] == lane) & (k < count_ref[...])
+            used = (slot_ref[:, k : k + 1] == lane) & (k < used_count)
             wide = weight_ref[:, k : k + 1].astype(jnp.float32)
             weights = weights + jnp.where(used, wide, jnp.float32(0.0))
         weights = weights.astype(jnp.bfloat16)
@@ -181,7 +193,9 @@
         along = lax.broadcasted_iota(jnp.int32, shape, 1) % LANES
         spread_ref[...] = jnp.where(down == along, full, 0.0).astype(jnp.bfloat16)
 
-    def body(own_ref, at_ref, column_ref, shift_ref, slot_ref, count_ref, weight_ref, *refs):
+    def body(
+        own_ref, at_ref, column_ref, count_ref, shift_ref, slot_ref, weight_ref, *refs
+    ):
         sources = refs[: len(stores)]
         (integ_ref, fock_ref, over_ref, local_ref, rest_ref, recip_ref, keep_ref, spread_ref) = (
             refs[len(stores) :]
@@ -221,7 +235,7 @@
     return pl.pallas_call(
         body,
         grid_spec=pltpu.PrefetchScalarGridSpec(
-            num_scalar_prefetch=4,
+            num_scalar_prefetch=5,
             grid=(half,),
             in_specs=[pl.BlockSpec(n.shape, lambda i, *_: (0, 0)) for n in near]
             + [pl.BlockSpec(s.shape, lambda i, *_: (0, 0, 0)) for s in stores]
@@ -246,7 +260,7 @@
         ),
         compiler_params=limits(20),
         name="prepare",
-    )(own, at, columns, shift, *near, *stores, integrals, fock_matrix, intersection)
+    )(own, at, columns, counts, shift, *near, *stores, integrals, fock_matrix, intersection)
 
 
 def finish(start, count, numbers, scale, prepared, arrived, stores, occ_count, last):
@@ -401,15 +415,19 @@
     far_step = pick(own_pick, step)
     own_far = pick(own_pick, far_slot[:, 0])
     own_place = pick(own_pick, place)
+
+    occ_energy, first_occ, second_occ, far_weight, _ = lax.optimization_barrier(
+        (occ_energy, first_occ, second_occ, far_weight, asked_lead)
+    )
+    orbitals = jnp.arange(occ_count, dtype=jnp.int32)
+
+    def energy_of(index):
+        found = index[:, None] == orbitals[None, :]
+        return jnp.sum(jnp.where(found, occ_energy[None, :], jnp.float32(0.0)), axis=1)
+
     far_scale = pick(own_pick, far_weight[:, 0].astype(jnp.float32))
     first = pick(own_pick, first_occ)
     second = pick(own_pick, second_occ)
-    orbitals = jnp.arange(occ_count, dtype=jnp.int32)
-
-    def energy_of(index):
-        found = index[:, None] == orbitals[None, :]
-        return jnp.sum(jnp.where(found, occ_energy[None, :], jnp.float32(0.0)), axis=1)
-
     shift = energy_of(first) + energy_of(second)
 
     by_slot = turn // 2 + jnp.where(turn % 2 == core, 0, half)
@@ -431,14 +449,10 @@
         )
         spot = jnp.where(far_step == 0, at_home, (far_step - 1) * cap + own_place)
         tables.append(jnp.concatenate([spot, first, second]))
-    near = [near_slot, near_count[:, None], near_weight]
+    near = [near_slot, near_weight]
     columns = [slot_ids, jnp.concatenate([own, other])]
     ats = [own, jnp.arange(half, dtype=jnp.int32)]
     slots = jnp.concatenate([own[:early], other[:early], own[early:], other[early:]])
-    (own, *moved, send_lead) = lax.optimization_barrier(
-        (own, *tables, *columns, *ats, slots, send_lead)
-    )
-    tables, columns, ats, slots = moved[:2], moved[2:4], moved[4:6], moved[6]
     stores = [amplitudes]
     whole = [amplitudes]
     for sweep in range(ITERS):
@@ -459,7 +473,7 @@
             arrived[d] = lax.ppermute(send, "row", sent(rows, d))
         arrived = [arrived[d] for d in range(1, rows)]
         prepared = prepare(
-            own, ats[again], columns[again], shift, near, whole,
+            own, ats[again], columns[again], near_count, shift, near, whole,
             integrals, fock_matrix, intersection,
         )
         spots = laid(arrived)

time: 133 us -> 127 us (0.955)
  waiting for transfers between devices: 61.1 us -> 54.8 us
    ppermute x2, waiting for transfers between devices: 30.3 us -> 26.7 us  [per_device(): arrived[1] = lax.ppermute(send_lead, 'row', sent(rows, 1))]
    unnamed x21 -> x29, local copies, waits for them, and re-layouts: 3.25 us -> 5.29 us
    ppermute x4, waiting for transfers between devices: 22.6 us -> 20.9 us  [per_device(): arrived[d] = lax.ppermute(send, 'row', sent(rows, d))]
  transfers between devices with their start and end apart: 17 -> 17, of which waited for: 10 -> 11; matrix products, arithmetic and copies ran while one was open for 3% -> 2% of each run, Pallas kernels for 14% -> 14%
where the time goes in v8:
time: 127 us
  waiting for transfers between devices  54.8 us (43%)
  starting transfers between devices  40 us (31%)
  Pallas kernels  22.5 us (18%)
  local copies, waits for them, and re-layouts  5.4 us (4%)
  other arithmetic  3.55 us (3%)
    ppermute x2, waiting for transfers between devices, per_device(): arrived[1] = lax.ppermute(send_lead, 'row', sent(rows, 1))  26.7 us
    ppermute x4, waiting for transfers between devices, per_device(): arrived[d] = lax.ppermute(send, 'row', sent(rows, d))  20.9 us
    ppermute x4, starting transfers between devices, add_over(): lax.ppermute(values, name, [(r, r ^ step) for r in range(size)])  15.6 us
    ppermute x2, starting transfers between devices, per_device(): arrived[1] = lax.ppermute(send_lead, 'row', sent(rows, 1))  8.9 us
    pallas_call x2, Pallas kernels, prepare(): pl.pallas_call(body, grid_spec=pltpu.PrefetchScalarGridSpec(num_scalar_pr...  7.09 us
    pallas_call x4, Pallas kernels, finish(): pl.pallas_call(body, out_shape=out_shape, in_specs=[pl.BlockSpec(memory_s...  6.56 us
    ppermute x4, starting transfers between devices, per_device(): arrived[d] = lax.ppermute(send, 'row', sent(rows, d))  6.32 us
    ppermute x4, waiting for transfers between devices, add_over(): lax.ppermute(values, name, [(r, r ^ step) for r in range(size)])  5.66 us
  transfers between devices with their start and end apart: 17, of which 11 were waited for; matrix products, arithmetic and copies ran while one was open for 2% of the time, Pallas kernels for 14%

profile of v8, /device:TPU:0, one launch (start us, length us, event | category | flops | bytes accessed | tf_op | source)
XLA Modules:
  0.0 127.2 jit_solution(10550324705828417400)
XLA Ops:
  1.3 5.1 %collective-permute-start.3 = (s32[16]{0:T(128)S(1)}, s32[16]{0:T(128)S(1)}, u32[]{:S(2)}, u32[]{:S(2)}) collective-permute-start(s32[16]{0:T(128)S(1)} %get-tuple-element.75), channel_id=1, source_target_pairs={{12,0},{8,4},{4,8},{0,12},{13,1},{9,5},{5,9},{1,13},{14,2},{10,6},... | collective-permute-start | bytes 200 | tf_op jit(solution)/shard_map/ppermute | solution.py:397
  6.4 2.9 %collective-permute-start = (s32[16]{0:T(128)S(1)}, s32[16]{0:T(128)S(1)}, u32[]{:S(2)}, u32[]{:S(2)}) collective-permute-start(s32[16]{0:T(128)S(1)} %get-tuple-element.75), channel_id=1, source_target_pairs={{4,0},{12,4},{0,8},{8,12},{5,1},{13,5},{1,9},{9,13},{6,2},{14,6},{... | collective-permute-start | bytes 200 | tf_op jit(solution)/shard_map/ppermute | solution.py:396
  10.6 2.7 %gather_first.2 = (s32[5]{0:T(128)S(1)}, bf16[4,256,256]{2,1,0:T(8,128)(2,1)S(1)}) custom-call(s32[2]{0:T(128)S(1)} %pad_add_fusion.1.place_ref, s32[16]{0:T(128)S(1)} %collective-permute-done.refs_0_, bf16[16,256,256]{2,1,0:T(8,128)(2,1)} %refs_3_.4), custom_call_target="tpu_custom_call" | custom-call | bytes 1048576 | tf_op jit(solution)/shard_map/gather_first/pallas_call | solution.py:110
  13.9 2.7 %gather_first.3 = (s32[10]{0:T(128)S(1)}, bf16[4,256,256]{2,1,0:T(8,128)(2,1)S(1)}, bf16[4,256,256]{2,1,0:T(8,128)(2,1)S(1)}) custom-call(s32[2]{0:T(128)S(1)} %pad_add_fusion.1.place_ref, s32[16]{0:T(128)S(1)} %collective-permute-done.2.refs_0_, s32[16]{0:T(128)S(1)} %collective-permute-done.3.refs_1_, bf16[16,256,256]{2,1,0:T(8,128)(2,1)} %refs_3_.4), custom_call_target="tpu_custom_call" | custom-call | bytes 2097152 | tf_op jit(solution)/shard_map/gather_first/pallas_call | solution.py:110
  16.6 2.5 %collective-permute-start.4 = (bf16[4,256,256]{2,1,0:T(8,128)(2,1)S(1)}, bf16[4,256,256]{2,1,0:T(8,128)(2,1)S(1)}, u32[]{:S(2)}, u32[]{:S(2)}) collective-permute-start(bf16[4,256,256]{2,1,0:T(8,128)(2,1)S(1)} %get-tuple-element.39), channel_id=1, source_target_pairs={{0,8},{4,0},{8,12},{12,4},{1,9},{5,1},{9,13},{13,5},{2,10},{6,2},{... | collective-permute-start | bytes 1572872 | tf_op jit(solution)/shard_map/ppermute | solution.py:473
  19.1 1.4 %collective-permute-start.5 = (bf16[4,256,256]{2,1,0:T(8,128)(2,1)S(1)}, bf16[4,256,256]{2,1,0:T(8,128)(2,1)S(1)}, u32[]{:S(2)}, u32[]{:S(2)}) collective-permute-start(bf16[4,256,256]{2,1,0:T(8,128)(2,1)S(1)} %get-tuple-element.40), channel_id=1, source_target_pairs={{0,12},{4,8},{8,4},{12,0},{1,13},{5,9},{9,5},{13,1},{2,14},{6,10},... | collective-permute-start | bytes 1572872 | tf_op jit(solution)/shard_map/ppermute | solution.py:473
  21.3 1.6 %copy-done.2 = bf16[16,256,256]{2,1,0:T(8,128)(2,1)S(1)} copy-done((bf16[16,256,256]{2,1,0:T(8,128)(2,1)S(1)}, bf16[16,256,256]{2,1,0:T(8,128)(2,1)}, u32[]{:S(2)}) %copy-start.2) | copy-done | bytes 2097176
  22.9 1.6 %copy-done.4 = bf16[16,256,256]{2,1,0:T(8,128)(2,1)S(1)} copy-done((bf16[16,256,256]{2,1,0:T(8,128)(2,1)S(1)}, bf16[16,256,256]{2,1,0:T(8,128)(2,1)}, u32[]{:S(2)}) %copy-start.4) | copy-done | bytes 2097176
  24.4 3.5 %prepare.2 = (f32[8,256,256]{2,1,0:T(8,128)S(1)}, f32[8,256,256]{2,1,0:T(8,128)S(1)}, f32[8,256,256]{2,1,0:T(8,128)S(1)}, bf16[8,256,256]{2,1,0:T(8,128)(2,1)S(1)}) custom-call(s32[8]{0:T(128)S(1)} %get-tuple-element.57.own_ref.at_ref, s32[8]{0:T(128)S(1)} %get-tuple-element.57.own_ref.at_ref, s32[16]{0:T(128)S(1)} %iota.26.column_ref, s32[16]{0:T(128)S(1)} %copy-done.8, ...), custom_call_target="tpu_custom_call" | custom-call | flops 805306368 | bytes 12582912 | tf_op jit(solution)/shard_map/prepare/pallas_call | solution.py:235
  28.3 23.4 %collective-permute-done.1.refs_0_ = bf16[4,256,256]{2,1,0:T(8,128)(2,1)S(1)} collective-permute-done((bf16[4,256,256]{2,1,0:T(8,128)(2,1)S(1)}, bf16[4,256,256]{2,1,0:T(8,128)(2,1)S(1)}, u32[]{:S(2)}, u32[]{:S(2)}) %collective-permute-start.1) | collective-permute-done | bytes 524320 | tf_op jit(solution)/shard_map/ppermute | solution.py:464
  51.6 1.2 finish.4.refs_0_
  52.9 1.2 finish.5.refs_2_
  54.8 1.4 %collective-permute-done.7.refs_3_ = bf16[4,256,256]{2,1,0:T(8,128)(2,1)S(1)} collective-permute-done((bf16[4,256,256]{2,1,0:T(8,128)(2,1)S(1)}, bf16[4,256,256]{2,1,0:T(8,128)(2,1)S(1)}, u32[]{:S(2)}, u32[]{:S(2)}) %collective-permute-start.7) | collective-permute-done | bytes 524320 | tf_op jit(solution)/shard_map/ppermute | solution.py:489
  56.3 0.7 gather_again.2
  57.0 8.4 %collective-permute-start.8 = (bf16[4,256,256]{2,1,0:T(8,128)(2,1)S(1)}, bf16[4,256,256]{2,1,0:T(8,128)(2,1)S(1)}, u32[]{:S(2)}, u32[]{:S(2)}) collective-permute-start(bf16[4,256,256]{2,1,0:T(8,128)(2,1)S(1)} %gather_again.2), channel_id=1, source_target_pairs={{0,4},{4,12},{8,0},{12,8},{1,5},{5,13},{9,1},{13,9},{2,6},{6,14},{... | collective-permute-start | bytes 1572872 | tf_op jit(solution)/shard_map/ppermute | solution.py:464
  65.3 0.8 gather_again.3
  66.2 2.4 %collective-permute-start.11 = (bf16[4,256,256]{2,1,0:T(8,128)(2,1)S(1)}, bf16[4,256,256]{2,1,0:T(8,128)(2,1)S(1)}, u32[]{:S(2)}, u32[]{:S(2)}) collective-permute-start(bf16[4,256,256]{2,1,0:T(8,128)(2,1)S(1)} %get-tuple-element.48), channel_id=1, source_target_pairs={{0,12},{4,8},{8,4},{12,0},{1,13},{5,9},{9,5},{13,1},{2,14},{6,10},... | collective-permute-start | bytes 1572872 | tf_op jit(solution)/shard_map/ppermute | solution.py:473
  68.9 1.4 %copy-done.3 = bf16[16,256,256]{2,1,0:T(8,128)(2,1)S(1)} copy-done((bf16[16,256,256]{2,1,0:T(8,128)(2,1)S(1)}, bf16[16,256,256]{2,1,0:T(8,128)(2,1)}, u32[]{:S(2)}) %copy-start.3) | copy-done | bytes 2097176
  70.9 3.5 %prepare.3 = (f32[8,256,256]{2,1,0:T(8,128)S(1)}, f32[8,256,256]{2,1,0:T(8,128)S(1)}, f32[8,256,256]{2,1,0:T(8,128)S(1)}, bf16[8,256,256]{2,1,0:T(8,128)(2,1)S(1)}) custom-call(s32[8]{0:T(128)S(1)} %get-tuple-element.57.own_ref.at_ref, s32[8]{0:T(128)S(1)} %iota.25.at_ref, s32[16]{0:T(128)S(1)} %pad_add_fusion.2.column_ref, s32[16]{0:T(128)S(1)} %copy-done.8, ...), custom_call_target="tpu_custom_call" | custom-call | flops 805306368 | bytes 12582912 | tf_op jit(solution)/shard_map/prepare/pallas_call | solution.py:235
  74.4 3.3 %collective-permute-done.8.refs_0_ = bf16[4,256,256]{2,1,0:T(8,128)(2,1)S(1)} collective-permute-done((bf16[4,256,256]{2,1,0:T(8,128)(2,1)S(1)}, bf16[4,256,256]{2,1,0:T(8,128)(2,1)S(1)}, u32[]{:S(2)}, u32[]{:S(2)}) %collective-permute-start.8) | collective-permute-done | bytes 524320 | tf_op jit(solution)/shard_map/ppermute | solution.py:464
  77.8 11.2 %collective-permute-done.9.refs_1_ = bf16[4,256,256]{2,1,0:T(8,128)(2,1)S(1)} collective-permute-done((bf16[4,256,256]{2,1,0:T(8,128)(2,1)S(1)}, bf16[4,256,256]{2,1,0:T(8,128)(2,1)S(1)}, u32[]{:S(2)}, u32[]{:S(2)}) %collective-permute-start.9) | collective-permute-done | bytes 524320 | tf_op jit(solution)/shard_map/ppermute | solution.py:473
  88.9 2.0 %finish.6 = (bf16[4,256,256]{2,1,0:T(8,128)(2,1)S(1)}, f32[1,64]{1,0:T(1,128)S(1)}) custom-call(s32[24]{0:T(128)S(1)} %get-tuple-element.67.number_ref, f32[8]{0:T(128)S(1)} %fusion.8.scale_ref, f32[8,256,256]{2,1,0:T(8,128)S(1)} %get-tuple-element.41.local_ref, f32[8,256,256]{2,1,0:T(8,128)S(1)} %get-tuple-element.42.rest_ref, ...), custom_call_target="tpu_custom_call" | custom-call | flops 268435456 | bytes 4718592 | tf_op jit(solution)/shard_map/finish/pallas_call | solution.py:312
  91.0 9.7 %collective-permute-done.11.refs_2_ = bf16[4,256,256]{2,1,0:T(8,128)(2,1)S(1)} collective-permute-done((bf16[4,256,256]{2,1,0:T(8,128)(2,1)S(1)}, bf16[4,256,256]{2,1,0:T(8,128)(2,1)S(1)}, u32[]{:S(2)}, u32[]{:S(2)}) %collective-permute-start.11) | collective-permute-done | bytes 524320 | tf_op jit(solution)/shard_map/ppermute | solution.py:473
  100.7 2.1 %finish.7 = (bf16[4,256,256]{2,1,0:T(8,128)(2,1)S(1)}, f32[1,64]{1,0:T(1,128)S(1)}) custom-call(s32[24]{0:T(128)S(1)} %get-tuple-element.67.number_ref, f32[8]{0:T(128)S(1)} %fusion.8.scale_ref, f32[8,256,256]{2,1,0:T(8,128)S(1)} %get-tuple-element.41.local_ref, f32[8,256,256]{2,1,0:T(8,128)S(1)} %get-tuple-element.42.rest_ref, ...), custom_call_target="tpu_custom_call" | custom-call | flops 268435456 | bytes 4718592 | tf_op jit(solution)/shard_map/finish/pallas_call | solution.py:312
  102.8 1.2 collective-permute-done.13
  103.9 1.5 %collective-permute-start.14 = (f32[64]{0:T(128)S(1)}, f32[64]{0:T(128)S(1)}, u32[]{:S(2)}, u32[]{:S(2)}) collective-permute-start(f32[64]{0:T(128)S(1)} %add.128), channel_id=1, source_target_pairs={{0,2},{2,0},{1,3},{3,1},{4,6},{6,4},{5,7},{7,5},{8,10},{10,8},{9,1... | collective-permute-start | bytes 776 | tf_op jit(solution)/shard_map/ppermute | solution.py:364
  105.9 1.6 %collective-permute-done.14 = f32[64]{0:T(128)S(1)} collective-permute-done((f32[64]{0:T(128)S(1)}, f32[64]{0:T(128)S(1)}, u32[]{:S(2)}, u32[]{:S(2)}) %collective-permute-start.14) | collective-permute-done | bytes 288 | tf_op jit(solution)/shard_map/ppermute | solution.py:364
  107.5 10.6 %collective-permute-start.15 = (f32[64]{0:T(128)S(1)}, f32[64]{0:T(128)S(1)}, u32[]{:S(2)}, u32[]{:S(2)}) collective-permute-start(f32[64]{0:T(128)S(1)} %add.129), channel_id=1, source_target_pairs={{0,4},{4,0},{8,12},{12,8},{1,5},{5,1},{9,13},{13,9},{2,6},{6,2},{1... | collective-permute-start | bytes 776 | tf_op jit(solution)/shard_map/ppermute | solution.py:364
  118.1 1.5 %collective-permute-done.15 = f32[64]{0:T(128)S(1)} collective-permute-done((f32[64]{0:T(128)S(1)}, f32[64]{0:T(128)S(1)}, u32[]{:S(2)}, u32[]{:S(2)}) %collective-permute-start.15) | collective-permute-done | bytes 288 | tf_op jit(solution)/shard_map/ppermute | solution.py:364
  119.6 3.6 %collective-permute-start.16 = (f32[64]{0:T(128)S(1)}, f32[64]{0:T(128)S(1)}, u32[]{:S(2)}, u32[]{:S(2)}) collective-permute-start(f32[64]{0:T(128)S(1)} %add.130), channel_id=1, source_target_pairs={{0,8},{4,12},{8,0},{12,4},{1,9},{5,13},{9,1},{13,5},{2,10},{6,14},... | collective-permute-start | bytes 776 | tf_op jit(solution)/shard_map/ppermute | solution.py:364
  123.2 1.5 %collective-permute-done.16 = f32[64]{0:T(128)S(1)} collective-permute-done((f32[64]{0:T(128)S(1)}, f32[64]{0:T(128)S(1)}, u32[]{:S(2)}, u32[]{:S(2)}) %collective-permute-start.16) | collective-permute-done | bytes 288 | tf_op jit(solution)/shard_map/ppermute | solution.py:364
  125.2 2.0 %put_in_slots.1 = bf16[16,256,256]{2,1,0:T(8,128)(2,1)} custom-call(s32[16]{0:T(128)S(1)} %pad_add_fusion.slot_ref, bf16[4,256,256]{2,1,0:T(8,128)(2,1)S(1)} %get-tuple-element.47.refs_0_, bf16[4,256,256]{2,1,0:T(8,128)(2,1)S(1)} %collective-permute-done.10.refs_1_, bf16[4,256,256]{2,1,0:T(8,128)(2,1)S(1)} %get-tuple-element.49.refs_2_, ...), custom_call_target="tpu_custom_call" | custom-call | bytes 4194304 | tf_op jit(solution)/shard_map/put_in_slots/pallas_call | solution.py:345
  (70 shorter events, 6.3 us)
Async XLA Ops:
  1.3 12.6 %collective-permute-start.3 = (s32[16]{0:T(128)S(1)}, s32[16]{0:T(128)S(1)}, u32[]{:S(2)}, u32[]{:S(2)}) collective-permute-start(s32[16]{0:T(128)S(1)} %get-tuple-element.75), channel_id=1, source_target_pairs={{12,0},{8,4},{4,8},{0,12},{13,1},{9,5},{5,9},{1,13},{14,2},{10,6},... | collective-permute-start | bytes 200 | tf_op jit(solution)/shard_map/ppermute | solution.py:397
  6.4 7.5 %collective-permute-start.2 = (s32[16]{0:T(128)S(1)}, s32[16]{0:T(128)S(1)}, u32[]{:S(2)}, u32[]{:S(2)}) collective-permute-start(s32[16]{0:T(128)S(1)} %get-tuple-element.75), channel_id=1, source_target_pairs={{8,0},{0,4},{12,8},{4,12},{9,1},{1,5},{13,9},{5,13},{10,2},{2,6},{... | collective-permute-start | bytes 200 | tf_op jit(solution)/shard_map/ppermute | solution.py:397
  6.4 4.2 %collective-permute-start = (s32[16]{0:T(128)S(1)}, s32[16]{0:T(128)S(1)}, u32[]{:S(2)}, u32[]{:S(2)}) collective-permute-start(s32[16]{0:T(128)S(1)} %get-tuple-element.75), channel_id=1, source_target_pairs={{4,0},{12,4},{0,8},{8,12},{5,1},{13,5},{1,9},{9,13},{6,2},{14,6},{... | collective-permute-start | bytes 200 | tf_op jit(solution)/shard_map/ppermute | solution.py:396
  10.4 10.1 %copy-start.9 = (s32[16,1]{0,1:T(1,128)S(1)}, s32[16,1]{0,1:T(1,128)}, u32[]{:S(2)}) copy-start(s32[16,1]{0,1:T(1,128)} %param.24) | copy-start | bytes 196
  10.4 10.1 %copy-start.11 = (s32[16]{0:T(128)S(1)}, s32[16]{0:T(128)}, u32[]{:S(2)}) copy-start(s32[16]{0:T(128)} %param.18) | copy-start | bytes 196
  10.4 10.1 %copy-start.12 = (s32[16]{0:T(128)S(1)}, s32[16]{0:T(128)}, u32[]{:S(2)}) copy-start(s32[16]{0:T(128)} %param.19) | copy-start | bytes 196
  10.5 10.4 %copy-start.10 = (f32[64]{0:T(128)S(1)}, f32[64]{0:T(128)}, u32[]{:S(2)}) copy-start(f32[64]{0:T(128)} %param.17) | copy-start | bytes 772
  10.5 10.7 %copy-start = (bf16[16,256,256]{2,1,0:T(8,128)(2,1)S(1)}, bf16[16,256,256]{2,1,0:T(8,128)(2,1)}, u32[]{:S(2)}) copy-start(bf16[16,256,256]{2,1,0:T(8,128)(2,1)} %refs_3_.4) | copy-start | bytes 6291460
  10.5 10.7 %copy-start.1 = (bf16[16,256,256]{2,1,0:T(8,128)(2,1)S(1)}, bf16[16,256,256]{2,1,0:T(8,128)(2,1)}, u32[]{:S(2)}) copy-start(bf16[16,256,256]{2,1,0:T(8,128)(2,1)} %refs_2_.7) | copy-start | bytes 6291460
  10.5 10.7 %copy-start.6 = (s32[16,11]{1,0:T(8,128)S(1)}, s32[16,11]{1,0:T(8,128)}, u32[]{:S(2)}) copy-start(s32[16,11]{1,0:T(8,128)} %slot_ref.3) | copy-start | bytes 2116
  10.5 10.7 %copy-start.7 = (bf16[16,11]{1,0:T(8,128)(2,1)S(1)}, bf16[16,11]{1,0:T(8,128)(2,1)}, u32[]{:S(2)}) copy-start(bf16[16,11]{1,0:T(8,128)(2,1)} %weight_ref.3) | copy-start | bytes 1060
  10.5 10.7 %copy-start.8 = (s32[16]{0:T(128)S(1)}, s32[16]{0:T(128)}, u32[]{:S(2)}) copy-start(s32[16]{0:T(128)} %count_ref.3) | copy-start | bytes 196
  13.4 38.3 %collective-permute-start.1 = (bf16[4,256,256]{2,1,0:T(8,128)(2,1)S(1)}, bf16[4,256,256]{2,1,0:T(8,128)(2,1)S(1)}, u32[]{:S(2)}, u32[]{:S(2)}) collective-permute-start(bf16[4,256,256]{2,1,0:T(8,128)(2,1)S(1)} %get-tuple-element.36), channel_id=1, source_target_pairs={{0,4},{4,12},{8,0},{12,8},{1,5},{5,13},{9,1},{13,9},{2,6},{6,14},{... | collective-permute-start | bytes 1572872 | tf_op jit(solution)/shard_map/ppermute | solution.py:464
  16.6 35.1 %collective-permute-start.4 = (bf16[4,256,256]{2,1,0:T(8,128)(2,1)S(1)}, bf16[4,256,256]{2,1,0:T(8,128)(2,1)S(1)}, u32[]{:S(2)}, u32[]{:S(2)}) collective-permute-start(bf16[4,256,256]{2,1,0:T(8,128)(2,1)S(1)} %get-tuple-element.39), channel_id=1, source_target_pairs={{0,8},{4,0},{8,12},{12,4},{1,9},{5,1},{9,13},{13,5},{2,10},{6,2},{... | collective-permute-start | bytes 1572872 | tf_op jit(solution)/shard_map/ppermute | solution.py:473
  19.1 33.9 %collective-permute-start.5 = (bf16[4,256,256]{2,1,0:T(8,128)(2,1)S(1)}, bf16[4,256,256]{2,1,0:T(8,128)(2,1)S(1)}, u32[]{:S(2)}, u32[]{:S(2)}) collective-permute-start(bf16[4,256,256]{2,1,0:T(8,128)(2,1)S(1)} %get-tuple-element.40), channel_id=1, source_target_pairs={{0,12},{4,8},{8,4},{12,0},{1,13},{5,9},{9,5},{13,1},{2,14},{6,10},... | collective-permute-start | bytes 1572872 | tf_op jit(solution)/shard_map/ppermute | solution.py:473
  21.3 1.6 %copy-start.2 = (bf16[16,256,256]{2,1,0:T(8,128)(2,1)S(1)}, bf16[16,256,256]{2,1,0:T(8,128)(2,1)}, u32[]{:S(2)}) copy-start(bf16[16,256,256]{2,1,0:T(8,128)(2,1)} %refs_3_.5) | copy-start | bytes 6291460
  22.9 1.6 %copy-start.4 = (bf16[16,256,256]{2,1,0:T(8,128)(2,1)S(1)}, bf16[16,256,256]{2,1,0:T(8,128)(2,1)}, u32[]{:S(2)}) copy-start(bf16[16,256,256]{2,1,0:T(8,128)(2,1)} %refs_4_.1) | copy-start | bytes 6291460
  24.4 3.6 %copy-start.13 = (bf16[16,1]{0,1:T(2,128)(2,1)S(1)}, bf16[16,1]{0,1:T(2,128)(2,1)}, u32[]{:S(2)}) copy-start(bf16[16,1]{0,1:T(2,128)(2,1)} %param.25) | copy-start | bytes 100
  52.9 2.0 %collective-permute-start.6 = (bf16[4,256,256]{2,1,0:T(8,128)(2,1)S(1)}, bf16[4,256,256]{2,1,0:T(8,128)(2,1)S(1)}, u32[]{:S(2)}, u32[]{:S(2)}) collective-permute-start(bf16[4,256,256]{2,1,0:T(8,128)(2,1)S(1)} %finish.4.refs_0_), channel_id=1, source_target_pairs={{0,1},{1,0},{2,3},{3,2},{4,5},{5,4},{6,7},{7,6},{8,9},{9,8},{10,11... | collective-permute-start | bytes 1572872 | tf_op jit(solution)/shard_map/ppermute | solution.py:485
  54.2 2.1 %collective-permute-start.7 = (bf16[4,256,256]{2,1,0:T(8,128)(2,1)S(1)}, bf16[4,256,256]{2,1,0:T(8,128)(2,1)S(1)}, u32[]{:S(2)}, u32[]{:S(2)}) collective-permute-start(bf16[4,256,256]{2,1,0:T(8,128)(2,1)S(1)} %finish.5.refs_2_), channel_id=1, source_target_pairs={{0,1},{1,0},{2,3},{3,2},{4,5},{5,4},{6,7},{7,6},{8,9},{9,8},{10,11... | collective-permute-start | bytes 1572872 | tf_op jit(solution)/shard_map/ppermute | solution.py:489
  57.0 20.8 %collective-permute-start.8 = (bf16[4,256,256]{2,1,0:T(8,128)(2,1)S(1)}, bf16[4,256,256]{2,1,0:T(8,128)(2,1)S(1)}, u32[]{:S(2)}, u32[]{:S(2)}) collective-permute-start(bf16[4,256,256]{2,1,0:T(8,128)(2,1)S(1)} %gather_again.2), channel_id=1, source_target_pairs={{0,4},{4,12},{8,0},{12,8},{1,5},{5,13},{9,1},{13,9},{2,6},{6,14},{... | collective-permute-start | bytes 1572872 | tf_op jit(solution)/shard_map/ppermute | solution.py:464
  66.2 22.8 %collective-permute-start.9 = (bf16[4,256,256]{2,1,0:T(8,128)(2,1)S(1)}, bf16[4,256,256]{2,1,0:T(8,128)(2,1)S(1)}, u32[]{:S(2)}, u32[]{:S(2)}) collective-permute-start(bf16[4,256,256]{2,1,0:T(8,128)(2,1)S(1)} %get-tuple-element.46), channel_id=1, source_target_pairs={{0,8},{4,0},{8,12},{12,4},{1,9},{5,1},{9,13},{13,5},{2,10},{6,2},{... | collective-permute-start | bytes 1572872 | tf_op jit(solution)/shard_map/ppermute | solution.py:473
  66.2 34.4 %collective-permute-start.11 = (bf16[4,256,256]{2,1,0:T(8,128)(2,1)S(1)}, bf16[4,256,256]{2,1,0:T(8,128)(2,1)S(1)}, u32[]{:S(2)}, u32[]{:S(2)}) collective-permute-start(bf16[4,256,256]{2,1,0:T(8,128)(2,1)S(1)} %get-tuple-element.48), channel_id=1, source_target_pairs={{0,12},{4,8},{8,4},{12,0},{1,13},{5,9},{9,5},{13,1},{2,14},{6,10},... | collective-permute-start | bytes 1572872 | tf_op jit(solution)/shard_map/ppermute | solution.py:473
  68.7 1.6 %copy-start.3 = (bf16[16,256,256]{2,1,0:T(8,128)(2,1)S(1)}, bf16[16,256,256]{2,1,0:T(8,128)(2,1)}, u32[]{:S(2)}) copy-start(bf16[16,256,256]{2,1,0:T(8,128)(2,1)} %refs_3_.5) | copy-start | bytes 6291460
  68.7 2.2 %copy-start.5 = (bf16[16,256,256]{2,1,0:T(8,128)(2,1)S(1)}, bf16[16,256,256]{2,1,0:T(8,128)(2,1)}, u32[]{:S(2)}) copy-start(bf16[16,256,256]{2,1,0:T(8,128)(2,1)} %refs_4_.1) | copy-start | bytes 6291460
  102.8 1.2 collective-permute-start.13
  103.9 3.6 %collective-permute-start.14 = (f32[64]{0:T(128)S(1)}, f32[64]{0:T(128)S(1)}, u32[]{:S(2)}, u32[]{:S(2)}) collective-permute-start(f32[64]{0:T(128)S(1)} %add.128), channel_id=1, source_target_pairs={{0,2},{2,0},{1,3},{3,1},{4,6},{6,4},{5,7},{7,5},{8,10},{10,8},{9,1... | collective-permute-start | bytes 776 | tf_op jit(solution)/shard_map/ppermute | solution.py:364
  105.4 19.8 %collective-permute-start.12 = (bf16[4,256,256]{2,1,0:T(8,128)(2,1)S(1)}, bf16[4,256,256]{2,1,0:T(8,128)(2,1)S(1)}, u32[]{:S(2)}, u32[]{:S(2)}) collective-permute-start(bf16[4,256,256]{2,1,0:T(8,128)(2,1)S(1)} %get-tuple-element.49.refs_2_), channel_id=1, source_target_pairs={{0,1},{1,0},{2,3},{3,2},{4,5},{5,4},{6,7},{7,6},{8,9},{9,8},{10,11... | collective-permute-start | bytes 1572872 | tf_op jit(solution)/shard_map/ppermute | solution.py:489
  105.4 19.8 %collective-permute-start.10 = (bf16[4,256,256]{2,1,0:T(8,128)(2,1)S(1)}, bf16[4,256,256]{2,1,0:T(8,128)(2,1)S(1)}, u32[]{:S(2)}, u32[]{:S(2)}) collective-permute-start(bf16[4,256,256]{2,1,0:T(8,128)(2,1)S(1)} %get-tuple-element.47.refs_0_), channel_id=1, source_target_pairs={{0,1},{1,0},{2,3},{3,2},{4,5},{5,4},{6,7},{7,6},{8,9},{9,8},{10,11... | collective-permute-start | bytes 1572872 | tf_op jit(solution)/shard_map/ppermute | solution.py:485
  107.5 12.1 %collective-permute-start.15 = (f32[64]{0:T(128)S(1)}, f32[64]{0:T(128)S(1)}, u32[]{:S(2)}, u32[]{:S(2)}) collective-permute-start(f32[64]{0:T(128)S(1)} %add.129), channel_id=1, source_target_pairs={{0,4},{4,0},{8,12},{12,8},{1,5},{5,1},{9,13},{13,9},{2,6},{6,2},{1... | collective-permute-start | bytes 776 | tf_op jit(solution)/shard_map/ppermute | solution.py:364
  119.6 5.1 %collective-permute-start.16 = (f32[64]{0:T(128)S(1)}, f32[64]{0:T(128)S(1)}, u32[]{:S(2)}, u32[]{:S(2)}) collective-permute-start(f32[64]{0:T(128)S(1)} %add.130), channel_id=1, source_target_pairs={{0,8},{4,12},{8,0},{12,4},{1,9},{5,13},{9,1},{13,5},{2,10},{6,14},... | collective-permute-start | bytes 776 | tf_op jit(solution)/shard_map/ppermute | solution.py:364

commit v9 on v8

--- a/solution.py
+++ b/solution.py
@@ -59,10 +59,11 @@
     return placed
 
 
-def gather_first(requests, shifts, place, amplitudes, rows, cap):
+def gather_first(requests, parts, place, amplitudes, rows, cap):
     pairs, domain = amplitudes.shape[:2]
-    count_of = len(shifts)
-    blocks = count_of * cap
+    steps = sorted({step for step, _, _ in parts})
+    count_of = len(steps)
+    blocks = sum(size for _, _, size in parts)
     bits = pairs.bit_length() - 1
 
     def body(place_ref, *refs):
@@ -73,7 +74,7 @@
         sem = refs[-1]
         me = place_ref[0]
         core = place_ref[1]
-        for n, step in enumerate(shifts):
+        for n, step in enumerate(steps):
             base = n * (cap + 1)
             asker = jnp.int32(0)
             for a, b in sent(rows, step):
@@ -98,48 +99,49 @@
                 asked[base + jnp.minimum(filled, cap)] = entries[p] - sources[p] * pairs
                 filled = filled + jnp.where((count & 1) == core, mine, 0)
                 count = count + mine
-            for k in range(cap):
-                pltpu.make_async_copy(
-                    store.at[asked[base + k]], outs[n].at[k], sem.at[n, k]
-                ).start()
-        for n in range(count_of):
-            for k in range(cap):
-                pltpu.make_async_copy(store.at[0], outs[n].at[k], sem.at[n, k]).wait()
-
-    shape = (cap, domain, domain)
+            for m, (of, begin, size) in enumerate(parts):
+                for k in range(size if of == step else 0):
+                    pltpu.make_async_copy(
+                        store.at[asked[base + begin + k]], outs[m].at[k], sem.at[m, k]
+                    ).start()
+        for m, (_, _, size) in enumerate(parts):
+            for k in range(size):
+                pltpu.make_async_copy(store.at[0], outs[m].at[k], sem.at[m, k]).wait()
+
     return pl.pallas_call(
         body,
         out_shape=[jax.ShapeDtypeStruct((count_of * (cap + 1),), jnp.int32)]
-        + [VMEM(shape, jnp.bfloat16)] * count_of,
+        + [VMEM((size, domain, domain), jnp.bfloat16) for _, _, size in parts],
         in_specs=[pl.BlockSpec(memory_space=SMEM)] * (count_of + 1)
         + [pl.BlockSpec(memory_space=pltpu.HBM)],
         out_specs=[pl.BlockSpec(memory_space=SMEM)]
-        + [pl.BlockSpec(memory_space=VMEM)] * count_of,
-        scratch_shapes=[pltpu.SemaphoreType.DMA((count_of, cap))],
+        + [pl.BlockSpec(memory_space=VMEM)] * len(parts),
+        scratch_shapes=[pltpu.SemaphoreType.DMA((len(parts), cap))],
         cost_estimate=cost(0, blocks * domain * domain * 4),
         compiler_params=limits(8),
         name="gather_first",
     )(place, *requests, pltpu.with_memory_space_constraint(amplitudes, pltpu.HBM))
 
 
-def gather_again(asked, where, stores, cap):
+def gather_again(asked, where, stores, parts, cap):
     domain = stores[0].shape[1]
-    lists = asked.shape[0] // (cap + 1)
-    blocks = lists * cap
+    steps = sorted({step for step, _, _ in parts})
+    blocks = sum(size for _, _, size in parts)
 
     def body(asked_ref, where_ref, *refs):
         sources = laid(refs[: len(stores)])
         outs = refs[len(stores) :]
-        for b in range(blocks):
-            spot = where_ref[asked_ref[b // cap * (cap + 1) + b % cap]]
-            fetch(sources, spot, outs[b // cap].at[b % cap])
+        for m, (step, begin, size) in enumerate(parts):
+            for k in range(size):
+                spot = where_ref[asked_ref[steps.index(step) * (cap + 1) + begin + k]]
+                fetch(sources, spot, outs[m].at[k])
 
     return pl.pallas_call(
         body,
-        out_shape=[VMEM((cap, domain, domain), jnp.bfloat16)] * lists,
+        out_shape=[VMEM((size, domain, domain), jnp.bfloat16) for _, _, size in parts],
         in_specs=[pl.BlockSpec(memory_space=SMEM)] * 2
         + [pl.BlockSpec(memory_space=VMEM)] * len(stores),
-        out_specs=[pl.BlockSpec(memory_space=VMEM)] * lists,
+        out_specs=[pl.BlockSpec(memory_space=VMEM)] * len(parts),
         cost_estimate=cost(0, blocks * domain * domain * 4),
         compiler_params=limits(8),
         name="gather_again",
@@ -392,10 +394,15 @@
     source = far_chip[:, 0]
     packed = source * pairs + far_slot[:, 0]
     here = jnp.stack([row, core]).astype(jnp.int32)
-    groups = [[1], list(range(2, rows))]
+    tail = max(1, cap // 2)
+    lead = [(1, 0, cap)]
+    rest = [(step, 0, cap) for step in range(2, rows - 1)]
+    rest += [(rows - 1, 0, cap - tail)] * (cap > tail) + [(rows - 1, cap - tail, tail)]
     request = lax.ppermute(packed, "row", asked_of(rows, 1))
-    requests = [lax.ppermute(packed, "row", asked_of(rows, d)) for d in groups[1]]
-    asked_lead, send_lead = gather_first([request], groups[0], here, amplitudes, rows, cap)
+    requests = [
+        lax.ppermute(packed, "row", asked_of(rows, d)) for d in range(2, rows)
+    ]
+    asked_lead, send_lead = gather_first([request], lead, here, amplitudes, rows, cap)
 
     step = step_of(rows, source, row)
     same = step[:, None] == step[None, :]
@@ -431,7 +438,7 @@
     shift = energy_of(first) + energy_of(second)
 
     by_slot = turn // 2 + jnp.where(turn % 2 == core, 0, half)
-    early = half - cap
+    early = half - tail
     swap = [(0, 1), (1, 0)]
     remote = (rows - 1) * cap
     local_spots = [
@@ -459,19 +466,15 @@
         last = sweep == ITERS - 1
         again = min(sweep, 1)
         if sweep > 0:
-            (send_lead,) = gather_again(asked_lead, local_spots[1], stores, cap)
-        arrived = {}
-        arrived[1] = lax.ppermute(send_lead, "row", sent(rows, 1))
+            (send_lead,) = gather_again(asked_lead, local_spots[1], stores, lead, cap)
+        arrived = [lax.ppermute(send_lead, "row", sent(rows, 1))]
         if sweep == 0:
             (*requests, _) = lax.optimization_barrier((*requests, send_lead))
-            asked, *sends = gather_first(
-                requests, groups[1], here, amplitudes, rows, cap
-            )
+            asked, *sends = gather_first(requests, rest, here, amplitudes, rows, cap)
         else:
-            sends = gather_again(asked, local_spots[1], stores, cap)
-        for d, send in zip(groups[1], sends):
-            arrived[d] = lax.ppermute(send, "row", sent(rows, d))
-        arrived = [arrived[d] for d in range(1, rows)]
+            sends = gather_again(asked, local_spots[1], stores, rest, cap)
+        for part, send in zip(rest, sends):
+            arrived.append(lax.ppermute(send, "row", sent(rows, part[0])))
         prepared = prepare(
             own, ats[again], columns[again], near_count, shift, near, whole,
             integrals, fock_matrix, intersection,
@@ -484,7 +487,7 @@
         )
         given_early = lax.ppermute(done_early[0], "rep", swap)
         done_late = finish(
-            early, cap, tables[again], far_scale, prepared, spots, homes, occ_count, last
+            early, tail, tables[again], far_scale, prepared, spots, homes, occ_count, last
         )
         given_late = lax.ppermute(done_late[0], "rep", swap)
         stores = [done_early[0], given_early, done_late[0], given_late]

time: 127 us -> 129 us (1.016)
  waiting for transfers between devices: 54.8 us -> 59.2 us
  local copies, waits for them, and re-layouts: 5.4 us -> 3.45 us
    ppermute x6 -> x8, waiting for transfers between devices: 47.6 us -> 51.5 us  [the longest x6 41.6 us: per_device(): arrived.append(lax.ppermute(send, 'row', sent(rows, part[0])))]
    unnamed x29, local copies, waits for them, and re-layouts: 5.29 us -> 3.29 us
    ppermute x6 -> x8, starting transfers between devices: 15.2 us -> 15.8 us  [the longest x6 9.17 us: per_device(): arrived.append(lax.ppermute(send, 'row', sent(rows, part[0])))]
  transfers between devices with their start and end apart: 17 -> 19, of which waited for: 11 -> 11; matrix products, arithmetic and copies ran while one was open for 2% -> 2% of each run, Pallas kernels for 14% -> 14%
where the time goes in v9:
time: 129 us
  waiting for transfers between devices  59.2 us (46%)
  starting transfers between devices  39.1 us (30%)
  Pallas kernels  22.7 us (18%)
  other arithmetic  3.56 us (3%)
  local copies, waits for them, and re-layouts  3.45 us (3%)
    ppermute x6, waiting for transfers between devices, per_device(): arrived.append(lax.ppermute(send, 'row', sent(rows, part[0])))  41.6 us
    ppermute x4, starting transfers between devices, add_over(): lax.ppermute(values, name, [(r, r ^ step) for r in range(size)])  15.1 us
    ppermute x2, waiting for transfers between devices, per_device(): arrived = [lax.ppermute(send_lead, 'row', sent(rows, 1))]  9.86 us
    ppermute x6, starting transfers between devices, per_device(): arrived.append(lax.ppermute(send, 'row', sent(rows, part[0])))  9.17 us
    pallas_call x2, Pallas kernels, prepare(): pl.pallas_call(body, grid_spec=pltpu.PrefetchScalarGridSpec(num_scalar_pr...  7.12 us
    ppermute x2, starting transfers between devices, per_device(): arrived = [lax.ppermute(send_lead, 'row', sent(rows, 1))]  6.66 us
    pallas_call x4, Pallas kernels, finish(): pl.pallas_call(body, out_shape=out_shape, in_specs=[pl.BlockSpec(memory_s...  6.64 us
    ppermute x4, waiting for transfers between devices, add_over(): lax.ppermute(values, name, [(r, r ^ step) for r in range(size)])  6.09 us
  transfers between devices with their start and end apart: 19, of which 11 were waited for; matrix products, arithmetic and copies ran while one was open for 2% of the time, Pallas kernels for 14%

profile of v9, /device:TPU:0, one launch (start us, length us, event | category | flops | bytes accessed | tf_op | source)
XLA Modules:
  0.0 128.9 jit_solution(18043454345754412894)
XLA Ops:
  1.3 5.1 %collective-permute-start.3 = (s32[16]{0:T(128)S(1)}, s32[16]{0:T(128)S(1)}, u32[]{:S(2)}, u32[]{:S(2)}) collective-permute-start(s32[16]{0:T(128)S(1)} %get-tuple-element.75), channel_id=1, source_target_pairs={{12,0},{8,4},{4,8},{0,12},{13,1},{9,5},{5,9},{1,13},{14,2},{10,6},... | collective-permute-start | bytes 200 | tf_op jit(solution)/shard_map/ppermute | solution.py:403
  6.4 2.9 %collective-permute-start = (s32[16]{0:T(128)S(1)}, s32[16]{0:T(128)S(1)}, u32[]{:S(2)}, u32[]{:S(2)}) collective-permute-start(s32[16]{0:T(128)S(1)} %get-tuple-element.75), channel_id=1, source_target_pairs={{4,0},{12,4},{0,8},{8,12},{5,1},{13,5},{1,9},{9,13},{6,2},{14,6},{... | collective-permute-start | bytes 200 | tf_op jit(solution)/shard_map/ppermute | solution.py:401
  10.6 2.8 %gather_first.2 = (s32[5]{0:T(128)S(1)}, bf16[4,256,256]{2,1,0:T(8,128)(2,1)S(1)}) custom-call(s32[2]{0:T(128)S(1)} %pad_add_fusion.1.place_ref, s32[16]{0:T(128)S(1)} %collective-permute-done.refs_0_, bf16[16,256,256]{2,1,0:T(8,128)(2,1)} %refs_4_.2), custom_call_target="tpu_custom_call" | custom-call | bytes 1048576 | tf_op jit(solution)/shard_map/gather_first/pallas_call | solution.py:111
  13.9 2.7 %gather_first.3 = (s32[10]{0:T(128)S(1)}, bf16[4,256,256]{2,1,0:T(8,128)(2,1)S(1)}, bf16[2,256,256]{2,1,0:T(8,128)(2,1)S(1)}, bf16[2,256,256]{2,1,0:T(8,128)(2,1)S(1)}) custom-call(s32[2]{0:T(128)S(1)} %pad_add_fusion.1.place_ref, s32[16]{0:T(128)S(1)} %collective-permute-done.2.refs_0_, s32[16]{0:T(128)S(1)} %collective-permute-done.3.refs_1_, ...), custom_call_target="tpu_custom_call" | custom-call | bytes 2097152 | tf_op jit(solution)/shard_map/gather_first/pallas_call | solution.py:111
  16.6 3.8 %collective-permute-start.5 = (bf16[2,256,256]{2,1,0:T(8,128)(2,1)S(1)}, bf16[2,256,256]{2,1,0:T(8,128)(2,1)S(1)}, u32[]{:S(2)}, u32[]{:S(2)}) collective-permute-start(bf16[2,256,256]{2,1,0:T(8,128)(2,1)S(1)} %get-tuple-element.42), channel_id=1, source_target_pairs={{0,12},{4,8},{8,4},{12,0},{1,13},{5,9},{9,5},{13,1},{2,14},{6,10},... | collective-permute-start | bytes 786440 | tf_op jit(solution)/shard_map/ppermute | solution.py:477
  21.3 1.6 %copy-done.2 = bf16[16,256,256]{2,1,0:T(8,128)(2,1)S(1)} copy-done((bf16[16,256,256]{2,1,0:T(8,128)(2,1)S(1)}, bf16[16,256,256]{2,1,0:T(8,128)(2,1)}, u32[]{:S(2)}) %copy-start.2) | copy-done | bytes 2097176
  22.9 1.6 %copy-done.4 = bf16[16,256,256]{2,1,0:T(8,128)(2,1)S(1)} copy-done((bf16[16,256,256]{2,1,0:T(8,128)(2,1)S(1)}, bf16[16,256,256]{2,1,0:T(8,128)(2,1)}, u32[]{:S(2)}) %copy-start.4) | copy-done | bytes 2097176
  24.5 3.6 %prepare.2 = (f32[8,256,256]{2,1,0:T(8,128)S(1)}, f32[8,256,256]{2,1,0:T(8,128)S(1)}, f32[8,256,256]{2,1,0:T(8,128)S(1)}, bf16[8,256,256]{2,1,0:T(8,128)(2,1)S(1)}) custom-call(s32[8]{0:T(128)S(1)} %get-tuple-element.61.own_ref.at_ref, s32[8]{0:T(128)S(1)} %get-tuple-element.61.own_ref.at_ref, s32[16]{0:T(128)S(1)} %iota.26.column_ref, s32[16]{0:T(128)S(1)} %copy-done.8, ...), custom_call_target="tpu_custom_call" | custom-call | flops 805306368 | bytes 12582912 | tf_op jit(solution)/shard_map/prepare/pallas_call | solution.py:237
  28.3 7.9 %collective-permute-done.5.refs_2_ = bf16[2,256,256]{2,1,0:T(8,128)(2,1)S(1)} collective-permute-done((bf16[2,256,256]{2,1,0:T(8,128)(2,1)S(1)}, bf16[2,256,256]{2,1,0:T(8,128)(2,1)S(1)}, u32[]{:S(2)}, u32[]{:S(2)}) %collective-permute-start.5) | collective-permute-done | bytes 262176 | tf_op jit(solution)/shard_map/ppermute | solution.py:477
  36.2 9.9 %collective-permute-done.1.refs_0_ = bf16[4,256,256]{2,1,0:T(8,128)(2,1)S(1)} collective-permute-done((bf16[4,256,256]{2,1,0:T(8,128)(2,1)S(1)}, bf16[4,256,256]{2,1,0:T(8,128)(2,1)S(1)}, u32[]{:S(2)}, u32[]{:S(2)}) %collective-permute-start.1) | collective-permute-done | bytes 524320 | tf_op jit(solution)/shard_map/ppermute | solution.py:470
  46.0 1.4 %finish.4.refs_0_ = bf16[6,256,256]{2,1,0:T(8,128)(2,1)S(1)} custom-call(s32[24]{0:T(128)S(1)} %get-tuple-element.70.number_ref, f32[8]{0:T(128)S(1)} %fusion.8.scale_ref, f32[8,256,256]{2,1,0:T(8,128)S(1)} %get-tuple-element.34.local_ref, f32[8,256,256]{2,1,0:T(8,128)S(1)} %get-tuple-element.35.rest_ref, f32[8,256,256]{2,1,0:T(8,128)S(1)} %get-tuple-element.36.recip_ref, ...), custom_call_target="tpu_custom_call" | custom-call | flops 402653184 | bytes 7077888 | tf_op jit(solution)/shard_map/finish/pallas_call | solution.py:314
  47.6 1.4 %collective-permute-start.6 = (bf16[2,256,256]{2,1,0:T(8,128)(2,1)S(1)}, bf16[2,256,256]{2,1,0:T(8,128)(2,1)S(1)}, u32[]{:S(2)}, u32[]{:S(2)}) collective-permute-start(bf16[2,256,256]{2,1,0:T(8,128)(2,1)S(1)} %get-tuple-element.43), channel_id=1, source_target_pairs={{0,12},{4,8},{8,4},{12,0},{1,13},{5,9},{9,5},{13,1},{2,14},{6,10},... | collective-permute-start | bytes 786440 | tf_op jit(solution)/shard_map/ppermute | solution.py:477
  48.9 9.2 %collective-permute-done.6.refs_3_ = bf16[2,256,256]{2,1,0:T(8,128)(2,1)S(1)} collective-permute-done((bf16[2,256,256]{2,1,0:T(8,128)(2,1)S(1)}, bf16[2,256,256]{2,1,0:T(8,128)(2,1)S(1)}, u32[]{:S(2)}, u32[]{:S(2)}) %collective-permute-start.6) | collective-permute-done | bytes 262176 | tf_op jit(solution)/shard_map/ppermute | solution.py:477
  58.2 1.0 finish.5.refs_2_
  59.3 1.5 %collective-permute-done.8.refs_3_ = bf16[2,256,256]{2,1,0:T(8,128)(2,1)S(1)} collective-permute-done((bf16[2,256,256]{2,1,0:T(8,128)(2,1)S(1)}, bf16[2,256,256]{2,1,0:T(8,128)(2,1)S(1)}, u32[]{:S(2)}, u32[]{:S(2)}) %collective-permute-start.8) | collective-permute-done | bytes 262176 | tf_op jit(solution)/shard_map/ppermute | solution.py:492
  61.5 6.1 %collective-permute-start.9 = (bf16[4,256,256]{2,1,0:T(8,128)(2,1)S(1)}, bf16[4,256,256]{2,1,0:T(8,128)(2,1)S(1)}, u32[]{:S(2)}, u32[]{:S(2)}) collective-permute-start(bf16[4,256,256]{2,1,0:T(8,128)(2,1)S(1)} %gather_again.2), channel_id=1, source_target_pairs={{0,4},{4,12},{8,0},{12,8},{1,5},{5,13},{9,1},{13,9},{2,6},{6,14},{... | collective-permute-start | bytes 1572872 | tf_op jit(solution)/shard_map/ppermute | solution.py:470
  67.6 0.8 gather_again.3
  68.7 2.4 %collective-permute-start.11 = (bf16[2,256,256]{2,1,0:T(8,128)(2,1)S(1)}, bf16[2,256,256]{2,1,0:T(8,128)(2,1)S(1)}, u32[]{:S(2)}, u32[]{:S(2)}) collective-permute-start(bf16[2,256,256]{2,1,0:T(8,128)(2,1)S(1)} %get-tuple-element.50), channel_id=1, source_target_pairs={{0,12},{4,8},{8,4},{12,0},{1,13},{5,9},{9,5},{13,1},{2,14},{6,10},... | collective-permute-start | bytes 786440 | tf_op jit(solution)/shard_map/ppermute | solution.py:477
  71.1 1.5 %collective-permute-start.13 = (bf16[2,256,256]{2,1,0:T(8,128)(2,1)S(1)}, bf16[2,256,256]{2,1,0:T(8,128)(2,1)S(1)}, u32[]{:S(2)}, u32[]{:S(2)}) collective-permute-start(bf16[2,256,256]{2,1,0:T(8,128)(2,1)S(1)} %get-tuple-element.52), channel_id=1, source_target_pairs={{0,12},{4,8},{8,4},{12,0},{1,13},{5,9},{9,5},{13,1},{2,14},{6,10},... | collective-permute-start | bytes 786440 | tf_op jit(solution)/shard_map/ppermute | solution.py:477
  72.7 3.6 %prepare.3 = (f32[8,256,256]{2,1,0:T(8,128)S(1)}, f32[8,256,256]{2,1,0:T(8,128)S(1)}, f32[8,256,256]{2,1,0:T(8,128)S(1)}, bf16[8,256,256]{2,1,0:T(8,128)(2,1)S(1)}) custom-call(s32[8]{0:T(128)S(1)} %get-tuple-element.61.own_ref.at_ref, s32[8]{0:T(128)S(1)} %iota.25.at_ref, s32[16]{0:T(128)S(1)} %pad_add_fusion.2.column_ref, s32[16]{0:T(128)S(1)} %copy-done.8, ...), custom_call_target="tpu_custom_call" | custom-call | flops 805306368 | bytes 12582912 | tf_op jit(solution)/shard_map/prepare/pallas_call | solution.py:237
  76.3 22.4 %collective-permute-done.11.refs_2_ = bf16[2,256,256]{2,1,0:T(8,128)(2,1)S(1)} collective-permute-done((bf16[2,256,256]{2,1,0:T(8,128)(2,1)S(1)}, bf16[2,256,256]{2,1,0:T(8,128)(2,1)S(1)}, u32[]{:S(2)}, u32[]{:S(2)}) %collective-permute-start.11) | collective-permute-done | bytes 262176 | tf_op jit(solution)/shard_map/ppermute | solution.py:477
  98.7 2.7 %finish.6 = (bf16[6,256,256]{2,1,0:T(8,128)(2,1)S(1)}, f32[1,64]{1,0:T(1,128)S(1)}) custom-call(s32[24]{0:T(128)S(1)} %get-tuple-element.71.number_ref, f32[8]{0:T(128)S(1)} %fusion.8.scale_ref, f32[8,256,256]{2,1,0:T(8,128)S(1)} %get-tuple-element.44.local_ref, f32[8,256,256]{2,1,0:T(8,128)S(1)} %get-tuple-element.45.rest_ref, ...), custom_call_target="tpu_custom_call" | custom-call | flops 402653184 | bytes 7077888 | tf_op jit(solution)/shard_map/finish/pallas_call | solution.py:314
  101.4 2.1 %collective-permute-done.13.refs_3_ = bf16[2,256,256]{2,1,0:T(8,128)(2,1)S(1)} collective-permute-done((bf16[2,256,256]{2,1,0:T(8,128)(2,1)S(1)}, bf16[2,256,256]{2,1,0:T(8,128)(2,1)S(1)}, u32[]{:S(2)}, u32[]{:S(2)}) %collective-permute-start.13) | collective-permute-done | bytes 262176 | tf_op jit(solution)/shard_map/ppermute | solution.py:477
  103.5 1.5 %finish.7 = (bf16[2,256,256]{2,1,0:T(8,128)(2,1)S(1)}, f32[1,64]{1,0:T(1,128)S(1)}) custom-call(s32[24]{0:T(128)S(1)} %get-tuple-element.71.number_ref, f32[8]{0:T(128)S(1)} %fusion.8.scale_ref, f32[8,256,256]{2,1,0:T(8,128)S(1)} %get-tuple-element.44.local_ref, f32[8,256,256]{2,1,0:T(8,128)S(1)} %get-tuple-element.45.rest_ref, ...), custom_call_target="tpu_custom_call" | custom-call | flops 134217728 | bytes 2359296 | tf_op jit(solution)/shard_map/finish/pallas_call | solution.py:314
  105.0 1.2 collective-permute-done.15
  106.1 1.5 %collective-permute-start.16 = (f32[64]{0:T(128)S(1)}, f32[64]{0:T(128)S(1)}, u32[]{:S(2)}, u32[]{:S(2)}) collective-permute-start(f32[64]{0:T(128)S(1)} %add.128), channel_id=1, source_target_pairs={{0,2},{2,0},{1,3},{3,1},{4,6},{6,4},{5,7},{7,5},{8,10},{10,8},{9,1... | collective-permute-start | bytes 776 | tf_op jit(solution)/shard_map/ppermute | solution.py:366
  107.6 2.1 %collective-permute-done.16 = f32[64]{0:T(128)S(1)} collective-permute-done((f32[64]{0:T(128)S(1)}, f32[64]{0:T(128)S(1)}, u32[]{:S(2)}, u32[]{:S(2)}) %collective-permute-start.16) | collective-permute-done | bytes 288 | tf_op jit(solution)/shard_map/ppermute | solution.py:366
  109.7 10.6 %collective-permute-start.17 = (f32[64]{0:T(128)S(1)}, f32[64]{0:T(128)S(1)}, u32[]{:S(2)}, u32[]{:S(2)}) collective-permute-start(f32[64]{0:T(128)S(1)} %add.129), channel_id=1, source_target_pairs={{0,4},{4,0},{8,12},{12,8},{1,5},{5,1},{9,13},{13,9},{2,6},{6,2},{1... | collective-permute-start | bytes 776 | tf_op jit(solution)/shard_map/ppermute | solution.py:366
  120.4 1.4 %collective-permute-done.17 = f32[64]{0:T(128)S(1)} collective-permute-done((f32[64]{0:T(128)S(1)}, f32[64]{0:T(128)S(1)}, u32[]{:S(2)}, u32[]{:S(2)}) %collective-permute-start.17) | collective-permute-done | bytes 288 | tf_op jit(solution)/shard_map/ppermute | solution.py:366
  121.8 3.1 %collective-permute-start.18 = (f32[64]{0:T(128)S(1)}, f32[64]{0:T(128)S(1)}, u32[]{:S(2)}, u32[]{:S(2)}) collective-permute-start(f32[64]{0:T(128)S(1)} %add.130), channel_id=1, source_target_pairs={{0,8},{4,12},{8,0},{12,4},{1,9},{5,13},{9,1},{13,5},{2,10},{6,14},... | collective-permute-start | bytes 776 | tf_op jit(solution)/shard_map/ppermute | solution.py:366
  125.0 1.5 %collective-permute-done.18 = f32[64]{0:T(128)S(1)} collective-permute-done((f32[64]{0:T(128)S(1)}, f32[64]{0:T(128)S(1)}, u32[]{:S(2)}, u32[]{:S(2)}) %collective-permute-start.18) | collective-permute-done | bytes 288 | tf_op jit(solution)/shard_map/ppermute | solution.py:366
  127.0 2.0 %put_in_slots.1 = bf16[16,256,256]{2,1,0:T(8,128)(2,1)} custom-call(s32[16]{0:T(128)S(1)} %pad_add_fusion.slot_ref, bf16[6,256,256]{2,1,0:T(8,128)(2,1)S(1)} %get-tuple-element.51.refs_0_, bf16[6,256,256]{2,1,0:T(8,128)(2,1)S(1)} %collective-permute-done.12.refs_1_, bf16[2,256,256]{2,1,0:T(8,128)(2,1)S(1)} %get-tuple-element.53.refs_2_, ...), custom_call_target="tpu_custom_call" | custom-call | bytes 4194304 | tf_op jit(solution)/shard_map/put_in_slots/pallas_call | solution.py:347
  (75 shorter events, 5.4 us)
Async XLA Ops:
  1.3 12.6 %collective-permute-start.3 = (s32[16]{0:T(128)S(1)}, s32[16]{0:T(128)S(1)}, u32[]{:S(2)}, u32[]{:S(2)}) collective-permute-start(s32[16]{0:T(128)S(1)} %get-tuple-element.75), channel_id=1, source_target_pairs={{12,0},{8,4},{4,8},{0,12},{13,1},{9,5},{5,9},{1,13},{14,2},{10,6},... | collective-permute-start | bytes 200 | tf_op jit(solution)/shard_map/ppermute | solution.py:403
  6.4 7.5 %collective-permute-start.2 = (s32[16]{0:T(128)S(1)}, s32[16]{0:T(128)S(1)}, u32[]{:S(2)}, u32[]{:S(2)}) collective-permute-start(s32[16]{0:T(128)S(1)} %get-tuple-element.75), channel_id=1, source_target_pairs={{8,0},{0,4},{12,8},{4,12},{9,1},{1,5},{13,9},{5,13},{10,2},{2,6},{... | collective-permute-start | bytes 200 | tf_op jit(solution)/shard_map/ppermute | solution.py:403
  6.4 4.2 %collective-permute-start = (s32[16]{0:T(128)S(1)}, s32[16]{0:T(128)S(1)}, u32[]{:S(2)}, u32[]{:S(2)}) collective-permute-start(s32[16]{0:T(128)S(1)} %get-tuple-element.75), channel_id=1, source_target_pairs={{4,0},{12,4},{0,8},{8,12},{5,1},{13,5},{1,9},{9,13},{6,2},{14,6},{... | collective-permute-start | bytes 200 | tf_op jit(solution)/shard_map/ppermute | solution.py:401
  10.4 10.1 %copy-start.9 = (s32[16,1]{0,1:T(1,128)S(1)}, s32[16,1]{0,1:T(1,128)}, u32[]{:S(2)}) copy-start(s32[16,1]{0,1:T(1,128)} %param.24) | copy-start | bytes 196
  10.4 10.0 %copy-start.11 = (s32[16]{0:T(128)S(1)}, s32[16]{0:T(128)}, u32[]{:S(2)}) copy-start(s32[16]{0:T(128)} %param.18) | copy-start | bytes 196
  10.4 10.0 %copy-start.12 = (s32[16]{0:T(128)S(1)}, s32[16]{0:T(128)}, u32[]{:S(2)}) copy-start(s32[16]{0:T(128)} %param.19) | copy-start | bytes 196
  10.5 10.4 %copy-start.10 = (f32[64]{0:T(128)S(1)}, f32[64]{0:T(128)}, u32[]{:S(2)}) copy-start(f32[64]{0:T(128)} %param.17) | copy-start | bytes 772
  10.5 10.7 %copy-start.13 = (bf16[16,1]{0,1:T(2,128)(2,1)S(1)}, bf16[16,1]{0,1:T(2,128)(2,1)}, u32[]{:S(2)}) copy-start(bf16[16,1]{0,1:T(2,128)(2,1)} %param.25) | copy-start | bytes 100
  10.5 10.7 %copy-start = (bf16[16,256,256]{2,1,0:T(8,128)(2,1)S(1)}, bf16[16,256,256]{2,1,0:T(8,128)(2,1)}, u32[]{:S(2)}) copy-start(bf16[16,256,256]{2,1,0:T(8,128)(2,1)} %refs_4_.2) | copy-start | bytes 6291460
  10.5 10.7 %copy-start.1 = (bf16[16,256,256]{2,1,0:T(8,128)(2,1)S(1)}, bf16[16,256,256]{2,1,0:T(8,128)(2,1)}, u32[]{:S(2)}) copy-start(bf16[16,256,256]{2,1,0:T(8,128)(2,1)} %refs_2_.5) | copy-start | bytes 6291460
  10.5 10.7 %copy-start.6 = (s32[16,11]{1,0:T(8,128)S(1)}, s32[16,11]{1,0:T(8,128)}, u32[]{:S(2)}) copy-start(s32[16,11]{1,0:T(8,128)} %slot_ref.3) | copy-start | bytes 2116
  10.5 10.7 %copy-start.7 = (bf16[16,11]{1,0:T(8,128)(2,1)S(1)}, bf16[16,11]{1,0:T(8,128)(2,1)}, u32[]{:S(2)}) copy-start(bf16[16,11]{1,0:T(8,128)(2,1)} %weight_ref.3) | copy-start | bytes 1060
  10.5 10.7 %copy-start.8 = (s32[16]{0:T(128)S(1)}, s32[16]{0:T(128)}, u32[]{:S(2)}) copy-start(s32[16]{0:T(128)} %count_ref.3) | copy-start | bytes 196
  13.4 32.6 %collective-permute-start.1 = (bf16[4,256,256]{2,1,0:T(8,128)(2,1)S(1)}, bf16[4,256,256]{2,1,0:T(8,128)(2,1)S(1)}, u32[]{:S(2)}, u32[]{:S(2)}) collective-permute-start(bf16[4,256,256]{2,1,0:T(8,128)(2,1)S(1)} %get-tuple-element.38), channel_id=1, source_target_pairs={{0,4},{4,12},{8,0},{12,8},{1,5},{5,13},{9,1},{13,9},{2,6},{6,14},{... | collective-permute-start | bytes 1572872 | tf_op jit(solution)/shard_map/ppermute | solution.py:470
  16.6 19.6 %collective-permute-start.5 = (bf16[2,256,256]{2,1,0:T(8,128)(2,1)S(1)}, bf16[2,256,256]{2,1,0:T(8,128)(2,1)S(1)}, u32[]{:S(2)}, u32[]{:S(2)}) collective-permute-start(bf16[2,256,256]{2,1,0:T(8,128)(2,1)S(1)} %get-tuple-element.42), channel_id=1, source_target_pairs={{0,12},{4,8},{8,4},{12,0},{1,13},{5,9},{9,5},{13,1},{2,14},{6,10},... | collective-permute-start | bytes 786440 | tf_op jit(solution)/shard_map/ppermute | solution.py:477
  20.4 25.6 %collective-permute-start.4 = (bf16[4,256,256]{2,1,0:T(8,128)(2,1)S(1)}, bf16[4,256,256]{2,1,0:T(8,128)(2,1)S(1)}, u32[]{:S(2)}, u32[]{:S(2)}) collective-permute-start(bf16[4,256,256]{2,1,0:T(8,128)(2,1)S(1)} %get-tuple-element.41), channel_id=1, source_target_pairs={{0,8},{4,0},{8,12},{12,4},{1,9},{5,1},{9,13},{13,5},{2,10},{6,2},{... | collective-permute-start | bytes 1572872 | tf_op jit(solution)/shard_map/ppermute | solution.py:477
  21.3 1.6 %copy-start.2 = (bf16[16,256,256]{2,1,0:T(8,128)(2,1)S(1)}, bf16[16,256,256]{2,1,0:T(8,128)(2,1)}, u32[]{:S(2)}) copy-start(bf16[16,256,256]{2,1,0:T(8,128)(2,1)} %refs_3_.5) | copy-start | bytes 6291460
  47.5 13.3 %collective-permute-start.7 = (bf16[6,256,256]{2,1,0:T(8,128)(2,1)S(1)}, bf16[6,256,256]{2,1,0:T(8,128)(2,1)S(1)}, u32[]{:S(2)}, u32[]{:S(2)}) collective-permute-start(bf16[6,256,256]{2,1,0:T(8,128)(2,1)S(1)} %finish.4.refs_0_), channel_id=1, source_target_pairs={{0,1},{1,0},{2,3},{3,2},{4,5},{5,4},{6,7},{7,6},{8,9},{9,8},{10,11... | collective-permute-start | bytes 2359304 | tf_op jit(solution)/shard_map/ppermute | solution.py:488
  47.6 10.6 %collective-permute-start.6 = (bf16[2,256,256]{2,1,0:T(8,128)(2,1)S(1)}, bf16[2,256,256]{2,1,0:T(8,128)(2,1)S(1)}, u32[]{:S(2)}, u32[]{:S(2)}) collective-permute-start(bf16[2,256,256]{2,1,0:T(8,128)(2,1)S(1)} %get-tuple-element.43), channel_id=1, source_target_pairs={{0,12},{4,8},{8,4},{12,0},{1,13},{5,9},{9,5},{13,1},{2,14},{6,10},... | collective-permute-start | bytes 786440 | tf_op jit(solution)/shard_map/ppermute | solution.py:477
  59.2 1.6 %collective-permute-start.8 = (bf16[2,256,256]{2,1,0:T(8,128)(2,1)S(1)}, bf16[2,256,256]{2,1,0:T(8,128)(2,1)S(1)}, u32[]{:S(2)}, u32[]{:S(2)}) collective-permute-start(bf16[2,256,256]{2,1,0:T(8,128)(2,1)S(1)} %finish.5.refs_2_), channel_id=1, source_target_pairs={{0,1},{1,0},{2,3},{3,2},{4,5},{5,4},{6,7},{7,6},{8,9},{9,8},{10,11... | collective-permute-start | bytes 786440 | tf_op jit(solution)/shard_map/ppermute | solution.py:492
  61.5 37.2 %collective-permute-start.9 = (bf16[4,256,256]{2,1,0:T(8,128)(2,1)S(1)}, bf16[4,256,256]{2,1,0:T(8,128)(2,1)S(1)}, u32[]{:S(2)}, u32[]{:S(2)}) collective-permute-start(bf16[4,256,256]{2,1,0:T(8,128)(2,1)S(1)} %gather_again.2), channel_id=1, source_target_pairs={{0,4},{4,12},{8,0},{12,8},{1,5},{5,13},{9,1},{13,9},{2,6},{6,14},{... | collective-permute-start | bytes 1572872 | tf_op jit(solution)/shard_map/ppermute | solution.py:470
  68.5 30.2 %collective-permute-start.10 = (bf16[4,256,256]{2,1,0:T(8,128)(2,1)S(1)}, bf16[4,256,256]{2,1,0:T(8,128)(2,1)S(1)}, u32[]{:S(2)}, u32[]{:S(2)}) collective-permute-start(bf16[4,256,256]{2,1,0:T(8,128)(2,1)S(1)} %get-tuple-element.49), channel_id=1, source_target_pairs={{0,8},{4,0},{8,12},{12,4},{1,9},{5,1},{9,13},{13,5},{2,10},{6,2},{... | collective-permute-start | bytes 1572872 | tf_op jit(solution)/shard_map/ppermute | solution.py:477
  68.6 4.1 %copy-start.3 = (bf16[16,256,256]{2,1,0:T(8,128)(2,1)S(1)}, bf16[16,256,256]{2,1,0:T(8,128)(2,1)}, u32[]{:S(2)}) copy-start(bf16[16,256,256]{2,1,0:T(8,128)(2,1)} %refs_3_.5) | copy-start | bytes 6291460
  68.6 4.1 %copy-start.5 = (bf16[16,256,256]{2,1,0:T(8,128)(2,1)S(1)}, bf16[16,256,256]{2,1,0:T(8,128)(2,1)}, u32[]{:S(2)}) copy-start(bf16[16,256,256]{2,1,0:T(8,128)(2,1)} %refs_4_.3) | copy-start | bytes 6291460
  68.7 30.0 %collective-permute-start.11 = (bf16[2,256,256]{2,1,0:T(8,128)(2,1)S(1)}, bf16[2,256,256]{2,1,0:T(8,128)(2,1)S(1)}, u32[]{:S(2)}, u32[]{:S(2)}) collective-permute-start(bf16[2,256,256]{2,1,0:T(8,128)(2,1)S(1)} %get-tuple-element.50), channel_id=1, source_target_pairs={{0,12},{4,8},{8,4},{12,0},{1,13},{5,9},{9,5},{13,1},{2,14},{6,10},... | collective-permute-start | bytes 786440 | tf_op jit(solution)/shard_map/ppermute | solution.py:477
  71.1 32.3 %collective-permute-start.13 = (bf16[2,256,256]{2,1,0:T(8,128)(2,1)S(1)}, bf16[2,256,256]{2,1,0:T(8,128)(2,1)S(1)}, u32[]{:S(2)}, u32[]{:S(2)}) collective-permute-start(bf16[2,256,256]{2,1,0:T(8,128)(2,1)S(1)} %get-tuple-element.52), channel_id=1, source_target_pairs={{0,12},{4,8},{8,4},{12,0},{1,13},{5,9},{9,5},{13,1},{2,14},{6,10},... | collective-permute-start | bytes 786440 | tf_op jit(solution)/shard_map/ppermute | solution.py:477
  101.4 25.6 %collective-permute-start.12 = (bf16[6,256,256]{2,1,0:T(8,128)(2,1)S(1)}, bf16[6,256,256]{2,1,0:T(8,128)(2,1)S(1)}, u32[]{:S(2)}, u32[]{:S(2)}) collective-permute-start(bf16[6,256,256]{2,1,0:T(8,128)(2,1)S(1)} %get-tuple-element.51.refs_0_), channel_id=1, source_target_pairs={{0,1},{1,0},{2,3},{3,2},{4,5},{5,4},{6,7},{7,6},{8,9},{9,8},{10,11... | collective-permute-start | bytes 2359304 | tf_op jit(solution)/shard_map/ppermute | solution.py:488
  105.0 1.2 collective-permute-start.15
  106.1 3.6 %collective-permute-start.16 = (f32[64]{0:T(128)S(1)}, f32[64]{0:T(128)S(1)}, u32[]{:S(2)}, u32[]{:S(2)}) collective-permute-start(f32[64]{0:T(128)S(1)} %add.128), channel_id=1, source_target_pairs={{0,2},{2,0},{1,3},{3,1},{4,6},{6,4},{5,7},{7,5},{8,10},{10,8},{9,1... | collective-permute-start | bytes 776 | tf_op jit(solution)/shard_map/ppermute | solution.py:366
  109.7 12.1 %collective-permute-start.17 = (f32[64]{0:T(128)S(1)}, f32[64]{0:T(128)S(1)}, u32[]{:S(2)}, u32[]{:S(2)}) collective-permute-start(f32[64]{0:T(128)S(1)} %add.129), channel_id=1, source_target_pairs={{0,4},{4,0},{8,12},{12,8},{1,5},{5,1},{9,13},{13,9},{2,6},{6,2},{1... | collective-permute-start | bytes 776 | tf_op jit(solution)/shard_map/ppermute | solution.py:366
  120.4 6.5 %collective-permute-start.14 = (bf16[2,256,256]{2,1,0:T(8,128)(2,1)S(1)}, bf16[2,256,256]{2,1,0:T(8,128)(2,1)S(1)}, u32[]{:S(2)}, u32[]{:S(2)}) collective-permute-start(bf16[2,256,256]{2,1,0:T(8,128)(2,1)S(1)} %get-tuple-element.53.refs_2_), channel_id=1, source_target_pairs={{0,1},{1,0},{2,3},{3,2},{4,5},{5,4},{6,7},{7,6},{8,9},{9,8},{10,11... | collective-permute-start | bytes 786440 | tf_op jit(solution)/shard_map/ppermute | solution.py:492
  121.8 4.6 %collective-permute-start.18 = (f32[64]{0:T(128)S(1)}, f32[64]{0:T(128)S(1)}, u32[]{:S(2)}, u32[]{:S(2)}) collective-permute-start(f32[64]{0:T(128)S(1)} %add.130), channel_id=1, source_target_pairs={{0,8},{4,12},{8,0},{12,4},{1,9},{5,13},{9,1},{13,5},{2,10},{6,14},... | collective-permute-start | bytes 776 | tf_op jit(solution)/shard_map/ppermute | solution.py:366
  (1 other events, 1.6 us)

commit v10 on v9

--- a/solution.py
+++ b/solution.py
@@ -33,6 +33,10 @@
     hop = jnp.where(hop < 0, hop + rows, hop)
     step = jnp.where(2 * hop <= rows, 2 * hop - 1, 2 * (rows - hop))
     return jnp.where(hop == 0, 0, step)
+
+
+def in_hbm(array):
+    return pltpu.with_memory_space_constraint(array, pltpu.HBM)
 
 
 def limits(mib):
@@ -120,7 +124,7 @@
         cost_estimate=cost(0, blocks * domain * domain * 4),
         compiler_params=limits(8),
         name="gather_first",
-    )(place, *requests, pltpu.with_memory_space_constraint(amplitudes, pltpu.HBM))
+    )(place, *requests, in_hbm(amplitudes))
 
 
 def gather_again(asked, where, stores, parts, cap):
@@ -148,7 +152,9 @@
     )(asked, where, *stores)
 
 
-def prepare(own, at, columns, counts, shift, near, stores, integrals, fock_matrix, intersection):
+def prepare(
+    own, at, home, columns, counts, shift, near, stores, integrals, fock_matrix, intersection
+):
     half = own.shape[0]
     domain = integrals.shape[1]
     total = columns.shape[0]
@@ -196,12 +202,13 @@
         spread_ref[...] = jnp.where(down == along, full, 0.0).astype(jnp.bfloat16)
 
     def body(
-        own_ref, at_ref, column_ref, count_ref, shift_ref, slot_ref, weight_ref, *refs
+        own_ref, at_ref, home_ref, column_ref, count_ref, shift_ref, slot_ref, weight_ref, *refs
     ):
         sources = refs[: len(stores)]
-        (integ_ref, fock_ref, over_ref, local_ref, rest_ref, recip_ref, keep_ref, spread_ref) = (
-            refs[len(stores) :]
-        )
+        (
+            integ_ref, fock_ref, over_ref,
+            local_ref, rest_ref, recip_ref, keep_ref, near_by_ref, spread_ref,
+        ) = refs[len(stores) :]
         i = pl.program_id(0)
 
         @pl.when(i == 0)
@@ -229,6 +236,7 @@
         recip_ref[0] = recip
         rest_ref[0] = wide - residual * recip
         keep_ref[0] = over_ref[0]
+        fetch(laid(sources), home_ref[i], near_by_ref.at[0])
 
     block = (1, domain, domain)
     mine = pl.BlockSpec(block, lambda i, own, *_: (own[i], 0, 0))
@@ -237,13 +245,14 @@
     return pl.pallas_call(
         body,
         grid_spec=pltpu.PrefetchScalarGridSpec(
-            num_scalar_prefetch=5,
+            num_scalar_prefetch=6,
             grid=(half,),
             in_specs=[pl.BlockSpec(n.shape, lambda i, *_: (0, 0)) for n in near]
             + [pl.BlockSpec(s.shape, lambda i, *_: (0, 0, 0)) for s in stores]
             + [mine, mine, mine],
             out_specs=[
                 pl.BlockSpec((half, strip, domain), lambda i, *_: (0, i, 0)),
+                in_turn,
                 in_turn,
                 in_turn,
                 in_turn,
@@ -255,6 +264,7 @@
             wide_shape,
             wide_shape,
             jax.ShapeDtypeStruct((half, domain, domain), jnp.bfloat16),
+            jax.ShapeDtypeStruct((half, domain, domain), jnp.bfloat16),
         ],
         cost_estimate=cost(
             2 * half * domain**3 * 3,
@@ -262,15 +272,19 @@
         ),
         compiler_params=limits(20),
         name="prepare",
-    )(own, at, columns, counts, shift, *near, *stores, integrals, fock_matrix, intersection)
-
-
-def finish(start, count, numbers, scale, prepared, arrived, stores, occ_count, last):
+    )(
+        own, at, home, columns, counts, shift, *near,
+        *[in_hbm(s) if s.shape[0] > half else s for s in stores],
+        in_hbm(integrals), in_hbm(fock_matrix), in_hbm(intersection),
+    )
+
+
+def finish(start, count, numbers, scale, prepared, arrived, occ_count, last):
     half, domain = prepared[0].shape[:2]
 
     def body(number_ref, scale_ref, local_ref, rest_ref, recip_ref, over_ref, *refs):
         candidates = [
-            (offset, ref) for offset, ref in zip([o for o, _ in arrived + stores], refs)
+            (offset, ref) for offset, ref in zip([o for o, _ in arrived], refs)
         ]
         outs = refs[len(candidates) : -1]
         hold = refs[-1]
@@ -316,13 +330,13 @@
         out_shape=out_shape,
         in_specs=[pl.BlockSpec(memory_space=SMEM)] * 2
         + [pl.BlockSpec(memory_space=VMEM)] * 4
-        + [pl.BlockSpec(memory_space=VMEM)] * len(arrived + stores),
+        + [pl.BlockSpec(memory_space=VMEM)] * len(arrived),
         out_specs=[pl.BlockSpec(memory_space=VMEM)] * len(out_shape),
         scratch_shapes=[VMEM((count, domain, domain), jnp.bfloat16)],
         cost_estimate=cost(2 * count * domain**3 * 2, count * domain * domain * 18),
         compiler_params=limits(16),
         name="finish",
-    )(numbers, scale, *prepared, *[a for _, a in arrived + stores])
+    )(numbers, scale, *prepared, *[a for _, a in arrived])
 
 
 def put_in_slots(slots, stores):
@@ -404,6 +418,15 @@
     ]
     asked_lead, send_lead = gather_first([request], lead, here, amplitudes, rows, cap)
 
+    (
+        source, far_slot, occ_energy, first_occ, second_occ, far_weight,
+        _,
+    ) = lax.optimization_barrier(
+        (
+            source, far_slot, occ_energy, first_occ, second_occ, far_weight,
+            asked_lead,
+        )
+    )
     step = step_of(rows, source, row)
     same = step[:, None] == step[None, :]
     before = (step[None, :] < step[:, None]) | (same & (slot_ids[None, :] < slot_ids[:, None]))
@@ -423,9 +446,6 @@
     own_far = pick(own_pick, far_slot[:, 0])
     own_place = pick(own_pick, place)
 
-    occ_energy, first_occ, second_occ, far_weight, _ = lax.optimization_barrier(
-        (occ_energy, first_occ, second_occ, far_weight, asked_lead)
-    )
     orbitals = jnp.arange(occ_count, dtype=jnp.int32)
 
     def energy_of(index):
@@ -449,13 +469,13 @@
             by_slot - half + jnp.where(by_slot % half < early, early, half),
         ),
     ]
-    tables = []
-    for where in (slot_ids, by_slot):
-        at_home = remote + jnp.sum(
-            jnp.where(own_far[:, None] == slot_ids[None, :], where[None, :], 0), axis=1
-        )
-        spot = jnp.where(far_step == 0, at_home, (far_step - 1) * cap + own_place)
-        tables.append(jnp.concatenate([spot, first, second]))
+    homes = [
+        jnp.sum(jnp.where(own_far[:, None] == slot_ids[None, :], where[None, :], 0), axis=1)
+        for where in (slot_ids, by_slot)
+    ]
+    at_home = remote + jnp.arange(half, dtype=jnp.int32)
+    spot = jnp.where(far_step == 0, at_home, (far_step - 1) * cap + own_place)
+    numbers = jnp.concatenate([spot, first, second])
     near = [near_slot, near_weight]
     columns = [slot_ids, jnp.concatenate([own, other])]
     ats = [own, jnp.arange(half, dtype=jnp.int32)]
@@ -475,19 +495,19 @@
             sends = gather_again(asked, local_spots[1], stores, rest, cap)
         for part, send in zip(rest, sends):
             arrived.append(lax.ppermute(send, "row", sent(rows, part[0])))
-        prepared = prepare(
-            own, ats[again], columns[again], near_count, shift, near, whole,
+        *prepared, at_home = prepare(
+            own, ats[again], homes[again], columns[again], near_count, shift, near, whole,
             integrals, fock_matrix, intersection,
         )
         spots = laid(arrived)
-        homes = laid(whole, remote)
+        at_home = [(remote, at_home)]
         done_early = finish(
-            0, early, tables[again], far_scale, prepared, spots[:-1], homes, occ_count,
+            0, early, numbers, far_scale, prepared, spots[:-1] + at_home, occ_count,
             last,
         )
         given_early = lax.ppermute(done_early[0], "rep", swap)
         done_late = finish(
-            early, tail, tables[again], far_scale, prepared, spots, homes, occ_count, last
+            early, tail, numbers, far_scale, prepared, spots + at_home, occ_count, last
         )
         given_late = lax.ppermute(done_late[0], "rep", swap)
         stores = [done_early[0], given_early, done_late[0], given_late]

time: 129 us -> 129 us (level)
  Pallas kernels: 22.7 us -> 29.8 us
  waiting for transfers between devices: 59.2 us -> 55.4 us
  local copies, waits for them, and re-layouts: 3.45 us -> 0.19 us
    pallas_call x2, Pallas kernels: 7.12 us -> 14.7 us  [prepare(): pl.pallas_call(body, grid_spec=pltpu.PrefetchScalarGridSpec(num_scalar_pr...]
    ppermute x6, waiting for transfers between devices: 41.6 us -> 36.9 us  [per_device(): arrived.append(lax.ppermute(send, 'row', sent(rows, part[0])))]
    unnamed x29 -> x18, local copies, waits for them, and re-layouts: 3.29 us -> 0.04 us
  transfers between devices with their start and end apart: 19 -> 19, of which waited for: 11 -> 11; matrix products, arithmetic and copies ran while one was open for 2% -> 2% of each run, Pallas kernels for 14% -> 20%
where the time goes in v10:
time: 129 us
  waiting for transfers between devices  55.4 us (43%)
  starting transfers between devices  39.5 us (31%)
  Pallas kernels  29.8 us (23%)
  other arithmetic  3.03 us (2%)
    ppermute x6, waiting for transfers between devices, per_device(): arrived.append(lax.ppermute(send, 'row', sent(rows, part[0])))  36.9 us
    ppermute x4, starting transfers between devices, add_over(): lax.ppermute(values, name, [(r, r ^ step) for r in range(size)])  15 us
    pallas_call x2, Pallas kernels, prepare(): pl.pallas_call(body, grid_spec=pltpu.PrefetchScalarGridSpec(num_scalar_pr...  14.7 us
    ppermute x2, waiting for transfers between devices, per_device(): arrived = [lax.ppermute(send_lead, 'row', sent(rows, 1))]  9.72 us
    ppermute x6, starting transfers between devices, per_device(): arrived.append(lax.ppermute(send, 'row', sent(rows, part[0])))  9.37 us
    ppermute x2, starting transfers between devices, per_device(): arrived = [lax.ppermute(send_lead, 'row', sent(rows, 1))]  7 us
    pallas_call x4, Pallas kernels, finish(): pl.pallas_call(body, out_shape=out_shape, in_specs=[pl.BlockSpec(memory_s...  6.62 us
    ppermute x4, waiting for transfers between devices, add_over(): lax.ppermute(values, name, [(r, r ^ step) for r in range(size)])  6.09 us
  transfers between devices with their start and end apart: 19, of which 11 were waited for; matrix products, arithmetic and copies ran while one was open for 2% of the time, Pallas kernels for 20%

profile of v10, /device:TPU:0, one launch (start us, length us, event | category | flops | bytes accessed | tf_op | source)
XLA Modules:
  0.0 128.8 jit_solution(2468054539414744829)
XLA Ops:
  1.4 5.1 %collective-permute-start.3 = (s32[16]{0:T(128)S(1)}, s32[16]{0:T(128)S(1)}, u32[]{:S(2)}, u32[]{:S(2)}) collective-permute-start(s32[16]{0:T(128)S(1)} %bitcast_add_fusion), channel_id=1, source_target_pairs={{12,0},{8,4},{4,8},{0,12},{13,1},{9,5},{5,9},{1,13},{14,2},{10,6},... | collective-permute-start | bytes 200 | tf_op jit(solution)/shard_map/ppermute | solution.py:417
  6.4 2.9 %collective-permute-start = (s32[16]{0:T(128)S(1)}, s32[16]{0:T(128)S(1)}, u32[]{:S(2)}, u32[]{:S(2)}) collective-permute-start(s32[16]{0:T(128)S(1)} %bitcast_add_fusion), channel_id=1, source_target_pairs={{4,0},{12,4},{0,8},{8,12},{5,1},{13,5},{1,9},{9,13},{6,2},{14,6},{... | collective-permute-start | bytes 200 | tf_op jit(solution)/shard_map/ppermute | solution.py:415
  9.5 1.2 collective-permute-done.refs_0_
  10.7 2.4 %gather_first.2 = (s32[5]{0:T(128)S(1)}, bf16[4,256,256]{2,1,0:T(8,128)(2,1)S(1)}) custom-call(s32[2]{0:T(128)S(1)} %pad_add_fusion.place_ref, s32[16]{0:T(128)S(1)} %collective-permute-done.refs_0_, bf16[16,256,256]{2,1,0:T(8,128)(2,1)} %refs_2_.4), custom_call_target="tpu_custom_call" | custom-call | bytes 1048576 | tf_op jit(solution)/shard_map/gather_first/pallas_call | solution.py:115
  13.0 0.9 collective-permute-start.1
  14.3 2.7 %gather_first.3 = (s32[10]{0:T(128)S(1)}, bf16[4,256,256]{2,1,0:T(8,128)(2,1)S(1)}, bf16[2,256,256]{2,1,0:T(8,128)(2,1)S(1)}, bf16[2,256,256]{2,1,0:T(8,128)(2,1)S(1)}) custom-call(s32[2]{0:T(128)S(1)} %pad_add_fusion.place_ref, s32[16]{0:T(128)S(1)} %collective-permute-done.2.refs_0_, s32[16]{0:T(128)S(1)} %collective-permute-done.3.refs_1_, ...), custom_call_target="tpu_custom_call" | custom-call | bytes 2097152 | tf_op jit(solution)/shard_map/gather_first/pallas_call | solution.py:115
  17.0 3.9 %collective-permute-start.5 = (bf16[2,256,256]{2,1,0:T(8,128)(2,1)S(1)}, bf16[2,256,256]{2,1,0:T(8,128)(2,1)S(1)}, u32[]{:S(2)}, u32[]{:S(2)}) collective-permute-start(bf16[2,256,256]{2,1,0:T(8,128)(2,1)S(1)} %get-tuple-element.48), channel_id=1, source_target_pairs={{0,12},{4,8},{8,4},{12,0},{1,13},{5,9},{9,5},{13,1},{2,14},{6,10},... | collective-permute-start | bytes 786440 | tf_op jit(solution)/shard_map/ppermute | solution.py:497
  21.7 7.7 %prepare.2 = (f32[8,256,256]{2,1,0:T(8,128)S(1)}, f32[8,256,256]{2,1,0:T(8,128)S(1)}, f32[8,256,256]{2,1,0:T(8,128)S(1)}, bf16[8,256,256]{2,1,0:T(8,128)(2,1)S(1)}, bf16[8,256,256]{2,1,0:T(8,128)(2,1)S(1)}) custom-call(s32[8]{0:T(128)S(1)} %get-tuple-element.69.own_ref.at_ref, s32[8]{0:T(128)S(1)} %get-tuple-element.69.own_ref.at_ref, ...), custom_call_target="tpu_custom_call" | custom-call | flops 805306368 | bytes 12582912 | tf_op jit(solution)/shard_map/prepare/pallas_call | solution.py:245
  29.7 6.5 %collective-permute-done.5.refs_2_ = bf16[2,256,256]{2,1,0:T(8,128)(2,1)S(1)} collective-permute-done((bf16[2,256,256]{2,1,0:T(8,128)(2,1)S(1)}, bf16[2,256,256]{2,1,0:T(8,128)(2,1)S(1)}, u32[]{:S(2)}, u32[]{:S(2)}) %collective-permute-start.5) | collective-permute-done | bytes 262176 | tf_op jit(solution)/shard_map/ppermute | solution.py:497
  36.2 9.7 %collective-permute-done.1.refs_0_ = bf16[4,256,256]{2,1,0:T(8,128)(2,1)S(1)} collective-permute-done((bf16[4,256,256]{2,1,0:T(8,128)(2,1)S(1)}, bf16[4,256,256]{2,1,0:T(8,128)(2,1)S(1)}, u32[]{:S(2)}, u32[]{:S(2)}) %collective-permute-start.1) | collective-permute-done | bytes 524320 | tf_op jit(solution)/shard_map/ppermute | solution.py:490
  45.9 1.4 %finish.4.refs_0_ = bf16[6,256,256]{2,1,0:T(8,128)(2,1)S(1)} custom-call(s32[24]{0:T(128)S(1)} %pad_add_fusion.2.number_ref, f32[8]{0:T(128)S(1)} %fusion.7.scale_ref, f32[8,256,256]{2,1,0:T(8,128)S(1)} %get-tuple-element.40.local_ref, f32[8,256,256]{2,1,0:T(8,128)S(1)} %get-tuple-element.41.rest_ref, f32[8,256,256]{2,1,0:T(8,128)S(1)} %get-tuple-element.42.recip_ref, ...), custom_call_target="tpu_custom_call" | custom-call | flops 402653184 | bytes 7077888 | tf_op jit(solution)/shard_map/finish/pallas_call | solution.py:328
  47.4 1.5 %collective-permute-start.6 = (bf16[2,256,256]{2,1,0:T(8,128)(2,1)S(1)}, bf16[2,256,256]{2,1,0:T(8,128)(2,1)S(1)}, u32[]{:S(2)}, u32[]{:S(2)}) collective-permute-start(bf16[2,256,256]{2,1,0:T(8,128)(2,1)S(1)} %get-tuple-element.50), channel_id=1, source_target_pairs={{0,12},{4,8},{8,4},{12,0},{1,13},{5,9},{9,5},{13,1},{2,14},{6,10},... | collective-permute-start | bytes 786440 | tf_op jit(solution)/shard_map/ppermute | solution.py:497
  49.0 9.1 %collective-permute-done.6.refs_3_ = bf16[2,256,256]{2,1,0:T(8,128)(2,1)S(1)} collective-permute-done((bf16[2,256,256]{2,1,0:T(8,128)(2,1)S(1)}, bf16[2,256,256]{2,1,0:T(8,128)(2,1)S(1)}, u32[]{:S(2)}, u32[]{:S(2)}) %collective-permute-start.6) | collective-permute-done | bytes 262176 | tf_op jit(solution)/shard_map/ppermute | solution.py:497
  58.0 1.0 finish.5.refs_2_
  59.2 1.5 %collective-permute-done.8.refs_3_ = bf16[2,256,256]{2,1,0:T(8,128)(2,1)S(1)} collective-permute-done((bf16[2,256,256]{2,1,0:T(8,128)(2,1)S(1)}, bf16[2,256,256]{2,1,0:T(8,128)(2,1)S(1)}, u32[]{:S(2)}, u32[]{:S(2)}) %collective-permute-start.8) | collective-permute-done | bytes 262176 | tf_op jit(solution)/shard_map/ppermute | solution.py:512
  61.4 6.1 %collective-permute-start.9 = (bf16[4,256,256]{2,1,0:T(8,128)(2,1)S(1)}, bf16[4,256,256]{2,1,0:T(8,128)(2,1)S(1)}, u32[]{:S(2)}, u32[]{:S(2)}) collective-permute-start(bf16[4,256,256]{2,1,0:T(8,128)(2,1)S(1)} %gather_again.2), channel_id=1, source_target_pairs={{0,4},{4,12},{8,0},{12,8},{1,5},{5,13},{9,1},{13,9},{2,6},{6,14},{... | collective-permute-start | bytes 1572872 | tf_op jit(solution)/shard_map/ppermute | solution.py:490
  67.5 0.8 gather_again.3
  68.5 2.4 %collective-permute-start.11 = (bf16[2,256,256]{2,1,0:T(8,128)(2,1)S(1)}, bf16[2,256,256]{2,1,0:T(8,128)(2,1)S(1)}, u32[]{:S(2)}, u32[]{:S(2)}) collective-permute-start(bf16[2,256,256]{2,1,0:T(8,128)(2,1)S(1)} %get-tuple-element.57), channel_id=1, source_target_pairs={{0,12},{4,8},{8,4},{12,0},{1,13},{5,9},{9,5},{13,1},{2,14},{6,10},... | collective-permute-start | bytes 786440 | tf_op jit(solution)/shard_map/ppermute | solution.py:497
  71.0 1.5 %collective-permute-start.13 = (bf16[2,256,256]{2,1,0:T(8,128)(2,1)S(1)}, bf16[2,256,256]{2,1,0:T(8,128)(2,1)S(1)}, u32[]{:S(2)}, u32[]{:S(2)}) collective-permute-start(bf16[2,256,256]{2,1,0:T(8,128)(2,1)S(1)} %get-tuple-element.60), channel_id=1, source_target_pairs={{0,12},{4,8},{8,4},{12,0},{1,13},{5,9},{9,5},{13,1},{2,14},{6,10},... | collective-permute-start | bytes 786440 | tf_op jit(solution)/shard_map/ppermute | solution.py:497
  72.6 6.9 %prepare.3 = (f32[8,256,256]{2,1,0:T(8,128)S(1)}, f32[8,256,256]{2,1,0:T(8,128)S(1)}, f32[8,256,256]{2,1,0:T(8,128)S(1)}, bf16[8,256,256]{2,1,0:T(8,128)(2,1)S(1)}, bf16[8,256,256]{2,1,0:T(8,128)(2,1)S(1)}) custom-call(s32[8]{0:T(128)S(1)} %get-tuple-element.69.own_ref.at_ref, s32[8]{0:T(128)S(1)} %iota.29.at_ref, s32[8]{0:T(128)S(1)} %get-tuple-element.71.home_ref, ...), custom_call_target="tpu_custom_call" | custom-call | flops 805306368 | bytes 12582912 | tf_op jit(solution)/shard_map/prepare/pallas_call | solution.py:245
  79.5 19.2 %collective-permute-done.11.refs_2_ = bf16[2,256,256]{2,1,0:T(8,128)(2,1)S(1)} collective-permute-done((bf16[2,256,256]{2,1,0:T(8,128)(2,1)S(1)}, bf16[2,256,256]{2,1,0:T(8,128)(2,1)S(1)}, u32[]{:S(2)}, u32[]{:S(2)}) %collective-permute-start.11) | collective-permute-done | bytes 262176 | tf_op jit(solution)/shard_map/ppermute | solution.py:497
  98.7 2.7 %finish.6 = (bf16[6,256,256]{2,1,0:T(8,128)(2,1)S(1)}, f32[1,64]{1,0:T(1,128)S(1)}) custom-call(s32[24]{0:T(128)S(1)} %pad_add_fusion.2.number_ref, f32[8]{0:T(128)S(1)} %fusion.7.scale_ref, f32[8,256,256]{2,1,0:T(8,128)S(1)} %get-tuple-element.51.local_ref, f32[8,256,256]{2,1,0:T(8,128)S(1)} %get-tuple-element.52.rest_ref, ...), custom_call_target="tpu_custom_call" | custom-call | flops 402653184 | bytes 7077888 | tf_op jit(solution)/shard_map/finish/pallas_call | solution.py:328
  101.4 2.1 %collective-permute-done.13.refs_3_ = bf16[2,256,256]{2,1,0:T(8,128)(2,1)S(1)} collective-permute-done((bf16[2,256,256]{2,1,0:T(8,128)(2,1)S(1)}, bf16[2,256,256]{2,1,0:T(8,128)(2,1)S(1)}, u32[]{:S(2)}, u32[]{:S(2)}) %collective-permute-start.13) | collective-permute-done | bytes 262176 | tf_op jit(solution)/shard_map/ppermute | solution.py:497
  103.5 1.5 %finish.7 = (bf16[2,256,256]{2,1,0:T(8,128)(2,1)S(1)}, f32[1,64]{1,0:T(1,128)S(1)}) custom-call(s32[24]{0:T(128)S(1)} %pad_add_fusion.2.number_ref, f32[8]{0:T(128)S(1)} %fusion.7.scale_ref, f32[8,256,256]{2,1,0:T(8,128)S(1)} %get-tuple-element.51.local_ref, f32[8,256,256]{2,1,0:T(8,128)S(1)} %get-tuple-element.52.rest_ref, ...), custom_call_target="tpu_custom_call" | custom-call | flops 134217728 | bytes 2359296 | tf_op jit(solution)/shard_map/finish/pallas_call | solution.py:328
  105.0 1.2 collective-permute-done.15
  106.2 1.5 %collective-permute-start.16 = (f32[64]{0:T(128)S(1)}, f32[64]{0:T(128)S(1)}, u32[]{:S(2)}, u32[]{:S(2)}) collective-permute-start(f32[64]{0:T(128)S(1)} %add.110), channel_id=1, source_target_pairs={{0,2},{2,0},{1,3},{3,1},{4,6},{6,4},{5,7},{7,5},{8,10},{10,8},{9,1... | collective-permute-start | bytes 776 | tf_op jit(solution)/shard_map/ppermute | solution.py:380
  107.6 2.1 %collective-permute-done.16 = f32[64]{0:T(128)S(1)} collective-permute-done((f32[64]{0:T(128)S(1)}, f32[64]{0:T(128)S(1)}, u32[]{:S(2)}, u32[]{:S(2)}) %collective-permute-start.16) | collective-permute-done | bytes 288 | tf_op jit(solution)/shard_map/ppermute | solution.py:380
  109.7 10.6 %collective-permute-start.17 = (f32[64]{0:T(128)S(1)}, f32[64]{0:T(128)S(1)}, u32[]{:S(2)}, u32[]{:S(2)}) collective-permute-start(f32[64]{0:T(128)S(1)} %add.111), channel_id=1, source_target_pairs={{0,4},{4,0},{8,12},{12,8},{1,5},{5,1},{9,13},{13,9},{2,6},{6,2},{1... | collective-permute-start | bytes 776 | tf_op jit(solution)/shard_map/ppermute | solution.py:380
  120.4 1.4 %collective-permute-done.17 = f32[64]{0:T(128)S(1)} collective-permute-done((f32[64]{0:T(128)S(1)}, f32[64]{0:T(128)S(1)}, u32[]{:S(2)}, u32[]{:S(2)}) %collective-permute-start.17) | collective-permute-done | bytes 288 | tf_op jit(solution)/shard_map/ppermute | solution.py:380
  121.8 2.9 %collective-permute-start.18 = (f32[64]{0:T(128)S(1)}, f32[64]{0:T(128)S(1)}, u32[]{:S(2)}, u32[]{:S(2)}) collective-permute-start(f32[64]{0:T(128)S(1)} %add.112), channel_id=1, source_target_pairs={{0,8},{4,12},{8,0},{12,4},{1,9},{5,13},{9,1},{13,5},{2,10},{6,14},... | collective-permute-start | bytes 776 | tf_op jit(solution)/shard_map/ppermute | solution.py:380
  124.8 1.5 %collective-permute-done.18 = f32[64]{0:T(128)S(1)} collective-permute-done((f32[64]{0:T(128)S(1)}, f32[64]{0:T(128)S(1)}, u32[]{:S(2)}, u32[]{:S(2)}) %collective-permute-start.18) | collective-permute-done | bytes 288 | tf_op jit(solution)/shard_map/ppermute | solution.py:380
  126.8 2.0 %put_in_slots.1 = bf16[16,256,256]{2,1,0:T(8,128)(2,1)} custom-call(s32[16]{0:T(128)S(1)} %pad_add_fusion.1.slot_ref, bf16[6,256,256]{2,1,0:T(8,128)(2,1)S(1)} %get-tuple-element.59.refs_0_, bf16[6,256,256]{2,1,0:T(8,128)(2,1)S(1)} %collective-permute-done.12.refs_1_, bf16[2,256,256]{2,1,0:T(8,128)(2,1)S(1)} %get-tuple-element.61.refs_2_, ...), custom_call_target="tpu_custom_call" | custom-call | bytes 4194304 | tf_op jit(solution)/shard_map/put_in_slots/pallas_call | solution.py:361
  (64 shorter events, 4.2 us)
Async XLA Ops:
  0.6 13.3 %copy-start.7 = (s32[16,1]{0,1:T(1,128)S(1)}, s32[16,1]{0,1:T(1,128)}, u32[]{:S(2)}) copy-start(s32[16,1]{0,1:T(1,128)} %param.23) | copy-start | bytes 196
  1.4 12.5 %collective-permute-start.3 = (s32[16]{0:T(128)S(1)}, s32[16]{0:T(128)S(1)}, u32[]{:S(2)}, u32[]{:S(2)}) collective-permute-start(s32[16]{0:T(128)S(1)} %bitcast_add_fusion), channel_id=1, source_target_pairs={{12,0},{8,4},{4,8},{0,12},{13,1},{9,5},{5,9},{1,13},{14,2},{10,6},... | collective-permute-start | bytes 200 | tf_op jit(solution)/shard_map/ppermute | solution.py:417
  6.4 7.5 %collective-permute-start.2 = (s32[16]{0:T(128)S(1)}, s32[16]{0:T(128)S(1)}, u32[]{:S(2)}, u32[]{:S(2)}) collective-permute-start(s32[16]{0:T(128)S(1)} %bitcast_add_fusion), channel_id=1, source_target_pairs={{8,0},{0,4},{12,8},{4,12},{9,1},{1,5},{13,9},{5,13},{10,2},{2,6},{... | collective-permute-start | bytes 200 | tf_op jit(solution)/shard_map/ppermute | solution.py:417
  6.4 4.2 %collective-permute-start = (s32[16]{0:T(128)S(1)}, s32[16]{0:T(128)S(1)}, u32[]{:S(2)}, u32[]{:S(2)}) collective-permute-start(s32[16]{0:T(128)S(1)} %bitcast_add_fusion), channel_id=1, source_target_pairs={{4,0},{12,4},{0,8},{8,12},{5,1},{13,5},{1,9},{9,13},{6,2},{14,6},{... | collective-permute-start | bytes 200 | tf_op jit(solution)/shard_map/ppermute | solution.py:415
  9.5 11.5 %copy-start.4 = (s32[16,1]{0,1:T(1,128)S(1)}, s32[16,1]{0,1:T(1,128)}, u32[]{:S(2)}) copy-start(s32[16,1]{0,1:T(1,128)} %param.24) | copy-start | bytes 196
  9.5 11.5 %copy-start.5 = (s32[16]{0:T(128)S(1)}, s32[16]{0:T(128)}, u32[]{:S(2)}) copy-start(s32[16]{0:T(128)} %param.19) | copy-start | bytes 196
  9.5 11.5 %copy-start.6 = (s32[16]{0:T(128)S(1)}, s32[16]{0:T(128)}, u32[]{:S(2)}) copy-start(s32[16]{0:T(128)} %param.18) | copy-start | bytes 196
  9.5 12.0 %copy-start.3 = (f32[64]{0:T(128)S(1)}, f32[64]{0:T(128)}, u32[]{:S(2)}) copy-start(f32[64]{0:T(128)} %param.17) | copy-start | bytes 772
  9.5 12.2 %copy-start.8 = (bf16[16,1]{0,1:T(2,128)(2,1)S(1)}, bf16[16,1]{0,1:T(2,128)(2,1)}, u32[]{:S(2)}) copy-start(bf16[16,1]{0,1:T(2,128)(2,1)} %param.25) | copy-start | bytes 100
  9.5 12.2 %copy-start = (s32[16,11]{1,0:T(8,128)S(1)}, s32[16,11]{1,0:T(8,128)}, u32[]{:S(2)}) copy-start(s32[16,11]{1,0:T(8,128)} %slot_ref.3) | copy-start | bytes 2116
  9.5 12.2 %copy-start.1 = (bf16[16,11]{1,0:T(8,128)(2,1)S(1)}, bf16[16,11]{1,0:T(8,128)(2,1)}, u32[]{:S(2)}) copy-start(bf16[16,11]{1,0:T(8,128)(2,1)} %weight_ref.3) | copy-start | bytes 1060
  9.5 12.2 %copy-start.2 = (s32[16]{0:T(128)S(1)}, s32[16]{0:T(128)}, u32[]{:S(2)}) copy-start(s32[16]{0:T(128)} %count_ref.3) | copy-start | bytes 196
  13.0 32.9 %collective-permute-start.1 = (bf16[4,256,256]{2,1,0:T(8,128)(2,1)S(1)}, bf16[4,256,256]{2,1,0:T(8,128)(2,1)S(1)}, u32[]{:S(2)}, u32[]{:S(2)}) collective-permute-start(bf16[4,256,256]{2,1,0:T(8,128)(2,1)S(1)} %get-tuple-element.44), channel_id=1, source_target_pairs={{0,4},{4,12},{8,0},{12,8},{1,5},{5,13},{9,1},{13,9},{2,6},{6,14},{... | collective-permute-start | bytes 1572872 | tf_op jit(solution)/shard_map/ppermute | solution.py:490
  17.0 19.2 %collective-permute-start.5 = (bf16[2,256,256]{2,1,0:T(8,128)(2,1)S(1)}, bf16[2,256,256]{2,1,0:T(8,128)(2,1)S(1)}, u32[]{:S(2)}, u32[]{:S(2)}) collective-permute-start(bf16[2,256,256]{2,1,0:T(8,128)(2,1)S(1)} %get-tuple-element.48), channel_id=1, source_target_pairs={{0,12},{4,8},{8,4},{12,0},{1,13},{5,9},{9,5},{13,1},{2,14},{6,10},... | collective-permute-start | bytes 786440 | tf_op jit(solution)/shard_map/ppermute | solution.py:497
  20.9 25.0 %collective-permute-start.4 = (bf16[4,256,256]{2,1,0:T(8,128)(2,1)S(1)}, bf16[4,256,256]{2,1,0:T(8,128)(2,1)S(1)}, u32[]{:S(2)}, u32[]{:S(2)}) collective-permute-start(bf16[4,256,256]{2,1,0:T(8,128)(2,1)S(1)} %get-tuple-element.47), channel_id=1, source_target_pairs={{0,8},{4,0},{8,12},{12,4},{1,9},{5,1},{9,13},{13,5},{2,10},{6,2},{... | collective-permute-start | bytes 1572872 | tf_op jit(solution)/shard_map/ppermute | solution.py:497
  47.4 13.3 %collective-permute-start.7 = (bf16[6,256,256]{2,1,0:T(8,128)(2,1)S(1)}, bf16[6,256,256]{2,1,0:T(8,128)(2,1)S(1)}, u32[]{:S(2)}, u32[]{:S(2)}) collective-permute-start(bf16[6,256,256]{2,1,0:T(8,128)(2,1)S(1)} %finish.4.refs_0_), channel_id=1, source_target_pairs={{0,1},{1,0},{2,3},{3,2},{4,5},{5,4},{6,7},{7,6},{8,9},{9,8},{10,11... | collective-permute-start | bytes 2359304 | tf_op jit(solution)/shard_map/ppermute | solution.py:508
  47.4 10.6 %collective-permute-start.6 = (bf16[2,256,256]{2,1,0:T(8,128)(2,1)S(1)}, bf16[2,256,256]{2,1,0:T(8,128)(2,1)S(1)}, u32[]{:S(2)}, u32[]{:S(2)}) collective-permute-start(bf16[2,256,256]{2,1,0:T(8,128)(2,1)S(1)} %get-tuple-element.50), channel_id=1, source_target_pairs={{0,12},{4,8},{8,4},{12,0},{1,13},{5,9},{9,5},{13,1},{2,14},{6,10},... | collective-permute-start | bytes 786440 | tf_op jit(solution)/shard_map/ppermute | solution.py:497
  59.1 1.6 %collective-permute-start.8 = (bf16[2,256,256]{2,1,0:T(8,128)(2,1)S(1)}, bf16[2,256,256]{2,1,0:T(8,128)(2,1)S(1)}, u32[]{:S(2)}, u32[]{:S(2)}) collective-permute-start(bf16[2,256,256]{2,1,0:T(8,128)(2,1)S(1)} %finish.5.refs_2_), channel_id=1, source_target_pairs={{0,1},{1,0},{2,3},{3,2},{4,5},{5,4},{6,7},{7,6},{8,9},{9,8},{10,11... | collective-permute-start | bytes 786440 | tf_op jit(solution)/shard_map/ppermute | solution.py:512
  61.4 37.3 %collective-permute-start.9 = (bf16[4,256,256]{2,1,0:T(8,128)(2,1)S(1)}, bf16[4,256,256]{2,1,0:T(8,128)(2,1)S(1)}, u32[]{:S(2)}, u32[]{:S(2)}) collective-permute-start(bf16[4,256,256]{2,1,0:T(8,128)(2,1)S(1)} %gather_again.2), channel_id=1, source_target_pairs={{0,4},{4,12},{8,0},{12,8},{1,5},{5,13},{9,1},{13,9},{2,6},{6,14},{... | collective-permute-start | bytes 1572872 | tf_op jit(solution)/shard_map/ppermute | solution.py:490
  68.3 30.4 %collective-permute-start.10 = (bf16[4,256,256]{2,1,0:T(8,128)(2,1)S(1)}, bf16[4,256,256]{2,1,0:T(8,128)(2,1)S(1)}, u32[]{:S(2)}, u32[]{:S(2)}) collective-permute-start(bf16[4,256,256]{2,1,0:T(8,128)(2,1)S(1)} %get-tuple-element.56), channel_id=1, source_target_pairs={{0,8},{4,0},{8,12},{12,4},{1,9},{5,1},{9,13},{13,5},{2,10},{6,2},{... | collective-permute-start | bytes 1572872 | tf_op jit(solution)/shard_map/ppermute | solution.py:497
  68.5 30.2 %collective-permute-start.11 = (bf16[2,256,256]{2,1,0:T(8,128)(2,1)S(1)}, bf16[2,256,256]{2,1,0:T(8,128)(2,1)S(1)}, u32[]{:S(2)}, u32[]{:S(2)}) collective-permute-start(bf16[2,256,256]{2,1,0:T(8,128)(2,1)S(1)} %get-tuple-element.57), channel_id=1, source_target_pairs={{0,12},{4,8},{8,4},{12,0},{1,13},{5,9},{9,5},{13,1},{2,14},{6,10},... | collective-permute-start | bytes 786440 | tf_op jit(solution)/shard_map/ppermute | solution.py:497
  71.0 32.5 %collective-permute-start.13 = (bf16[2,256,256]{2,1,0:T(8,128)(2,1)S(1)}, bf16[2,256,256]{2,1,0:T(8,128)(2,1)S(1)}, u32[]{:S(2)}, u32[]{:S(2)}) collective-permute-start(bf16[2,256,256]{2,1,0:T(8,128)(2,1)S(1)} %get-tuple-element.60), channel_id=1, source_target_pairs={{0,12},{4,8},{8,4},{12,0},{1,13},{5,9},{9,5},{13,1},{2,14},{6,10},... | collective-permute-start | bytes 786440 | tf_op jit(solution)/shard_map/ppermute | solution.py:497
  101.4 25.5 %collective-permute-start.12 = (bf16[6,256,256]{2,1,0:T(8,128)(2,1)S(1)}, bf16[6,256,256]{2,1,0:T(8,128)(2,1)S(1)}, u32[]{:S(2)}, u32[]{:S(2)}) collective-permute-start(bf16[6,256,256]{2,1,0:T(8,128)(2,1)S(1)} %get-tuple-element.59.refs_0_), channel_id=1, source_target_pairs={{0,1},{1,0},{2,3},{3,2},{4,5},{5,4},{6,7},{7,6},{8,9},{9,8},{10,11... | collective-permute-start | bytes 2359304 | tf_op jit(solution)/shard_map/ppermute | solution.py:508
  105.0 1.2 collective-permute-start.15
  106.2 3.6 %collective-permute-start.16 = (f32[64]{0:T(128)S(1)}, f32[64]{0:T(128)S(1)}, u32[]{:S(2)}, u32[]{:S(2)}) collective-permute-start(f32[64]{0:T(128)S(1)} %add.110), channel_id=1, source_target_pairs={{0,2},{2,0},{1,3},{3,1},{4,6},{6,4},{5,7},{7,5},{8,10},{10,8},{9,1... | collective-permute-start | bytes 776 | tf_op jit(solution)/shard_map/ppermute | solution.py:380
  109.7 12.1 %collective-permute-start.17 = (f32[64]{0:T(128)S(1)}, f32[64]{0:T(128)S(1)}, u32[]{:S(2)}, u32[]{:S(2)}) collective-permute-start(f32[64]{0:T(128)S(1)} %add.111), channel_id=1, source_target_pairs={{0,4},{4,0},{8,12},{12,8},{1,5},{5,1},{9,13},{13,9},{2,6},{6,2},{1... | collective-permute-start | bytes 776 | tf_op jit(solution)/shard_map/ppermute | solution.py:380
  120.4 6.4 %collective-permute-start.14 = (bf16[2,256,256]{2,1,0:T(8,128)(2,1)S(1)}, bf16[2,256,256]{2,1,0:T(8,128)(2,1)S(1)}, u32[]{:S(2)}, u32[]{:S(2)}) collective-permute-start(bf16[2,256,256]{2,1,0:T(8,128)(2,1)S(1)} %get-tuple-element.61.refs_2_), channel_id=1, source_target_pairs={{0,1},{1,0},{2,3},{3,2},{4,5},{5,4},{6,7},{7,6},{8,9},{9,8},{10,11... | collective-permute-start | bytes 786440 | tf_op jit(solution)/shard_map/ppermute | solution.py:512
  121.8 4.5 %collective-permute-start.18 = (f32[64]{0:T(128)S(1)}, f32[64]{0:T(128)S(1)}, u32[]{:S(2)}, u32[]{:S(2)}) collective-permute-start(f32[64]{0:T(128)S(1)} %add.112), channel_id=1, source_target_pairs={{0,8},{4,12},{8,0},{12,4},{1,9},{5,13},{9,1},{13,5},{2,10},{6,14},... | collective-permute-start | bytes 776 | tf_op jit(solution)/shard_map/ppermute | solution.py:380

commit v11 on v10

--- a/solution.py
+++ b/solution.py
@@ -127,29 +127,29 @@
     )(place, *requests, in_hbm(amplitudes))
 
 
-def gather_again(asked, where, stores, parts, cap):
+def gather_again(spots, stores, parts, cap):
     domain = stores[0].shape[1]
     steps = sorted({step for step, _, _ in parts})
     blocks = sum(size for _, _, size in parts)
 
-    def body(asked_ref, where_ref, *refs):
+    def body(spot_ref, *refs):
         sources = laid(refs[: len(stores)])
         outs = refs[len(stores) :]
         for m, (step, begin, size) in enumerate(parts):
             for k in range(size):
-                spot = where_ref[asked_ref[steps.index(step) * (cap + 1) + begin + k]]
+                spot = spot_ref[steps.index(step) * (cap + 1) + begin + k]
                 fetch(sources, spot, outs[m].at[k])
 
     return pl.pallas_call(
         body,
         out_shape=[VMEM((size, domain, domain), jnp.bfloat16) for _, _, size in parts],
-        in_specs=[pl.BlockSpec(memory_space=SMEM)] * 2
+        in_specs=[pl.BlockSpec(memory_space=SMEM)]
         + [pl.BlockSpec(memory_space=VMEM)] * len(stores),
         out_specs=[pl.BlockSpec(memory_space=VMEM)] * len(parts),
         cost_estimate=cost(0, blocks * domain * domain * 4),
         compiler_params=limits(8),
         name="gather_again",
-    )(asked, where, *stores)
+    )(spots, *stores)
 
 
 def prepare(
@@ -298,7 +298,7 @@
             density = jnp.zeros((1, occ_count), jnp.float32)
         for n in range(count):
             i = start + n
-            coupled = local_ref[i] + scale_ref[i] * hold[n].astype(jnp.float32)
+            coupled = local_ref[i] + scale_ref[i : i + 1, :] * hold[n].astype(jnp.float32)
             over = over_ref[i]
             projected = jnp.dot(
                 over, coupled.astype(jnp.bfloat16), preferred_element_type=jnp.float32
@@ -328,8 +328,8 @@
     return pl.pallas_call(
         body,
         out_shape=out_shape,
-        in_specs=[pl.BlockSpec(memory_space=SMEM)] * 2
-        + [pl.BlockSpec(memory_space=VMEM)] * 4
+        in_specs=[pl.BlockSpec(memory_space=SMEM)]
+        + [pl.BlockSpec(memory_space=VMEM)] * 5
         + [pl.BlockSpec(memory_space=VMEM)] * len(arrived),
         out_specs=[pl.BlockSpec(memory_space=VMEM)] * len(out_shape),
         scratch_shapes=[VMEM((count, domain, domain), jnp.bfloat16)],
@@ -339,9 +339,10 @@
     )(numbers, scale, *prepared, *[a for _, a in arrived])
 
 
-def put_in_slots(slots, stores):
+def put_in_slots(slots, stores, total, whole=None):
     domain = stores[0].shape[1]
-    total = slots.shape[0]
+    blocks = sum(s.shape[0] for s in stores)
+    given = [] if whole is None else [whole]
 
     def body(slot_ref, *refs):
         sources = refs[: len(stores)]
@@ -362,23 +363,26 @@
         body,
         out_shape=jax.ShapeDtypeStruct((total, domain, domain), jnp.bfloat16),
         in_specs=[pl.BlockSpec(memory_space=SMEM)]
-        + [pl.BlockSpec(memory_space=VMEM)] * len(stores),
+        + [pl.BlockSpec(memory_space=VMEM)] * len(stores)
+        + [pl.BlockSpec(memory_space=ANY)] * len(given),
         out_specs=pl.BlockSpec(memory_space=ANY),
-        scratch_shapes=[pltpu.SemaphoreType.DMA((total,))],
-        cost_estimate=cost(0, total * domain * domain * 4),
+        scratch_shapes=[pltpu.SemaphoreType.DMA((blocks,))],
+        input_output_aliases={1 + len(stores): 0} if given else {},
+        cost_estimate=cost(0, blocks * domain * domain * 4),
         compiler_params=limits(8),
         name="put_in_slots",
-    )(slots, *stores)
+    )(slots, *stores, *given)
 
 
 def add_over(values, name):
     size = lax.axis_size(name)
     if size & (size - 1):
         return lax.psum(values, name)
-    step = 1
-    while step < size:
+    steps = [1 << bit for bit in range(size.bit_length() - 1)]
+    if name == "row":
+        steps = [size - 1] + steps[:-1]
+    for step in steps:
         values = values + lax.ppermute(values, name, [(r, r ^ step) for r in range(size)])
-        step *= 2
     return values
 
 
@@ -453,6 +457,7 @@
         return jnp.sum(jnp.where(found, occ_energy[None, :], jnp.float32(0.0)), axis=1)
 
     far_scale = pick(own_pick, far_weight[:, 0].astype(jnp.float32))
+    far_scale = jnp.broadcast_to(far_scale[:, None], (half, domain))
     first = pick(own_pick, first_occ)
     second = pick(own_pick, second_occ)
     shift = energy_of(first) + energy_of(second)
@@ -479,20 +484,25 @@
     near = [near_slot, near_weight]
     columns = [slot_ids, jnp.concatenate([own, other])]
     ats = [own, jnp.arange(half, dtype=jnp.int32)]
-    slots = jnp.concatenate([own[:early], other[:early], own[early:], other[early:]])
+    slots = jnp.concatenate([other[:early], own[early:], other[early:]])
+
+    def spots_of(slots_asked):
+        found = slots_asked[:, None] == slot_ids[None, :]
+        return jnp.sum(jnp.where(found, local_spots[1][None, :], 0), axis=1)
+
     stores = [amplitudes]
     whole = [amplitudes]
     for sweep in range(ITERS):
         last = sweep == ITERS - 1
         again = min(sweep, 1)
         if sweep > 0:
-            (send_lead,) = gather_again(asked_lead, local_spots[1], stores, lead, cap)
+            (send_lead,) = gather_again(spots_of(asked_lead), stores, lead, cap)
         arrived = [lax.ppermute(send_lead, "row", sent(rows, 1))]
         if sweep == 0:
             (*requests, _) = lax.optimization_barrier((*requests, send_lead))
             asked, *sends = gather_first(requests, rest, here, amplitudes, rows, cap)
         else:
-            sends = gather_again(asked, local_spots[1], stores, rest, cap)
+            sends = gather_again(spots_of(asked), stores, rest, cap)
         for part, send in zip(rest, sends):
             arrived.append(lax.ppermute(send, "row", sent(rows, part[0])))
         *prepared, at_home = prepare(
@@ -506,6 +516,8 @@
             last,
         )
         given_early = lax.ppermute(done_early[0], "rep", swap)
+        if last:
+            final = put_in_slots(own[:early], [done_early[0]], pairs)
         done_late = finish(
             early, tail, numbers, far_scale, prepared, spots + at_home, occ_count, last
         )
@@ -515,7 +527,7 @@
             jnp.concatenate([done_early[0], done_late[0]], axis=0),
             jnp.concatenate([given_early, given_late], axis=0),
         ]
-    final = put_in_slots(slots, stores)
+    final = put_in_slots(slots, stores[1:], pairs, final)
     occ_sum = (done_early[1] + done_late[1])[0]
     occ_sum = add_over(occ_sum, "rep")
     occ_sum = add_over(occ_sum, "col")

time: 129 us -> 128 us (level)
  starting transfers between devices: 39.5 us -> 37.2 us
    ppermute x4, starting transfers between devices: 15 us -> 12.6 us  [add_over(): lax.ppermute(values, name, [(r, r ^ step) for r in range(size)])]
    pallas_call x1 -> x2, Pallas kernels: 1.98 us -> 3.14 us  [put_in_slots(): pl.pallas_call(body, out_shape=jax.ShapeDtypeStruct((total, domain, domai...]
  transfers between devices with their start and end apart: 19 -> 19, of which waited for: 11 -> 10; matrix products, arithmetic and copies ran while one was open for 2% -> 2% of each run, Pallas kernels for 20% -> 21%
where the time goes in v11:
time: 128 us
  waiting for transfers between devices  55.1 us (43%)
  starting transfers between devices  37.2 us (29%)
  Pallas kernels  30.9 us (24%)
  other arithmetic  3.39 us (3%)
    ppermute x6, waiting for transfers between devices, per_device(): arrived.append(lax.ppermute(send, 'row', sent(rows, part[0])))  36.9 us
    pallas_call x2, Pallas kernels, prepare(): pl.pallas_call(body, grid_spec=pltpu.PrefetchScalarGridSpec(num_scalar_pr...  14.6 us
    ppermute x4, starting transfers between devices, add_over(): lax.ppermute(values, name, [(r, r ^ step) for r in range(size)])  12.6 us
    ppermute x2, waiting for transfers between devices, per_device(): arrived = [lax.ppermute(send_lead, 'row', sent(rows, 1))]  9.72 us
    ppermute x6, starting transfers between devices, per_device(): arrived.append(lax.ppermute(send, 'row', sent(rows, part[0])))  9.37 us
    ppermute x2, starting transfers between devices, per_device(): arrived = [lax.ppermute(send_lead, 'row', sent(rows, 1))]  7 us
    pallas_call x4, Pallas kernels, finish(): pl.pallas_call(body, out_shape=out_shape, in_specs=[pl.BlockSpec(memory_s...  6.58 us
    ppermute x4, waiting for transfers between devices, add_over(): lax.ppermute(values, name, [(r, r ^ step) for r in range(size)])  6.08 us
  transfers between devices with their start and end apart: 19, of which 10 were waited for; matrix products, arithmetic and copies ran while one was open for 2% of the time, Pallas kernels for 21%

profile of v11, /device:TPU:0, one launch (start us, length us, event | category | flops | bytes accessed | tf_op | source)
XLA Modules:
  0.0 127.7 jit_solution(7438191075992982698)
XLA Ops:
  1.4 5.1 %collective-permute-start.3 = (s32[16]{0:T(128)S(1)}, s32[16]{0:T(128)S(1)}, u32[]{:S(2)}, u32[]{:S(2)}) collective-permute-start(s32[16]{0:T(128)S(1)} %bitcast_add_fusion), channel_id=1, source_target_pairs={{12,0},{8,4},{4,8},{0,12},{13,1},{9,5},{5,9},{1,13},{14,2},{10,6},... | collective-permute-start | bytes 200 | tf_op jit(solution)/shard_map/ppermute | solution.py:421
  6.4 2.9 %collective-permute-start = (s32[16]{0:T(128)S(1)}, s32[16]{0:T(128)S(1)}, u32[]{:S(2)}, u32[]{:S(2)}) collective-permute-start(s32[16]{0:T(128)S(1)} %bitcast_add_fusion), channel_id=1, source_target_pairs={{4,0},{12,4},{0,8},{8,12},{5,1},{13,5},{1,9},{9,13},{6,2},{14,6},{... | collective-permute-start | bytes 200 | tf_op jit(solution)/shard_map/ppermute | solution.py:419
  9.5 1.2 collective-permute-done.refs_0_
  10.7 2.4 %gather_first.2 = (s32[5]{0:T(128)S(1)}, bf16[4,256,256]{2,1,0:T(8,128)(2,1)S(1)}) custom-call(s32[2]{0:T(128)S(1)} %pad_add_fusion.place_ref, s32[16]{0:T(128)S(1)} %collective-permute-done.refs_0_, bf16[16,256,256]{2,1,0:T(8,128)(2,1)} %refs_2_.4), custom_call_target="tpu_custom_call" | custom-call | bytes 1048576 | tf_op jit(solution)/shard_map/gather_first/pallas_call | solution.py:115
  13.0 0.9 collective-permute-start.1
  14.3 2.7 %gather_first.3 = (s32[10]{0:T(128)S(1)}, bf16[4,256,256]{2,1,0:T(8,128)(2,1)S(1)}, bf16[2,256,256]{2,1,0:T(8,128)(2,1)S(1)}, bf16[2,256,256]{2,1,0:T(8,128)(2,1)S(1)}) custom-call(s32[2]{0:T(128)S(1)} %pad_add_fusion.place_ref, s32[16]{0:T(128)S(1)} %collective-permute-done.2.refs_0_, s32[16]{0:T(128)S(1)} %collective-permute-done.3.refs_1_, ...), custom_call_target="tpu_custom_call" | custom-call | bytes 2097152 | tf_op jit(solution)/shard_map/gather_first/pallas_call | solution.py:115
  17.0 3.9 %collective-permute-start.5 = (bf16[2,256,256]{2,1,0:T(8,128)(2,1)S(1)}, bf16[2,256,256]{2,1,0:T(8,128)(2,1)S(1)}, u32[]{:S(2)}, u32[]{:S(2)}) collective-permute-start(bf16[2,256,256]{2,1,0:T(8,128)(2,1)S(1)} %get-tuple-element.48), channel_id=1, source_target_pairs={{0,12},{4,8},{8,4},{12,0},{1,13},{5,9},{9,5},{13,1},{2,14},{6,10},... | collective-permute-start | bytes 786440 | tf_op jit(solution)/shard_map/ppermute | solution.py:507
  21.7 7.7 %prepare.2 = (f32[8,256,256]{2,1,0:T(8,128)S(1)}, f32[8,256,256]{2,1,0:T(8,128)S(1)}, f32[8,256,256]{2,1,0:T(8,128)S(1)}, bf16[8,256,256]{2,1,0:T(8,128)(2,1)S(1)}, bf16[8,256,256]{2,1,0:T(8,128)(2,1)S(1)}) custom-call(s32[8]{0:T(128)S(1)} %get-tuple-element.69.own_ref.at_ref, s32[8]{0:T(128)S(1)} %get-tuple-element.69.own_ref.at_ref, ...), custom_call_target="tpu_custom_call" | custom-call | flops 805306368 | bytes 12582912 | tf_op jit(solution)/shard_map/prepare/pallas_call | solution.py:245
  29.7 6.5 %collective-permute-done.5.refs_2_ = bf16[2,256,256]{2,1,0:T(8,128)(2,1)S(1)} collective-permute-done((bf16[2,256,256]{2,1,0:T(8,128)(2,1)S(1)}, bf16[2,256,256]{2,1,0:T(8,128)(2,1)S(1)}, u32[]{:S(2)}, u32[]{:S(2)}) %collective-permute-start.5) | collective-permute-done | bytes 262176 | tf_op jit(solution)/shard_map/ppermute | solution.py:507
  36.2 9.7 %collective-permute-done.1.refs_0_ = bf16[4,256,256]{2,1,0:T(8,128)(2,1)S(1)} collective-permute-done((bf16[4,256,256]{2,1,0:T(8,128)(2,1)S(1)}, bf16[4,256,256]{2,1,0:T(8,128)(2,1)S(1)}, u32[]{:S(2)}, u32[]{:S(2)}) %collective-permute-start.1) | collective-permute-done | bytes 524320 | tf_op jit(solution)/shard_map/ppermute | solution.py:500
  46.0 1.4 %finish.4.refs_0_ = bf16[6,256,256]{2,1,0:T(8,128)(2,1)S(1)} custom-call(s32[24]{0:T(128)S(1)} %pad_add_fusion.2.number_ref, f32[8,256]{1,0:T(8,128)S(1)} %broadcast_in_dim.186.scale_ref, f32[8,256,256]{2,1,0:T(8,128)S(1)} %get-tuple-element.40.local_ref, f32[8,256,256]{2,1,0:T(8,128)S(1)} %get-tuple-element.41.rest_ref, ...), custom_call_target="tpu_custom_call" | custom-call | flops 402653184 | bytes 7077888 | tf_op jit(solution)/shard_map/finish/pallas_call | solution.py:328
  47.5 1.5 %collective-permute-start.6 = (bf16[2,256,256]{2,1,0:T(8,128)(2,1)S(1)}, bf16[2,256,256]{2,1,0:T(8,128)(2,1)S(1)}, u32[]{:S(2)}, u32[]{:S(2)}) collective-permute-start(bf16[2,256,256]{2,1,0:T(8,128)(2,1)S(1)} %get-tuple-element.50), channel_id=1, source_target_pairs={{0,12},{4,8},{8,4},{12,0},{1,13},{5,9},{9,5},{13,1},{2,14},{6,10},... | collective-permute-start | bytes 786440 | tf_op jit(solution)/shard_map/ppermute | solution.py:507
  49.0 9.1 %collective-permute-done.6.refs_3_ = bf16[2,256,256]{2,1,0:T(8,128)(2,1)S(1)} collective-permute-done((bf16[2,256,256]{2,1,0:T(8,128)(2,1)S(1)}, bf16[2,256,256]{2,1,0:T(8,128)(2,1)S(1)}, u32[]{:S(2)}, u32[]{:S(2)}) %collective-permute-start.6) | collective-permute-done | bytes 262176 | tf_op jit(solution)/shard_map/ppermute | solution.py:507
  58.1 1.0 finish.5.refs_2_
  59.6 1.2 collective-permute-done.8.refs_3_
  61.4 6.1 %collective-permute-start.9 = (bf16[4,256,256]{2,1,0:T(8,128)(2,1)S(1)}, bf16[4,256,256]{2,1,0:T(8,128)(2,1)S(1)}, u32[]{:S(2)}, u32[]{:S(2)}) collective-permute-start(bf16[4,256,256]{2,1,0:T(8,128)(2,1)S(1)} %gather_again.2), channel_id=1, source_target_pairs={{0,4},{4,12},{8,0},{12,8},{1,5},{5,13},{9,1},{13,9},{2,6},{6,14},{... | collective-permute-start | bytes 1572872 | tf_op jit(solution)/shard_map/ppermute | solution.py:500
  67.6 0.8 gather_again.3
  68.5 2.4 %collective-permute-start.11 = (bf16[2,256,256]{2,1,0:T(8,128)(2,1)S(1)}, bf16[2,256,256]{2,1,0:T(8,128)(2,1)S(1)}, u32[]{:S(2)}, u32[]{:S(2)}) collective-permute-start(bf16[2,256,256]{2,1,0:T(8,128)(2,1)S(1)} %get-tuple-element.57), channel_id=1, source_target_pairs={{0,12},{4,8},{8,4},{12,0},{1,13},{5,9},{9,5},{13,1},{2,14},{6,10},... | collective-permute-start | bytes 786440 | tf_op jit(solution)/shard_map/ppermute | solution.py:507
  71.0 1.5 %collective-permute-start.13 = (bf16[2,256,256]{2,1,0:T(8,128)(2,1)S(1)}, bf16[2,256,256]{2,1,0:T(8,128)(2,1)S(1)}, u32[]{:S(2)}, u32[]{:S(2)}) collective-permute-start(bf16[2,256,256]{2,1,0:T(8,128)(2,1)S(1)} %get-tuple-element.60), channel_id=1, source_target_pairs={{0,12},{4,8},{8,4},{12,0},{1,13},{5,9},{9,5},{13,1},{2,14},{6,10},... | collective-permute-start | bytes 786440 | tf_op jit(solution)/shard_map/ppermute | solution.py:507
  72.6 6.9 %prepare.3 = (f32[8,256,256]{2,1,0:T(8,128)S(1)}, f32[8,256,256]{2,1,0:T(8,128)S(1)}, f32[8,256,256]{2,1,0:T(8,128)S(1)}, bf16[8,256,256]{2,1,0:T(8,128)(2,1)S(1)}, bf16[8,256,256]{2,1,0:T(8,128)(2,1)S(1)}) custom-call(s32[8]{0:T(128)S(1)} %get-tuple-element.69.own_ref.at_ref, s32[8]{0:T(128)S(1)} %iota.31.at_ref, s32[8]{0:T(128)S(1)} %get-tuple-element.71.home_ref, ...), custom_call_target="tpu_custom_call" | custom-call | flops 805306368 | bytes 12582912 | tf_op jit(solution)/shard_map/prepare/pallas_call | solution.py:245
  79.5 19.2 %collective-permute-done.11.refs_2_ = bf16[2,256,256]{2,1,0:T(8,128)(2,1)S(1)} collective-permute-done((bf16[2,256,256]{2,1,0:T(8,128)(2,1)S(1)}, bf16[2,256,256]{2,1,0:T(8,128)(2,1)S(1)}, u32[]{:S(2)}, u32[]{:S(2)}) %collective-permute-start.11) | collective-permute-done | bytes 262176 | tf_op jit(solution)/shard_map/ppermute | solution.py:507
  98.7 2.6 %finish.6 = (bf16[6,256,256]{2,1,0:T(8,128)(2,1)S(1)}, f32[1,64]{1,0:T(1,128)S(1)}) custom-call(s32[24]{0:T(128)S(1)} %pad_add_fusion.2.number_ref, f32[8,256]{1,0:T(8,128)S(1)} %broadcast_in_dim.186.scale_ref, f32[8,256,256]{2,1,0:T(8,128)S(1)} %get-tuple-element.51.local_ref, f32[8,256,256]{2,1,0:T(8,128)S(1)} %get-tuple-element.52.rest_ref, ...), custom_call_target="tpu_custom_call" | custom-call | flops 402653184 | bytes 7077888 | tf_op jit(solution)/shard_map/finish/pallas_call | solution.py:328
  101.4 2.1 %collective-permute-done.13.refs_3_ = bf16[2,256,256]{2,1,0:T(8,128)(2,1)S(1)} collective-permute-done((bf16[2,256,256]{2,1,0:T(8,128)(2,1)S(1)}, bf16[2,256,256]{2,1,0:T(8,128)(2,1)S(1)}, u32[]{:S(2)}, u32[]{:S(2)}) %collective-permute-start.13) | collective-permute-done | bytes 262176 | tf_op jit(solution)/shard_map/ppermute | solution.py:507
  103.5 1.5 %finish.7 = (bf16[2,256,256]{2,1,0:T(8,128)(2,1)S(1)}, f32[1,64]{1,0:T(1,128)S(1)}) custom-call(s32[24]{0:T(128)S(1)} %pad_add_fusion.2.number_ref, f32[8,256]{1,0:T(8,128)S(1)} %broadcast_in_dim.186.scale_ref, f32[8,256,256]{2,1,0:T(8,128)S(1)} %get-tuple-element.51.local_ref, f32[8,256,256]{2,1,0:T(8,128)S(1)} %get-tuple-element.52.rest_ref, ...), custom_call_target="tpu_custom_call" | custom-call | flops 134217728 | bytes 2359296 | tf_op jit(solution)/shard_map/finish/pallas_call | solution.py:328
  105.0 1.2 collective-permute-done.15
  106.2 1.5 %collective-permute-start.16 = (f32[64]{0:T(128)S(1)}, f32[64]{0:T(128)S(1)}, u32[]{:S(2)}, u32[]{:S(2)}) collective-permute-start(f32[64]{0:T(128)S(1)} %add.135), channel_id=1, source_target_pairs={{0,2},{2,0},{1,3},{3,1},{4,6},{6,4},{5,7},{7,5},{8,10},{10,8},{9,1... | collective-permute-start | bytes 776 | tf_op jit(solution)/shard_map/ppermute | solution.py:385
  107.7 2.1 %collective-permute-done.16 = f32[64]{0:T(128)S(1)} collective-permute-done((f32[64]{0:T(128)S(1)}, f32[64]{0:T(128)S(1)}, u32[]{:S(2)}, u32[]{:S(2)}) %collective-permute-start.16) | collective-permute-done | bytes 288 | tf_op jit(solution)/shard_map/ppermute | solution.py:385
  109.8 2.4 %collective-permute-start.17 = (f32[64]{0:T(128)S(1)}, f32[64]{0:T(128)S(1)}, u32[]{:S(2)}, u32[]{:S(2)}) collective-permute-start(f32[64]{0:T(128)S(1)} %add.136), channel_id=1, source_target_pairs={{0,12},{4,8},{8,4},{12,0},{1,13},{5,9},{9,5},{13,1},{2,14},{6,10},... | collective-permute-start | bytes 776 | tf_op jit(solution)/shard_map/ppermute | solution.py:385
  112.3 2.8 %collective-permute-done.17 = f32[64]{0:T(128)S(1)} collective-permute-done((f32[64]{0:T(128)S(1)}, f32[64]{0:T(128)S(1)}, u32[]{:S(2)}, u32[]{:S(2)}) %collective-permute-start.17) | collective-permute-done | bytes 288 | tf_op jit(solution)/shard_map/ppermute | solution.py:385
  115.1 8.8 %collective-permute-start.18 = (f32[64]{0:T(128)S(1)}, f32[64]{0:T(128)S(1)}, u32[]{:S(2)}, u32[]{:S(2)}) collective-permute-start(f32[64]{0:T(128)S(1)} %add.137), channel_id=1, source_target_pairs={{0,4},{4,0},{8,12},{12,8},{1,5},{5,1},{9,13},{13,9},{2,6},{6,2},{1... | collective-permute-start | bytes 776 | tf_op jit(solution)/shard_map/ppermute | solution.py:385
  124.0 1.5 %put_in_slots.2.refs_3_ = bf16[16,256,256]{2,1,0:T(8,128)(2,1)} custom-call(s32[6]{0:T(128)S(1)} %bitcast.14, bf16[6,256,256]{2,1,0:T(8,128)(2,1)S(1)} %get-tuple-element.59.refs_0_), custom_call_target="tpu_custom_call" | custom-call | bytes 1572864 | tf_op jit(solution)/shard_map/put_in_slots/pallas_call | solution.py:362
  126.0 1.7 %put_in_slots.3 = bf16[16,256,256]{2,1,0:T(8,128)(2,1)} custom-call(s32[10]{0:T(128)S(1)} %pad_add_fusion.1.slot_ref, bf16[6,256,256]{2,1,0:T(8,128)(2,1)S(1)} %collective-permute-done.12.refs_0_, bf16[2,256,256]{2,1,0:T(8,128)(2,1)S(1)} %get-tuple-element.61.refs_1_, ...), custom_call_target="tpu_custom_call", output_to_operand_aliasing={{}: (4, {})} | custom-call | bytes 2621440 | tf_op jit(solution)/shard_map/put_in_slots/pallas_call | solution.py:362
  (67 shorter events, 4.6 us)
Async XLA Ops:
  0.6 13.3 %copy-start.7 = (s32[16,1]{0,1:T(1,128)S(1)}, s32[16,1]{0,1:T(1,128)}, u32[]{:S(2)}) copy-start(s32[16,1]{0,1:T(1,128)} %param.23) | copy-start | bytes 196
  1.4 12.5 %collective-permute-start.3 = (s32[16]{0:T(128)S(1)}, s32[16]{0:T(128)S(1)}, u32[]{:S(2)}, u32[]{:S(2)}) collective-permute-start(s32[16]{0:T(128)S(1)} %bitcast_add_fusion), channel_id=1, source_target_pairs={{12,0},{8,4},{4,8},{0,12},{13,1},{9,5},{5,9},{1,13},{14,2},{10,6},... | collective-permute-start | bytes 200 | tf_op jit(solution)/shard_map/ppermute | solution.py:421
  6.4 7.5 %collective-permute-start.2 = (s32[16]{0:T(128)S(1)}, s32[16]{0:T(128)S(1)}, u32[]{:S(2)}, u32[]{:S(2)}) collective-permute-start(s32[16]{0:T(128)S(1)} %bitcast_add_fusion), channel_id=1, source_target_pairs={{8,0},{0,4},{12,8},{4,12},{9,1},{1,5},{13,9},{5,13},{10,2},{2,6},{... | collective-permute-start | bytes 200 | tf_op jit(solution)/shard_map/ppermute | solution.py:421
  6.4 4.2 %collective-permute-start = (s32[16]{0:T(128)S(1)}, s32[16]{0:T(128)S(1)}, u32[]{:S(2)}, u32[]{:S(2)}) collective-permute-start(s32[16]{0:T(128)S(1)} %bitcast_add_fusion), channel_id=1, source_target_pairs={{4,0},{12,4},{0,8},{8,12},{5,1},{13,5},{1,9},{9,13},{6,2},{14,6},{... | collective-permute-start | bytes 200 | tf_op jit(solution)/shard_map/ppermute | solution.py:419
  9.4 11.5 %copy-start.4 = (s32[16,1]{0,1:T(1,128)S(1)}, s32[16,1]{0,1:T(1,128)}, u32[]{:S(2)}) copy-start(s32[16,1]{0,1:T(1,128)} %param.24) | copy-start | bytes 196
  9.4 11.5 %copy-start.5 = (s32[16]{0:T(128)S(1)}, s32[16]{0:T(128)}, u32[]{:S(2)}) copy-start(s32[16]{0:T(128)} %param.19) | copy-start | bytes 196
  9.5 11.5 %copy-start.6 = (s32[16]{0:T(128)S(1)}, s32[16]{0:T(128)}, u32[]{:S(2)}) copy-start(s32[16]{0:T(128)} %param.18) | copy-start | bytes 196
  9.5 12.0 %copy-start.3 = (f32[64]{0:T(128)S(1)}, f32[64]{0:T(128)}, u32[]{:S(2)}) copy-start(f32[64]{0:T(128)} %param.17) | copy-start | bytes 772
  9.5 12.2 %copy-start.8 = (bf16[16,1]{0,1:T(2,128)(2,1)S(1)}, bf16[16,1]{0,1:T(2,128)(2,1)}, u32[]{:S(2)}) copy-start(bf16[16,1]{0,1:T(2,128)(2,1)} %param.25) | copy-start | bytes 100
  9.5 12.2 %copy-start = (s32[16,11]{1,0:T(8,128)S(1)}, s32[16,11]{1,0:T(8,128)}, u32[]{:S(2)}) copy-start(s32[16,11]{1,0:T(8,128)} %slot_ref.3) | copy-start | bytes 2116
  9.5 12.2 %copy-start.1 = (bf16[16,11]{1,0:T(8,128)(2,1)S(1)}, bf16[16,11]{1,0:T(8,128)(2,1)}, u32[]{:S(2)}) copy-start(bf16[16,11]{1,0:T(8,128)(2,1)} %weight_ref.3) | copy-start | bytes 1060
  9.5 12.2 %copy-start.2 = (s32[16]{0:T(128)S(1)}, s32[16]{0:T(128)}, u32[]{:S(2)}) copy-start(s32[16]{0:T(128)} %count_ref.3) | copy-start | bytes 196
  13.0 32.9 %collective-permute-start.1 = (bf16[4,256,256]{2,1,0:T(8,128)(2,1)S(1)}, bf16[4,256,256]{2,1,0:T(8,128)(2,1)S(1)}, u32[]{:S(2)}, u32[]{:S(2)}) collective-permute-start(bf16[4,256,256]{2,1,0:T(8,128)(2,1)S(1)} %get-tuple-element.44), channel_id=1, source_target_pairs={{0,4},{4,12},{8,0},{12,8},{1,5},{5,13},{9,1},{13,9},{2,6},{6,14},{... | collective-permute-start | bytes 1572872 | tf_op jit(solution)/shard_map/ppermute | solution.py:500
  17.0 19.2 %collective-permute-start.5 = (bf16[2,256,256]{2,1,0:T(8,128)(2,1)S(1)}, bf16[2,256,256]{2,1,0:T(8,128)(2,1)S(1)}, u32[]{:S(2)}, u32[]{:S(2)}) collective-permute-start(bf16[2,256,256]{2,1,0:T(8,128)(2,1)S(1)} %get-tuple-element.48), channel_id=1, source_target_pairs={{0,12},{4,8},{8,4},{12,0},{1,13},{5,9},{9,5},{13,1},{2,14},{6,10},... | collective-permute-start | bytes 786440 | tf_op jit(solution)/shard_map/ppermute | solution.py:507
  20.9 25.0 %collective-permute-start.4 = (bf16[4,256,256]{2,1,0:T(8,128)(2,1)S(1)}, bf16[4,256,256]{2,1,0:T(8,128)(2,1)S(1)}, u32[]{:S(2)}, u32[]{:S(2)}) collective-permute-start(bf16[4,256,256]{2,1,0:T(8,128)(2,1)S(1)} %get-tuple-element.47), channel_id=1, source_target_pairs={{0,8},{4,0},{8,12},{12,4},{1,9},{5,1},{9,13},{13,5},{2,10},{6,2},{... | collective-permute-start | bytes 1572872 | tf_op jit(solution)/shard_map/ppermute | solution.py:507
  47.4 13.3 %collective-permute-start.7 = (bf16[6,256,256]{2,1,0:T(8,128)(2,1)S(1)}, bf16[6,256,256]{2,1,0:T(8,128)(2,1)S(1)}, u32[]{:S(2)}, u32[]{:S(2)}) collective-permute-start(bf16[6,256,256]{2,1,0:T(8,128)(2,1)S(1)} %finish.4.refs_0_), channel_id=1, source_target_pairs={{0,1},{1,0},{2,3},{3,2},{4,5},{5,4},{6,7},{7,6},{8,9},{9,8},{10,11... | collective-permute-start | bytes 2359304 | tf_op jit(solution)/shard_map/ppermute | solution.py:518
  47.5 10.6 %collective-permute-start.6 = (bf16[2,256,256]{2,1,0:T(8,128)(2,1)S(1)}, bf16[2,256,256]{2,1,0:T(8,128)(2,1)S(1)}, u32[]{:S(2)}, u32[]{:S(2)}) collective-permute-start(bf16[2,256,256]{2,1,0:T(8,128)(2,1)S(1)} %get-tuple-element.50), channel_id=1, source_target_pairs={{0,12},{4,8},{8,4},{12,0},{1,13},{5,9},{9,5},{13,1},{2,14},{6,10},... | collective-permute-start | bytes 786440 | tf_op jit(solution)/shard_map/ppermute | solution.py:507
  59.1 1.6 %collective-permute-start.8 = (bf16[2,256,256]{2,1,0:T(8,128)(2,1)S(1)}, bf16[2,256,256]{2,1,0:T(8,128)(2,1)S(1)}, u32[]{:S(2)}, u32[]{:S(2)}) collective-permute-start(bf16[2,256,256]{2,1,0:T(8,128)(2,1)S(1)} %finish.5.refs_2_), channel_id=1, source_target_pairs={{0,1},{1,0},{2,3},{3,2},{4,5},{5,4},{6,7},{7,6},{8,9},{9,8},{10,11... | collective-permute-start | bytes 786440 | tf_op jit(solution)/shard_map/ppermute | solution.py:524
  61.4 37.3 %collective-permute-start.9 = (bf16[4,256,256]{2,1,0:T(8,128)(2,1)S(1)}, bf16[4,256,256]{2,1,0:T(8,128)(2,1)S(1)}, u32[]{:S(2)}, u32[]{:S(2)}) collective-permute-start(bf16[4,256,256]{2,1,0:T(8,128)(2,1)S(1)} %gather_again.2), channel_id=1, source_target_pairs={{0,4},{4,12},{8,0},{12,8},{1,5},{5,13},{9,1},{13,9},{2,6},{6,14},{... | collective-permute-start | bytes 1572872 | tf_op jit(solution)/shard_map/ppermute | solution.py:500
  68.4 30.4 %collective-permute-start.10 = (bf16[4,256,256]{2,1,0:T(8,128)(2,1)S(1)}, bf16[4,256,256]{2,1,0:T(8,128)(2,1)S(1)}, u32[]{:S(2)}, u32[]{:S(2)}) collective-permute-start(bf16[4,256,256]{2,1,0:T(8,128)(2,1)S(1)} %get-tuple-element.56), channel_id=1, source_target_pairs={{0,8},{4,0},{8,12},{12,4},{1,9},{5,1},{9,13},{13,5},{2,10},{6,2},{... | collective-permute-start | bytes 1572872 | tf_op jit(solution)/shard_map/ppermute | solution.py:507
  68.5 30.2 %collective-permute-start.11 = (bf16[2,256,256]{2,1,0:T(8,128)(2,1)S(1)}, bf16[2,256,256]{2,1,0:T(8,128)(2,1)S(1)}, u32[]{:S(2)}, u32[]{:S(2)}) collective-permute-start(bf16[2,256,256]{2,1,0:T(8,128)(2,1)S(1)} %get-tuple-element.57), channel_id=1, source_target_pairs={{0,12},{4,8},{8,4},{12,0},{1,13},{5,9},{9,5},{13,1},{2,14},{6,10},... | collective-permute-start | bytes 786440 | tf_op jit(solution)/shard_map/ppermute | solution.py:507
  71.0 32.6 %collective-permute-start.13 = (bf16[2,256,256]{2,1,0:T(8,128)(2,1)S(1)}, bf16[2,256,256]{2,1,0:T(8,128)(2,1)S(1)}, u32[]{:S(2)}, u32[]{:S(2)}) collective-permute-start(bf16[2,256,256]{2,1,0:T(8,128)(2,1)S(1)} %get-tuple-element.60), channel_id=1, source_target_pairs={{0,12},{4,8},{8,4},{12,0},{1,13},{5,9},{9,5},{13,1},{2,14},{6,10},... | collective-permute-start | bytes 786440 | tf_op jit(solution)/shard_map/ppermute | solution.py:507
  101.4 24.6 %collective-permute-start.12 = (bf16[6,256,256]{2,1,0:T(8,128)(2,1)S(1)}, bf16[6,256,256]{2,1,0:T(8,128)(2,1)S(1)}, u32[]{:S(2)}, u32[]{:S(2)}) collective-permute-start(bf16[6,256,256]{2,1,0:T(8,128)(2,1)S(1)} %get-tuple-element.59.refs_0_), channel_id=1, source_target_pairs={{0,1},{1,0},{2,3},{3,2},{4,5},{5,4},{6,7},{7,6},{8,9},{9,8},{10,11... | collective-permute-start | bytes 2359304 | tf_op jit(solution)/shard_map/ppermute | solution.py:518
  105.0 1.2 collective-permute-start.15
  106.2 3.6 %collective-permute-start.16 = (f32[64]{0:T(128)S(1)}, f32[64]{0:T(128)S(1)}, u32[]{:S(2)}, u32[]{:S(2)}) collective-permute-start(f32[64]{0:T(128)S(1)} %add.135), channel_id=1, source_target_pairs={{0,2},{2,0},{1,3},{3,1},{4,6},{6,4},{5,7},{7,5},{8,10},{10,8},{9,1... | collective-permute-start | bytes 776 | tf_op jit(solution)/shard_map/ppermute | solution.py:385
  109.8 5.4 %collective-permute-start.17 = (f32[64]{0:T(128)S(1)}, f32[64]{0:T(128)S(1)}, u32[]{:S(2)}, u32[]{:S(2)}) collective-permute-start(f32[64]{0:T(128)S(1)} %add.136), channel_id=1, source_target_pairs={{0,12},{4,8},{8,4},{12,0},{1,13},{5,9},{9,5},{13,1},{2,14},{6,10},... | collective-permute-start | bytes 776 | tf_op jit(solution)/shard_map/ppermute | solution.py:385
  112.3 13.7 %collective-permute-start.14 = (bf16[2,256,256]{2,1,0:T(8,128)(2,1)S(1)}, bf16[2,256,256]{2,1,0:T(8,128)(2,1)S(1)}, u32[]{:S(2)}, u32[]{:S(2)}) collective-permute-start(bf16[2,256,256]{2,1,0:T(8,128)(2,1)S(1)} %get-tuple-element.61.refs_1_), channel_id=1, source_target_pairs={{0,1},{1,0},{2,3},{3,2},{4,5},{5,4},{6,7},{7,6},{8,9},{9,8},{10,11... | collective-permute-start | bytes 786440 | tf_op jit(solution)/shard_map/ppermute | solution.py:524
  115.1 10.3 %collective-permute-start.18 = (f32[64]{0:T(128)S(1)}, f32[64]{0:T(128)S(1)}, u32[]{:S(2)}, u32[]{:S(2)}) collective-permute-start(f32[64]{0:T(128)S(1)} %add.137), channel_id=1, source_target_pairs={{0,4},{4,0},{8,12},{12,8},{1,5},{5,1},{9,13},{13,9},{2,6},{6,2},{1... | collective-permute-start | bytes 776 | tf_op jit(solution)/shard_map/ppermute | solution.py:385

commit v12 on v11

--- a/solution.py
+++ b/solution.py
@@ -127,29 +127,29 @@
     )(place, *requests, in_hbm(amplitudes))
 
 
-def gather_again(spots, stores, parts, cap):
+def gather_again(asked, where, stores, parts, cap):
     domain = stores[0].shape[1]
     steps = sorted({step for step, _, _ in parts})
     blocks = sum(size for _, _, size in parts)
 
-    def body(spot_ref, *refs):
+    def body(asked_ref, where_ref, *refs):
         sources = laid(refs[: len(stores)])
         outs = refs[len(stores) :]
         for m, (step, begin, size) in enumerate(parts):
             for k in range(size):
-                spot = spot_ref[steps.index(step) * (cap + 1) + begin + k]
+                spot = where_ref[asked_ref[steps.index(step) * (cap + 1) + begin + k]]
                 fetch(sources, spot, outs[m].at[k])
 
     return pl.pallas_call(
         body,
         out_shape=[VMEM((size, domain, domain), jnp.bfloat16) for _, _, size in parts],
-        in_specs=[pl.BlockSpec(memory_space=SMEM)]
+        in_specs=[pl.BlockSpec(memory_space=SMEM)] * 2
         + [pl.BlockSpec(memory_space=VMEM)] * len(stores),
         out_specs=[pl.BlockSpec(memory_space=VMEM)] * len(parts),
         cost_estimate=cost(0, blocks * domain * domain * 4),
         compiler_params=limits(8),
         name="gather_again",
-    )(spots, *stores)
+    )(asked, where, *stores)
 
 
 def prepare(
@@ -298,7 +298,7 @@
             density = jnp.zeros((1, occ_count), jnp.float32)
         for n in range(count):
             i = start + n
-            coupled = local_ref[i] + scale_ref[i : i + 1, :] * hold[n].astype(jnp.float32)
+            coupled = local_ref[i] + scale_ref[i] * hold[n].astype(jnp.float32)
             over = over_ref[i]
             projected = jnp.dot(
                 over, coupled.astype(jnp.bfloat16), preferred_element_type=jnp.float32
@@ -328,8 +328,8 @@
     return pl.pallas_call(
         body,
         out_shape=out_shape,
-        in_specs=[pl.BlockSpec(memory_space=SMEM)]
-        + [pl.BlockSpec(memory_space=VMEM)] * 5
+        in_specs=[pl.BlockSpec(memory_space=SMEM)] * 2
+        + [pl.BlockSpec(memory_space=VMEM)] * 4
         + [pl.BlockSpec(memory_space=VMEM)] * len(arrived),
         out_specs=[pl.BlockSpec(memory_space=VMEM)] * len(out_shape),
         scratch_shapes=[VMEM((count, domain, domain), jnp.bfloat16)],
@@ -414,11 +414,11 @@
     here = jnp.stack([row, core]).astype(jnp.int32)
     tail = max(1, cap // 2)
     lead = [(1, 0, cap)]
-    rest = [(step, 0, cap) for step in range(2, rows - 1)]
-    rest += [(rows - 1, 0, cap - tail)] * (cap > tail) + [(rows - 1, cap - tail, tail)]
+    inner = [(step, 0, cap) for step in range(2, rows - 1)]
+    outer = [(rows - 1, 0, cap - tail)] * (cap > tail) + [(rows - 1, cap - tail, tail)]
     request = lax.ppermute(packed, "row", asked_of(rows, 1))
     requests = [
-        lax.ppermute(packed, "row", asked_of(rows, d)) for d in range(2, rows)
+        lax.ppermute(packed, "row", asked_of(rows, d)) for d in range(2, rows - 1)
     ]
     asked_lead, send_lead = gather_first([request], lead, here, amplitudes, rows, cap)
 
@@ -457,7 +457,6 @@
         return jnp.sum(jnp.where(found, occ_energy[None, :], jnp.float32(0.0)), axis=1)
 
     far_scale = pick(own_pick, far_weight[:, 0].astype(jnp.float32))
-    far_scale = jnp.broadcast_to(far_scale[:, None], (half, domain))
     first = pick(own_pick, first_occ)
     second = pick(own_pick, second_occ)
     shift = energy_of(first) + energy_of(second)
@@ -485,25 +484,24 @@
     columns = [slot_ids, jnp.concatenate([own, other])]
     ats = [own, jnp.arange(half, dtype=jnp.int32)]
     slots = jnp.concatenate([other[:early], own[early:], other[early:]])
-
-    def spots_of(slots_asked):
-        found = slots_asked[:, None] == slot_ids[None, :]
-        return jnp.sum(jnp.where(found, local_spots[1][None, :], 0), axis=1)
-
     stores = [amplitudes]
     whole = [amplitudes]
     for sweep in range(ITERS):
         last = sweep == ITERS - 1
         again = min(sweep, 1)
         if sweep > 0:
-            (send_lead,) = gather_again(spots_of(asked_lead), stores, lead, cap)
+            (send_lead,) = gather_again(asked_lead, local_spots[1], stores, lead, cap)
         arrived = [lax.ppermute(send_lead, "row", sent(rows, 1))]
         if sweep == 0:
+            request = lax.ppermute(packed, "row", asked_of(rows, rows - 1))
             (*requests, _) = lax.optimization_barrier((*requests, send_lead))
-            asked, *sends = gather_first(requests, rest, here, amplitudes, rows, cap)
+            asked, *sends = gather_first(requests, inner, here, amplitudes, rows, cap)
+            request, _ = lax.optimization_barrier((request, sends[0]))
+            asked_last, *sends_last = gather_first([request], outer, here, amplitudes, rows, cap)
         else:
-            sends = gather_again(spots_of(asked), stores, rest, cap)
-        for part, send in zip(rest, sends):
+            sends = gather_again(asked, local_spots[1], stores, inner, cap)
+            sends_last = gather_again(asked_last, local_spots[1], stores, outer, cap)
+        for part, send in zip(inner + outer, [*sends, *sends_last]):
             arrived.append(lax.ppermute(send, "row", sent(rows, part[0])))
         *prepared, at_home = prepare(
             own, ats[again], homes[again], columns[again], near_count, shift, near, whole,

time: 128 us -> 128 us (level)
  Pallas kernels: 30.9 us -> 33.7 us
  waiting for transfers between devices: 55.1 us -> 52.5 us
    ppermute x2, waiting for transfers between devices: 9.72 us -> 1.33 us  [per_device(): arrived = [lax.ppermute(send_lead, 'row', sent(rows, 1))]]
    ppermute x6, waiting for transfers between devices: 36.9 us -> 42.3 us  [per_device(): arrived.append(lax.ppermute(send, 'row', sent(rows, part[0])))]
    ppermute x0 -> x1, starting transfers between devices: none -> 5.08 us  [per_device(): request = lax.ppermute(packed, 'row', asked_of(rows, rows - 1))]
    ppermute x2 -> x1, starting transfers between devices: 5.08 us -> 0.01 us  [per_device(): lax.ppermute(packed, 'row', asked_of(rows, d))]
    pallas_call x2 -> x3, Pallas kernels: 5.05 us -> 7.19 us  [gather_first(): pl.pallas_call(body, out_shape=[jax.ShapeDtypeStruct((count_of * (cap + 1...]
  transfers between devices with their start and end apart: 19 -> 19, of which waited for: 10 -> 10; matrix products, arithmetic and copies ran while one was open for 2% -> 2% of each run, Pallas kernels for 21% -> 23%
where the time goes in v12:
time: 128 us
  waiting for transfers between devices  52.5 us (41%)
  starting transfers between devices  37.3 us (29%)
  Pallas kernels  33.7 us (26%)
  other arithmetic  3.03 us (2%)
    ppermute x6, waiting for transfers between devices, per_device(): arrived.append(lax.ppermute(send, 'row', sent(rows, part[0])))  42.3 us
    pallas_call x2, Pallas kernels, prepare(): pl.pallas_call(body, grid_spec=pltpu.PrefetchScalarGridSpec(num_scalar_pr...  14.7 us
    ppermute x4, starting transfers between devices, add_over(): lax.ppermute(values, name, [(r, r ^ step) for r in range(size)])  12.6 us
    ppermute x6, starting transfers between devices, per_device(): arrived.append(lax.ppermute(send, 'row', sent(rows, part[0])))  9.51 us
    pallas_call x3, Pallas kernels, gather_first(): pl.pallas_call(body, out_shape=[jax.ShapeDtypeStruct((count_of * (cap + 1...  7.19 us
    ppermute x2, starting transfers between devices, per_device(): arrived = [lax.ppermute(send_lead, 'row', sent(rows, 1))]  7 us
    pallas_call x4, Pallas kernels, finish(): pl.pallas_call(body, out_shape=out_shape, in_specs=[pl.BlockSpec(memory_s...  6.62 us
    ppermute x4, waiting for transfers between devices, add_over(): lax.ppermute(values, name, [(r, r ^ step) for r in range(size)])  6.09 us
  transfers between devices with their start and end apart: 19, of which 10 were waited for; matrix products, arithmetic and copies ran while one was open for 2% of the time, Pallas kernels for 23%

profile of v12, /device:TPU:0, one launch (start us, length us, event | category | flops | bytes accessed | tf_op | source)
XLA Modules:
  0.0 127.6 jit_solution(844699030254593960)
XLA Ops:
  1.4 5.1 %collective-permute-start.4 = (s32[16]{0:T(128)S(1)}, s32[16]{0:T(128)S(1)}, u32[]{:S(2)}, u32[]{:S(2)}) collective-permute-start(s32[16]{0:T(128)S(1)} %bitcast_add_fusion), channel_id=1, source_target_pairs={{12,0},{8,4},{4,8},{0,12},{13,1},{9,5},{5,9},{1,13},{14,2},{10,6},... | collective-permute-start | bytes 200 | tf_op jit(solution)/shard_map/ppermute | solution.py:496
  6.4 2.9 %collective-permute-start = (s32[16]{0:T(128)S(1)}, s32[16]{0:T(128)S(1)}, u32[]{:S(2)}, u32[]{:S(2)}) collective-permute-start(s32[16]{0:T(128)S(1)} %bitcast_add_fusion), channel_id=1, source_target_pairs={{4,0},{12,4},{0,8},{8,12},{5,1},{13,5},{1,9},{9,13},{6,2},{14,6},{... | collective-permute-start | bytes 200 | tf_op jit(solution)/shard_map/ppermute | solution.py:419
  9.5 1.2 collective-permute-done.refs_0_
  10.7 2.4 %gather_first.3 = (s32[5]{0:T(128)S(1)}, bf16[4,256,256]{2,1,0:T(8,128)(2,1)S(1)}) custom-call(s32[2]{0:T(128)S(1)} %pad_add_fusion.place_ref, s32[16]{0:T(128)S(1)} %collective-permute-done.refs_0_, bf16[16,256,256]{2,1,0:T(8,128)(2,1)} %refs_1_.7), custom_call_target="tpu_custom_call" | custom-call | bytes 1048576 | tf_op jit(solution)/shard_map/gather_first/pallas_call | solution.py:115
  14.4 2.4 %gather_first.4 = (s32[5]{0:T(128)S(1)}, bf16[4,256,256]{2,1,0:T(8,128)(2,1)S(1)}) custom-call(s32[2]{0:T(128)S(1)} %pad_add_fusion.place_ref, s32[16]{0:T(128)S(1)} %collective-permute-done.2.refs_0_, bf16[16,256,256]{2,1,0:T(8,128)(2,1)} %refs_1_.7), custom_call_target="tpu_custom_call" | custom-call | bytes 1048576 | tf_op jit(solution)/shard_map/gather_first/pallas_call | solution.py:115
  16.8 2.4 %collective-permute-start.3 = (bf16[4,256,256]{2,1,0:T(8,128)(2,1)S(1)}, bf16[4,256,256]{2,1,0:T(8,128)(2,1)S(1)}, u32[]{:S(2)}, u32[]{:S(2)}) collective-permute-start(bf16[4,256,256]{2,1,0:T(8,128)(2,1)S(1)} %get-tuple-element.46), channel_id=1, source_target_pairs={{0,8},{4,0},{8,12},{12,4},{1,9},{5,1},{9,13},{13,5},{2,10},{6,2},{... | collective-permute-start | bytes 1572872 | tf_op jit(solution)/shard_map/ppermute | solution.py:505
  19.2 2.4 %gather_first.5 = (s32[5]{0:T(128)S(1)}, bf16[2,256,256]{2,1,0:T(8,128)(2,1)S(1)}, bf16[2,256,256]{2,1,0:T(8,128)(2,1)S(1)}) custom-call(s32[2]{0:T(128)S(1)} %pad_add_fusion.place_ref, s32[16]{0:T(128)S(1)} %collective-permute-done.4.refs_0_, bf16[16,256,256]{2,1,0:T(8,128)(2,1)} %refs_1_.7), custom_call_target="tpu_custom_call" | custom-call | bytes 1048576 | tf_op jit(solution)/shard_map/gather_first/pallas_call | solution.py:115
  21.7 1.5 %collective-permute-start.5 = (bf16[2,256,256]{2,1,0:T(8,128)(2,1)S(1)}, bf16[2,256,256]{2,1,0:T(8,128)(2,1)S(1)}, u32[]{:S(2)}, u32[]{:S(2)}) collective-permute-start(bf16[2,256,256]{2,1,0:T(8,128)(2,1)S(1)} %get-tuple-element.48), channel_id=1, source_target_pairs={{0,12},{4,8},{8,4},{12,0},{1,13},{5,9},{9,5},{13,1},{2,14},{6,10},... | collective-permute-start | bytes 786440 | tf_op jit(solution)/shard_map/ppermute | solution.py:505
  24.0 7.7 %prepare.2 = (f32[8,256,256]{2,1,0:T(8,128)S(1)}, f32[8,256,256]{2,1,0:T(8,128)S(1)}, f32[8,256,256]{2,1,0:T(8,128)S(1)}, bf16[8,256,256]{2,1,0:T(8,128)(2,1)S(1)}, bf16[8,256,256]{2,1,0:T(8,128)(2,1)S(1)}) custom-call(s32[8]{0:T(128)S(1)} %get-tuple-element.69.own_ref.at_ref, s32[8]{0:T(128)S(1)} %get-tuple-element.69.own_ref.at_ref, ...), custom_call_target="tpu_custom_call" | custom-call | flops 805306368 | bytes 12582912 | tf_op jit(solution)/shard_map/prepare/pallas_call | solution.py:245
  32.0 12.6 %collective-permute-done.5.refs_2_ = bf16[2,256,256]{2,1,0:T(8,128)(2,1)S(1)} collective-permute-done((bf16[2,256,256]{2,1,0:T(8,128)(2,1)S(1)}, bf16[2,256,256]{2,1,0:T(8,128)(2,1)S(1)}, u32[]{:S(2)}, u32[]{:S(2)}) %collective-permute-start.5) | collective-permute-done | bytes 262176 | tf_op jit(solution)/shard_map/ppermute | solution.py:505
  44.6 1.3 %collective-permute-done.1.refs_0_ = bf16[4,256,256]{2,1,0:T(8,128)(2,1)S(1)} collective-permute-done((bf16[4,256,256]{2,1,0:T(8,128)(2,1)S(1)}, bf16[4,256,256]{2,1,0:T(8,128)(2,1)S(1)}, u32[]{:S(2)}, u32[]{:S(2)}) %collective-permute-start.1) | collective-permute-done | bytes 524320 | tf_op jit(solution)/shard_map/ppermute | solution.py:494
  45.9 1.4 %finish.4.refs_0_ = bf16[6,256,256]{2,1,0:T(8,128)(2,1)S(1)} custom-call(s32[24]{0:T(128)S(1)} %pad_add_fusion.2.number_ref, f32[8]{0:T(128)S(1)} %fusion.7.scale_ref, f32[8,256,256]{2,1,0:T(8,128)S(1)} %get-tuple-element.40.local_ref, f32[8,256,256]{2,1,0:T(8,128)S(1)} %get-tuple-element.41.rest_ref, f32[8,256,256]{2,1,0:T(8,128)S(1)} %get-tuple-element.42.recip_ref, ...), custom_call_target="tpu_custom_call" | custom-call | flops 402653184 | bytes 7077888 | tf_op jit(solution)/shard_map/finish/pallas_call | solution.py:328
  47.4 1.5 %collective-permute-start.6 = (bf16[2,256,256]{2,1,0:T(8,128)(2,1)S(1)}, bf16[2,256,256]{2,1,0:T(8,128)(2,1)S(1)}, u32[]{:S(2)}, u32[]{:S(2)}) collective-permute-start(bf16[2,256,256]{2,1,0:T(8,128)(2,1)S(1)} %get-tuple-element.50), channel_id=1, source_target_pairs={{0,12},{4,8},{8,4},{12,0},{1,13},{5,9},{9,5},{13,1},{2,14},{6,10},... | collective-permute-start | bytes 786440 | tf_op jit(solution)/shard_map/ppermute | solution.py:505
  49.0 9.1 %collective-permute-done.6.refs_3_ = bf16[2,256,256]{2,1,0:T(8,128)(2,1)S(1)} collective-permute-done((bf16[2,256,256]{2,1,0:T(8,128)(2,1)S(1)}, bf16[2,256,256]{2,1,0:T(8,128)(2,1)S(1)}, u32[]{:S(2)}, u32[]{:S(2)}) %collective-permute-start.6) | collective-permute-done | bytes 262176 | tf_op jit(solution)/shard_map/ppermute | solution.py:505
  58.0 1.0 finish.5.refs_2_
  59.2 1.5 %collective-permute-done.8.refs_3_ = bf16[2,256,256]{2,1,0:T(8,128)(2,1)S(1)} collective-permute-done((bf16[2,256,256]{2,1,0:T(8,128)(2,1)S(1)}, bf16[2,256,256]{2,1,0:T(8,128)(2,1)S(1)}, u32[]{:S(2)}, u32[]{:S(2)}) %collective-permute-start.8) | collective-permute-done | bytes 262176 | tf_op jit(solution)/shard_map/ppermute | solution.py:522
  61.4 6.1 %collective-permute-start.9 = (bf16[4,256,256]{2,1,0:T(8,128)(2,1)S(1)}, bf16[4,256,256]{2,1,0:T(8,128)(2,1)S(1)}, u32[]{:S(2)}, u32[]{:S(2)}) collective-permute-start(bf16[4,256,256]{2,1,0:T(8,128)(2,1)S(1)} %gather_again.3), channel_id=1, source_target_pairs={{0,4},{4,12},{8,0},{12,8},{1,5},{5,13},{9,1},{13,9},{2,6},{6,14},{... | collective-permute-start | bytes 1572872 | tf_op jit(solution)/shard_map/ppermute | solution.py:494
  69.0 2.4 %collective-permute-start.11 = (bf16[2,256,256]{2,1,0:T(8,128)(2,1)S(1)}, bf16[2,256,256]{2,1,0:T(8,128)(2,1)S(1)}, u32[]{:S(2)}, u32[]{:S(2)}) collective-permute-start(bf16[2,256,256]{2,1,0:T(8,128)(2,1)S(1)} %get-tuple-element.57), channel_id=1, source_target_pairs={{0,12},{4,8},{8,4},{12,0},{1,13},{5,9},{9,5},{13,1},{2,14},{6,10},... | collective-permute-start | bytes 786440 | tf_op jit(solution)/shard_map/ppermute | solution.py:505
  71.6 1.5 %collective-permute-start.13 = (bf16[2,256,256]{2,1,0:T(8,128)(2,1)S(1)}, bf16[2,256,256]{2,1,0:T(8,128)(2,1)S(1)}, u32[]{:S(2)}, u32[]{:S(2)}) collective-permute-start(bf16[2,256,256]{2,1,0:T(8,128)(2,1)S(1)} %get-tuple-element.60), channel_id=1, source_target_pairs={{0,12},{4,8},{8,4},{12,0},{1,13},{5,9},{9,5},{13,1},{2,14},{6,10},... | collective-permute-start | bytes 786440 | tf_op jit(solution)/shard_map/ppermute | solution.py:505
  73.2 6.9 %prepare.3 = (f32[8,256,256]{2,1,0:T(8,128)S(1)}, f32[8,256,256]{2,1,0:T(8,128)S(1)}, f32[8,256,256]{2,1,0:T(8,128)S(1)}, bf16[8,256,256]{2,1,0:T(8,128)(2,1)S(1)}, bf16[8,256,256]{2,1,0:T(8,128)(2,1)S(1)}) custom-call(s32[8]{0:T(128)S(1)} %get-tuple-element.69.own_ref.at_ref, s32[8]{0:T(128)S(1)} %iota.29.at_ref, s32[8]{0:T(128)S(1)} %get-tuple-element.71.home_ref, ...), custom_call_target="tpu_custom_call" | custom-call | flops 805306368 | bytes 12582912 | tf_op jit(solution)/shard_map/prepare/pallas_call | solution.py:245
  80.1 18.5 %collective-permute-done.11.refs_2_ = bf16[2,256,256]{2,1,0:T(8,128)(2,1)S(1)} collective-permute-done((bf16[2,256,256]{2,1,0:T(8,128)(2,1)S(1)}, bf16[2,256,256]{2,1,0:T(8,128)(2,1)S(1)}, u32[]{:S(2)}, u32[]{:S(2)}) %collective-permute-start.11) | collective-permute-done | bytes 262176 | tf_op jit(solution)/shard_map/ppermute | solution.py:505
  98.7 2.7 %finish.6 = (bf16[6,256,256]{2,1,0:T(8,128)(2,1)S(1)}, f32[1,64]{1,0:T(1,128)S(1)}) custom-call(s32[24]{0:T(128)S(1)} %pad_add_fusion.2.number_ref, f32[8]{0:T(128)S(1)} %fusion.7.scale_ref, f32[8,256,256]{2,1,0:T(8,128)S(1)} %get-tuple-element.51.local_ref, f32[8,256,256]{2,1,0:T(8,128)S(1)} %get-tuple-element.52.rest_ref, ...), custom_call_target="tpu_custom_call" | custom-call | flops 402653184 | bytes 7077888 | tf_op jit(solution)/shard_map/finish/pallas_call | solution.py:328
  101.4 2.1 %collective-permute-done.13.refs_3_ = bf16[2,256,256]{2,1,0:T(8,128)(2,1)S(1)} collective-permute-done((bf16[2,256,256]{2,1,0:T(8,128)(2,1)S(1)}, bf16[2,256,256]{2,1,0:T(8,128)(2,1)S(1)}, u32[]{:S(2)}, u32[]{:S(2)}) %collective-permute-start.13) | collective-permute-done | bytes 262176 | tf_op jit(solution)/shard_map/ppermute | solution.py:505
  103.5 1.5 %finish.7 = (bf16[2,256,256]{2,1,0:T(8,128)(2,1)S(1)}, f32[1,64]{1,0:T(1,128)S(1)}) custom-call(s32[24]{0:T(128)S(1)} %pad_add_fusion.2.number_ref, f32[8]{0:T(128)S(1)} %fusion.7.scale_ref, f32[8,256,256]{2,1,0:T(8,128)S(1)} %get-tuple-element.51.local_ref, f32[8,256,256]{2,1,0:T(8,128)S(1)} %get-tuple-element.52.rest_ref, ...), custom_call_target="tpu_custom_call" | custom-call | flops 134217728 | bytes 2359296 | tf_op jit(solution)/shard_map/finish/pallas_call | solution.py:328
  105.0 1.2 collective-permute-done.15
  106.2 1.5 %collective-permute-start.16 = (f32[64]{0:T(128)S(1)}, f32[64]{0:T(128)S(1)}, u32[]{:S(2)}, u32[]{:S(2)}) collective-permute-start(f32[64]{0:T(128)S(1)} %add.110), channel_id=1, source_target_pairs={{0,2},{2,0},{1,3},{3,1},{4,6},{6,4},{5,7},{7,5},{8,10},{10,8},{9,1... | collective-permute-start | bytes 776 | tf_op jit(solution)/shard_map/ppermute | solution.py:385
  107.6 2.1 %collective-permute-done.16 = f32[64]{0:T(128)S(1)} collective-permute-done((f32[64]{0:T(128)S(1)}, f32[64]{0:T(128)S(1)}, u32[]{:S(2)}, u32[]{:S(2)}) %collective-permute-start.16) | collective-permute-done | bytes 288 | tf_op jit(solution)/shard_map/ppermute | solution.py:385
  109.7 2.4 %collective-permute-start.17 = (f32[64]{0:T(128)S(1)}, f32[64]{0:T(128)S(1)}, u32[]{:S(2)}, u32[]{:S(2)}) collective-permute-start(f32[64]{0:T(128)S(1)} %add.111), channel_id=1, source_target_pairs={{0,12},{4,8},{8,4},{12,0},{1,13},{5,9},{9,5},{13,1},{2,14},{6,10},... | collective-permute-start | bytes 776 | tf_op jit(solution)/shard_map/ppermute | solution.py:385
  112.2 2.9 %collective-permute-done.17 = f32[64]{0:T(128)S(1)} collective-permute-done((f32[64]{0:T(128)S(1)}, f32[64]{0:T(128)S(1)}, u32[]{:S(2)}, u32[]{:S(2)}) %collective-permute-start.17) | collective-permute-done | bytes 288 | tf_op jit(solution)/shard_map/ppermute | solution.py:385
  115.1 8.8 %collective-permute-start.18 = (f32[64]{0:T(128)S(1)}, f32[64]{0:T(128)S(1)}, u32[]{:S(2)}, u32[]{:S(2)}) collective-permute-start(f32[64]{0:T(128)S(1)} %add.112), channel_id=1, source_target_pairs={{0,4},{4,0},{8,12},{12,8},{1,5},{5,1},{9,13},{13,9},{2,6},{6,2},{1... | collective-permute-start | bytes 776 | tf_op jit(solution)/shard_map/ppermute | solution.py:385
  123.9 1.5 %put_in_slots.2.refs_3_ = bf16[16,256,256]{2,1,0:T(8,128)(2,1)} custom-call(s32[6]{0:T(128)S(1)} %bitcast.14, bf16[6,256,256]{2,1,0:T(8,128)(2,1)S(1)} %get-tuple-element.59.refs_0_), custom_call_target="tpu_custom_call" | custom-call | bytes 1572864 | tf_op jit(solution)/shard_map/put_in_slots/pallas_call | solution.py:362
  125.9 1.7 %put_in_slots.3 = bf16[16,256,256]{2,1,0:T(8,128)(2,1)} custom-call(s32[10]{0:T(128)S(1)} %pad_add_fusion.1.slot_ref, bf16[6,256,256]{2,1,0:T(8,128)(2,1)S(1)} %collective-permute-done.12.refs_0_, bf16[2,256,256]{2,1,0:T(8,128)(2,1)S(1)} %get-tuple-element.61.refs_1_, ...), custom_call_target="tpu_custom_call", output_to_operand_aliasing={{}: (4, {})} | custom-call | bytes 2621440 | tf_op jit(solution)/shard_map/put_in_slots/pallas_call | solution.py:362
  (67 shorter events, 6.4 us)
Async XLA Ops:
  0.6 13.3 %copy-start.7 = (s32[16,1]{0,1:T(1,128)S(1)}, s32[16,1]{0,1:T(1,128)}, u32[]{:S(2)}) copy-start(s32[16,1]{0,1:T(1,128)} %param.23) | copy-start | bytes 196
  1.4 17.9 %collective-permute-start.4 = (s32[16]{0:T(128)S(1)}, s32[16]{0:T(128)S(1)}, u32[]{:S(2)}, u32[]{:S(2)}) collective-permute-start(s32[16]{0:T(128)S(1)} %bitcast_add_fusion), channel_id=1, source_target_pairs={{12,0},{8,4},{4,8},{0,12},{13,1},{9,5},{5,9},{1,13},{14,2},{10,6},... | collective-permute-start | bytes 200 | tf_op jit(solution)/shard_map/ppermute | solution.py:496
  6.4 7.5 %collective-permute-start.2 = (s32[16]{0:T(128)S(1)}, s32[16]{0:T(128)S(1)}, u32[]{:S(2)}, u32[]{:S(2)}) collective-permute-start(s32[16]{0:T(128)S(1)} %bitcast_add_fusion), channel_id=1, source_target_pairs={{8,0},{0,4},{12,8},{4,12},{9,1},{1,5},{13,9},{5,13},{10,2},{2,6},{... | collective-permute-start | bytes 200 | tf_op jit(solution)/shard_map/ppermute | solution.py:421
  6.4 4.2 %collective-permute-start = (s32[16]{0:T(128)S(1)}, s32[16]{0:T(128)S(1)}, u32[]{:S(2)}, u32[]{:S(2)}) collective-permute-start(s32[16]{0:T(128)S(1)} %bitcast_add_fusion), channel_id=1, source_target_pairs={{4,0},{12,4},{0,8},{8,12},{5,1},{13,5},{1,9},{9,13},{6,2},{14,6},{... | collective-permute-start | bytes 200 | tf_op jit(solution)/shard_map/ppermute | solution.py:419
  13.0 32.9 %collective-permute-start.1 = (bf16[4,256,256]{2,1,0:T(8,128)(2,1)S(1)}, bf16[4,256,256]{2,1,0:T(8,128)(2,1)S(1)}, u32[]{:S(2)}, u32[]{:S(2)}) collective-permute-start(bf16[4,256,256]{2,1,0:T(8,128)(2,1)S(1)} %get-tuple-element.44), channel_id=1, source_target_pairs={{0,4},{4,12},{8,0},{12,8},{1,5},{5,13},{9,1},{13,9},{2,6},{6,14},{... | collective-permute-start | bytes 1572872 | tf_op jit(solution)/shard_map/ppermute | solution.py:494
  14.3 8.9 %copy-start.4 = (s32[16,1]{0,1:T(1,128)S(1)}, s32[16,1]{0,1:T(1,128)}, u32[]{:S(2)}) copy-start(s32[16,1]{0,1:T(1,128)} %param.24) | copy-start | bytes 196
  14.3 8.9 %copy-start.5 = (s32[16]{0:T(128)S(1)}, s32[16]{0:T(128)}, u32[]{:S(2)}) copy-start(s32[16]{0:T(128)} %param.19) | copy-start | bytes 196
  14.3 8.9 %copy-start.6 = (s32[16]{0:T(128)S(1)}, s32[16]{0:T(128)}, u32[]{:S(2)}) copy-start(s32[16]{0:T(128)} %param.18) | copy-start | bytes 196
  14.3 9.4 %copy-start.3 = (f32[64]{0:T(128)S(1)}, f32[64]{0:T(128)}, u32[]{:S(2)}) copy-start(f32[64]{0:T(128)} %param.17) | copy-start | bytes 772
  14.4 9.6 %copy-start.8 = (bf16[16,1]{0,1:T(2,128)(2,1)S(1)}, bf16[16,1]{0,1:T(2,128)(2,1)}, u32[]{:S(2)}) copy-start(bf16[16,1]{0,1:T(2,128)(2,1)} %param.25) | copy-start | bytes 100
  14.4 9.6 %copy-start = (s32[16,11]{1,0:T(8,128)S(1)}, s32[16,11]{1,0:T(8,128)}, u32[]{:S(2)}) copy-start(s32[16,11]{1,0:T(8,128)} %slot_ref.3) | copy-start | bytes 2116
  14.4 9.6 %copy-start.1 = (bf16[16,11]{1,0:T(8,128)(2,1)S(1)}, bf16[16,11]{1,0:T(8,128)(2,1)}, u32[]{:S(2)}) copy-start(bf16[16,11]{1,0:T(8,128)(2,1)} %weight_ref.3) | copy-start | bytes 1060
  14.4 9.6 %copy-start.2 = (s32[16]{0:T(128)S(1)}, s32[16]{0:T(128)}, u32[]{:S(2)}) copy-start(s32[16]{0:T(128)} %count_ref.3) | copy-start | bytes 196
  16.8 27.8 %collective-permute-start.3 = (bf16[4,256,256]{2,1,0:T(8,128)(2,1)S(1)}, bf16[4,256,256]{2,1,0:T(8,128)(2,1)S(1)}, u32[]{:S(2)}, u32[]{:S(2)}) collective-permute-start(bf16[4,256,256]{2,1,0:T(8,128)(2,1)S(1)} %get-tuple-element.46), channel_id=1, source_target_pairs={{0,8},{4,0},{8,12},{12,4},{1,9},{5,1},{9,13},{13,5},{2,10},{6,2},{... | collective-permute-start | bytes 1572872 | tf_op jit(solution)/shard_map/ppermute | solution.py:505
  21.7 22.9 %collective-permute-start.5 = (bf16[2,256,256]{2,1,0:T(8,128)(2,1)S(1)}, bf16[2,256,256]{2,1,0:T(8,128)(2,1)S(1)}, u32[]{:S(2)}, u32[]{:S(2)}) collective-permute-start(bf16[2,256,256]{2,1,0:T(8,128)(2,1)S(1)} %get-tuple-element.48), channel_id=1, source_target_pairs={{0,12},{4,8},{8,4},{12,0},{1,13},{5,9},{9,5},{13,1},{2,14},{6,10},... | collective-permute-start | bytes 786440 | tf_op jit(solution)/shard_map/ppermute | solution.py:505
  47.4 13.3 %collective-permute-start.7 = (bf16[6,256,256]{2,1,0:T(8,128)(2,1)S(1)}, bf16[6,256,256]{2,1,0:T(8,128)(2,1)S(1)}, u32[]{:S(2)}, u32[]{:S(2)}) collective-permute-start(bf16[6,256,256]{2,1,0:T(8,128)(2,1)S(1)} %finish.4.refs_0_), channel_id=1, source_target_pairs={{0,1},{1,0},{2,3},{3,2},{4,5},{5,4},{6,7},{7,6},{8,9},{9,8},{10,11... | collective-permute-start | bytes 2359304 | tf_op jit(solution)/shard_map/ppermute | solution.py:516
  47.4 10.6 %collective-permute-start.6 = (bf16[2,256,256]{2,1,0:T(8,128)(2,1)S(1)}, bf16[2,256,256]{2,1,0:T(8,128)(2,1)S(1)}, u32[]{:S(2)}, u32[]{:S(2)}) collective-permute-start(bf16[2,256,256]{2,1,0:T(8,128)(2,1)S(1)} %get-tuple-element.50), channel_id=1, source_target_pairs={{0,12},{4,8},{8,4},{12,0},{1,13},{5,9},{9,5},{13,1},{2,14},{6,10},... | collective-permute-start | bytes 786440 | tf_op jit(solution)/shard_map/ppermute | solution.py:505
  59.1 1.6 %collective-permute-start.8 = (bf16[2,256,256]{2,1,0:T(8,128)(2,1)S(1)}, bf16[2,256,256]{2,1,0:T(8,128)(2,1)S(1)}, u32[]{:S(2)}, u32[]{:S(2)}) collective-permute-start(bf16[2,256,256]{2,1,0:T(8,128)(2,1)S(1)} %finish.5.refs_2_), channel_id=1, source_target_pairs={{0,1},{1,0},{2,3},{3,2},{4,5},{5,4},{6,7},{7,6},{8,9},{9,8},{10,11... | collective-permute-start | bytes 786440 | tf_op jit(solution)/shard_map/ppermute | solution.py:522
  61.4 37.3 %collective-permute-start.9 = (bf16[4,256,256]{2,1,0:T(8,128)(2,1)S(1)}, bf16[4,256,256]{2,1,0:T(8,128)(2,1)S(1)}, u32[]{:S(2)}, u32[]{:S(2)}) collective-permute-start(bf16[4,256,256]{2,1,0:T(8,128)(2,1)S(1)} %gather_again.3), channel_id=1, source_target_pairs={{0,4},{4,12},{8,0},{12,8},{1,5},{5,13},{9,1},{13,9},{2,6},{6,14},{... | collective-permute-start | bytes 1572872 | tf_op jit(solution)/shard_map/ppermute | solution.py:494
  68.2 30.5 %collective-permute-start.10 = (bf16[4,256,256]{2,1,0:T(8,128)(2,1)S(1)}, bf16[4,256,256]{2,1,0:T(8,128)(2,1)S(1)}, u32[]{:S(2)}, u32[]{:S(2)}) collective-permute-start(bf16[4,256,256]{2,1,0:T(8,128)(2,1)S(1)} %gather_again.4), channel_id=1, source_target_pairs={{0,8},{4,0},{8,12},{12,4},{1,9},{5,1},{9,13},{13,5},{2,10},{6,2},{... | collective-permute-start | bytes 1572872 | tf_op jit(solution)/shard_map/ppermute | solution.py:505
  69.0 29.7 %collective-permute-start.11 = (bf16[2,256,256]{2,1,0:T(8,128)(2,1)S(1)}, bf16[2,256,256]{2,1,0:T(8,128)(2,1)S(1)}, u32[]{:S(2)}, u32[]{:S(2)}) collective-permute-start(bf16[2,256,256]{2,1,0:T(8,128)(2,1)S(1)} %get-tuple-element.57), channel_id=1, source_target_pairs={{0,12},{4,8},{8,4},{12,0},{1,13},{5,9},{9,5},{13,1},{2,14},{6,10},... | collective-permute-start | bytes 786440 | tf_op jit(solution)/shard_map/ppermute | solution.py:505
  71.6 31.9 %collective-permute-start.13 = (bf16[2,256,256]{2,1,0:T(8,128)(2,1)S(1)}, bf16[2,256,256]{2,1,0:T(8,128)(2,1)S(1)}, u32[]{:S(2)}, u32[]{:S(2)}) collective-permute-start(bf16[2,256,256]{2,1,0:T(8,128)(2,1)S(1)} %get-tuple-element.60), channel_id=1, source_target_pairs={{0,12},{4,8},{8,4},{12,0},{1,13},{5,9},{9,5},{13,1},{2,14},{6,10},... | collective-permute-start | bytes 786440 | tf_op jit(solution)/shard_map/ppermute | solution.py:505
  101.4 24.6 %collective-permute-start.12 = (bf16[6,256,256]{2,1,0:T(8,128)(2,1)S(1)}, bf16[6,256,256]{2,1,0:T(8,128)(2,1)S(1)}, u32[]{:S(2)}, u32[]{:S(2)}) collective-permute-start(bf16[6,256,256]{2,1,0:T(8,128)(2,1)S(1)} %get-tuple-element.59.refs_0_), channel_id=1, source_target_pairs={{0,1},{1,0},{2,3},{3,2},{4,5},{5,4},{6,7},{7,6},{8,9},{9,8},{10,11... | collective-permute-start | bytes 2359304 | tf_op jit(solution)/shard_map/ppermute | solution.py:516
  105.0 1.2 collective-permute-start.15
  106.2 3.6 %collective-permute-start.16 = (f32[64]{0:T(128)S(1)}, f32[64]{0:T(128)S(1)}, u32[]{:S(2)}, u32[]{:S(2)}) collective-permute-start(f32[64]{0:T(128)S(1)} %add.110), channel_id=1, source_target_pairs={{0,2},{2,0},{1,3},{3,1},{4,6},{6,4},{5,7},{7,5},{8,10},{10,8},{9,1... | collective-permute-start | bytes 776 | tf_op jit(solution)/shard_map/ppermute | solution.py:385
  109.7 5.4 %collective-permute-start.17 = (f32[64]{0:T(128)S(1)}, f32[64]{0:T(128)S(1)}, u32[]{:S(2)}, u32[]{:S(2)}) collective-permute-start(f32[64]{0:T(128)S(1)} %add.111), channel_id=1, source_target_pairs={{0,12},{4,8},{8,4},{12,0},{1,13},{5,9},{9,5},{13,1},{2,14},{6,10},... | collective-permute-start | bytes 776 | tf_op jit(solution)/shard_map/ppermute | solution.py:385
  112.2 13.7 %collective-permute-start.14 = (bf16[2,256,256]{2,1,0:T(8,128)(2,1)S(1)}, bf16[2,256,256]{2,1,0:T(8,128)(2,1)S(1)}, u32[]{:S(2)}, u32[]{:S(2)}) collective-permute-start(bf16[2,256,256]{2,1,0:T(8,128)(2,1)S(1)} %get-tuple-element.61.refs_1_), channel_id=1, source_target_pairs={{0,1},{1,0},{2,3},{3,2},{4,5},{5,4},{6,7},{7,6},{8,9},{9,8},{10,11... | collective-permute-start | bytes 786440 | tf_op jit(solution)/shard_map/ppermute | solution.py:522
  115.1 10.3 %collective-permute-start.18 = (f32[64]{0:T(128)S(1)}, f32[64]{0:T(128)S(1)}, u32[]{:S(2)}, u32[]{:S(2)}) collective-permute-start(f32[64]{0:T(128)S(1)} %add.112), channel_id=1, source_target_pairs={{0,4},{4,0},{8,12},{12,8},{1,5},{5,1},{9,13},{13,9},{2,6},{6,2},{1... | collective-permute-start | bytes 776 | tf_op jit(solution)/shard_map/ppermute | solution.py:385

commit v13 on v12

--- a/solution.py
+++ b/solution.py
@@ -414,11 +414,11 @@
     here = jnp.stack([row, core]).astype(jnp.int32)
     tail = max(1, cap // 2)
     lead = [(1, 0, cap)]
-    inner = [(step, 0, cap) for step in range(2, rows - 1)]
-    outer = [(rows - 1, 0, cap - tail)] * (cap > tail) + [(rows - 1, cap - tail, tail)]
+    rest = [(step, 0, cap) for step in range(2, rows - 1)]
+    rest += [(rows - 1, 0, cap - tail)] * (cap > tail) + [(rows - 1, cap - tail, tail)]
     request = lax.ppermute(packed, "row", asked_of(rows, 1))
     requests = [
-        lax.ppermute(packed, "row", asked_of(rows, d)) for d in range(2, rows - 1)
+        lax.ppermute(packed, "row", asked_of(rows, d)) for d in range(2, rows)
     ]
     asked_lead, send_lead = gather_first([request], lead, here, amplitudes, rows, cap)
 
@@ -493,15 +493,11 @@
             (send_lead,) = gather_again(asked_lead, local_spots[1], stores, lead, cap)
         arrived = [lax.ppermute(send_lead, "row", sent(rows, 1))]
         if sweep == 0:
-            request = lax.ppermute(packed, "row", asked_of(rows, rows - 1))
             (*requests, _) = lax.optimization_barrier((*requests, send_lead))
-            asked, *sends = gather_first(requests, inner, here, amplitudes, rows, cap)
-            request, _ = lax.optimization_barrier((request, sends[0]))
-            asked_last, *sends_last = gather_first([request], outer, here, amplitudes, rows, cap)
+            asked, *sends = gather_first(requests, rest, here, amplitudes, rows, cap)
         else:
-            sends = gather_again(asked, local_spots[1], stores, inner, cap)
-            sends_last = gather_again(asked_last, local_spots[1], stores, outer, cap)
-        for part, send in zip(inner + outer, [*sends, *sends_last]):
+            sends = gather_again(asked, local_spots[1], stores, rest, cap)
+        for part, send in zip(rest, sends):
             arrived.append(lax.ppermute(send, "row", sent(rows, part[0])))
         *prepared, at_home = prepare(
             own, ats[again], homes[again], columns[again], near_count, shift, near, whole,

time: 128 us -> 128 us (level)
  waiting for transfers between devices: 52.5 us -> 55.3 us
  Pallas kernels: 33.7 us -> 31 us
    ppermute x2, waiting for transfers between devices: 1.33 us -> 9.72 us  [per_device(): arrived = [lax.ppermute(send_lead, 'row', sent(rows, 1))]]
    ppermute x6, waiting for transfers between devices: 42.3 us -> 36.9 us  [per_device(): arrived.append(lax.ppermute(send, 'row', sent(rows, part[0])))]
    ppermute x1 -> x0, starting transfers between devices: 5.08 us -> none  [per_device(): request = lax.ppermute(packed, 'row', asked_of(rows, rows - 1))]
    ppermute x1 -> x2, starting transfers between devices: 0.01 us -> 5.08 us  [per_device(): lax.ppermute(packed, 'row', asked_of(rows, d))]
    pallas_call x3 -> x2, Pallas kernels: 7.19 us -> 5.05 us  [gather_first(): pl.pallas_call(body, out_shape=[jax.ShapeDtypeStruct((count_of * (cap + 1...]
  transfers between devices with their start and end apart: 19 -> 19, of which waited for: 10 -> 10; matrix products, arithmetic and copies ran while one was open for 2% -> 2% of each run, Pallas kernels for 23% -> 21%
where the time goes in v13:
time: 128 us
  waiting for transfers between devices  55.3 us (43%)
  starting transfers between devices  37.2 us (29%)
  Pallas kernels  31 us (24%)
  other arithmetic  3.03 us (2%)
    ppermute x6, waiting for transfers between devices, per_device(): arrived.append(lax.ppermute(send, 'row', sent(rows, part[0])))  36.9 us
    pallas_call x2, Pallas kernels, prepare(): pl.pallas_call(body, grid_spec=pltpu.PrefetchScalarGridSpec(num_scalar_pr...  14.7 us
    ppermute x4, starting transfers between devices, add_over(): lax.ppermute(values, name, [(r, r ^ step) for r in range(size)])  12.6 us
    ppermute x2, waiting for transfers between devices, per_device(): arrived = [lax.ppermute(send_lead, 'row', sent(rows, 1))]  9.72 us
    ppermute x6, starting transfers between devices, per_device(): arrived.append(lax.ppermute(send, 'row', sent(rows, part[0])))  9.37 us
    ppermute x2, starting transfers between devices, per_device(): arrived = [lax.ppermute(send_lead, 'row', sent(rows, 1))]  7 us
    pallas_call x4, Pallas kernels, finish(): pl.pallas_call(body, out_shape=out_shape, in_specs=[pl.BlockSpec(memory_s...  6.62 us
    ppermute x4, waiting for transfers between devices, add_over(): lax.ppermute(values, name, [(r, r ^ step) for r in range(size)])  6.08 us
  transfers between devices with their start and end apart: 19, of which 10 were waited for; matrix products, arithmetic and copies ran while one was open for 2% of the time, Pallas kernels for 21%

profile of v13, /device:TPU:0, one launch (start us, length us, event | category | flops | bytes accessed | tf_op | source)
XLA Modules:
  0.0 127.6 jit_solution(6725909742502334935)
XLA Ops:
  1.4 5.1 %collective-permute-start.3 = (s32[16]{0:T(128)S(1)}, s32[16]{0:T(128)S(1)}, u32[]{:S(2)}, u32[]{:S(2)}) collective-permute-start(s32[16]{0:T(128)S(1)} %bitcast_add_fusion), channel_id=1, source_target_pairs={{12,0},{8,4},{4,8},{0,12},{13,1},{9,5},{5,9},{1,13},{14,2},{10,6},... | collective-permute-start | bytes 200 | tf_op jit(solution)/shard_map/ppermute | solution.py:421
  6.4 2.9 %collective-permute-start = (s32[16]{0:T(128)S(1)}, s32[16]{0:T(128)S(1)}, u32[]{:S(2)}, u32[]{:S(2)}) collective-permute-start(s32[16]{0:T(128)S(1)} %bitcast_add_fusion), channel_id=1, source_target_pairs={{4,0},{12,4},{0,8},{8,12},{5,1},{13,5},{1,9},{9,13},{6,2},{14,6},{... | collective-permute-start | bytes 200 | tf_op jit(solution)/shard_map/ppermute | solution.py:419
  9.5 1.2 collective-permute-done.refs_0_
  10.7 2.4 %gather_first.2 = (s32[5]{0:T(128)S(1)}, bf16[4,256,256]{2,1,0:T(8,128)(2,1)S(1)}) custom-call(s32[2]{0:T(128)S(1)} %pad_add_fusion.place_ref, s32[16]{0:T(128)S(1)} %collective-permute-done.refs_0_, bf16[16,256,256]{2,1,0:T(8,128)(2,1)} %refs_2_.4), custom_call_target="tpu_custom_call" | custom-call | bytes 1048576 | tf_op jit(solution)/shard_map/gather_first/pallas_call | solution.py:115
  13.0 0.9 collective-permute-start.1
  14.3 2.7 %gather_first.3 = (s32[10]{0:T(128)S(1)}, bf16[4,256,256]{2,1,0:T(8,128)(2,1)S(1)}, bf16[2,256,256]{2,1,0:T(8,128)(2,1)S(1)}, bf16[2,256,256]{2,1,0:T(8,128)(2,1)S(1)}) custom-call(s32[2]{0:T(128)S(1)} %pad_add_fusion.place_ref, s32[16]{0:T(128)S(1)} %collective-permute-done.2.refs_0_, s32[16]{0:T(128)S(1)} %collective-permute-done.3.refs_1_, ...), custom_call_target="tpu_custom_call" | custom-call | bytes 2097152 | tf_op jit(solution)/shard_map/gather_first/pallas_call | solution.py:115
  17.0 3.9 %collective-permute-start.5 = (bf16[2,256,256]{2,1,0:T(8,128)(2,1)S(1)}, bf16[2,256,256]{2,1,0:T(8,128)(2,1)S(1)}, u32[]{:S(2)}, u32[]{:S(2)}) collective-permute-start(bf16[2,256,256]{2,1,0:T(8,128)(2,1)S(1)} %get-tuple-element.48), channel_id=1, source_target_pairs={{0,12},{4,8},{8,4},{12,0},{1,13},{5,9},{9,5},{13,1},{2,14},{6,10},... | collective-permute-start | bytes 786440 | tf_op jit(solution)/shard_map/ppermute | solution.py:501
  21.7 7.7 %prepare.2 = (f32[8,256,256]{2,1,0:T(8,128)S(1)}, f32[8,256,256]{2,1,0:T(8,128)S(1)}, f32[8,256,256]{2,1,0:T(8,128)S(1)}, bf16[8,256,256]{2,1,0:T(8,128)(2,1)S(1)}, bf16[8,256,256]{2,1,0:T(8,128)(2,1)S(1)}) custom-call(s32[8]{0:T(128)S(1)} %get-tuple-element.69.own_ref.at_ref, s32[8]{0:T(128)S(1)} %get-tuple-element.69.own_ref.at_ref, ...), custom_call_target="tpu_custom_call" | custom-call | flops 805306368 | bytes 12582912 | tf_op jit(solution)/shard_map/prepare/pallas_call | solution.py:245
  29.7 6.5 %collective-permute-done.5.refs_2_ = bf16[2,256,256]{2,1,0:T(8,128)(2,1)S(1)} collective-permute-done((bf16[2,256,256]{2,1,0:T(8,128)(2,1)S(1)}, bf16[2,256,256]{2,1,0:T(8,128)(2,1)S(1)}, u32[]{:S(2)}, u32[]{:S(2)}) %collective-permute-start.5) | collective-permute-done | bytes 262176 | tf_op jit(solution)/shard_map/ppermute | solution.py:501
  36.2 9.7 %collective-permute-done.1.refs_0_ = bf16[4,256,256]{2,1,0:T(8,128)(2,1)S(1)} collective-permute-done((bf16[4,256,256]{2,1,0:T(8,128)(2,1)S(1)}, bf16[4,256,256]{2,1,0:T(8,128)(2,1)S(1)}, u32[]{:S(2)}, u32[]{:S(2)}) %collective-permute-start.1) | collective-permute-done | bytes 524320 | tf_op jit(solution)/shard_map/ppermute | solution.py:494
  45.9 1.4 %finish.4.refs_0_ = bf16[6,256,256]{2,1,0:T(8,128)(2,1)S(1)} custom-call(s32[24]{0:T(128)S(1)} %pad_add_fusion.2.number_ref, f32[8]{0:T(128)S(1)} %fusion.7.scale_ref, f32[8,256,256]{2,1,0:T(8,128)S(1)} %get-tuple-element.40.local_ref, f32[8,256,256]{2,1,0:T(8,128)S(1)} %get-tuple-element.41.rest_ref, f32[8,256,256]{2,1,0:T(8,128)S(1)} %get-tuple-element.42.recip_ref, ...), custom_call_target="tpu_custom_call" | custom-call | flops 402653184 | bytes 7077888 | tf_op jit(solution)/shard_map/finish/pallas_call | solution.py:328
  47.4 1.5 %collective-permute-start.6 = (bf16[2,256,256]{2,1,0:T(8,128)(2,1)S(1)}, bf16[2,256,256]{2,1,0:T(8,128)(2,1)S(1)}, u32[]{:S(2)}, u32[]{:S(2)}) collective-permute-start(bf16[2,256,256]{2,1,0:T(8,128)(2,1)S(1)} %get-tuple-element.50), channel_id=1, source_target_pairs={{0,12},{4,8},{8,4},{12,0},{1,13},{5,9},{9,5},{13,1},{2,14},{6,10},... | collective-permute-start | bytes 786440 | tf_op jit(solution)/shard_map/ppermute | solution.py:501
  49.0 9.1 %collective-permute-done.6.refs_3_ = bf16[2,256,256]{2,1,0:T(8,128)(2,1)S(1)} collective-permute-done((bf16[2,256,256]{2,1,0:T(8,128)(2,1)S(1)}, bf16[2,256,256]{2,1,0:T(8,128)(2,1)S(1)}, u32[]{:S(2)}, u32[]{:S(2)}) %collective-permute-start.6) | collective-permute-done | bytes 262176 | tf_op jit(solution)/shard_map/ppermute | solution.py:501
  58.0 1.0 finish.5.refs_2_
  59.2 1.5 %collective-permute-done.8.refs_3_ = bf16[2,256,256]{2,1,0:T(8,128)(2,1)S(1)} collective-permute-done((bf16[2,256,256]{2,1,0:T(8,128)(2,1)S(1)}, bf16[2,256,256]{2,1,0:T(8,128)(2,1)S(1)}, u32[]{:S(2)}, u32[]{:S(2)}) %collective-permute-start.8) | collective-permute-done | bytes 262176 | tf_op jit(solution)/shard_map/ppermute | solution.py:518
  61.4 6.1 %collective-permute-start.9 = (bf16[4,256,256]{2,1,0:T(8,128)(2,1)S(1)}, bf16[4,256,256]{2,1,0:T(8,128)(2,1)S(1)}, u32[]{:S(2)}, u32[]{:S(2)}) collective-permute-start(bf16[4,256,256]{2,1,0:T(8,128)(2,1)S(1)} %gather_again.2), channel_id=1, source_target_pairs={{0,4},{4,12},{8,0},{12,8},{1,5},{5,13},{9,1},{13,9},{2,6},{6,14},{... | collective-permute-start | bytes 1572872 | tf_op jit(solution)/shard_map/ppermute | solution.py:494
  67.5 0.8 gather_again.3
  68.5 2.4 %collective-permute-start.11 = (bf16[2,256,256]{2,1,0:T(8,128)(2,1)S(1)}, bf16[2,256,256]{2,1,0:T(8,128)(2,1)S(1)}, u32[]{:S(2)}, u32[]{:S(2)}) collective-permute-start(bf16[2,256,256]{2,1,0:T(8,128)(2,1)S(1)} %get-tuple-element.57), channel_id=1, source_target_pairs={{0,12},{4,8},{8,4},{12,0},{1,13},{5,9},{9,5},{13,1},{2,14},{6,10},... | collective-permute-start | bytes 786440 | tf_op jit(solution)/shard_map/ppermute | solution.py:501
  71.0 1.5 %collective-permute-start.13 = (bf16[2,256,256]{2,1,0:T(8,128)(2,1)S(1)}, bf16[2,256,256]{2,1,0:T(8,128)(2,1)S(1)}, u32[]{:S(2)}, u32[]{:S(2)}) collective-permute-start(bf16[2,256,256]{2,1,0:T(8,128)(2,1)S(1)} %get-tuple-element.60), channel_id=1, source_target_pairs={{0,12},{4,8},{8,4},{12,0},{1,13},{5,9},{9,5},{13,1},{2,14},{6,10},... | collective-permute-start | bytes 786440 | tf_op jit(solution)/shard_map/ppermute | solution.py:501
  72.6 6.9 %prepare.3 = (f32[8,256,256]{2,1,0:T(8,128)S(1)}, f32[8,256,256]{2,1,0:T(8,128)S(1)}, f32[8,256,256]{2,1,0:T(8,128)S(1)}, bf16[8,256,256]{2,1,0:T(8,128)(2,1)S(1)}, bf16[8,256,256]{2,1,0:T(8,128)(2,1)S(1)}) custom-call(s32[8]{0:T(128)S(1)} %get-tuple-element.69.own_ref.at_ref, s32[8]{0:T(128)S(1)} %iota.29.at_ref, s32[8]{0:T(128)S(1)} %get-tuple-element.71.home_ref, ...), custom_call_target="tpu_custom_call" | custom-call | flops 805306368 | bytes 12582912 | tf_op jit(solution)/shard_map/prepare/pallas_call | solution.py:245
  79.5 19.2 %collective-permute-done.11.refs_2_ = bf16[2,256,256]{2,1,0:T(8,128)(2,1)S(1)} collective-permute-done((bf16[2,256,256]{2,1,0:T(8,128)(2,1)S(1)}, bf16[2,256,256]{2,1,0:T(8,128)(2,1)S(1)}, u32[]{:S(2)}, u32[]{:S(2)}) %collective-permute-start.11) | collective-permute-done | bytes 262176 | tf_op jit(solution)/shard_map/ppermute | solution.py:501
  98.7 2.7 %finish.6 = (bf16[6,256,256]{2,1,0:T(8,128)(2,1)S(1)}, f32[1,64]{1,0:T(1,128)S(1)}) custom-call(s32[24]{0:T(128)S(1)} %pad_add_fusion.2.number_ref, f32[8]{0:T(128)S(1)} %fusion.7.scale_ref, f32[8,256,256]{2,1,0:T(8,128)S(1)} %get-tuple-element.51.local_ref, f32[8,256,256]{2,1,0:T(8,128)S(1)} %get-tuple-element.52.rest_ref, ...), custom_call_target="tpu_custom_call" | custom-call | flops 402653184 | bytes 7077888 | tf_op jit(solution)/shard_map/finish/pallas_call | solution.py:328
  101.4 2.1 %collective-permute-done.13.refs_3_ = bf16[2,256,256]{2,1,0:T(8,128)(2,1)S(1)} collective-permute-done((bf16[2,256,256]{2,1,0:T(8,128)(2,1)S(1)}, bf16[2,256,256]{2,1,0:T(8,128)(2,1)S(1)}, u32[]{:S(2)}, u32[]{:S(2)}) %collective-permute-start.13) | collective-permute-done | bytes 262176 | tf_op jit(solution)/shard_map/ppermute | solution.py:501
  103.5 1.5 %finish.7 = (bf16[2,256,256]{2,1,0:T(8,128)(2,1)S(1)}, f32[1,64]{1,0:T(1,128)S(1)}) custom-call(s32[24]{0:T(128)S(1)} %pad_add_fusion.2.number_ref, f32[8]{0:T(128)S(1)} %fusion.7.scale_ref, f32[8,256,256]{2,1,0:T(8,128)S(1)} %get-tuple-element.51.local_ref, f32[8,256,256]{2,1,0:T(8,128)S(1)} %get-tuple-element.52.rest_ref, ...), custom_call_target="tpu_custom_call" | custom-call | flops 134217728 | bytes 2359296 | tf_op jit(solution)/shard_map/finish/pallas_call | solution.py:328
  105.0 1.2 collective-permute-done.15
  106.2 1.5 %collective-permute-start.16 = (f32[64]{0:T(128)S(1)}, f32[64]{0:T(128)S(1)}, u32[]{:S(2)}, u32[]{:S(2)}) collective-permute-start(f32[64]{0:T(128)S(1)} %add.110), channel_id=1, source_target_pairs={{0,2},{2,0},{1,3},{3,1},{4,6},{6,4},{5,7},{7,5},{8,10},{10,8},{9,1... | collective-permute-start | bytes 776 | tf_op jit(solution)/shard_map/ppermute | solution.py:385
  107.6 2.1 %collective-permute-done.16 = f32[64]{0:T(128)S(1)} collective-permute-done((f32[64]{0:T(128)S(1)}, f32[64]{0:T(128)S(1)}, u32[]{:S(2)}, u32[]{:S(2)}) %collective-permute-start.16) | collective-permute-done | bytes 288 | tf_op jit(solution)/shard_map/ppermute | solution.py:385
  109.7 2.4 %collective-permute-start.17 = (f32[64]{0:T(128)S(1)}, f32[64]{0:T(128)S(1)}, u32[]{:S(2)}, u32[]{:S(2)}) collective-permute-start(f32[64]{0:T(128)S(1)} %add.111), channel_id=1, source_target_pairs={{0,12},{4,8},{8,4},{12,0},{1,13},{5,9},{9,5},{13,1},{2,14},{6,10},... | collective-permute-start | bytes 776 | tf_op jit(solution)/shard_map/ppermute | solution.py:385
  112.2 2.9 %collective-permute-done.17 = f32[64]{0:T(128)S(1)} collective-permute-done((f32[64]{0:T(128)S(1)}, f32[64]{0:T(128)S(1)}, u32[]{:S(2)}, u32[]{:S(2)}) %collective-permute-start.17) | collective-permute-done | bytes 288 | tf_op jit(solution)/shard_map/ppermute | solution.py:385
  115.1 8.8 %collective-permute-start.18 = (f32[64]{0:T(128)S(1)}, f32[64]{0:T(128)S(1)}, u32[]{:S(2)}, u32[]{:S(2)}) collective-permute-start(f32[64]{0:T(128)S(1)} %add.112), channel_id=1, source_target_pairs={{0,4},{4,0},{8,12},{12,8},{1,5},{5,1},{9,13},{13,9},{2,6},{6,2},{1... | collective-permute-start | bytes 776 | tf_op jit(solution)/shard_map/ppermute | solution.py:385
  123.9 1.5 %put_in_slots.2.refs_3_ = bf16[16,256,256]{2,1,0:T(8,128)(2,1)} custom-call(s32[6]{0:T(128)S(1)} %bitcast.14, bf16[6,256,256]{2,1,0:T(8,128)(2,1)S(1)} %get-tuple-element.59.refs_0_), custom_call_target="tpu_custom_call" | custom-call | bytes 1572864 | tf_op jit(solution)/shard_map/put_in_slots/pallas_call | solution.py:362
  125.9 1.7 %put_in_slots.3 = bf16[16,256,256]{2,1,0:T(8,128)(2,1)} custom-call(s32[10]{0:T(128)S(1)} %pad_add_fusion.1.slot_ref, bf16[6,256,256]{2,1,0:T(8,128)(2,1)S(1)} %collective-permute-done.12.refs_0_, bf16[2,256,256]{2,1,0:T(8,128)(2,1)S(1)} %get-tuple-element.61.refs_1_, ...), custom_call_target="tpu_custom_call", output_to_operand_aliasing={{}: (4, {})} | custom-call | bytes 2621440 | tf_op jit(solution)/shard_map/put_in_slots/pallas_call | solution.py:362
  (65 shorter events, 4.2 us)
Async XLA Ops:
  0.6 13.3 %copy-start.7 = (s32[16,1]{0,1:T(1,128)S(1)}, s32[16,1]{0,1:T(1,128)}, u32[]{:S(2)}) copy-start(s32[16,1]{0,1:T(1,128)} %param.23) | copy-start | bytes 196
  1.4 12.5 %collective-permute-start.3 = (s32[16]{0:T(128)S(1)}, s32[16]{0:T(128)S(1)}, u32[]{:S(2)}, u32[]{:S(2)}) collective-permute-start(s32[16]{0:T(128)S(1)} %bitcast_add_fusion), channel_id=1, source_target_pairs={{12,0},{8,4},{4,8},{0,12},{13,1},{9,5},{5,9},{1,13},{14,2},{10,6},... | collective-permute-start | bytes 200 | tf_op jit(solution)/shard_map/ppermute | solution.py:421
  6.4 7.5 %collective-permute-start.2 = (s32[16]{0:T(128)S(1)}, s32[16]{0:T(128)S(1)}, u32[]{:S(2)}, u32[]{:S(2)}) collective-permute-start(s32[16]{0:T(128)S(1)} %bitcast_add_fusion), channel_id=1, source_target_pairs={{8,0},{0,4},{12,8},{4,12},{9,1},{1,5},{13,9},{5,13},{10,2},{2,6},{... | collective-permute-start | bytes 200 | tf_op jit(solution)/shard_map/ppermute | solution.py:421
  6.4 4.2 %collective-permute-start = (s32[16]{0:T(128)S(1)}, s32[16]{0:T(128)S(1)}, u32[]{:S(2)}, u32[]{:S(2)}) collective-permute-start(s32[16]{0:T(128)S(1)} %bitcast_add_fusion), channel_id=1, source_target_pairs={{4,0},{12,4},{0,8},{8,12},{5,1},{13,5},{1,9},{9,13},{6,2},{14,6},{... | collective-permute-start | bytes 200 | tf_op jit(solution)/shard_map/ppermute | solution.py:419
  9.5 11.5 %copy-start.4 = (s32[16,1]{0,1:T(1,128)S(1)}, s32[16,1]{0,1:T(1,128)}, u32[]{:S(2)}) copy-start(s32[16,1]{0,1:T(1,128)} %param.24) | copy-start | bytes 196
  9.5 11.5 %copy-start.5 = (s32[16]{0:T(128)S(1)}, s32[16]{0:T(128)}, u32[]{:S(2)}) copy-start(s32[16]{0:T(128)} %param.19) | copy-start | bytes 196
  9.5 11.5 %copy-start.6 = (s32[16]{0:T(128)S(1)}, s32[16]{0:T(128)}, u32[]{:S(2)}) copy-start(s32[16]{0:T(128)} %param.18) | copy-start | bytes 196
  9.5 12.0 %copy-start.3 = (f32[64]{0:T(128)S(1)}, f32[64]{0:T(128)}, u32[]{:S(2)}) copy-start(f32[64]{0:T(128)} %param.17) | copy-start | bytes 772
  9.5 12.2 %copy-start.8 = (bf16[16,1]{0,1:T(2,128)(2,1)S(1)}, bf16[16,1]{0,1:T(2,128)(2,1)}, u32[]{:S(2)}) copy-start(bf16[16,1]{0,1:T(2,128)(2,1)} %param.25) | copy-start | bytes 100
  9.5 12.2 %copy-start = (s32[16,11]{1,0:T(8,128)S(1)}, s32[16,11]{1,0:T(8,128)}, u32[]{:S(2)}) copy-start(s32[16,11]{1,0:T(8,128)} %slot_ref.3) | copy-start | bytes 2116
  9.5 12.2 %copy-start.1 = (bf16[16,11]{1,0:T(8,128)(2,1)S(1)}, bf16[16,11]{1,0:T(8,128)(2,1)}, u32[]{:S(2)}) copy-start(bf16[16,11]{1,0:T(8,128)(2,1)} %weight_ref.3) | copy-start | bytes 1060
  9.5 12.2 %copy-start.2 = (s32[16]{0:T(128)S(1)}, s32[16]{0:T(128)}, u32[]{:S(2)}) copy-start(s32[16]{0:T(128)} %count_ref.3) | copy-start | bytes 196
  13.0 32.9 %collective-permute-start.1 = (bf16[4,256,256]{2,1,0:T(8,128)(2,1)S(1)}, bf16[4,256,256]{2,1,0:T(8,128)(2,1)S(1)}, u32[]{:S(2)}, u32[]{:S(2)}) collective-permute-start(bf16[4,256,256]{2,1,0:T(8,128)(2,1)S(1)} %get-tuple-element.44), channel_id=1, source_target_pairs={{0,4},{4,12},{8,0},{12,8},{1,5},{5,13},{9,1},{13,9},{2,6},{6,14},{... | collective-permute-start | bytes 1572872 | tf_op jit(solution)/shard_map/ppermute | solution.py:494
  17.0 19.2 %collective-permute-start.5 = (bf16[2,256,256]{2,1,0:T(8,128)(2,1)S(1)}, bf16[2,256,256]{2,1,0:T(8,128)(2,1)S(1)}, u32[]{:S(2)}, u32[]{:S(2)}) collective-permute-start(bf16[2,256,256]{2,1,0:T(8,128)(2,1)S(1)} %get-tuple-element.48), channel_id=1, source_target_pairs={{0,12},{4,8},{8,4},{12,0},{1,13},{5,9},{9,5},{13,1},{2,14},{6,10},... | collective-permute-start | bytes 786440 | tf_op jit(solution)/shard_map/ppermute | solution.py:501
  20.9 25.0 %collective-permute-start.4 = (bf16[4,256,256]{2,1,0:T(8,128)(2,1)S(1)}, bf16[4,256,256]{2,1,0:T(8,128)(2,1)S(1)}, u32[]{:S(2)}, u32[]{:S(2)}) collective-permute-start(bf16[4,256,256]{2,1,0:T(8,128)(2,1)S(1)} %get-tuple-element.47), channel_id=1, source_target_pairs={{0,8},{4,0},{8,12},{12,4},{1,9},{5,1},{9,13},{13,5},{2,10},{6,2},{... | collective-permute-start | bytes 1572872 | tf_op jit(solution)/shard_map/ppermute | solution.py:501
  47.4 13.3 %collective-permute-start.7 = (bf16[6,256,256]{2,1,0:T(8,128)(2,1)S(1)}, bf16[6,256,256]{2,1,0:T(8,128)(2,1)S(1)}, u32[]{:S(2)}, u32[]{:S(2)}) collective-permute-start(bf16[6,256,256]{2,1,0:T(8,128)(2,1)S(1)} %finish.4.refs_0_), channel_id=1, source_target_pairs={{0,1},{1,0},{2,3},{3,2},{4,5},{5,4},{6,7},{7,6},{8,9},{9,8},{10,11... | collective-permute-start | bytes 2359304 | tf_op jit(solution)/shard_map/ppermute | solution.py:512
  47.4 10.6 %collective-permute-start.6 = (bf16[2,256,256]{2,1,0:T(8,128)(2,1)S(1)}, bf16[2,256,256]{2,1,0:T(8,128)(2,1)S(1)}, u32[]{:S(2)}, u32[]{:S(2)}) collective-permute-start(bf16[2,256,256]{2,1,0:T(8,128)(2,1)S(1)} %get-tuple-element.50), channel_id=1, source_target_pairs={{0,12},{4,8},{8,4},{12,0},{1,13},{5,9},{9,5},{13,1},{2,14},{6,10},... | collective-permute-start | bytes 786440 | tf_op jit(solution)/shard_map/ppermute | solution.py:501
  59.1 1.6 %collective-permute-start.8 = (bf16[2,256,256]{2,1,0:T(8,128)(2,1)S(1)}, bf16[2,256,256]{2,1,0:T(8,128)(2,1)S(1)}, u32[]{:S(2)}, u32[]{:S(2)}) collective-permute-start(bf16[2,256,256]{2,1,0:T(8,128)(2,1)S(1)} %finish.5.refs_2_), channel_id=1, source_target_pairs={{0,1},{1,0},{2,3},{3,2},{4,5},{5,4},{6,7},{7,6},{8,9},{9,8},{10,11... | collective-permute-start | bytes 786440 | tf_op jit(solution)/shard_map/ppermute | solution.py:518
  61.4 37.3 %collective-permute-start.9 = (bf16[4,256,256]{2,1,0:T(8,128)(2,1)S(1)}, bf16[4,256,256]{2,1,0:T(8,128)(2,1)S(1)}, u32[]{:S(2)}, u32[]{:S(2)}) collective-permute-start(bf16[4,256,256]{2,1,0:T(8,128)(2,1)S(1)} %gather_again.2), channel_id=1, source_target_pairs={{0,4},{4,12},{8,0},{12,8},{1,5},{5,13},{9,1},{13,9},{2,6},{6,14},{... | collective-permute-start | bytes 1572872 | tf_op jit(solution)/shard_map/ppermute | solution.py:494
  68.3 30.4 %collective-permute-start.10 = (bf16[4,256,256]{2,1,0:T(8,128)(2,1)S(1)}, bf16[4,256,256]{2,1,0:T(8,128)(2,1)S(1)}, u32[]{:S(2)}, u32[]{:S(2)}) collective-permute-start(bf16[4,256,256]{2,1,0:T(8,128)(2,1)S(1)} %get-tuple-element.56), channel_id=1, source_target_pairs={{0,8},{4,0},{8,12},{12,4},{1,9},{5,1},{9,13},{13,5},{2,10},{6,2},{... | collective-permute-start | bytes 1572872 | tf_op jit(solution)/shard_map/ppermute | solution.py:501
  68.5 30.2 %collective-permute-start.11 = (bf16[2,256,256]{2,1,0:T(8,128)(2,1)S(1)}, bf16[2,256,256]{2,1,0:T(8,128)(2,1)S(1)}, u32[]{:S(2)}, u32[]{:S(2)}) collective-permute-start(bf16[2,256,256]{2,1,0:T(8,128)(2,1)S(1)} %get-tuple-element.57), channel_id=1, source_target_pairs={{0,12},{4,8},{8,4},{12,0},{1,13},{5,9},{9,5},{13,1},{2,14},{6,10},... | collective-permute-start | bytes 786440 | tf_op jit(solution)/shard_map/ppermute | solution.py:501
  71.0 32.5 %collective-permute-start.13 = (bf16[2,256,256]{2,1,0:T(8,128)(2,1)S(1)}, bf16[2,256,256]{2,1,0:T(8,128)(2,1)S(1)}, u32[]{:S(2)}, u32[]{:S(2)}) collective-permute-start(bf16[2,256,256]{2,1,0:T(8,128)(2,1)S(1)} %get-tuple-element.60), channel_id=1, source_target_pairs={{0,12},{4,8},{8,4},{12,0},{1,13},{5,9},{9,5},{13,1},{2,14},{6,10},... | collective-permute-start | bytes 786440 | tf_op jit(solution)/shard_map/ppermute | solution.py:501
  101.4 24.6 %collective-permute-start.12 = (bf16[6,256,256]{2,1,0:T(8,128)(2,1)S(1)}, bf16[6,256,256]{2,1,0:T(8,128)(2,1)S(1)}, u32[]{:S(2)}, u32[]{:S(2)}) collective-permute-start(bf16[6,256,256]{2,1,0:T(8,128)(2,1)S(1)} %get-tuple-element.59.refs_0_), channel_id=1, source_target_pairs={{0,1},{1,0},{2,3},{3,2},{4,5},{5,4},{6,7},{7,6},{8,9},{9,8},{10,11... | collective-permute-start | bytes 2359304 | tf_op jit(solution)/shard_map/ppermute | solution.py:512
  105.0 1.2 collective-permute-start.15
  106.2 3.6 %collective-permute-start.16 = (f32[64]{0:T(128)S(1)}, f32[64]{0:T(128)S(1)}, u32[]{:S(2)}, u32[]{:S(2)}) collective-permute-start(f32[64]{0:T(128)S(1)} %add.110), channel_id=1, source_target_pairs={{0,2},{2,0},{1,3},{3,1},{4,6},{6,4},{5,7},{7,5},{8,10},{10,8},{9,1... | collective-permute-start | bytes 776 | tf_op jit(solution)/shard_map/ppermute | solution.py:385
  109.7 5.4 %collective-permute-start.17 = (f32[64]{0:T(128)S(1)}, f32[64]{0:T(128)S(1)}, u32[]{:S(2)}, u32[]{:S(2)}) collective-permute-start(f32[64]{0:T(128)S(1)} %add.111), channel_id=1, source_target_pairs={{0,12},{4,8},{8,4},{12,0},{1,13},{5,9},{9,5},{13,1},{2,14},{6,10},... | collective-permute-start | bytes 776 | tf_op jit(solution)/shard_map/ppermute | solution.py:385
  112.2 13.7 %collective-permute-start.14 = (bf16[2,256,256]{2,1,0:T(8,128)(2,1)S(1)}, bf16[2,256,256]{2,1,0:T(8,128)(2,1)S(1)}, u32[]{:S(2)}, u32[]{:S(2)}) collective-permute-start(bf16[2,256,256]{2,1,0:T(8,128)(2,1)S(1)} %get-tuple-element.61.refs_1_), channel_id=1, source_target_pairs={{0,1},{1,0},{2,3},{3,2},{4,5},{5,4},{6,7},{7,6},{8,9},{9,8},{10,11... | collective-permute-start | bytes 786440 | tf_op jit(solution)/shard_map/ppermute | solution.py:518
  115.1 10.3 %collective-permute-start.18 = (f32[64]{0:T(128)S(1)}, f32[64]{0:T(128)S(1)}, u32[]{:S(2)}, u32[]{:S(2)}) collective-permute-start(f32[64]{0:T(128)S(1)} %add.112), channel_id=1, source_target_pairs={{0,4},{4,0},{8,12},{12,8},{1,5},{5,1},{9,13},{13,9},{2,6},{6,2},{1... | collective-permute-start | bytes 776 | tf_op jit(solution)/shard_map/ppermute | solution.py:385
